TPU v7x, 256 devices: a whole 4x4x8 slice. The times are simulated.
256 devices in a mesh: row: 8 (over x, core), col: 32 (over z, y).
Axes of the slice: x: 4, y: 4, z: 8, core: 2. Of those that a mesh axis runs over, the one named last changes fastest.
Arguments:
- ancestor_order: int32 [2, 48], replicated, may hold values from 0 to 47, each once within a row
- factor_rows: bfloat16 [2, 24576, 512], P(None, ('row', 'col')), may hold values from -0.0390625 to 0.0390625
- factor_inverse: bfloat16 [2, 512, 512], replicated
- ancestor_inverse: bfloat16 [24576, 24576], P('col', 'row'), may hold values from -6 to 6
- diagonal_inverse: float32 [2, 512, 512], P(None, None, 'row'), may hold values from -6 to 6
Outputs:
- offdiag_inverse: bfloat16 [2, 24576, 512], P(None, 'col', 'row')
- diag_updated: float32 [2, 512, 512], P(None, None, 'row')
Inputs may be any that keep to these rules, and one draw needn't show every extreme that they name: `ancestor_order`: each row lists every ancestor block once; its first 40 entries are the blocks coupled to that supernode.
All inputs are finite; a program needn't handle non-finite values.
Results may differ from a plain program's by a relative error of at most 0.011.
Values may be sent and summed in bfloat16 or wider, within the bound.
No kernel may reach another device: no remote copies, remote signals or barrier semaphores. Data moves between devices by JAX's collectives and lax.ppermute only.
A program may use at most 128 MiB of HBM per device.

v0:
```python
import jax
import jax.numpy as jnp
from jax import lax
from jax.sharding import Mesh
from jax.sharding import PartitionSpec as P

NSEL = 40
COL = ("col_0", "col_1")
ROW_COL = ("row", "col_0", "col_1")


def gathered_by_axis(array, axes, dim):
    result = array
    for number in range(len(axes) - 1, -1, -1):
        result = lax.all_gather(result, axes[number], axis=dim, tiled=True)
    return result


def from_root(array, axis, root):
    return lax.dynamic_index_in_dim(lax.all_gather(array, axis), root, 0, keepdims=False)


def split_up(array, dim, devices):
    dims = array.shape
    tiles = array.reshape(*dims[:dim], devices, dims[dim] // devices, *dims[dim + 1 :])
    return jnp.moveaxis(tiles, dim, 0)


def sum_at_owner(array, axis, dim):
    tiles = split_up(array, dim, lax.axis_size(axis))
    arrived = lax.all_to_all(tiles, axis, split_axis=0, concat_axis=0, tiled=True)
    return arrived.sum(axis=0)


def filled_up(lines, devices):
    spare = -len(lines) % devices
    return jnp.pad(lines, [(0, spare)] + [(0, 0)] * (lines.ndim - 1))


def reduced_to_own(tiles, axes, turns):
    dims = [lax.axis_size(a) for a in axes]
    tiles = tiles.reshape(*dims, *tiles.shape[1:])
    tiles = tiles.transpose(*turns, *range(len(axes), tiles.ndim))
    tiles = tiles.reshape(-1, *tiles.shape[len(axes) :])
    for k in turns:
        tiles = lax.psum_scatter(tiles, axes[k], scatter_dimension=0, tiled=True)
    return tiles[0]


def gather_in_order(array, axes, turns):
    tiles = array
    for k in turns:
        tiles = lax.all_gather(tiles, axes[k])
    done = turns[::-1]
    back = [done.index(k) for k in range(len(axes))]
    tiles = tiles.transpose(*back, *range(len(axes), tiles.ndim))
    return tiles.reshape(-1, *array.shape)


def sum_by_parts(array, axes, turns):
    devices, lines = (lax.axis_size(axes), array.reshape(-1, *array.shape[1:][-1:]))
    tiles = filled_up(lines, devices).reshape(devices, -1, *lines.shape[1:])
    own = reduced_to_own(tiles, axes, turns)
    whole = gather_in_order(own, axes, turns[::-1]).reshape(-1, *lines.shape[1:])
    return whole[: len(lines)].reshape(array.shape)


def process(listing, pieces, factor_inv, inverse_block, diag_inv):
    piece_rows = pieces.shape[1]
    block_width = pieces.shape[2]
    row_count = lax.axis_size("row")
    col_count = lax.axis_size(COL)
    row_index = lax.axis_index("row")
    col_index = lax.axis_index(COL)
    chosen = listing[:, :NSEL]
    first_row = (row_index * col_count + col_index) * piece_rows
    own_labels = (first_row + jnp.arange(piece_rows, dtype=jnp.int32)) // block_width
    own_keep = jnp.any(chosen[:, :, None] == own_labels[None, None, :], axis=1).astype(jnp.float32)
    normed = jnp.einsum("srk,skj->srj", pieces, factor_inv, preferred_element_type=jnp.float32)
    normed = (normed * own_keep[:, :, None]).astype(jnp.bfloat16)
    row_panel = gathered_by_axis(normed, COL, 1)
    column_rows = inverse_block.shape[0]
    per_row = col_count // row_count
    offset = col_index % per_row * column_rows
    column_part = lax.dynamic_slice_in_dim(row_panel, offset, column_rows, 1)
    columns = from_root(column_part, "row", col_index // per_row)
    partial_value = jnp.einsum(
        "pq,sqj->spj", inverse_block, row_panel, preferred_element_type=jnp.float32
    )
    lifted = columns.astype(jnp.float32)
    shares = sum_at_owner(partial_value, "row", 2)
    local_terms = jnp.einsum("spk,spj->skj", lifted, shares, precision=lax.Precision.HIGHEST)
    correction = sum_by_parts(local_terms.astype(jnp.bfloat16), COL, (0, 1)).astype(jnp.float32)
    col_labels = (col_index * column_rows + jnp.arange(column_rows, dtype=jnp.int32)) // block_width
    col_keep = jnp.any(chosen[:, :, None] == col_labels[None, None, :], axis=1).astype(jnp.float32)
    offdiag = (-(shares * col_keep[:, :, None])).astype(jnp.bfloat16)
    return (offdiag, diag_inv + correction)


def body(ancestor_order, factor_rows, factor_inverse, ancestor_inverse, diagonal_inverse):
    return process(ancestor_order, factor_rows, factor_inverse, ancestor_inverse, diagonal_inverse)


def solution(mesh):
    torus = Mesh(mesh.devices.reshape(mesh.shape["row"], 8, 4), ("row", "col_0", "col_1"))
    placed = (P(), P(None, ROW_COL, None), P(), P(COL, "row"), P(None, None, "row"))
    return jax.shard_map(
        body,
        mesh=torus,
        in_specs=placed,
        out_specs=(P(None, COL, "row"), P(None, None, "row")),
        check_vma=False,
    )
```

profile of v0, /device:TPU:6, one launch (start us, length us, event | category | flops | bytes accessed | tf_op | source)
XLA Modules:
  0.0 317.0 jit_solution(10247332286624158810)
XLA Ops:
  7.2 0.0 copy-start
  7.2 0.0 all-gather.5.cloned.1.call-start
  7.3 0.8 compare_reduce_fusion.1
  8.1 0.3 copy-done
  8.4 1.2 fusion.5
  9.6 14.6 %all_gather.21 = bf16[2,384,512]{2,1,0:T(8,128)(2,1)} all-gather(bf16[2,96,512]{2,1,0:T(8,128)(2,1)S(1)} %fusion.5), channel_id=1, replica_groups=mesh['row'=8,'col_0'=8,'col_1'=4] {'col_1'}, dimensions={1}, use_global_device_ids=true | all-gather | bytes 983040 | tf_op jit(solution)/shard_map/all_gather | solution.py:15
  24.2 0.0 all-gather.5.cloned.1.call-update
  24.2 0.0 all-gather.7.cloned.1.call-start
  24.3 77.5 %all-gather.5.cloned.1.call-done = bf16[2,3072,512]{2,1,0:T(8,128)(2,1)} async-done(((bf16[2,384,512]{2,1,0:T(8,128)(2,1)}), bf16[2,3072,512]{2,1,0:T(8,128)(2,1)}) %all-gather.5.cloned.1.call-update) | async-done | bytes 6291472 | tf_op jit(solution)/shard_map/all_gather | solution.py:15
  101.8 2.7 constant_dynamic-slice_fusion
  104.4 0.0 all-gather.7.cloned.1.call-update
  104.5 8.6 %fusion = f32[2,512,768]{2,1,0:T(8,128)S(1)} fusion(bf16[2,3072,512]{2,1,0:T(8,128)(2,1)} %all-gather.5.cloned.1.call-done, bf16[768,3072]{1,0:T(8,128)(2,1)} %param.8), kind=kOutput, calls=%fused_computation | convolution fusion | flops 4831838208 | bytes 14155776 | tf_op jit(solution)/shard_map/pq,sqj->spj/dot_general | solution.py:87
  113.1 1.9 copy.24
  115.1 4.9 %all-to-all-start = ((f32[8,2,768,64]{2,3,1,0:T(8,128)}), f32[8,2,768,64]{2,3,1,0:T(8,128)}, u32[]{:S(2)}, u32[]{:S(2)}) async-start(f32[8,2,768,64]{2,3,1,0:T(8,128)} %bitcast.25), calls=%async_computation | async-start | bytes 6291456 | tf_op jit(solution)/shard_map/all_to_all | solution.py:31
  120.0 0.0 reduce-scatter.3.cloned.1.call-start
  120.1 70.4 %all-to-all-done = f32[8,2,768,64]{2,3,1,0:T(8,128)} async-done(((f32[8,2,768,64]{2,3,1,0:T(8,128)}), f32[8,2,768,64]{2,3,1,0:T(8,128)}, u32[]{:S(2)}, u32[]{:S(2)}) %all-to-all-start) | async-done | bytes 3145760 | tf_op jit(solution)/shard_map/all_to_all | solution.py:31
  190.5 2.2 reduce_sum.9
  192.6 12.4 %all-gather.7.cloned.1.call-done = bf16[16,768,512]{2,1,0:T(8,128)(2,1)} async-done(((bf16[2,768,512]{2,1,0:T(8,128)(2,1)}), bf16[16,768,512]{2,1,0:T(8,128)(2,1)}) %all-gather.7.cloned.1.call-update) | async-done | bytes 12582928 | tf_op jit(solution)/shard_map/all_gather | solution.py:20
  205.1 2.3 fusion.6
  207.4 0.8 copy.19
  208.2 0.0 reduce-scatter.3.cloned.1.call-update
  208.3 0.0 reduce-scatter.5.cloned.1.call-start
  208.3 0.1 compare_reduce_fusion
  208.5 0.2 copy.20
  208.7 38.3 %reduce-scatter.3.cloned.1.call-done = bf16[4,32,64]{2,1,0:T(8,128)(2,1)} async-done(((bf16[32,32,64]{2,1,0:T(8,128)(2,1)}), bf16[4,32,64]{2,1,0:T(8,128)(2,1)}) %reduce-scatter.3.cloned.1.call-update) | async-done | bytes 16400 | tf_op jit(solution)/shard_map/reduce_scatter | solution.py:46
  247.0 0.0 reduce-scatter.5.cloned.1.call-update
  247.1 0.7 negate_convert_fusion
  247.8 23.3 %reduce-scatter.5.cloned.1.call-done = bf16[1,32,64]{2,1,0:T(8,128)(2,1)} async-done(((bf16[4,32,64]{2,1,0:T(8,128)(2,1)}), bf16[1,32,64]{2,1,0:T(8,128)(2,1)}) %reduce-scatter.5.cloned.1.call-update) | async-done | bytes 4112 | tf_op jit(solution)/shard_map/reduce_scatter | solution.py:46
  271.1 12.1 %all_gather.25 = bf16[4,32,64]{2,1,0:T(8,128)(2,1)S(1)} all-gather(bf16[1,32,64]{2,1,0:T(8,128)(2,1)} %reduce-scatter.5.cloned.1.call-done), channel_id=1, replica_groups=mesh['row'=8,'col_0'=8,'col_1'=4] {'col_1'}, dimensions={0}, use_global_device_ids=true | all-gather | bytes 20480 | tf_op jit(solution)/shard_map/all_gather | solution.py:53
  283.2 26.3 %all-gather.1 = bf16[32,32,64]{2,1,0:T(8,128)(2,1)S(1)} all-gather(bf16[4,32,64]{2,1,0:T(8,128)(2,1)S(1)} %all_gather.25), channel_id=3, replica_groups=mesh['row'=8,'col_0'=8,'col_1'=4] {'col_0'}, dimensions={0}, use_global_device_ids=true | all-gather | bytes 147456 | tf_op jit(solution)/shard_map/all_gather | solution.py:53
  309.5 0.1 convert_add_fusion
  309.6 0.9 copy.21
  (8 shorter events, 0.0 us)
Async XLA Ops:
  7.2 1.2 copy-start
  7.2 94.6 %all-gather.5.cloned.1.call-start = ((), (), s32[]{:S(2)}) async-start(), calls=%async_computation.3 | async-start | bytes 7077888 | tf_op jit(solution)/shard_map/all_gather | solution.py:15
  24.2 180.8 %all-gather.7.cloned.1.call-start = ((), (), s32[]{:S(2)}) async-start(), calls=%async_computation.6 | async-start | bytes 14155776 | tf_op jit(solution)/shard_map/all_gather | solution.py:20
  115.1 75.4 %all-to-all-start = ((f32[8,2,768,64]{2,3,1,0:T(8,128)}), f32[8,2,768,64]{2,3,1,0:T(8,128)}, u32[]{:S(2)}, u32[]{:S(2)}) async-start(f32[8,2,768,64]{2,3,1,0:T(8,128)} %bitcast.25), calls=%async_computation | async-start | bytes 6291456 | tf_op jit(solution)/shard_map/all_to_all | solution.py:31
  120.0 88.3 %copy-start.2 = (s32[2,48]{1,0:T(2,128)S(1)}, s32[2,48]{1,0:T(2,128)}, u32[]{:S(2)}) copy-start(s32[2,48]{1,0:T(2,128)} %param.5) | copy-start | bytes 1156
  120.0 88.5 %copy-start.1 = (f32[2,512,64]{1,2,0:T(8,128)S(1)}, f32[2,512,64]{1,2,0:T(8,128)}, u32[]{:S(2)}) copy-start(f32[2,512,64]{1,2,0:T(8,128)} %param.9) | copy-start | bytes 786436
  120.0 127.0 %reduce-scatter.3.cloned.1.call-start = ((), (), s32[]{:S(2)}) async-start(), calls=%async_computation.4 | async-start | bytes 294912 | tf_op jit(solution)/shard_map/reduce_scatter | solution.py:46
  208.3 62.9 %reduce-scatter.5.cloned.1.call-start = ((), (), s32[]{:S(2)}) async-start(), calls=%async_computation.5 | async-start | bytes 40960 | tf_op jit(solution)/shard_map/reduce_scatter | solution.py:46
Sparse Core Ops, SparseCore 0:
  24.4 77.3 all-gather.4
  104.6 100.4 all-gather.6
  208.4 38.5 reduce-scatter.2
  249.5 21.5 reduce-scatter.4
where the time goes:
time: 317 us
  waiting for transfers between devices  222 us (70%)
  blocking collectives  53 us (17%)
  between operations  13.9 us (4%)
  matrix products  12.2 us (4%)
  local copies, waits for them, and re-layouts  6.86 us (2%)
  starting transfers between devices  5.09 us (2%)
  other arithmetic  3.93 us (1%)
    all_gather x1, waiting for transfers between devices, gathered_by_axis(): result = lax.all_gather(result, axes[number], axis=dim, tiled=True)  77.5 us
    all_to_all x1, waiting for transfers between devices, sum_at_owner(): lax.all_to_all(tiles, axis, split_axis=0, concat_axis=0, tiled=True)  70.4 us
    reduce_scatter x2, waiting for transfers between devices, reduced_to_own(): tiles = lax.psum_scatter(tiles, axes[k], scatter_dimension=0, tiled=True)  61.7 us
    all_gather x2, blocking collectives, gather_in_order(): tiles = lax.all_gather(tiles, axes[k])  38.4 us
    all_gather x1, blocking collectives, gathered_by_axis(): result = lax.all_gather(result, axes[number], axis=dim, tiled=True)  14.6 us
    all_gather x1, waiting for transfers between devices, from_root(): lax.all_gather(array, axis)  12.4 us
    dot_general x1, matrix products, process(): jnp.einsum('pq,sqj->spj', inverse_block, row_panel, preferred_element_typ...  8.63 us
  transfers between devices with their start and end apart: 5, of which 5 were waited for; matrix products, arithmetic and copies ran while one was open for 4% of the time, Pallas kernels for 0%

commit v1 on v0

v1 whole, which is shorter than its diff:
```python
import jax
import jax.numpy as jnp
from jax import lax
from jax.sharding import Mesh
from jax.sharding import PartitionSpec as P

NSEL = 40
XS, CORES, ZS, YS = 4, 2, 8, 4
ROW = ("x", "core")
COL = ("z", "y")
ALL = ("x", "core", "z", "y")
F32 = jnp.float32
BF16 = jnp.bfloat16


def shift(array, axis, size, by):
    return lax.ppermute(array, axis, [(i, (i + by) % size) for i in range(size)])


def direct_ring(array, axis, size):
    return [array] + [shift(array, axis, size, d if d <= size // 2 else d - size) for d in range(1, size)]


def relay_ring(array, axis, size, halved):
    got = [array] + [None] * (size - 1)
    right = left = array
    for step in range(1, size // 2):
        right = shift(right, axis, size, 1)
        left = shift(left, axis, size, -1)
        got[step], got[size - step] = right, left
    if halved:
        half = array.shape[0] // 2
        got[size // 2] = jnp.concatenate(
            [shift(right[:half], axis, size, 1), shift(left[half:], axis, size, -1)], axis=0
        )
    else:
        got[size // 2] = shift(right, axis, size, 1)
    return got


def placed_by_owner(got, own, axis):
    size, width = len(got), got[0].shape[axis]
    dims = list(got[0].shape)
    dims[axis] *= size
    whole = jnp.zeros(dims, got[0].dtype)
    for d, chunk in enumerate(got):
        whole = lax.dynamic_update_slice_in_dim(whole, chunk, (own - d) % size * width, axis)
    return whole


def panel_y_then_z(piece):
    part = placed_by_owner(direct_ring(piece, "y", YS), lax.axis_index("y"), 0)
    return lax.all_gather(part, "z", axis=0, tiled=True)


def panel_z_then_y(piece):
    part = placed_by_owner(relay_ring(piece[None], "z", ZS, False), lax.axis_index("z"), 0)
    whole = placed_by_owner(
        [g[:, None] for g in relay_ring(part, "y", YS, True)], lax.axis_index("y"), 1
    )
    return whole.reshape(-1, piece.shape[-1])


def sum_over_row(tiles):
    x, core = lax.axis_index("x"), lax.axis_index("core")
    kept = lax.dynamic_index_in_dim(tiles, core, 1, keepdims=False)
    given = lax.dynamic_index_in_dim(tiles, 1 - core, 1, keepdims=False)
    pair = kept.astype(F32) + lax.ppermute(given, "core", [(0, 1), (1, 0)]).astype(F32)
    pair = lax.optimization_barrier(pair.astype(BF16))
    tile = lambda k: lax.dynamic_index_in_dim(pair, (x + k) % XS, 0, keepdims=False)
    far = tile(2)
    opposite = jnp.stack([shift(far[0], "x", XS, 2), shift(far[1], "x", XS, -2)])
    near = shift(tile(1), "x", XS, 1).astype(F32) + shift(tile(3), "x", XS, -1).astype(F32)
    return (tile(0).astype(F32) + opposite.astype(F32)) + near


def summed_by_pairs(array, axis, size):
    other = lambda k: lax.ppermute(array, axis, [(i, i ^ k) for i in range(size)]).astype(F32)
    total = array.astype(F32) + other(1)
    if size == 4:
        total = total + (other(2) + other(3))
    return lax.optimization_barrier(total.astype(BF16))


SWAP = [
    ((a * ZS + b) * YS + y, (b * ZS + a) * YS + y)
    for a in range(XS * CORES)
    for b in range(ZS)
    for y in range(YS)
]


def body(listing, pieces, factor_inv, inverse_block, diag_inv):
    piece_rows, width = pieces.shape[1:]
    row = lax.axis_index(ROW)
    col = lax.axis_index(COL)
    y = lax.axis_index("y")
    chosen = listing[:, :NSEL]

    def keep_of(first, count):
        labels = (first + jnp.arange(count, dtype=jnp.int32)) // width
        return jnp.any(chosen[:, :, None] == labels[None, None, :], axis=1).astype(F32)

    own_keep = keep_of((row * ZS * YS + col) * piece_rows, piece_rows)
    normed = jnp.einsum("srk,skj->srj", pieces, factor_inv, preferred_element_type=F32)
    normed = (normed * own_keep[:, :, None]).astype(BF16)
    panels = [panel_y_then_z(normed[0]), panel_z_then_y(normed[1])]

    rows = inverse_block.shape[0]
    slab = width // (XS * CORES)
    partial = [
        jnp.einsum("qj,pq->jp", panel, inverse_block, preferred_element_type=F32)
        .astype(BF16)
        .reshape(XS, CORES, 1, slab, rows)
        for panel in panels
    ]
    product = sum_over_row(jnp.concatenate(partial, axis=2))
    col_keep = keep_of(col * rows, rows)
    offdiag = (-(product * col_keep[:, None, :])).astype(BF16)

    turned = lax.ppermute(offdiag, ALL, SWAP)
    own_slabs = [lax.dynamic_slice_in_dim(panel, y * rows, rows, 0) for panel in panels]
    terms = jnp.stack(
        [-jnp.dot(turned[s], own_slabs[s], preferred_element_type=F32) for s in range(len(panels))]
    ).astype(BF16)
    for axis, size in (("core", CORES), ("y", YS), ("x", XS)):
        terms = summed_by_pairs(terms, axis, size)
    correction = lax.ppermute(terms, ALL, SWAP).astype(F32)
    return offdiag.transpose(0, 2, 1), diag_inv + correction.transpose(0, 2, 1)


def solution(mesh):
    torus = Mesh(mesh.devices.reshape(XS, CORES, ZS, YS), ALL)
    return jax.shard_map(
        body,
        mesh=torus,
        in_specs=(P(), P(None, ALL, None), P(), P(COL, ROW), P(None, None, ROW)),
        out_specs=(P(None, COL, ROW), P(None, None, ROW)),
        check_vma=False,
    )
```

time: 317 us -> 174 us (0.55)
  the two profiles are of different devices: /device:TPU:6 before, /device:TPU:7 now
where the time goes in v1:
time: 174 us; the launch traced here: 173 us
  waiting for transfers between devices  84.3 us (48%)
  starting transfers between devices  53.5 us (31%)
  matrix products  15 us (9%)
  between operations  14.5 us (8%)
  local copies, waits for them, and re-layouts  3.69 us (2%)
  other arithmetic  2.43 us (1%)
    ppermute x18, waiting for transfers between devices, shift(): lax.ppermute(array, axis, [(i, (i + by) % size) for i in range(size)])  41.9 us
    ppermute x18, starting transfers between devices, shift(): lax.ppermute(array, axis, [(i, (i + by) % size) for i in range(size)])  26.7 us
    ppermute x7, waiting for transfers between devices, summed_by_pairs(): lax.ppermute(array, axis, [(i, i ^ k) for i in range(size)]).astype(F32)  16.4 us
    ppermute x1, waiting for transfers between devices, body(): turned = lax.ppermute(offdiag, ALL, SWAP)  14.9 us
    dot_general x2, matrix products, body(): jnp.einsum('qj,pq->jp', panel, inverse_block, preferred_element_type=F32)  11 us
    ppermute x1, starting transfers between devices, sum_over_row(): lax.ppermute(given, 'core', [(0, 1), (1, 0)]).astype(F32)  9.4 us
    ppermute x1, waiting for transfers between devices, body(): correction = lax.ppermute(terms, ALL, SWAP).astype(F32)  9.16 us
    ppermute x7, starting transfers between devices, summed_by_pairs(): lax.ppermute(array, axis, [(i, i ^ k) for i in range(size)]).astype(F32)  8.54 us
  transfers between devices with their start and end apart: 29, of which 19 were waited for; matrix products, arithmetic and copies ran while one was open for 3% of the time, Pallas kernels for 0%

profile of v1, /device:TPU:7, one launch (start us, length us, event | category | flops | bytes accessed | tf_op | source)
XLA Modules:
  0.0 173.4 jit_solution(17273010654180611636)
XLA Ops:
  11.1 2.6 %collective-permute-start.1 = (bf16[96,512]{1,0:T(8,128)(2,1)S(1)}, bf16[96,512]{1,0:T(8,128)(2,1)S(1)}, u32[]{:S(2)}, u32[]{:S(2)}) collective-permute-start(bf16[96,512]{1,0:T(8,128)(2,1)S(1)} %get-tuple-element.10), channel_id=1, source_target_pairs={{0,2},{1,3},{2,0},{3,1},{4,6},{5,7},{6,4},{7,5},{8,10},{9,11},{10,... | collective-permute-start | bytes 294920 | tf_op jit(solution)/shard_map/ppermute | solution.py:17
  15.0 2.8 %collective-permute-done.1 = bf16[96,512]{1,0:T(8,128)(2,1)S(1)} collective-permute-done((bf16[96,512]{1,0:T(8,128)(2,1)S(1)}, bf16[96,512]{1,0:T(8,128)(2,1)S(1)}, u32[]{:S(2)}, u32[]{:S(2)}) %collective-permute-start.1) | collective-permute-done | bytes 98336 | tf_op jit(solution)/shard_map/ppermute | solution.py:17
  18.6 1.7 collective-permute-start.3
  20.3 4.0 %collective-permute-start.7 = (bf16[1,96,512]{2,1,0:T(8,128)(2,1)S(1)}, bf16[1,96,512]{2,1,0:T(8,128)(2,1)S(1)}, u32[]{:S(2)}, u32[]{:S(2)}) collective-permute-start(bf16[1,96,512]{2,1,0:T(8,128)(2,1)S(1)} %get-tuple-element.8), channel_id=1, source_target_pairs={{0,28},{4,0},{8,4},{12,8},{16,12},{20,16},{24,20},{28,24},{1,29},{... | collective-permute-start | bytes 294920 | tf_op jit(solution)/shard_map/ppermute | solution.py:17
  24.3 1.9 %collective-permute-done.3 = bf16[1,96,512]{2,1,0:T(8,128)(2,1)S(1)} collective-permute-done((bf16[1,96,512]{2,1,0:T(8,128)(2,1)S(1)}, bf16[1,96,512]{2,1,0:T(8,128)(2,1)S(1)}, u32[]{:S(2)}, u32[]{:S(2)}) %collective-permute-start.3) | collective-permute-done | bytes 98336 | tf_op jit(solution)/shard_map/ppermute | solution.py:17
  26.2 2.8 %collective-permute-start.8 = (bf16[1,96,512]{2,1,0:T(8,128)(2,1)S(1)}, bf16[1,96,512]{2,1,0:T(8,128)(2,1)S(1)}, u32[]{:S(2)}, u32[]{:S(2)}) collective-permute-start(bf16[1,96,512]{2,1,0:T(8,128)(2,1)S(1)} %collective-permute-done.7), channel_id=1, source_target_pairs={{0,28},{4,0},{8,4},{12,8},{16,12},{20,16},{24,20},{28,24},{1,29},{... | collective-permute-start | bytes 294920 | tf_op jit(solution)/shard_map/ppermute | solution.py:17
  29.0 1.9 %collective-permute-done.4 = bf16[1,96,512]{2,1,0:T(8,128)(2,1)S(1)} collective-permute-done((bf16[1,96,512]{2,1,0:T(8,128)(2,1)S(1)}, bf16[1,96,512]{2,1,0:T(8,128)(2,1)S(1)}, u32[]{:S(2)}, u32[]{:S(2)}) %collective-permute-start.4) | collective-permute-done | bytes 98336 | tf_op jit(solution)/shard_map/ppermute | solution.py:17
  30.9 2.8 %collective-permute-start.9 = (bf16[1,96,512]{2,1,0:T(8,128)(2,1)S(1)}, bf16[1,96,512]{2,1,0:T(8,128)(2,1)S(1)}, u32[]{:S(2)}, u32[]{:S(2)}) collective-permute-start(bf16[1,96,512]{2,1,0:T(8,128)(2,1)S(1)} %collective-permute-done.8), channel_id=1, source_target_pairs={{0,28},{4,0},{8,4},{12,8},{16,12},{20,16},{24,20},{28,24},{1,29},{... | collective-permute-start | bytes 294920 | tf_op jit(solution)/shard_map/ppermute | solution.py:17
  33.7 1.9 %collective-permute-done.5 = bf16[1,96,512]{2,1,0:T(8,128)(2,1)S(1)} collective-permute-done((bf16[1,96,512]{2,1,0:T(8,128)(2,1)S(1)}, bf16[1,96,512]{2,1,0:T(8,128)(2,1)S(1)}, u32[]{:S(2)}, u32[]{:S(2)}) %collective-permute-start.5) | collective-permute-done | bytes 98336 | tf_op jit(solution)/shard_map/ppermute | solution.py:17
  35.6 8.0 %collective-permute-done.6 = bf16[1,96,512]{2,1,0:T(8,128)(2,1)S(1)} collective-permute-done((bf16[1,96,512]{2,1,0:T(8,128)(2,1)S(1)}, bf16[1,96,512]{2,1,0:T(8,128)(2,1)S(1)}, u32[]{:S(2)}, u32[]{:S(2)}) %collective-permute-start.6) | collective-permute-done | bytes 98336 | tf_op jit(solution)/shard_map/ppermute | solution.py:17
  44.4 2.1 %collective-permute-start.12 = (bf16[8,96,512]{2,1,0:T(8,128)(2,1)S(1)}, bf16[8,96,512]{2,1,0:T(8,128)(2,1)S(1)}, u32[]{:S(2)}, u32[]{:S(2)}) collective-permute-start(bf16[8,96,512]{2,1,0:T(8,128)(2,1)S(1)} %constant_dynamic-update-slice_fusion), channel_id=1, source_target_pairs={{0,3},{1,0},{2,1},{3,2},{4,7},{5,4},{6,5},{7,6},{8,11},{9,8},{10,9... | collective-permute-start | bytes 2359304 | tf_op jit(solution)/shard_map/ppermute | solution.py:17
  46.5 9.9 %collective-permute-done.10 = bf16[8,96,512]{2,1,0:T(8,128)(2,1)S(1)} collective-permute-done((bf16[8,96,512]{2,1,0:T(8,128)(2,1)S(1)}, bf16[8,96,512]{2,1,0:T(8,128)(2,1)S(1)}, u32[]{:S(2)}, u32[]{:S(2)}) %collective-permute-start.10) | collective-permute-done | bytes 786464 | tf_op jit(solution)/shard_map/ppermute | solution.py:17
  56.5 2.9 %collective-permute-start.13 = (bf16[4,96,512]{2,1,0:T(8,128)(2,1)S(1)}, bf16[4,96,512]{2,1,0:T(8,128)(2,1)S(1)}, u32[]{:S(2)}, u32[]{:S(2)}) collective-permute-start(bf16[4,96,512]{2,1,0:T(8,128)(2,1)S(1)} %slice.41), channel_id=1, source_target_pairs={{0,3},{1,0},{2,1},{3,2},{4,7},{5,4},{6,5},{7,6},{8,11},{9,8},{10,9... | collective-permute-start | bytes 1179656 | tf_op jit(solution)/shard_map/ppermute | solution.py:17
  59.9 9.0 %collective-permute-done.11 = bf16[4,96,512]{2,1,0:T(8,128)(2,1)S(1)} collective-permute-done((bf16[4,96,512]{2,1,0:T(8,128)(2,1)S(1)}, bf16[4,96,512]{2,1,0:T(8,128)(2,1)S(1)}, u32[]{:S(2)}, u32[]{:S(2)}) %collective-permute-start.11) | collective-permute-done | bytes 393248 | tf_op jit(solution)/shard_map/ppermute | solution.py:17
  69.1 1.7 copy-done.1
  70.8 5.1 %convolution_convert_fusion = bf16[512,768]{1,0:T(8,128)(2,1)S(1)} fusion(bf16[3072,512]{1,0:T(8,128)(2,1)S(1)} %bitcast.64, bf16[768,3072]{1,0:T(8,128)(2,1)} %param.8), kind=kOutput, calls=%fused_computation.6 | convolution fusion | flops 2416312320 | bytes 8650752 | tf_op jit(solution)/shard_map/qj,pq->jp/dot_general | solution.py:112
  75.8 6.0 %convolution_convert_fusion.1 = bf16[512,768]{1,0:T(8,128)(2,1)S(1)} fusion(bf16[3072,512]{1,0:T(8,128)(2,1)} %all-gather.2.cloned.1.call-done, bf16[768,3072]{1,0:T(8,128)(2,1)} %param.8), kind=kOutput, calls=%fused_computation.7 | convolution fusion | flops 2416312320 | bytes 8650752 | tf_op jit(solution)/shard_map/qj,pq->jp/dot_general | solution.py:112
  82.0 9.4 %collective-permute-start.14 = (bf16[4,2,64,768]{3,2,1,0:T(8,128)(2,1)S(1)}, bf16[4,2,64,768]{3,2,1,0:T(8,128)(2,1)S(1)}, u32[]{:S(2)}, u32[]{:S(2)}) collective-permute-start(bf16[4,2,64,768]{3,2,1,0:T(8,128)(2,1)S(1)} %bitcast.66), channel_id=1, source_target_pairs={{0,32},{32,0},{1,33},{33,1},{2,34},{34,2},{3,35},{35,3},{4,36},{36... | collective-permute-start | bytes 2359304 | tf_op jit(solution)/shard_map/ppermute | solution.py:68
  91.4 1.9 %collective-permute-done.14 = bf16[4,2,64,768]{3,2,1,0:T(8,128)(2,1)S(1)} collective-permute-done((bf16[4,2,64,768]{3,2,1,0:T(8,128)(2,1)S(1)}, bf16[4,2,64,768]{3,2,1,0:T(8,128)(2,1)S(1)}, u32[]{:S(2)}, u32[]{:S(2)}) %collective-permute-start.14) | collective-permute-done | bytes 786464 | tf_op jit(solution)/shard_map/ppermute | solution.py:68
  96.3 1.9 %collective-permute-start.16 = (bf16[64,768]{1,0:T(8,128)(2,1)S(1)}, bf16[64,768]{1,0:T(8,128)(2,1)S(1)}, u32[]{:S(2)}, u32[]{:S(2)}) collective-permute-start(bf16[64,768]{1,0:T(8,128)(2,1)S(1)} %get-tuple-element.5), channel_id=1, source_target_pairs={{0,128},{64,192},{128,0},{192,64},{1,129},{65,193},{129,1},{193,65... | collective-permute-start | bytes 294920 | tf_op jit(solution)/shard_map/ppermute | solution.py:17
  98.3 4.0 %collective-permute-done.15 = bf16[64,768]{1,0:T(8,128)(2,1)S(1)} collective-permute-done((bf16[64,768]{1,0:T(8,128)(2,1)S(1)}, bf16[64,768]{1,0:T(8,128)(2,1)S(1)}, u32[]{:S(2)}, u32[]{:S(2)}) %collective-permute-start.15) | collective-permute-done | bytes 98336 | tf_op jit(solution)/shard_map/ppermute | solution.py:17
  102.4 2.4 %collective-permute-done.16 = bf16[64,768]{1,0:T(8,128)(2,1)S(1)} collective-permute-done((bf16[64,768]{1,0:T(8,128)(2,1)S(1)}, bf16[64,768]{1,0:T(8,128)(2,1)S(1)}, u32[]{:S(2)}, u32[]{:S(2)}) %collective-permute-start.16) | collective-permute-done | bytes 98336 | tf_op jit(solution)/shard_map/ppermute | solution.py:17
  104.9 3.5 %collective-permute-start.19 = (bf16[2,64,768]{2,1,0:T(8,128)(2,1)S(1)}, bf16[2,64,768]{2,1,0:T(8,128)(2,1)S(1)}, u32[]{:S(2)}, u32[]{:S(2)}) collective-permute-start(bf16[2,64,768]{2,1,0:T(8,128)(2,1)S(1)} %fusion.14), channel_id=1, source_target_pairs={{0,0},{1,1},{2,2},{3,3},{4,32},{5,33},{6,34},{7,35},{8,64},{9,65},... | collective-permute-start | bytes 589832 | tf_op jit(solution)/shard_map/ppermute | solution.py:121
  108.5 14.9 %collective-permute-done.19 = bf16[2,64,768]{2,1,0:T(8,128)(2,1)S(1)} collective-permute-done((bf16[2,64,768]{2,1,0:T(8,128)(2,1)S(1)}, bf16[2,64,768]{2,1,0:T(8,128)(2,1)S(1)}, u32[]{:S(2)}, u32[]{:S(2)}) %collective-permute-start.19) | collective-permute-done | bytes 196640 | tf_op jit(solution)/shard_map/ppermute | solution.py:121
  128.1 4.1 %collective-permute-start.22 = (bf16[2,64,512]{2,1,0:T(8,128)(2,1)S(1)}, bf16[2,64,512]{2,1,0:T(8,128)(2,1)S(1)}, u32[]{:S(2)}, u32[]{:S(2)}) collective-permute-start(bf16[2,64,512]{2,1,0:T(8,128)(2,1)S(1)} %add_convert_fusion.2), channel_id=1, source_target_pairs={{0,2},{1,3},{2,0},{3,1},{4,6},{5,7},{6,4},{7,5},{8,10},{9,11},{10,... | collective-permute-start | bytes 393224 | tf_op jit(solution)/shard_map/ppermute | solution.py:78
  132.7 5.8 %collective-permute-done.22 = bf16[2,64,512]{2,1,0:T(8,128)(2,1)S(1)} collective-permute-done((bf16[2,64,512]{2,1,0:T(8,128)(2,1)S(1)}, bf16[2,64,512]{2,1,0:T(8,128)(2,1)S(1)}, u32[]{:S(2)}, u32[]{:S(2)}) %collective-permute-start.22) | collective-permute-done | bytes 131104 | tf_op jit(solution)/shard_map/ppermute | solution.py:78
  138.5 2.5 %collective-permute-done.23 = bf16[2,64,512]{2,1,0:T(8,128)(2,1)S(1)} collective-permute-done((bf16[2,64,512]{2,1,0:T(8,128)(2,1)S(1)}, bf16[2,64,512]{2,1,0:T(8,128)(2,1)S(1)}, u32[]{:S(2)}, u32[]{:S(2)}) %collective-permute-start.23) | collective-permute-done | bytes 131104 | tf_op jit(solution)/shard_map/ppermute | solution.py:78
  142.1 3.0 %collective-permute-start.26 = (bf16[2,64,512]{2,1,0:T(8,128)(2,1)S(1)}, bf16[2,64,512]{2,1,0:T(8,128)(2,1)S(1)}, u32[]{:S(2)}, u32[]{:S(2)}) collective-permute-start(bf16[2,64,512]{2,1,0:T(8,128)(2,1)S(1)} %add_convert_fusion.1), channel_id=1, source_target_pairs={{0,192},{64,128},{128,64},{192,0},{1,193},{65,129},{129,65},{193,1... | collective-permute-start | bytes 393224 | tf_op jit(solution)/shard_map/ppermute | solution.py:78
  145.3 2.7 %collective-permute-done.25 = bf16[2,64,512]{2,1,0:T(8,128)(2,1)S(1)} collective-permute-done((bf16[2,64,512]{2,1,0:T(8,128)(2,1)S(1)}, bf16[2,64,512]{2,1,0:T(8,128)(2,1)S(1)}, u32[]{:S(2)}, u32[]{:S(2)}) %collective-permute-start.25) | collective-permute-done | bytes 131104 | tf_op jit(solution)/shard_map/ppermute | solution.py:78
  148.0 3.3 %collective-permute-done.26 = bf16[2,64,512]{2,1,0:T(8,128)(2,1)S(1)} collective-permute-done((bf16[2,64,512]{2,1,0:T(8,128)(2,1)S(1)}, bf16[2,64,512]{2,1,0:T(8,128)(2,1)S(1)}, u32[]{:S(2)}, u32[]{:S(2)}) %collective-permute-start.26) | collective-permute-done | bytes 131104 | tf_op jit(solution)/shard_map/ppermute | solution.py:78
  151.4 5.3 %collective-permute-start.27 = (bf16[2,64,512]{2,1,0:T(8,128)(2,1)S(1)}, bf16[2,64,512]{2,1,0:T(8,128)(2,1)S(1)}, u32[]{:S(2)}, u32[]{:S(2)}) collective-permute-start(bf16[2,64,512]{2,1,0:T(8,128)(2,1)S(1)} %add_convert_fusion), channel_id=1, source_target_pairs={{0,0},{1,1},{2,2},{3,3},{4,32},{5,33},{6,34},{7,35},{8,64},{9,65},... | collective-permute-start | bytes 393224 | tf_op jit(solution)/shard_map/ppermute | solution.py:128
  156.7 9.2 %collective-permute-done.27 = bf16[2,64,512]{2,1,0:T(8,128)(2,1)S(1)} collective-permute-done((bf16[2,64,512]{2,1,0:T(8,128)(2,1)S(1)}, bf16[2,64,512]{2,1,0:T(8,128)(2,1)S(1)}, u32[]{:S(2)}, u32[]{:S(2)}) %collective-permute-start.27) | collective-permute-done | bytes 131104 | tf_op jit(solution)/shard_map/ppermute | solution.py:128
  (82 shorter events, 18.1 us)
Async XLA Ops:
  7.2 68.7 %all-gather.2.cloned.1.call-start = ((), (), s32[]{:S(2)}) async-start(), calls=%async_computation | async-start | bytes 3538944 | tf_op jit(solution)/shard_map/all_gather | solution.py:53
  9.7 5.2 %collective-permute-start = (bf16[96,512]{1,0:T(8,128)(2,1)S(1)}, bf16[96,512]{1,0:T(8,128)(2,1)S(1)}, u32[]{:S(2)}, u32[]{:S(2)}) collective-permute-start(bf16[96,512]{1,0:T(8,128)(2,1)S(1)} %get-tuple-element.10), channel_id=1, source_target_pairs={{0,1},{1,2},{2,3},{3,0},{4,5},{5,6},{6,7},{7,4},{8,9},{9,10},{10,1... | collective-permute-start | bytes 294920 | tf_op jit(solution)/shard_map/ppermute | solution.py:17
  11.1 6.6 %collective-permute-start.1 = (bf16[96,512]{1,0:T(8,128)(2,1)S(1)}, bf16[96,512]{1,0:T(8,128)(2,1)S(1)}, u32[]{:S(2)}, u32[]{:S(2)}) collective-permute-start(bf16[96,512]{1,0:T(8,128)(2,1)S(1)} %get-tuple-element.10), channel_id=1, source_target_pairs={{0,2},{1,3},{2,0},{3,1},{4,6},{5,7},{6,4},{7,5},{8,10},{9,11},{10,... | collective-permute-start | bytes 294920 | tf_op jit(solution)/shard_map/ppermute | solution.py:17
  13.7 4.0 %collective-permute-start.2 = (bf16[96,512]{1,0:T(8,128)(2,1)S(1)}, bf16[96,512]{1,0:T(8,128)(2,1)S(1)}, u32[]{:S(2)}, u32[]{:S(2)}) collective-permute-start(bf16[96,512]{1,0:T(8,128)(2,1)S(1)} %get-tuple-element.10), channel_id=1, source_target_pairs={{0,3},{1,0},{2,1},{3,2},{4,7},{5,4},{6,5},{7,6},{8,11},{9,8},{10,9... | collective-permute-start | bytes 294920 | tf_op jit(solution)/shard_map/ppermute | solution.py:17
  18.6 7.7 %collective-permute-start.3 = (bf16[1,96,512]{2,1,0:T(8,128)(2,1)S(1)}, bf16[1,96,512]{2,1,0:T(8,128)(2,1)S(1)}, u32[]{:S(2)}, u32[]{:S(2)}) collective-permute-start(bf16[1,96,512]{2,1,0:T(8,128)(2,1)S(1)} %get-tuple-element.8), channel_id=1, source_target_pairs={{0,4},{4,8},{8,12},{12,16},{16,20},{20,24},{24,28},{28,0},{1,5},{5... | collective-permute-start | bytes 294920 | tf_op jit(solution)/shard_map/ppermute | solution.py:17
  20.3 5.9 %collective-permute-start.7 = (bf16[1,96,512]{2,1,0:T(8,128)(2,1)S(1)}, bf16[1,96,512]{2,1,0:T(8,128)(2,1)S(1)}, u32[]{:S(2)}, u32[]{:S(2)}) collective-permute-start(bf16[1,96,512]{2,1,0:T(8,128)(2,1)S(1)} %get-tuple-element.8), channel_id=1, source_target_pairs={{0,28},{4,0},{8,4},{12,8},{16,12},{20,16},{24,20},{28,24},{1,29},{... | collective-permute-start | bytes 294920 | tf_op jit(solution)/shard_map/ppermute | solution.py:17
  26.2 4.7 %collective-permute-start.4 = (bf16[1,96,512]{2,1,0:T(8,128)(2,1)S(1)}, bf16[1,96,512]{2,1,0:T(8,128)(2,1)S(1)}, u32[]{:S(2)}, u32[]{:S(2)}) collective-permute-start(bf16[1,96,512]{2,1,0:T(8,128)(2,1)S(1)} %collective-permute-done.3), channel_id=1, source_target_pairs={{0,4},{4,8},{8,12},{12,16},{16,20},{20,24},{24,28},{28,0},{1,5},{5... | collective-permute-start | bytes 294920 | tf_op jit(solution)/shard_map/ppermute | solution.py:17
  26.2 4.7 %collective-permute-start.8 = (bf16[1,96,512]{2,1,0:T(8,128)(2,1)S(1)}, bf16[1,96,512]{2,1,0:T(8,128)(2,1)S(1)}, u32[]{:S(2)}, u32[]{:S(2)}) collective-permute-start(bf16[1,96,512]{2,1,0:T(8,128)(2,1)S(1)} %collective-permute-done.7), channel_id=1, source_target_pairs={{0,28},{4,0},{8,4},{12,8},{16,12},{20,16},{24,20},{28,24},{1,29},{... | collective-permute-start | bytes 294920 | tf_op jit(solution)/shard_map/ppermute | solution.py:17
  30.9 4.7 %collective-permute-start.5 = (bf16[1,96,512]{2,1,0:T(8,128)(2,1)S(1)}, bf16[1,96,512]{2,1,0:T(8,128)(2,1)S(1)}, u32[]{:S(2)}, u32[]{:S(2)}) collective-permute-start(bf16[1,96,512]{2,1,0:T(8,128)(2,1)S(1)} %collective-permute-done.4), channel_id=1, source_target_pairs={{0,4},{4,8},{8,12},{12,16},{16,20},{20,24},{24,28},{28,0},{1,5},{5... | collective-permute-start | bytes 294920 | tf_op jit(solution)/shard_map/ppermute | solution.py:17
  30.9 12.8 %collective-permute-start.9 = (bf16[1,96,512]{2,1,0:T(8,128)(2,1)S(1)}, bf16[1,96,512]{2,1,0:T(8,128)(2,1)S(1)}, u32[]{:S(2)}, u32[]{:S(2)}) collective-permute-start(bf16[1,96,512]{2,1,0:T(8,128)(2,1)S(1)} %collective-permute-done.8), channel_id=1, source_target_pairs={{0,28},{4,0},{8,4},{12,8},{16,12},{20,16},{24,20},{28,24},{1,29},{... | collective-permute-start | bytes 294920 | tf_op jit(solution)/shard_map/ppermute | solution.py:17
  35.6 8.1 %collective-permute-start.6 = (bf16[1,96,512]{2,1,0:T(8,128)(2,1)S(1)}, bf16[1,96,512]{2,1,0:T(8,128)(2,1)S(1)}, u32[]{:S(2)}, u32[]{:S(2)}) collective-permute-start(bf16[1,96,512]{2,1,0:T(8,128)(2,1)S(1)} %collective-permute-done.5), channel_id=1, source_target_pairs={{0,4},{4,8},{8,12},{12,16},{16,20},{20,24},{24,28},{28,0},{1,5},{5... | collective-permute-start | bytes 294920 | tf_op jit(solution)/shard_map/ppermute | solution.py:17
  43.8 12.6 %collective-permute-start.10 = (bf16[8,96,512]{2,1,0:T(8,128)(2,1)S(1)}, bf16[8,96,512]{2,1,0:T(8,128)(2,1)S(1)}, u32[]{:S(2)}, u32[]{:S(2)}) collective-permute-start(bf16[8,96,512]{2,1,0:T(8,128)(2,1)S(1)} %constant_dynamic-update-slice_fusion), channel_id=1, source_target_pairs={{0,1},{1,2},{2,3},{3,0},{4,5},{5,6},{6,7},{7,4},{8,9},{9,10},{10,1... | collective-permute-start | bytes 2359304 | tf_op jit(solution)/shard_map/ppermute | solution.py:17
  44.4 12.1 %collective-permute-start.12 = (bf16[8,96,512]{2,1,0:T(8,128)(2,1)S(1)}, bf16[8,96,512]{2,1,0:T(8,128)(2,1)S(1)}, u32[]{:S(2)}, u32[]{:S(2)}) collective-permute-start(bf16[8,96,512]{2,1,0:T(8,128)(2,1)S(1)} %constant_dynamic-update-slice_fusion), channel_id=1, source_target_pairs={{0,3},{1,0},{2,1},{3,2},{4,7},{5,4},{6,5},{7,6},{8,11},{9,8},{10,9... | collective-permute-start | bytes 2359304 | tf_op jit(solution)/shard_map/ppermute | solution.py:17
  56.4 12.5 %collective-permute-start.11 = (bf16[4,96,512]{2,1,0:T(8,128)(2,1)S(1)}, bf16[4,96,512]{2,1,0:T(8,128)(2,1)S(1)}, u32[]{:S(2)}, u32[]{:S(2)}) collective-permute-start(bf16[4,96,512]{2,1,0:T(8,128)(2,1)S(1)} %slice.40), channel_id=1, source_target_pairs={{0,1},{1,2},{2,3},{3,0},{4,5},{5,6},{6,7},{7,4},{8,9},{9,10},{10,1... | collective-permute-start | bytes 1179656 | tf_op jit(solution)/shard_map/ppermute | solution.py:17
  56.5 12.4 %collective-permute-start.13 = (bf16[4,96,512]{2,1,0:T(8,128)(2,1)S(1)}, bf16[4,96,512]{2,1,0:T(8,128)(2,1)S(1)}, u32[]{:S(2)}, u32[]{:S(2)}) collective-permute-start(bf16[4,96,512]{2,1,0:T(8,128)(2,1)S(1)} %slice.41), channel_id=1, source_target_pairs={{0,3},{1,0},{2,1},{3,2},{4,7},{5,4},{6,5},{7,6},{8,11},{9,8},{10,9... | collective-permute-start | bytes 1179656 | tf_op jit(solution)/shard_map/ppermute | solution.py:17
  82.0 16.2 %copy-start.5 = (s32[2,48]{1,0:T(2,128)S(1)}, s32[2,48]{1,0:T(2,128)}, u32[]{:S(2)}) copy-start(s32[2,48]{1,0:T(2,128)} %param.5) | copy-start | bytes 1156
  82.0 11.3 %collective-permute-start.14 = (bf16[4,2,64,768]{3,2,1,0:T(8,128)(2,1)S(1)}, bf16[4,2,64,768]{3,2,1,0:T(8,128)(2,1)S(1)}, u32[]{:S(2)}, u32[]{:S(2)}) collective-permute-start(bf16[4,2,64,768]{3,2,1,0:T(8,128)(2,1)S(1)} %bitcast.66), channel_id=1, source_target_pairs={{0,32},{32,0},{1,33},{33,1},{2,34},{34,2},{3,35},{35,3},{4,36},{36... | collective-permute-start | bytes 2359304 | tf_op jit(solution)/shard_map/ppermute | solution.py:68
  93.5 72.3 %copy-start.3 = (f32[2,512,64]{1,2,0:T(8,128)S(1)}, f32[2,512,64]{1,2,0:T(8,128)}, u32[]{:S(2)}) copy-start(f32[2,512,64]{1,2,0:T(8,128)} %param.9) | copy-start | bytes 786436
  93.6 11.2 %collective-permute-start.17 = (bf16[2,64,768]{2,1,0:T(8,128)(2,1)S(1)}, bf16[2,64,768]{2,1,0:T(8,128)(2,1)S(1)}, u32[]{:S(2)}, u32[]{:S(2)}) collective-permute-start(bf16[2,64,768]{2,1,0:T(8,128)(2,1)S(1)} %get-tuple-element.6), channel_id=1, source_target_pairs={{0,64},{64,128},{128,192},{192,0},{1,65},{65,129},{129,193},{193,1... | collective-permute-start | bytes 589832 | tf_op jit(solution)/shard_map/ppermute | solution.py:17
  93.8 11.0 %collective-permute-start.18 = (bf16[2,64,768]{2,1,0:T(8,128)(2,1)S(1)}, bf16[2,64,768]{2,1,0:T(8,128)(2,1)S(1)}, u32[]{:S(2)}, u32[]{:S(2)}) collective-permute-start(bf16[2,64,768]{2,1,0:T(8,128)(2,1)S(1)} %get-tuple-element.7), channel_id=1, source_target_pairs={{0,192},{64,0},{128,64},{192,128},{1,193},{65,1},{129,65},{193,129... | collective-permute-start | bytes 589832 | tf_op jit(solution)/shard_map/ppermute | solution.py:17
  95.1 7.2 %collective-permute-start.15 = (bf16[64,768]{1,0:T(8,128)(2,1)S(1)}, bf16[64,768]{1,0:T(8,128)(2,1)S(1)}, u32[]{:S(2)}, u32[]{:S(2)}) collective-permute-start(bf16[64,768]{1,0:T(8,128)(2,1)S(1)} %get-tuple-element.4), channel_id=1, source_target_pairs={{0,128},{64,192},{128,0},{192,64},{1,129},{65,193},{129,1},{193,65... | collective-permute-start | bytes 294920 | tf_op jit(solution)/shard_map/ppermute | solution.py:17
  96.3 8.5 %collective-permute-start.16 = (bf16[64,768]{1,0:T(8,128)(2,1)S(1)}, bf16[64,768]{1,0:T(8,128)(2,1)S(1)}, u32[]{:S(2)}, u32[]{:S(2)}) collective-permute-start(bf16[64,768]{1,0:T(8,128)(2,1)S(1)} %get-tuple-element.5), channel_id=1, source_target_pairs={{0,128},{64,192},{128,0},{192,64},{1,129},{65,193},{129,1},{193,65... | collective-permute-start | bytes 294920 | tf_op jit(solution)/shard_map/ppermute | solution.py:17
  104.9 61.7 %copy-start.4 = (bf16[2,64,768]{2,1,0:T(8,128)(2,1)}, bf16[2,64,768]{2,1,0:T(8,128)(2,1)S(1)}, u32[]{:S(2)}) copy-start(bf16[2,64,768]{2,1,0:T(8,128)(2,1)S(1)} %fusion.14) | copy-start | bytes 589828
  104.9 18.4 %collective-permute-start.19 = (bf16[2,64,768]{2,1,0:T(8,128)(2,1)S(1)}, bf16[2,64,768]{2,1,0:T(8,128)(2,1)S(1)}, u32[]{:S(2)}, u32[]{:S(2)}) collective-permute-start(bf16[2,64,768]{2,1,0:T(8,128)(2,1)S(1)} %fusion.14), channel_id=1, source_target_pairs={{0,0},{1,1},{2,2},{3,3},{4,32},{5,33},{6,34},{7,35},{8,64},{9,65},... | collective-permute-start | bytes 589832 | tf_op jit(solution)/shard_map/ppermute | solution.py:121
  126.2 1.4 collective-permute-start.20
  127.7 5.0 %collective-permute-start.21 = (bf16[2,64,512]{2,1,0:T(8,128)(2,1)S(1)}, bf16[2,64,512]{2,1,0:T(8,128)(2,1)S(1)}, u32[]{:S(2)}, u32[]{:S(2)}) collective-permute-start(bf16[2,64,512]{2,1,0:T(8,128)(2,1)S(1)} %add_convert_fusion.2), channel_id=1, source_target_pairs={{0,1},{1,0},{2,3},{3,2},{4,5},{5,4},{6,7},{7,6},{8,9},{9,8},{10,11... | collective-permute-start | bytes 393224 | tf_op jit(solution)/shard_map/ppermute | solution.py:78
  128.1 10.4 %collective-permute-start.22 = (bf16[2,64,512]{2,1,0:T(8,128)(2,1)S(1)}, bf16[2,64,512]{2,1,0:T(8,128)(2,1)S(1)}, u32[]{:S(2)}, u32[]{:S(2)}) collective-permute-start(bf16[2,64,512]{2,1,0:T(8,128)(2,1)S(1)} %add_convert_fusion.2), channel_id=1, source_target_pairs={{0,2},{1,3},{2,0},{3,1},{4,6},{5,7},{6,4},{7,5},{8,10},{9,11},{10,... | collective-permute-start | bytes 393224 | tf_op jit(solution)/shard_map/ppermute | solution.py:78
  132.2 8.8 %collective-permute-start.23 = (bf16[2,64,512]{2,1,0:T(8,128)(2,1)S(1)}, bf16[2,64,512]{2,1,0:T(8,128)(2,1)S(1)}, u32[]{:S(2)}, u32[]{:S(2)}) collective-permute-start(bf16[2,64,512]{2,1,0:T(8,128)(2,1)S(1)} %add_convert_fusion.2), channel_id=1, source_target_pairs={{0,3},{1,2},{2,1},{3,0},{4,7},{5,6},{6,5},{7,4},{8,11},{9,10},{10,... | collective-permute-start | bytes 393224 | tf_op jit(solution)/shard_map/ppermute | solution.py:78
  141.1 4.2 %collective-permute-start.24 = (bf16[2,64,512]{2,1,0:T(8,128)(2,1)S(1)}, bf16[2,64,512]{2,1,0:T(8,128)(2,1)S(1)}, u32[]{:S(2)}, u32[]{:S(2)}) collective-permute-start(bf16[2,64,512]{2,1,0:T(8,128)(2,1)S(1)} %add_convert_fusion.1), channel_id=1, source_target_pairs={{0,64},{64,0},{128,192},{192,128},{1,65},{65,1},{129,193},{193,129... | collective-permute-start | bytes 393224 | tf_op jit(solution)/shard_map/ppermute | solution.py:78
  141.2 6.8 %collective-permute-start.25 = (bf16[2,64,512]{2,1,0:T(8,128)(2,1)S(1)}, bf16[2,64,512]{2,1,0:T(8,128)(2,1)S(1)}, u32[]{:S(2)}, u32[]{:S(2)}) collective-permute-start(bf16[2,64,512]{2,1,0:T(8,128)(2,1)S(1)} %add_convert_fusion.1), channel_id=1, source_target_pairs={{0,128},{64,192},{128,0},{192,64},{1,129},{65,193},{129,1},{193,65... | collective-permute-start | bytes 393224 | tf_op jit(solution)/shard_map/ppermute | solution.py:78
  142.1 9.2 %collective-permute-start.26 = (bf16[2,64,512]{2,1,0:T(8,128)(2,1)S(1)}, bf16[2,64,512]{2,1,0:T(8,128)(2,1)S(1)}, u32[]{:S(2)}, u32[]{:S(2)}) collective-permute-start(bf16[2,64,512]{2,1,0:T(8,128)(2,1)S(1)} %add_convert_fusion.1), channel_id=1, source_target_pairs={{0,192},{64,128},{128,64},{192,0},{1,193},{65,129},{129,65},{193,1... | collective-permute-start | bytes 393224 | tf_op jit(solution)/shard_map/ppermute | solution.py:78
  151.4 14.5 %collective-permute-start.27 = (bf16[2,64,512]{2,1,0:T(8,128)(2,1)S(1)}, bf16[2,64,512]{2,1,0:T(8,128)(2,1)S(1)}, u32[]{:S(2)}, u32[]{:S(2)}) collective-permute-start(bf16[2,64,512]{2,1,0:T(8,128)(2,1)S(1)} %add_convert_fusion), channel_id=1, source_target_pairs={{0,0},{1,1},{2,2},{3,3},{4,32},{5,33},{6,34},{7,35},{8,64},{9,65},... | collective-permute-start | bytes 393224 | tf_op jit(solution)/shard_map/ppermute | solution.py:128
  (3 other events, 3.7 us)
Sparse Core Ops, SparseCore 0:
  18.7 51.3 all-gather.1

commit v2 on v1

--- a/solution.py
+++ b/solution.py
@@ -54,47 +54,92 @@
 
 
 def panel_z_then_y(piece):
-    part = placed_by_owner(relay_ring(piece[None], "z", ZS, False), lax.axis_index("z"), 0)
+    part = placed_by_owner(direct_ring(piece[None], "z", ZS), lax.axis_index("z"), 0)
     whole = placed_by_owner(
         [g[:, None] for g in relay_ring(part, "y", YS, True)], lax.axis_index("y"), 1
     )
     return whole.reshape(-1, piece.shape[-1])
 
 
-def sum_over_row(tiles):
+def device(x, core, z, y):
+    return ((x * CORES + core) * ZS + z) * YS + y
+
+
+def to_cores(own_slabs):
+    x, core, z = lax.axis_index("x"), lax.axis_index("core"), lax.axis_index("z")
+    home = (x == z // CORES) & (core == z % CORES)
+    total = jnp.where(home, jnp.where(core == 0, own_slabs[0], own_slabs[1]), jnp.zeros((), BF16))
+    across = jnp.where(core == 0, own_slabs[1], own_slabs[0])
+    pairs = lambda by, s: [
+        (device(r // CORES, r % CORES, r, y), device((r // CORES + by) % XS, s, r, y))
+        for r in range(ZS)
+        for y in range(YS)
+    ]
+    for s, shifts in ((0, (1, -1, 2)), (1, (1, -1, -2))):
+        for by in shifts:
+            total = total + lax.ppermute(own_slabs[s], ALL, pairs(by, s))
+    swapped = [
+        (device(r // CORES, r % CORES, r, y), device(r // CORES, 1 - r % CORES, r, y))
+        for r in range(ZS)
+        for y in range(YS)
+    ]
+    return total + lax.ppermute(across, ALL, swapped)
+
+
+def sum_over_row(partial):
     x, core = lax.axis_index("x"), lax.axis_index("core")
-    kept = lax.dynamic_index_in_dim(tiles, core, 1, keepdims=False)
-    given = lax.dynamic_index_in_dim(tiles, 1 - core, 1, keepdims=False)
-    pair = kept.astype(F32) + lax.ppermute(given, "core", [(0, 1), (1, 0)]).astype(F32)
+    moved = lax.ppermute(partial[0], "core", [(1, 0)]).astype(F32) + lax.ppermute(
+        partial[1], "core", [(0, 1)]
+    ).astype(F32)
+    pair = jnp.where(core == 0, partial[0], partial[1]).astype(F32) + moved
     pair = lax.optimization_barrier(pair.astype(BF16))
+    pair = pair.reshape(XS, -1, pair.shape[1])
     tile = lambda k: lax.dynamic_index_in_dim(pair, (x + k) % XS, 0, keepdims=False)
     far = tile(2)
-    opposite = jnp.stack([shift(far[0], "x", XS, 2), shift(far[1], "x", XS, -2)])
+    half = far.shape[0] // 2
+    opposite = jnp.concatenate(
+        [shift(far[:half], "x", XS, 2), shift(far[half:], "x", XS, -2)], axis=0
+    )
     near = shift(tile(1), "x", XS, 1).astype(F32) + shift(tile(3), "x", XS, -1).astype(F32)
     return (tile(0).astype(F32) + opposite.astype(F32)) + near
 
 
-def summed_by_pairs(array, axis, size):
-    other = lambda k: lax.ppermute(array, axis, [(i, i ^ k) for i in range(size)]).astype(F32)
-    total = array.astype(F32) + other(1)
-    if size == 4:
-        total = total + (other(2) + other(3))
-    return lax.optimization_barrier(total.astype(BF16))
+def exchanged(array, axis, size, by):
+    return lax.ppermute(array, axis, [(i, i ^ by) for i in range(size)])
 
 
-SWAP = [
-    ((a * ZS + b) * YS + y, (b * ZS + a) * YS + y)
-    for a in range(XS * CORES)
-    for b in range(ZS)
-    for y in range(YS)
-]
+def summed_over_col(array):
+    y = lax.axis_index("y")
+    quarters = array.reshape(YS, -1, array.shape[1])
+    own = lambda k: lax.dynamic_index_in_dim(quarters, y ^ k, 0, keepdims=False)
+    wide = [own(0)] + [exchanged(own(k), "y", YS, k) for k in range(1, YS)]
+    wide = [w.astype(F32) for w in wide]
+    part = lax.optimization_barrier(((wide[0] + wide[1]) + (wide[2] + wide[3])).astype(BF16))
+    wide = [part.astype(F32)] + [exchanged(part, "z", ZS, k).astype(F32) for k in range(1, 4)]
+    part = lax.optimization_barrier(((wide[0] + wide[1]) + (wide[2] + wide[3])).astype(BF16))
+    part = part.astype(F32) + exchanged(part, "z", ZS, 4).astype(F32)
+    part = lax.optimization_barrier(part.astype(BF16))
+    whole = jnp.zeros(quarters.shape, BF16)
+    for k in range(YS):
+        got = part if k == 0 else exchanged(part, "y", YS, k)
+        whole = lax.dynamic_update_slice_in_dim(whole, got[None], y ^ k, 0)
+    return whole.reshape(array.shape)
+
+
+def own_slab_of_both(array):
+    core = lax.axis_index("core")
+    slabs = array.reshape(CORES, -1, array.shape[1])
+    kept = lax.dynamic_index_in_dim(slabs, core, 0, keepdims=False)
+    given = lax.dynamic_index_in_dim(slabs, 1 - core, 0, keepdims=False)
+    got = lax.ppermute(given, "core", [(0, 1), (1, 0)])
+    return jnp.stack([jnp.where(core == 0, kept, got), jnp.where(core == 0, got, kept)])
 
 
 def body(listing, pieces, factor_inv, inverse_block, diag_inv):
     piece_rows, width = pieces.shape[1:]
     row = lax.axis_index(ROW)
     col = lax.axis_index(COL)
-    y = lax.axis_index("y")
+    core, y = lax.axis_index("core"), lax.axis_index("y")
     chosen = listing[:, :NSEL]
 
     def keep_of(first, count):
@@ -107,26 +152,23 @@
     panels = [panel_y_then_z(normed[0]), panel_z_then_y(normed[1])]
 
     rows = inverse_block.shape[0]
-    slab = width // (XS * CORES)
     partial = [
-        jnp.einsum("qj,pq->jp", panel, inverse_block, preferred_element_type=F32)
-        .astype(BF16)
-        .reshape(XS, CORES, 1, slab, rows)
+        jnp.einsum("qj,pq->jp", panel, inverse_block, preferred_element_type=F32).astype(BF16)
         for panel in panels
     ]
-    product = sum_over_row(jnp.concatenate(partial, axis=2))
-    col_keep = keep_of(col * rows, rows)
-    offdiag = (-(product * col_keep[:, None, :])).astype(BF16)
+    factor_slab = to_cores(
+        [lax.dynamic_slice_in_dim(panel, y * rows, rows, 0) for panel in panels]
+    )
+    product = sum_over_row(partial)
+    col_keep = lax.dynamic_index_in_dim(keep_of(col * rows, rows), core, 0)
+    offdiag = lax.optimization_barrier((-(product * col_keep)).astype(BF16))
 
-    turned = lax.ppermute(offdiag, ALL, SWAP)
-    own_slabs = [lax.dynamic_slice_in_dim(panel, y * rows, rows, 0) for panel in panels]
-    terms = jnp.stack(
-        [-jnp.dot(turned[s], own_slabs[s], preferred_element_type=F32) for s in range(len(panels))]
-    ).astype(BF16)
-    for axis, size in (("core", CORES), ("y", YS), ("x", XS)):
-        terms = summed_by_pairs(terms, axis, size)
-    correction = lax.ppermute(terms, ALL, SWAP).astype(F32)
-    return offdiag.transpose(0, 2, 1), diag_inv + correction.transpose(0, 2, 1)
+    term = -jnp.dot(offdiag, factor_slab, preferred_element_type=F32)
+    correction = own_slab_of_both(summed_over_col(term.astype(BF16)))
+    return (
+        own_slab_of_both(offdiag).transpose(0, 2, 1),
+        diag_inv + correction.astype(F32).transpose(0, 2, 1),
+    )
 
 
 def solution(mesh):

time: 174 us -> 205 us (1.18)
  the two profiles are of different devices: /device:TPU:7 before, /device:TPU:1 now
where the time goes in v2:
time: 205 us; the launch traced here: 201 us
  starting transfers between devices  98.1 us (48%)
  waiting for transfers between devices  60.4 us (29%)
  between operations  14.6 us (7%)
  matrix products  14.2 us (7%)
  other arithmetic  7.41 us (4%)
  local copies, waits for them, and re-layouts  6.21 us (3%)
    ppermute x18, waiting for transfers between devices, shift(): lax.ppermute(array, axis, [(i, (i + by) % size) for i in range(size)])  45.5 us
    ppermute x10, starting transfers between devices, exchanged(): return lax.ppermute(array, axis, [(i, i ^ by) for i in range(size)])  41.3 us
    ppermute x18, starting transfers between devices, shift(): lax.ppermute(array, axis, [(i, (i + by) % size) for i in range(size)])  33.4 us
    ppermute x10, waiting for transfers between devices, exchanged(): return lax.ppermute(array, axis, [(i, i ^ by) for i in range(size)])  14.6 us
    dot_general x2, matrix products, body(): jnp.einsum('qj,pq->jp', panel, inverse_block, preferred_element_type=F32)  9.58 us
    ppermute x6, starting transfers between devices, to_cores(): total = total + lax.ppermute(own_slabs[s], ALL, pairs(by, s))  9.32 us
    ppermute x1, starting transfers between devices, sum_over_row(): lax.ppermute(partial[0], 'core', [(1, 0)]).astype(F32)  8.56 us
    unnamed x16, local copies, waits for them, and re-layouts  4.9 us
  transfers between devices with their start and end apart: 40, of which 18 were waited for; matrix products, arithmetic and copies ran while one was open for 8% of the time, Pallas kernels for 0%

profile of v2, /device:TPU:1, one launch (start us, length us, event | category | flops | bytes accessed | tf_op | source)
XLA Modules:
  0.0 200.8 jit_solution(15441403225088898654)
XLA Ops:
  9.7 2.2 %collective-permute-start = (bf16[96,512]{1,0:T(8,128)(2,1)S(1)}, bf16[96,512]{1,0:T(8,128)(2,1)S(1)}, u32[]{:S(2)}, u32[]{:S(2)}) collective-permute-start(bf16[96,512]{1,0:T(8,128)(2,1)S(1)} %get-tuple-element.13), channel_id=1, source_target_pairs={{0,1},{1,2},{2,3},{3,0},{4,5},{5,6},{6,7},{7,4},{8,9},{9,10},{10,1... | collective-permute-start | bytes 294920 | tf_op jit(solution)/shard_map/ppermute | solution.py:17
  12.0 2.6 %collective-permute-start.1 = (bf16[96,512]{1,0:T(8,128)(2,1)S(1)}, bf16[96,512]{1,0:T(8,128)(2,1)S(1)}, u32[]{:S(2)}, u32[]{:S(2)}) collective-permute-start(bf16[96,512]{1,0:T(8,128)(2,1)S(1)} %get-tuple-element.13), channel_id=1, source_target_pairs={{0,2},{1,3},{2,0},{3,1},{4,6},{5,7},{6,4},{7,5},{8,10},{9,11},{10,... | collective-permute-start | bytes 294920 | tf_op jit(solution)/shard_map/ppermute | solution.py:17
  15.8 2.8 %collective-permute-done.1 = bf16[96,512]{1,0:T(8,128)(2,1)S(1)} collective-permute-done((bf16[96,512]{1,0:T(8,128)(2,1)S(1)}, bf16[96,512]{1,0:T(8,128)(2,1)S(1)}, u32[]{:S(2)}, u32[]{:S(2)}) %collective-permute-start.1) | collective-permute-done | bytes 98336 | tf_op jit(solution)/shard_map/ppermute | solution.py:17
  21.1 3.0 %collective-permute-start.4 = (bf16[1,96,512]{2,1,0:T(8,128)(2,1)S(1)}, bf16[1,96,512]{2,1,0:T(8,128)(2,1)S(1)}, u32[]{:S(2)}, u32[]{:S(2)}) collective-permute-start(bf16[1,96,512]{2,1,0:T(8,128)(2,1)S(1)} %get-tuple-element.15), channel_id=1, source_target_pairs={{0,8},{4,12},{8,16},{12,20},{16,24},{20,28},{24,0},{28,4},{1,9},{5... | collective-permute-start | bytes 294920 | tf_op jit(solution)/shard_map/ppermute | solution.py:17
  24.1 3.7 %collective-permute-start.5 = (bf16[1,96,512]{2,1,0:T(8,128)(2,1)S(1)}, bf16[1,96,512]{2,1,0:T(8,128)(2,1)S(1)}, u32[]{:S(2)}, u32[]{:S(2)}) collective-permute-start(bf16[1,96,512]{2,1,0:T(8,128)(2,1)S(1)} %get-tuple-element.15), channel_id=1, source_target_pairs={{0,12},{4,16},{8,20},{12,24},{16,28},{20,0},{24,4},{28,8},{1,13},{... | collective-permute-start | bytes 294920 | tf_op jit(solution)/shard_map/ppermute | solution.py:17
  28.3 4.5 %collective-permute-start.7 = (bf16[1,96,512]{2,1,0:T(8,128)(2,1)S(1)}, bf16[1,96,512]{2,1,0:T(8,128)(2,1)S(1)}, u32[]{:S(2)}, u32[]{:S(2)}) collective-permute-start(bf16[1,96,512]{2,1,0:T(8,128)(2,1)S(1)} %get-tuple-element.15), channel_id=1, source_target_pairs={{0,20},{4,24},{8,28},{12,0},{16,4},{20,8},{24,12},{28,16},{1,21},{... | collective-permute-start | bytes 294920 | tf_op jit(solution)/shard_map/ppermute | solution.py:17
  32.8 2.4 %collective-permute-start.8 = (bf16[1,96,512]{2,1,0:T(8,128)(2,1)S(1)}, bf16[1,96,512]{2,1,0:T(8,128)(2,1)S(1)}, u32[]{:S(2)}, u32[]{:S(2)}) collective-permute-start(bf16[1,96,512]{2,1,0:T(8,128)(2,1)S(1)} %get-tuple-element.15), channel_id=1, source_target_pairs={{0,24},{4,28},{8,0},{12,4},{16,8},{20,12},{24,16},{28,20},{1,25},{... | collective-permute-start | bytes 294920 | tf_op jit(solution)/shard_map/ppermute | solution.py:17
  36.1 2.2 %collective-permute-done.6 = bf16[1,96,512]{2,1,0:T(8,128)(2,1)S(1)} collective-permute-done((bf16[1,96,512]{2,1,0:T(8,128)(2,1)S(1)}, bf16[1,96,512]{2,1,0:T(8,128)(2,1)S(1)}, u32[]{:S(2)}, u32[]{:S(2)}) %collective-permute-start.6) | collective-permute-done | bytes 98336 | tf_op jit(solution)/shard_map/ppermute | solution.py:17
  38.2 2.2 %collective-permute-done.7 = bf16[1,96,512]{2,1,0:T(8,128)(2,1)S(1)} collective-permute-done((bf16[1,96,512]{2,1,0:T(8,128)(2,1)S(1)}, bf16[1,96,512]{2,1,0:T(8,128)(2,1)S(1)}, u32[]{:S(2)}, u32[]{:S(2)}) %collective-permute-start.7) | collective-permute-done | bytes 98336 | tf_op jit(solution)/shard_map/ppermute | solution.py:17
  40.5 11.1 %collective-permute-done.8 = bf16[1,96,512]{2,1,0:T(8,128)(2,1)S(1)} collective-permute-done((bf16[1,96,512]{2,1,0:T(8,128)(2,1)S(1)}, bf16[1,96,512]{2,1,0:T(8,128)(2,1)S(1)}, u32[]{:S(2)}, u32[]{:S(2)}) %collective-permute-start.8) | collective-permute-done | bytes 98336 | tf_op jit(solution)/shard_map/ppermute | solution.py:17
  51.6 2.9 %collective-permute-done.9 = bf16[1,96,512]{2,1,0:T(8,128)(2,1)S(1)} collective-permute-done((bf16[1,96,512]{2,1,0:T(8,128)(2,1)S(1)}, bf16[1,96,512]{2,1,0:T(8,128)(2,1)S(1)}, u32[]{:S(2)}, u32[]{:S(2)}) %collective-permute-start.9) | collective-permute-done | bytes 98336 | tf_op jit(solution)/shard_map/ppermute | solution.py:17
  54.6 1.8 collective-permute-start.12
  56.4 14.0 %collective-permute-done.12 = bf16[8,96,512]{2,1,0:T(8,128)(2,1)S(1)} collective-permute-done((bf16[8,96,512]{2,1,0:T(8,128)(2,1)S(1)}, bf16[8,96,512]{2,1,0:T(8,128)(2,1)S(1)}, u32[]{:S(2)}, u32[]{:S(2)}) %collective-permute-start.12) | collective-permute-done | bytes 786464 | tf_op jit(solution)/shard_map/ppermute | solution.py:17
  70.4 2.9 %collective-permute-start.13 = (bf16[4,96,512]{2,1,0:T(8,128)(2,1)S(1)}, bf16[4,96,512]{2,1,0:T(8,128)(2,1)S(1)}, u32[]{:S(2)}, u32[]{:S(2)}) collective-permute-start(bf16[4,96,512]{2,1,0:T(8,128)(2,1)S(1)} %slice.39), channel_id=1, source_target_pairs={{0,3},{1,0},{2,1},{3,2},{4,7},{5,4},{6,5},{7,6},{8,11},{9,8},{10,9... | collective-permute-start | bytes 1179656 | tf_op jit(solution)/shard_map/ppermute | solution.py:17
  74.2 4.4 %collective-permute-done.13 = bf16[4,96,512]{2,1,0:T(8,128)(2,1)S(1)} collective-permute-done((bf16[4,96,512]{2,1,0:T(8,128)(2,1)S(1)}, bf16[4,96,512]{2,1,0:T(8,128)(2,1)S(1)}, u32[]{:S(2)}, u32[]{:S(2)}) %collective-permute-start.13) | collective-permute-done | bytes 393248 | tf_op jit(solution)/shard_map/ppermute | solution.py:17
  78.6 2.9 %collective-permute-done.11 = bf16[4,96,512]{2,1,0:T(8,128)(2,1)S(1)} collective-permute-done((bf16[4,96,512]{2,1,0:T(8,128)(2,1)S(1)}, bf16[4,96,512]{2,1,0:T(8,128)(2,1)S(1)}, u32[]{:S(2)}, u32[]{:S(2)}) %collective-permute-start.11) | collective-permute-done | bytes 393248 | tf_op jit(solution)/shard_map/ppermute | solution.py:17
  82.0 2.8 %slice-done = s8[4194304]{0:T(1024)(128)(4,1)S(1)} async-done(((s8[4718592]{0:T(1024)(128)(4,1)}), s8[4194304]{0:T(1024)(128)(4,1)S(1)}, s32[]{:S(2)}) %slice-start) | async-done | bytes 4194328
  84.9 2.7 %convolution_convert_fusion = bf16[512,768]{1,0:T(8,128)(2,1)S(1)} fusion(bf16[3072,512]{1,0:T(8,128)(2,1)S(1)} %bitcast.85, bf16[768,3072]{1,0:T(8,128)(2,1)S(1)} %bitcast.99), kind=kOutput, calls=%fused_computation.1 | convolution fusion | flops 2416312320 | bytes 8650752 | tf_op jit(solution)/shard_map/qj,pq->jp/dot_general | solution.py:156
  88.9 6.9 %convolution_convert_fusion.1 = bf16[512,768]{1,0:T(8,128)(2,1)} fusion(bf16[3072,512]{1,0:T(8,128)(2,1)} %all-gather.2.cloned.1.call-done, bf16[768,3072]{1,0:T(8,128)(2,1)} %param.8), kind=kOutput, calls=%fused_computation.2 | convolution fusion | flops 2416312320 | bytes 8650752 | tf_op jit(solution)/shard_map/qj,pq->jp/dot_general | solution.py:156
  95.9 8.6 %collective-permute-start.14 = (bf16[512,768]{1,0:T(8,128)(2,1)}, bf16[512,768]{1,0:T(8,128)(2,1)}, u32[]{:S(2)}, u32[]{:S(2)}) collective-permute-start(bf16[512,768]{1,0:T(8,128)(2,1)} %convolution_convert_fusion.1), channel_id=1, source_target_pairs={{32,0},{33,1},{34,2},{35,3},{36,4},{37,5},{38,6},{39,7},{40,8},{41... | collective-permute-start | bytes 2359304 | tf_op jit(solution)/shard_map/ppermute | solution.py:91
  104.4 2.9 %broadcast_select_fusion = (bf16[768,512]{1,0:T(8,128)(2,1)}, bf16[768,512]{1,0:T(8,128)(2,1)S(1)}, bf16[768,512]{1,0:T(8,128)(2,1)}) fusion(pred[]{:T(512)S(6)} %eq.63, bf16[3072,512]{1,0:T(8,128)(2,1)} %all-gather.2.cloned.1.call-done, s32[]{:T(128)S(6)} %select_n.297, bf16[3072,512]{1,0:T(8,128)(2,1)} %bitcast.86), kind=kLoop, calls=%fused_computation.21 | loop fusion | flops 393216 | bytes 3932165 | tf_op jit(solution)/shard_map/jit(_where)/select_n | solution.py:72
  113.0 2.9 %collective-permute-start.19 = (bf16[128,768]{1,0:T(8,128)(2,1)S(1)}, bf16[128,768]{1,0:T(8,128)(2,1)S(1)}, u32[]{:S(2)}, u32[]{:S(2)}) collective-permute-start(bf16[128,768]{1,0:T(8,128)(2,1)S(1)} %get-tuple-element.8), channel_id=1, source_target_pairs={{0,192},{64,0},{128,64},{192,128},{1,193},{65,1},{129,65},{193,129... | collective-permute-start | bytes 589832 | tf_op jit(solution)/shard_map/ppermute | solution.py:17
  120.6 2.9 %collective-permute-done.17 = bf16[64,768]{1,0:T(8,128)(2,1)S(1)} collective-permute-done((bf16[64,768]{1,0:T(8,128)(2,1)S(1)}, bf16[64,768]{1,0:T(8,128)(2,1)S(1)}, u32[]{:S(2)}, u32[]{:S(2)}) %collective-permute-start.17) | collective-permute-done | bytes 98336 | tf_op jit(solution)/shard_map/ppermute | solution.py:17
  130.0 3.3 %fusion.1 = bf16[128,512]{1,0:T(8,128)(2,1)S(1)} fusion(bf16[128,768]{1,0:T(8,128)(2,1)S(1)} %fusion.17, bf16[768,512]{1,0:T(8,128)(2,1)} %collective-permute-done.27, bf16[768,512]{1,0:T(8,128)(2,1)} %collective-permute-done.26, bf16[768,512]{1,0:T(8,128)(2,1)} %collective-permute-done.25, bf16[768,512]{1,0:T(8,128)(2,1)} %collective-permute-done.24, ...), kind=kOutput, calls=%fused_computation.6 | convolution fusion | flops 104333312 | bytes 7405570 | tf_op jit(solution)/shard_map/dot_general | solution.py:166
  133.8 2.9 %collective-permute-start.28 = (bf16[32,512]{1,0:T(8,128)(2,1)S(1)}, bf16[32,512]{1,0:T(8,128)(2,1)S(1)}, u32[]{:S(2)}, u32[]{:S(2)}) collective-permute-start(bf16[32,512]{1,0:T(8,128)(2,1)S(1)} %get-tuple-element.16), channel_id=1, source_target_pairs={{0,1},{1,0},{2,3},{3,2},{4,5},{5,4},{6,7},{7,6},{8,9},{9,8},{10,11... | collective-permute-start | bytes 98312 | tf_op jit(solution)/shard_map/ppermute | solution.py:108
  138.4 11.7 %collective-permute-start.33 = (bf16[32,512]{1,0:T(8,128)(2,1)S(1)}, bf16[32,512]{1,0:T(8,128)(2,1)S(1)}, u32[]{:S(2)}, u32[]{:S(2)}) collective-permute-start(bf16[32,512]{1,0:T(8,128)(2,1)S(1)} %fusion.22), channel_id=1, source_target_pairs={{0,12},{4,8},{8,4},{12,0},{16,28},{20,24},{24,20},{28,16},{1,13},{... | collective-permute-start | bytes 98312 | tf_op jit(solution)/shard_map/ppermute | solution.py:108
  150.1 22.2 %collective-permute-start.32 = (bf16[32,512]{1,0:T(8,128)(2,1)S(1)}, bf16[32,512]{1,0:T(8,128)(2,1)S(1)}, u32[]{:S(2)}, u32[]{:S(2)}) collective-permute-start(bf16[32,512]{1,0:T(8,128)(2,1)S(1)} %fusion.22), channel_id=1, source_target_pairs={{0,8},{4,12},{8,0},{12,4},{16,24},{20,28},{24,16},{28,20},{1,9},{5... | collective-permute-start | bytes 98312 | tf_op jit(solution)/shard_map/ppermute | solution.py:108
  172.3 2.6 %collective-permute-done.32 = bf16[32,512]{1,0:T(8,128)(2,1)S(1)} collective-permute-done((bf16[32,512]{1,0:T(8,128)(2,1)S(1)}, bf16[32,512]{1,0:T(8,128)(2,1)S(1)}, u32[]{:S(2)}, u32[]{:S(2)}) %collective-permute-start.32) | collective-permute-done | bytes 32800 | tf_op jit(solution)/shard_map/ppermute | solution.py:108
  175.5 6.5 %collective-permute-done.34 = bf16[32,512]{1,0:T(8,128)(2,1)S(1)} collective-permute-done((bf16[32,512]{1,0:T(8,128)(2,1)S(1)}, bf16[32,512]{1,0:T(8,128)(2,1)S(1)}, u32[]{:S(2)}, u32[]{:S(2)}) %collective-permute-start.34) | collective-permute-done | bytes 32800 | tf_op jit(solution)/shard_map/ppermute | solution.py:108
  183.2 2.2 %collective-permute-start.36 = (bf16[32,512]{1,0:T(8,128)(2,1)S(1)}, bf16[32,512]{1,0:T(8,128)(2,1)S(1)}, u32[]{:S(2)}, u32[]{:S(2)}) collective-permute-start(bf16[32,512]{1,0:T(8,128)(2,1)S(1)} %add_convert_fusion.1), channel_id=1, source_target_pairs={{0,2},{1,3},{2,0},{3,1},{4,6},{5,7},{6,4},{7,5},{8,10},{9,11},{10,... | collective-permute-start | bytes 98312 | tf_op jit(solution)/shard_map/ppermute | solution.py:108
  187.4 2.3 %collective-permute-done.37 = bf16[32,512]{1,0:T(8,128)(2,1)S(1)} collective-permute-done((bf16[32,512]{1,0:T(8,128)(2,1)S(1)}, bf16[32,512]{1,0:T(8,128)(2,1)S(1)}, u32[]{:S(2)}, u32[]{:S(2)}) %collective-permute-start.37) | collective-permute-done | bytes 32800 | tf_op jit(solution)/shard_map/ppermute | solution.py:108
  189.8 2.6 %collective-permute-start.38 = (bf16[64,512]{1,0:T(8,128)(2,1)S(1)}, bf16[64,512]{1,0:T(8,128)(2,1)S(1)}, u32[]{:S(2)}, u32[]{:S(2)}) collective-permute-start(bf16[64,512]{1,0:T(8,128)(2,1)S(1)} %dynamic-slice_bitcast_fusion.5), channel_id=1, source_target_pairs={{0,32},{32,0},{1,33},{33,1},{2,34},{34,2},{3,35},{35,3},{4,36},{36... | collective-permute-start | bytes 196616 | tf_op jit(solution)/shard_map/ppermute | solution.py:134
  (118 shorter events, 34.6 us)
Async XLA Ops:
  7.2 81.7 %all-gather.2.cloned.1.call-start = ((), (), s32[]{:S(2)}) async-start(), calls=%async_computation | async-start | bytes 3538944 | tf_op jit(solution)/shard_map/all_gather | solution.py:53
  9.7 6.0 %collective-permute-start = (bf16[96,512]{1,0:T(8,128)(2,1)S(1)}, bf16[96,512]{1,0:T(8,128)(2,1)S(1)}, u32[]{:S(2)}, u32[]{:S(2)}) collective-permute-start(bf16[96,512]{1,0:T(8,128)(2,1)S(1)} %get-tuple-element.13), channel_id=1, source_target_pairs={{0,1},{1,2},{2,3},{3,0},{4,5},{5,6},{6,7},{7,4},{8,9},{9,10},{10,1... | collective-permute-start | bytes 294920 | tf_op jit(solution)/shard_map/ppermute | solution.py:17
  12.0 6.6 %collective-permute-start.1 = (bf16[96,512]{1,0:T(8,128)(2,1)S(1)}, bf16[96,512]{1,0:T(8,128)(2,1)S(1)}, u32[]{:S(2)}, u32[]{:S(2)}) collective-permute-start(bf16[96,512]{1,0:T(8,128)(2,1)S(1)} %get-tuple-element.13), channel_id=1, source_target_pairs={{0,2},{1,3},{2,0},{3,1},{4,6},{5,7},{6,4},{7,5},{8,10},{9,11},{10,... | collective-permute-start | bytes 294920 | tf_op jit(solution)/shard_map/ppermute | solution.py:17
  19.4 13.4 %collective-permute-start.3 = (bf16[1,96,512]{2,1,0:T(8,128)(2,1)S(1)}, bf16[1,96,512]{2,1,0:T(8,128)(2,1)S(1)}, u32[]{:S(2)}, u32[]{:S(2)}) collective-permute-start(bf16[1,96,512]{2,1,0:T(8,128)(2,1)S(1)} %get-tuple-element.15), channel_id=1, source_target_pairs={{0,4},{4,8},{8,12},{12,16},{16,20},{20,24},{24,28},{28,0},{1,5},{5... | collective-permute-start | bytes 294920 | tf_op jit(solution)/shard_map/ppermute | solution.py:17
  21.1 14.1 %collective-permute-start.4 = (bf16[1,96,512]{2,1,0:T(8,128)(2,1)S(1)}, bf16[1,96,512]{2,1,0:T(8,128)(2,1)S(1)}, u32[]{:S(2)}, u32[]{:S(2)}) collective-permute-start(bf16[1,96,512]{2,1,0:T(8,128)(2,1)S(1)} %get-tuple-element.15), channel_id=1, source_target_pairs={{0,8},{4,12},{8,16},{12,20},{16,24},{20,28},{24,0},{28,4},{1,9},{5... | collective-permute-start | bytes 294920 | tf_op jit(solution)/shard_map/ppermute | solution.py:17
  24.1 11.9 %collective-permute-start.5 = (bf16[1,96,512]{2,1,0:T(8,128)(2,1)S(1)}, bf16[1,96,512]{2,1,0:T(8,128)(2,1)S(1)}, u32[]{:S(2)}, u32[]{:S(2)}) collective-permute-start(bf16[1,96,512]{2,1,0:T(8,128)(2,1)S(1)} %get-tuple-element.15), channel_id=1, source_target_pairs={{0,12},{4,16},{8,20},{12,24},{16,28},{20,0},{24,4},{28,8},{1,13},{... | collective-permute-start | bytes 294920 | tf_op jit(solution)/shard_map/ppermute | solution.py:17
  27.9 10.4 %collective-permute-start.6 = (bf16[1,96,512]{2,1,0:T(8,128)(2,1)S(1)}, bf16[1,96,512]{2,1,0:T(8,128)(2,1)S(1)}, u32[]{:S(2)}, u32[]{:S(2)}) collective-permute-start(bf16[1,96,512]{2,1,0:T(8,128)(2,1)S(1)} %get-tuple-element.15), channel_id=1, source_target_pairs={{0,16},{4,20},{8,24},{12,28},{16,0},{20,4},{24,8},{28,12},{1,17},{... | collective-permute-start | bytes 294920 | tf_op jit(solution)/shard_map/ppermute | solution.py:17
  28.3 12.1 %collective-permute-start.7 = (bf16[1,96,512]{2,1,0:T(8,128)(2,1)S(1)}, bf16[1,96,512]{2,1,0:T(8,128)(2,1)S(1)}, u32[]{:S(2)}, u32[]{:S(2)}) collective-permute-start(bf16[1,96,512]{2,1,0:T(8,128)(2,1)S(1)} %get-tuple-element.15), channel_id=1, source_target_pairs={{0,20},{4,24},{8,28},{12,0},{16,4},{20,8},{24,12},{28,16},{1,21},{... | collective-permute-start | bytes 294920 | tf_op jit(solution)/shard_map/ppermute | solution.py:17
  32.8 18.8 %collective-permute-start.8 = (bf16[1,96,512]{2,1,0:T(8,128)(2,1)S(1)}, bf16[1,96,512]{2,1,0:T(8,128)(2,1)S(1)}, u32[]{:S(2)}, u32[]{:S(2)}) collective-permute-start(bf16[1,96,512]{2,1,0:T(8,128)(2,1)S(1)} %get-tuple-element.15), channel_id=1, source_target_pairs={{0,24},{4,28},{8,0},{12,4},{16,8},{20,12},{24,16},{28,20},{1,25},{... | collective-permute-start | bytes 294920 | tf_op jit(solution)/shard_map/ppermute | solution.py:17
  35.2 19.4 %collective-permute-start.9 = (bf16[1,96,512]{2,1,0:T(8,128)(2,1)S(1)}, bf16[1,96,512]{2,1,0:T(8,128)(2,1)S(1)}, u32[]{:S(2)}, u32[]{:S(2)}) collective-permute-start(bf16[1,96,512]{2,1,0:T(8,128)(2,1)S(1)} %get-tuple-element.15), channel_id=1, source_target_pairs={{0,28},{4,0},{8,4},{12,8},{16,12},{20,16},{24,20},{28,24},{1,29},{... | collective-permute-start | bytes 294920 | tf_op jit(solution)/shard_map/ppermute | solution.py:17
  54.6 15.8 %collective-permute-start.12 = (bf16[8,96,512]{2,1,0:T(8,128)(2,1)S(1)}, bf16[8,96,512]{2,1,0:T(8,128)(2,1)S(1)}, u32[]{:S(2)}, u32[]{:S(2)}) collective-permute-start(bf16[8,96,512]{2,1,0:T(8,128)(2,1)S(1)} %constant_dynamic-update-slice_fusion), channel_id=1, source_target_pairs={{0,3},{1,0},{2,1},{3,2},{4,7},{5,4},{6,5},{7,6},{8,11},{9,8},{10,9... | collective-permute-start | bytes 2359304 | tf_op jit(solution)/shard_map/ppermute | solution.py:17
  56.4 17.0 %collective-permute-start.10 = (bf16[8,96,512]{2,1,0:T(8,128)(2,1)S(1)}, bf16[8,96,512]{2,1,0:T(8,128)(2,1)S(1)}, u32[]{:S(2)}, u32[]{:S(2)}) collective-permute-start(bf16[8,96,512]{2,1,0:T(8,128)(2,1)S(1)} %constant_dynamic-update-slice_fusion), channel_id=1, source_target_pairs={{0,1},{1,2},{2,3},{3,0},{4,5},{5,6},{6,7},{7,4},{8,9},{9,10},{10,1... | collective-permute-start | bytes 2359304 | tf_op jit(solution)/shard_map/ppermute | solution.py:17
  70.4 8.2 %collective-permute-start.13 = (bf16[4,96,512]{2,1,0:T(8,128)(2,1)S(1)}, bf16[4,96,512]{2,1,0:T(8,128)(2,1)S(1)}, u32[]{:S(2)}, u32[]{:S(2)}) collective-permute-start(bf16[4,96,512]{2,1,0:T(8,128)(2,1)S(1)} %slice.39), channel_id=1, source_target_pairs={{0,3},{1,0},{2,1},{3,2},{4,7},{5,4},{6,5},{7,6},{8,11},{9,8},{10,9... | collective-permute-start | bytes 1179656 | tf_op jit(solution)/shard_map/ppermute | solution.py:17
  73.4 8.1 %collective-permute-start.11 = (bf16[4,96,512]{2,1,0:T(8,128)(2,1)S(1)}, bf16[4,96,512]{2,1,0:T(8,128)(2,1)S(1)}, u32[]{:S(2)}, u32[]{:S(2)}) collective-permute-start(bf16[4,96,512]{2,1,0:T(8,128)(2,1)S(1)} %slice.38), channel_id=1, source_target_pairs={{0,1},{1,2},{2,3},{3,0},{4,5},{5,6},{6,7},{7,4},{8,9},{9,10},{10,1... | collective-permute-start | bytes 1179656 | tf_op jit(solution)/shard_map/ppermute | solution.py:17
  87.6 22.7 %collective-permute-start.15 = (bf16[512,768]{1,0:T(8,128)(2,1)S(1)}, bf16[512,768]{1,0:T(8,128)(2,1)S(1)}, u32[]{:S(2)}, u32[]{:S(2)}) collective-permute-start(bf16[512,768]{1,0:T(8,128)(2,1)S(1)} %convolution_convert_fusion), channel_id=1, source_target_pairs={{0,32},{1,33},{2,34},{3,35},{4,36},{5,37},{6,38},{7,39},{8,40},{9,... | collective-permute-start | bytes 2359304 | tf_op jit(solution)/shard_map/ppermute | solution.py:91
  95.9 15.4 %collective-permute-start.14 = (bf16[512,768]{1,0:T(8,128)(2,1)}, bf16[512,768]{1,0:T(8,128)(2,1)}, u32[]{:S(2)}, u32[]{:S(2)}) collective-permute-start(bf16[512,768]{1,0:T(8,128)(2,1)} %convolution_convert_fusion.1), channel_id=1, source_target_pairs={{32,0},{33,1},{34,2},{35,3},{36,4},{37,5},{38,6},{39,7},{40,8},{41... | collective-permute-start | bytes 2359304 | tf_op jit(solution)/shard_map/ppermute | solution.py:91
  107.3 10.2 %collective-permute-start.27 = (bf16[768,512]{1,0:T(8,128)(2,1)}, bf16[768,512]{1,0:T(8,128)(2,1)}, u32[]{:S(2)}, u32[]{:S(2)}) collective-permute-start(bf16[768,512]{1,0:T(8,128)(2,1)} %get-tuple-element.2), channel_id=1, source_target_pairs={{0,32},{1,33},{2,34},{3,35},{36,4},{37,5},{38,6},{39,7},{72,104},{... | collective-permute-start | bytes 2359304 | tf_op jit(solution)/shard_map/ppermute | solution.py:86
  108.8 10.2 %collective-permute-start.26 = (bf16[768,512]{1,0:T(8,128)(2,1)}, bf16[768,512]{1,0:T(8,128)(2,1)}, u32[]{:S(2)}, u32[]{:S(2)}) collective-permute-start(bf16[768,512]{1,0:T(8,128)(2,1)} %get-tuple-element.4), channel_id=1, source_target_pairs={{0,160},{1,161},{2,162},{3,163},{36,164},{37,165},{38,166},{39,167... | collective-permute-start | bytes 2359304 | tf_op jit(solution)/shard_map/ppermute | solution.py:80
  113.0 13.5 %collective-permute-start.19 = (bf16[128,768]{1,0:T(8,128)(2,1)S(1)}, bf16[128,768]{1,0:T(8,128)(2,1)S(1)}, u32[]{:S(2)}, u32[]{:S(2)}) collective-permute-start(bf16[128,768]{1,0:T(8,128)(2,1)S(1)} %get-tuple-element.8), channel_id=1, source_target_pairs={{0,192},{64,0},{128,64},{192,128},{1,193},{65,1},{129,65},{193,129... | collective-permute-start | bytes 589832 | tf_op jit(solution)/shard_map/ppermute | solution.py:17
  115.9 12.1 %collective-permute-start.18 = (bf16[128,768]{1,0:T(8,128)(2,1)S(1)}, bf16[128,768]{1,0:T(8,128)(2,1)S(1)}, u32[]{:S(2)}, u32[]{:S(2)}) collective-permute-start(bf16[128,768]{1,0:T(8,128)(2,1)S(1)} %get-tuple-element.7), channel_id=1, source_target_pairs={{0,64},{64,128},{128,192},{192,0},{1,65},{65,129},{129,193},{193,1... | collective-permute-start | bytes 589832 | tf_op jit(solution)/shard_map/ppermute | solution.py:17
  115.9 7.5 %collective-permute-start.17 = (bf16[64,768]{1,0:T(8,128)(2,1)S(1)}, bf16[64,768]{1,0:T(8,128)(2,1)S(1)}, u32[]{:S(2)}, u32[]{:S(2)}) collective-permute-start(bf16[64,768]{1,0:T(8,128)(2,1)S(1)} %get-tuple-element.6), channel_id=1, source_target_pairs={{0,128},{64,192},{128,0},{192,64},{1,129},{65,193},{129,1},{193,65... | collective-permute-start | bytes 294920 | tf_op jit(solution)/shard_map/ppermute | solution.py:17
  117.5 7.4 %collective-permute-start.16 = (bf16[64,768]{1,0:T(8,128)(2,1)S(1)}, bf16[64,768]{1,0:T(8,128)(2,1)S(1)}, u32[]{:S(2)}, u32[]{:S(2)}) collective-permute-start(bf16[64,768]{1,0:T(8,128)(2,1)S(1)} %get-tuple-element.5), channel_id=1, source_target_pairs={{0,128},{64,192},{128,0},{192,64},{1,129},{65,193},{129,1},{193,65... | collective-permute-start | bytes 294920 | tf_op jit(solution)/shard_map/ppermute | solution.py:17
  119.0 11.0 %collective-permute-start.25 = (bf16[768,512]{1,0:T(8,128)(2,1)}, bf16[768,512]{1,0:T(8,128)(2,1)}, u32[]{:S(2)}, u32[]{:S(2)}) collective-permute-start(bf16[768,512]{1,0:T(8,128)(2,1)} %get-tuple-element.4), channel_id=1, source_target_pairs={{0,224},{1,225},{2,226},{3,227},{36,228},{37,229},{38,230},{39,231... | collective-permute-start | bytes 2359304 | tf_op jit(solution)/shard_map/ppermute | solution.py:80
  123.4 6.5 %collective-permute-start.24 = (bf16[768,512]{1,0:T(8,128)(2,1)}, bf16[768,512]{1,0:T(8,128)(2,1)}, u32[]{:S(2)}, u32[]{:S(2)}) collective-permute-start(bf16[768,512]{1,0:T(8,128)(2,1)} %get-tuple-element.4), channel_id=1, source_target_pairs={{0,96},{1,97},{2,98},{3,99},{36,100},{37,101},{38,102},{39,103},{7... | collective-permute-start | bytes 2359304 | tf_op jit(solution)/shard_map/ppermute | solution.py:80
  125.0 5.0 %collective-permute-start.23 = (bf16[768,512]{1,0:T(8,128)(2,1)S(1)}, bf16[768,512]{1,0:T(8,128)(2,1)}, u32[]{:S(2)}, u32[]{:S(2)}) collective-permute-start(bf16[768,512]{1,0:T(8,128)(2,1)S(1)} %get-tuple-element.3), channel_id=1, source_target_pairs={{0,128},{1,129},{2,130},{3,131},{36,132},{37,133},{38,134},{39,135... | collective-permute-start | bytes 2359304 | tf_op jit(solution)/shard_map/ppermute | solution.py:80
  133.5 4.6 %collective-permute-start.29 = (bf16[32,512]{1,0:T(8,128)(2,1)S(1)}, bf16[32,512]{1,0:T(8,128)(2,1)S(1)}, u32[]{:S(2)}, u32[]{:S(2)}) collective-permute-start(bf16[32,512]{1,0:T(8,128)(2,1)S(1)} %get-tuple-element.18), channel_id=1, source_target_pairs={{0,2},{1,3},{2,0},{3,1},{4,6},{5,7},{6,4},{7,5},{8,10},{9,11},{10,... | collective-permute-start | bytes 98312 | tf_op jit(solution)/shard_map/ppermute | solution.py:108
  133.8 4.6 %collective-permute-start.28 = (bf16[32,512]{1,0:T(8,128)(2,1)S(1)}, bf16[32,512]{1,0:T(8,128)(2,1)S(1)}, u32[]{:S(2)}, u32[]{:S(2)}) collective-permute-start(bf16[32,512]{1,0:T(8,128)(2,1)S(1)} %get-tuple-element.16), channel_id=1, source_target_pairs={{0,1},{1,0},{2,3},{3,2},{4,5},{5,4},{6,7},{7,6},{8,9},{9,8},{10,11... | collective-permute-start | bytes 98312 | tf_op jit(solution)/shard_map/ppermute | solution.py:108
  138.4 33.9 %collective-permute-start.33 = (bf16[32,512]{1,0:T(8,128)(2,1)S(1)}, bf16[32,512]{1,0:T(8,128)(2,1)S(1)}, u32[]{:S(2)}, u32[]{:S(2)}) collective-permute-start(bf16[32,512]{1,0:T(8,128)(2,1)S(1)} %fusion.22), channel_id=1, source_target_pairs={{0,12},{4,8},{8,4},{12,0},{16,28},{20,24},{24,20},{28,16},{1,13},{... | collective-permute-start | bytes 98312 | tf_op jit(solution)/shard_map/ppermute | solution.py:108
  150.1 24.8 %collective-permute-start.32 = (bf16[32,512]{1,0:T(8,128)(2,1)S(1)}, bf16[32,512]{1,0:T(8,128)(2,1)S(1)}, u32[]{:S(2)}, u32[]{:S(2)}) collective-permute-start(bf16[32,512]{1,0:T(8,128)(2,1)S(1)} %fusion.22), channel_id=1, source_target_pairs={{0,8},{4,12},{8,0},{12,4},{16,24},{20,28},{24,16},{28,20},{1,9},{5... | collective-permute-start | bytes 98312 | tf_op jit(solution)/shard_map/ppermute | solution.py:108
  175.1 6.9 %collective-permute-start.34 = (bf16[32,512]{1,0:T(8,128)(2,1)S(1)}, bf16[32,512]{1,0:T(8,128)(2,1)S(1)}, u32[]{:S(2)}, u32[]{:S(2)}) collective-permute-start(bf16[32,512]{1,0:T(8,128)(2,1)S(1)} %add_convert_fusion.2), channel_id=1, source_target_pairs={{0,16},{4,20},{8,24},{12,28},{16,0},{20,4},{24,8},{28,12},{1,17},{... | collective-permute-start | bytes 98312 | tf_op jit(solution)/shard_map/ppermute | solution.py:108
  175.3 10.7 %collective-permute-start.20 = (bf16[64,768]{1,0:T(8,128)(2,1)S(1)}, bf16[64,768]{1,0:T(8,128)(2,1)S(1)}, u32[]{:S(2)}, u32[]{:S(2)}) collective-permute-start(bf16[64,768]{1,0:T(8,128)(2,1)S(1)} %dynamic-slice_bitcast_fusion.4), channel_id=1, source_target_pairs={{0,32},{32,0},{1,33},{33,1},{2,34},{34,2},{3,35},{35,3},{4,36},{36... | collective-permute-start | bytes 294920 | tf_op jit(solution)/shard_map/ppermute | solution.py:134
  185.3 4.4 %collective-permute-start.37 = (bf16[32,512]{1,0:T(8,128)(2,1)S(1)}, bf16[32,512]{1,0:T(8,128)(2,1)S(1)}, u32[]{:S(2)}, u32[]{:S(2)}) collective-permute-start(bf16[32,512]{1,0:T(8,128)(2,1)S(1)} %add_convert_fusion.1), channel_id=1, source_target_pairs={{0,3},{1,2},{2,1},{3,0},{4,7},{5,6},{6,5},{7,4},{8,11},{9,10},{10,... | collective-permute-start | bytes 98312 | tf_op jit(solution)/shard_map/ppermute | solution.py:108
  (16 other events, 128.9 us)
Sparse Core Ops, SparseCore 0:
  19.5 59.9 all-gather.1

commit v3 on v2

--- a/solution.py
+++ b/solution.py
@@ -53,37 +53,31 @@
     return lax.all_gather(part, "z", axis=0, tiled=True)
 
 
-def panel_z_then_y(piece):
-    part = placed_by_owner(direct_ring(piece[None], "z", ZS), lax.axis_index("z"), 0)
-    whole = placed_by_owner(
-        [g[:, None] for g in relay_ring(part, "y", YS, True)], lax.axis_index("y"), 1
-    )
-    return whole.reshape(-1, piece.shape[-1])
+def chunks_z_then_y(piece):
+    part = placed_by_owner(relay_ring(piece[None], "z", ZS, False), lax.axis_index("z"), 0)
+    return [g[:, None] for g in relay_ring(part, "y", YS, True)]
 
 
 def device(x, core, z, y):
     return ((x * CORES + core) * ZS + z) * YS + y
 
 
-def to_cores(own_slabs):
-    x, core, z = lax.axis_index("x"), lax.axis_index("core"), lax.axis_index("z")
-    home = (x == z // CORES) & (core == z % CORES)
-    total = jnp.where(home, jnp.where(core == 0, own_slabs[0], own_slabs[1]), jnp.zeros((), BF16))
-    across = jnp.where(core == 0, own_slabs[1], own_slabs[0])
-    pairs = lambda by, s: [
-        (device(r // CORES, r % CORES, r, y), device((r // CORES + by) % XS, s, r, y))
-        for r in range(ZS)
-        for y in range(YS)
-    ]
-    for s, shifts in ((0, (1, -1, 2)), (1, (1, -1, -2))):
-        for by in shifts:
-            total = total + lax.ppermute(own_slabs[s], ALL, pairs(by, s))
-    swapped = [
-        (device(r // CORES, r % CORES, r, y), device(r // CORES, 1 - r % CORES, r, y))
-        for r in range(ZS)
-        for y in range(YS)
-    ]
-    return total + lax.ppermute(across, ALL, swapped)
+def along_x(array, by, inward):
+    pairs = []
+    for core in range(CORES):
+        for z in range(ZS):
+            for y in range(YS):
+                root = device(z // CORES, core, z, y)
+                other = device((z // CORES + by) % XS, core, z, y)
+                pairs.append((other, root) if inward else (root, other))
+    return lax.ppermute(array, ALL, pairs)
+
+
+def along_x_far(array, inward):
+    half = array.shape[0] // 2
+    return jnp.concatenate(
+        [along_x(array[:half], 2, inward), along_x(array[half:], -2, inward)], axis=0
+    )
 
 
 def sum_over_row(partial):
@@ -104,26 +98,12 @@
     return (tile(0).astype(F32) + opposite.astype(F32)) + near
 
 
-def exchanged(array, axis, size, by):
-    return lax.ppermute(array, axis, [(i, i ^ by) for i in range(size)])
-
-
 def summed_over_col(array):
-    y = lax.axis_index("y")
-    quarters = array.reshape(YS, -1, array.shape[1])
-    own = lambda k: lax.dynamic_index_in_dim(quarters, y ^ k, 0, keepdims=False)
-    wide = [own(0)] + [exchanged(own(k), "y", YS, k) for k in range(1, YS)]
-    wide = [w.astype(F32) for w in wide]
-    part = lax.optimization_barrier(((wide[0] + wide[1]) + (wide[2] + wide[3])).astype(BF16))
-    wide = [part.astype(F32)] + [exchanged(part, "z", ZS, k).astype(F32) for k in range(1, 4)]
-    part = lax.optimization_barrier(((wide[0] + wide[1]) + (wide[2] + wide[3])).astype(BF16))
-    part = part.astype(F32) + exchanged(part, "z", ZS, 4).astype(F32)
-    part = lax.optimization_barrier(part.astype(BF16))
-    whole = jnp.zeros(quarters.shape, BF16)
-    for k in range(YS):
-        got = part if k == 0 else exchanged(part, "y", YS, k)
-        whole = lax.dynamic_update_slice_in_dim(whole, got[None], y ^ k, 0)
-    return whole.reshape(array.shape)
+    shares = array.reshape(ZS * YS, -1, array.shape[1])
+    mine = lax.all_to_all(shares, COL, split_axis=0, concat_axis=0, tiled=True)
+    mine = mine.astype(F32).sum(axis=0).astype(BF16)
+    copies = jnp.broadcast_to(mine[None], shares.shape)
+    return lax.all_to_all(copies, COL, split_axis=0, concat_axis=0, tiled=True).reshape(array.shape)
 
 
 def own_slab_of_both(array):
@@ -139,7 +119,7 @@
     piece_rows, width = pieces.shape[1:]
     row = lax.axis_index(ROW)
     col = lax.axis_index(COL)
-    core, y = lax.axis_index("core"), lax.axis_index("y")
+    core, z, y = lax.axis_index("core"), lax.axis_index("z"), lax.axis_index("y")
     chosen = listing[:, :NSEL]
 
     def keep_of(first, count):
@@ -149,22 +129,36 @@
     own_keep = keep_of((row * ZS * YS + col) * piece_rows, piece_rows)
     normed = jnp.einsum("srk,skj->srj", pieces, factor_inv, preferred_element_type=F32)
     normed = (normed * own_keep[:, :, None]).astype(BF16)
-    panels = [panel_y_then_z(normed[0]), panel_z_then_y(normed[1])]
+    rows = inverse_block.shape[0]
 
-    rows = inverse_block.shape[0]
-    partial = [
-        jnp.einsum("qj,pq->jp", panel, inverse_block, preferred_element_type=F32).astype(BF16)
-        for panel in panels
-    ]
-    factor_slab = to_cores(
-        [lax.dynamic_slice_in_dim(panel, y * rows, rows, 0) for panel in panels]
+    def partial_of(panel):
+        return jnp.einsum("qj,pq->jp", panel, inverse_block, preferred_element_type=F32).astype(BF16)
+
+    chunks = chunks_z_then_y(normed[1])
+    panels = [panel_y_then_z(normed[0])]
+    partial = [partial_of(panels[0])]
+    partial[0], chunks = lax.optimization_barrier((partial[0], chunks))
+    panels.append(placed_by_owner(chunks, y, 1).reshape(panels[0].shape))
+    partial.append(partial_of(panels[1]))
+
+    slabs = [lax.dynamic_slice_in_dim(panel, y * rows, rows, 0) for panel in panels]
+    across = lax.ppermute(
+        jnp.where(core == 0, slabs[1], slabs[0]), "core", [(0, 1), (1, 0)]
     )
+    holder = core == z % CORES
+    factor_slab = jnp.where(holder, jnp.where(core == 0, slabs[0], slabs[1]), across)
+
     product = sum_over_row(partial)
     col_keep = lax.dynamic_index_in_dim(keep_of(col * rows, rows), core, 0)
     offdiag = lax.optimization_barrier((-(product * col_keep)).astype(BF16))
 
-    term = -jnp.dot(offdiag, factor_slab, preferred_element_type=F32)
-    correction = own_slab_of_both(summed_over_col(term.astype(BF16)))
+    tiles = [offdiag, along_x(offdiag, 1, True), along_x_far(offdiag, True), along_x(offdiag, -1, True)]
+    terms = -jnp.dot(jnp.concatenate(tiles, axis=0), factor_slab, preferred_element_type=F32)
+    terms = lax.optimization_barrier(terms.astype(BF16)).reshape(XS, -1, width)
+    term = jnp.where(lax.axis_index("x") == z // CORES, terms[0], jnp.zeros((), BF16))
+    term = term + along_x(terms[1], 1, False) + along_x_far(terms[2], False)
+    term = term + along_x(terms[3], -1, False)
+    correction = own_slab_of_both(summed_over_col(term))
     return (
         own_slab_of_both(offdiag).transpose(0, 2, 1),
         diag_inv + correction.astype(F32).transpose(0, 2, 1),

time: 205 us -> 183 us (0.89); the launches traced: 201 us -> 183 us
  starting transfers between devices: 98.1 us -> 81.4 us
  local copies, waits for them, and re-layouts: 6.21 us -> 9.14 us
    ppermute x17 -> x9, starting transfers between devices: 52 us -> 13.4 us  [the longest x8 10.7 us: along_x(): return lax.ppermute(array, ALL, pairs)]
    all_to_all x0 -> x2, starting transfers between devices: none -> 15.6 us  [the longest x1 10.5 us: summed_over_col(): mine = lax.all_to_all(shares, COL, split_axis=0, concat_axis=0, tiled=True)]
    all_to_all x0 -> x2, waiting for transfers between devices: none -> 13.7 us  [the longest x1 9.3 us: summed_over_col(): lax.all_to_all(copies, COL, split_axis=0, concat_axis=0, tiled=True)]
    ppermute x18, waiting for transfers between devices: 45.5 us -> 36.2 us  [shift(): lax.ppermute(array, axis, [(i, (i + by) % size) for i in range(size)])]
    ppermute x2, starting transfers between devices: 2.81 us -> 11 us  [own_slab_of_both(): got = lax.ppermute(given, 'core', [(0, 1), (1, 0)])]
    ppermute x17 -> x9, waiting for transfers between devices: 14.7 us -> 7.34 us  [the longest x8 7.34 us: along_x(): return lax.ppermute(array, ALL, pairs)]
    ppermute x18, starting transfers between devices: 33.4 us -> 28.4 us  [shift(): lax.ppermute(array, axis, [(i, (i + by) % size) for i in range(size)])]
    ppermute x1, starting transfers between devices: 8.56 us -> 11.7 us  [sum_over_row(): lax.ppermute(partial[0], 'core', [(1, 0)]).astype(F32)]
  transfers between devices with their start and end apart: 40 -> 34, of which waited for: 18 -> 17; matrix products, arithmetic and copies ran while one was open for 8% -> 3% of each run, Pallas kernels for 0% -> 0%
where the time goes in v3:
time: 183 us
  starting transfers between devices  81.4 us (44%)
  waiting for transfers between devices  59.3 us (32%)
  between operations  14.8 us (8%)
  matrix products  12.5 us (7%)
  local copies, waits for them, and re-layouts  9.14 us (5%)
  other arithmetic  5.68 us (3%)
    ppermute x18, waiting for transfers between devices, shift(): lax.ppermute(array, axis, [(i, (i + by) % size) for i in range(size)])  36.2 us
    ppermute x18, starting transfers between devices, shift(): lax.ppermute(array, axis, [(i, (i + by) % size) for i in range(size)])  28.4 us
    ppermute x1, starting transfers between devices, sum_over_row(): lax.ppermute(partial[0], 'core', [(1, 0)]).astype(F32)  11.7 us
    ppermute x2, starting transfers between devices, own_slab_of_both(): got = lax.ppermute(given, 'core', [(0, 1), (1, 0)])  11 us
    ppermute x8, starting transfers between devices, along_x(): return lax.ppermute(array, ALL, pairs)  10.7 us
    all_to_all x1, starting transfers between devices, summed_over_col(): mine = lax.all_to_all(shares, COL, split_axis=0, concat_axis=0, tiled=True)  10.5 us
    dot_general x2, matrix products, partial_of(): jnp.einsum('qj,pq->jp', panel, inverse_block, preferred_element_type=F32)  9.48 us
    all_to_all x1, waiting for transfers between devices, summed_over_col(): lax.all_to_all(copies, COL, split_axis=0, concat_axis=0, tiled=True)  9.3 us
  transfers between devices with their start and end apart: 34, of which 17 were waited for; matrix products, arithmetic and copies ran while one was open for 3% of the time, Pallas kernels for 0%

profile of v3, /device:TPU:1, one launch (start us, length us, event | category | flops | bytes accessed | tf_op | source)
XLA Modules:
  0.0 182.8 jit_solution(6671919035976353792)
XLA Ops:
  9.7 2.2 %collective-permute-start = (bf16[96,512]{1,0:T(8,128)(2,1)S(1)}, bf16[96,512]{1,0:T(8,128)(2,1)S(1)}, u32[]{:S(2)}, u32[]{:S(2)}) collective-permute-start(bf16[96,512]{1,0:T(8,128)(2,1)S(1)} %get-tuple-element.28), channel_id=1, source_target_pairs={{0,1},{1,2},{2,3},{3,0},{4,5},{5,6},{6,7},{7,4},{8,9},{9,10},{10,1... | collective-permute-start | bytes 294920 | tf_op jit(solution)/shard_map/ppermute | solution.py:17
  12.0 2.6 %collective-permute-start.1 = (bf16[96,512]{1,0:T(8,128)(2,1)S(1)}, bf16[96,512]{1,0:T(8,128)(2,1)S(1)}, u32[]{:S(2)}, u32[]{:S(2)}) collective-permute-start(bf16[96,512]{1,0:T(8,128)(2,1)S(1)} %get-tuple-element.28), channel_id=1, source_target_pairs={{0,2},{1,3},{2,0},{3,1},{4,6},{5,7},{6,4},{7,5},{8,10},{9,11},{10,... | collective-permute-start | bytes 294920 | tf_op jit(solution)/shard_map/ppermute | solution.py:17
  15.8 2.8 %collective-permute-done.1 = bf16[96,512]{1,0:T(8,128)(2,1)S(1)} collective-permute-done((bf16[96,512]{1,0:T(8,128)(2,1)S(1)}, bf16[96,512]{1,0:T(8,128)(2,1)S(1)}, u32[]{:S(2)}, u32[]{:S(2)}) %collective-permute-start.1) | collective-permute-done | bytes 98336 | tf_op jit(solution)/shard_map/ppermute | solution.py:17
  19.4 1.7 collective-permute-start.3
  21.1 4.0 %collective-permute-start.7 = (bf16[1,96,512]{2,1,0:T(8,128)(2,1)S(1)}, bf16[1,96,512]{2,1,0:T(8,128)(2,1)S(1)}, u32[]{:S(2)}, u32[]{:S(2)}) collective-permute-start(bf16[1,96,512]{2,1,0:T(8,128)(2,1)S(1)} %get-tuple-element.26), channel_id=1, source_target_pairs={{0,28},{4,0},{8,4},{12,8},{16,12},{20,16},{24,20},{28,24},{1,29},{... | collective-permute-start | bytes 294920 | tf_op jit(solution)/shard_map/ppermute | solution.py:17
  25.2 1.9 %collective-permute-done.3 = bf16[1,96,512]{2,1,0:T(8,128)(2,1)S(1)} collective-permute-done((bf16[1,96,512]{2,1,0:T(8,128)(2,1)S(1)}, bf16[1,96,512]{2,1,0:T(8,128)(2,1)S(1)}, u32[]{:S(2)}, u32[]{:S(2)}) %collective-permute-start.3) | collective-permute-done | bytes 98336 | tf_op jit(solution)/shard_map/ppermute | solution.py:17
  27.1 2.8 %collective-permute-start.8 = (bf16[1,96,512]{2,1,0:T(8,128)(2,1)S(1)}, bf16[1,96,512]{2,1,0:T(8,128)(2,1)S(1)}, u32[]{:S(2)}, u32[]{:S(2)}) collective-permute-start(bf16[1,96,512]{2,1,0:T(8,128)(2,1)S(1)} %collective-permute-done.7), channel_id=1, source_target_pairs={{0,28},{4,0},{8,4},{12,8},{16,12},{20,16},{24,20},{28,24},{1,29},{... | collective-permute-start | bytes 294920 | tf_op jit(solution)/shard_map/ppermute | solution.py:17
  29.9 1.9 %collective-permute-done.4 = bf16[1,96,512]{2,1,0:T(8,128)(2,1)S(1)} collective-permute-done((bf16[1,96,512]{2,1,0:T(8,128)(2,1)S(1)}, bf16[1,96,512]{2,1,0:T(8,128)(2,1)S(1)}, u32[]{:S(2)}, u32[]{:S(2)}) %collective-permute-start.4) | collective-permute-done | bytes 98336 | tf_op jit(solution)/shard_map/ppermute | solution.py:17
  31.8 2.8 %collective-permute-start.9 = (bf16[1,96,512]{2,1,0:T(8,128)(2,1)S(1)}, bf16[1,96,512]{2,1,0:T(8,128)(2,1)S(1)}, u32[]{:S(2)}, u32[]{:S(2)}) collective-permute-start(bf16[1,96,512]{2,1,0:T(8,128)(2,1)S(1)} %collective-permute-done.8), channel_id=1, source_target_pairs={{0,28},{4,0},{8,4},{12,8},{16,12},{20,16},{24,20},{28,24},{1,29},{... | collective-permute-start | bytes 294920 | tf_op jit(solution)/shard_map/ppermute | solution.py:17
  34.5 1.9 %collective-permute-done.5 = bf16[1,96,512]{2,1,0:T(8,128)(2,1)S(1)} collective-permute-done((bf16[1,96,512]{2,1,0:T(8,128)(2,1)S(1)}, bf16[1,96,512]{2,1,0:T(8,128)(2,1)S(1)}, u32[]{:S(2)}, u32[]{:S(2)}) %collective-permute-start.5) | collective-permute-done | bytes 98336 | tf_op jit(solution)/shard_map/ppermute | solution.py:17
  36.5 8.0 %collective-permute-done.6 = bf16[1,96,512]{2,1,0:T(8,128)(2,1)S(1)} collective-permute-done((bf16[1,96,512]{2,1,0:T(8,128)(2,1)S(1)}, bf16[1,96,512]{2,1,0:T(8,128)(2,1)S(1)}, u32[]{:S(2)}, u32[]{:S(2)}) %collective-permute-start.6) | collective-permute-done | bytes 98336 | tf_op jit(solution)/shard_map/ppermute | solution.py:17
  45.3 2.1 %collective-permute-start.12 = (bf16[8,96,512]{2,1,0:T(8,128)(2,1)S(1)}, bf16[8,96,512]{2,1,0:T(8,128)(2,1)S(1)}, u32[]{:S(2)}, u32[]{:S(2)}) collective-permute-start(bf16[8,96,512]{2,1,0:T(8,128)(2,1)S(1)} %constant_dynamic-update-slice_fusion.9), channel_id=1, source_target_pairs={{0,3},{1,0},{2,1},{3,2},{4,7},{5,4},{6,5},{7,6},{8,11},{9,8},{10,9... | collective-permute-start | bytes 2359304 | tf_op jit(solution)/shard_map/ppermute | solution.py:17
  47.3 9.9 %collective-permute-done.10 = bf16[8,96,512]{2,1,0:T(8,128)(2,1)S(1)} collective-permute-done((bf16[8,96,512]{2,1,0:T(8,128)(2,1)S(1)}, bf16[8,96,512]{2,1,0:T(8,128)(2,1)S(1)}, u32[]{:S(2)}, u32[]{:S(2)}) %collective-permute-start.10) | collective-permute-done | bytes 786464 | tf_op jit(solution)/shard_map/ppermute | solution.py:17
  58.8 2.7 %collective-permute-start.13 = (bf16[4,96,512]{2,1,0:T(8,128)(2,1)}, bf16[4,96,512]{2,1,0:T(8,128)(2,1)}, u32[]{:S(2)}, u32[]{:S(2)}) collective-permute-start(bf16[4,96,512]{2,1,0:T(8,128)(2,1)} %slice.75), channel_id=1, source_target_pairs={{0,3},{1,0},{2,1},{3,2},{4,7},{5,4},{6,5},{7,6},{8,11},{9,8},{10,9... | collective-permute-start | bytes 1179656 | tf_op jit(solution)/shard_map/ppermute | solution.py:17
  61.5 8.2 %collective-permute-done.11 = bf16[4,96,512]{2,1,0:T(8,128)(2,1)} collective-permute-done((bf16[4,96,512]{2,1,0:T(8,128)(2,1)}, bf16[4,96,512]{2,1,0:T(8,128)(2,1)}, u32[]{:S(2)}, u32[]{:S(2)}) %collective-permute-start.11) | collective-permute-done | bytes 393248 | tf_op jit(solution)/shard_map/ppermute | solution.py:17
  71.0 6.8 %convolution_convert_fusion.1 = bf16[512,768]{1,0:T(8,128)(2,1)} fusion(bf16[3072,512]{1,0:T(8,128)(2,1)} %all-gather.2.cloned.1.call-done, bf16[768,3072]{1,0:T(8,128)(2,1)} %param.8), kind=kOutput, calls=%fused_computation.2 | convolution fusion | flops 2416312320 | bytes 8650752 | tf_op jit(solution)/shard_map/qj,pq->jp/dot_general | solution.py:135
  79.5 2.8 %slice-done = s8[4194304]{0:T(1024)(128)(4,1)S(1)} async-done(((s8[4718592]{0:T(1024)(128)(4,1)}), s8[4194304]{0:T(1024)(128)(4,1)S(1)}, s32[]{:S(2)}) %slice-start) | async-done | bytes 4194328
  82.5 2.7 %convolution_convert_fusion = bf16[512,768]{1,0:T(8,128)(2,1)S(1)} fusion(bf16[3072,512]{1,0:T(8,128)(2,1)S(1)} %bitcast.61, bf16[768,3072]{1,0:T(8,128)(2,1)S(1)} %bitcast.75), kind=kOutput, calls=%fused_computation.1 | convolution fusion | flops 2416312320 | bytes 8650752 | tf_op jit(solution)/shard_map/qj,pq->jp/dot_general | solution.py:135
  86.4 11.7 %collective-permute-start.14 = (bf16[512,768]{1,0:T(8,128)(2,1)}, bf16[512,768]{1,0:T(8,128)(2,1)S(1)}, u32[]{:S(2)}, u32[]{:S(2)}) collective-permute-start(bf16[512,768]{1,0:T(8,128)(2,1)} %convolution_convert_fusion.1), channel_id=1, source_target_pairs={{32,0},{33,1},{34,2},{35,3},{36,4},{37,5},{38,6},{39,7},{40,8},{41... | collective-permute-start | bytes 2359304 | tf_op jit(solution)/shard_map/ppermute | solution.py:85
  98.4 1.8 collective-permute-done.14
  103.4 1.6 collective-permute-start.16
  107.8 2.7 %collective-permute-start.25 = (bf16[768,512]{1,0:T(8,128)(2,1)S(1)}, bf16[768,512]{1,0:T(8,128)(2,1)S(1)}, u32[]{:S(2)}, u32[]{:S(2)}) collective-permute-start(bf16[768,512]{1,0:T(8,128)(2,1)S(1)} %broadcast_select_fusion), channel_id=1, source_target_pairs={{0,32},{32,0},{1,33},{33,1},{2,34},{34,2},{3,35},{35,3},{4,36},{36... | collective-permute-start | bytes 2359304 | tf_op jit(solution)/shard_map/ppermute | solution.py:145
  110.5 1.5 collective-permute-done.17
  118.6 3.2 %collective-permute-done.22 = bf16[64,768]{1,0:T(8,128)(2,1)S(1)} collective-permute-done((bf16[64,768]{1,0:T(8,128)(2,1)S(1)}, bf16[64,768]{1,0:T(8,128)(2,1)S(1)}, u32[]{:S(2)}, u32[]{:S(2)}) %collective-permute-start.22) | collective-permute-done | bytes 98336 | tf_op jit(solution)/shard_map/ppermute | solution.py:73
  123.8 1.8 fusion
  129.7 1.5 collective-permute-start.28
  133.1 10.5 %all-to-all-start = ((bf16[32,4,512]{2,1,0:T(4,128)(2,1)}), bf16[32,4,512]{2,1,0:T(4,128)(2,1)S(1)}, u32[]{:S(2)}, u32[]{:S(2)}) async-start(bf16[32,4,512]{2,1,0:T(4,128)(2,1)} %reshape.76), calls=%async_computation | async-start | bytes 262144 | tf_op jit(solution)/shard_map/all_to_all | solution.py:103
  143.6 5.0 %collective-permute-start.20 = (bf16[64,768]{1,0:T(8,128)(2,1)S(1)}, bf16[64,768]{1,0:T(8,128)(2,1)S(1)}, u32[]{:S(2)}, u32[]{:S(2)}) collective-permute-start(bf16[64,768]{1,0:T(8,128)(2,1)S(1)} %dynamic-slice_bitcast_fusion.4), channel_id=1, source_target_pairs={{0,32},{32,0},{1,33},{33,1},{2,34},{34,2},{3,35},{35,3},{4,36},{36... | collective-permute-start | bytes 294920 | tf_op jit(solution)/shard_map/ppermute | solution.py:114
  148.5 4.4 %all-to-all-done = bf16[32,4,512]{2,1,0:T(4,128)(2,1)S(1)} async-done(((bf16[32,4,512]{2,1,0:T(4,128)(2,1)}), bf16[32,4,512]{2,1,0:T(4,128)(2,1)S(1)}, u32[]{:S(2)}, u32[]{:S(2)}) %all-to-all-start) | async-done | bytes 131104 | tf_op jit(solution)/shard_map/all_to_all | solution.py:103
  153.7 5.1 %all-to-all-start.1 = ((bf16[32,4,512]{2,1,0:T(4,128)(2,1)}), bf16[32,4,512]{2,1,0:T(4,128)(2,1)S(1)}, u32[]{:S(2)}, u32[]{:S(2)}) async-start(bf16[32,4,512]{2,1,0:T(4,128)(2,1)} %broadcast_in_dim.44), calls=%async_computation.1 | async-start | bytes 262144 | tf_op jit(solution)/shard_map/all_to_all | solution.py:106
  158.9 9.3 %all-to-all-done.1 = bf16[32,4,512]{2,1,0:T(4,128)(2,1)S(1)} async-done(((bf16[32,4,512]{2,1,0:T(4,128)(2,1)}), bf16[32,4,512]{2,1,0:T(4,128)(2,1)S(1)}, u32[]{:S(2)}, u32[]{:S(2)}) %all-to-all-start.1) | async-done | bytes 131104 | tf_op jit(solution)/shard_map/all_to_all | solution.py:106
  168.2 6.0 %collective-permute-start.30 = (bf16[64,512]{1,0:T(8,128)(2,1)S(1)}, bf16[64,512]{1,0:T(8,128)(2,1)S(1)}, u32[]{:S(2)}, u32[]{:S(2)}) collective-permute-start(bf16[64,512]{1,0:T(8,128)(2,1)S(1)} %dynamic-slice_bitcast_fusion.5), channel_id=1, source_target_pairs={{0,32},{32,0},{1,33},{33,1},{2,34},{34,2},{3,35},{35,3},{4,36},{36... | collective-permute-start | bytes 196616 | tf_op jit(solution)/shard_map/ppermute | solution.py:114
  (115 shorter events, 34.2 us)
Async XLA Ops:
  7.2 63.8 %all-gather.2.cloned.1.call-start = ((), (), s32[]{:S(2)}) async-start(), calls=%async_computation.2 | async-start | bytes 3538944 | tf_op jit(solution)/shard_map/all_gather | solution.py:53
  9.7 6.0 %collective-permute-start = (bf16[96,512]{1,0:T(8,128)(2,1)S(1)}, bf16[96,512]{1,0:T(8,128)(2,1)S(1)}, u32[]{:S(2)}, u32[]{:S(2)}) collective-permute-start(bf16[96,512]{1,0:T(8,128)(2,1)S(1)} %get-tuple-element.28), channel_id=1, source_target_pairs={{0,1},{1,2},{2,3},{3,0},{4,5},{5,6},{6,7},{7,4},{8,9},{9,10},{10,1... | collective-permute-start | bytes 294920 | tf_op jit(solution)/shard_map/ppermute | solution.py:17
  12.0 6.6 %collective-permute-start.1 = (bf16[96,512]{1,0:T(8,128)(2,1)S(1)}, bf16[96,512]{1,0:T(8,128)(2,1)S(1)}, u32[]{:S(2)}, u32[]{:S(2)}) collective-permute-start(bf16[96,512]{1,0:T(8,128)(2,1)S(1)} %get-tuple-element.28), channel_id=1, source_target_pairs={{0,2},{1,3},{2,0},{3,1},{4,6},{5,7},{6,4},{7,5},{8,10},{9,11},{10,... | collective-permute-start | bytes 294920 | tf_op jit(solution)/shard_map/ppermute | solution.py:17
  14.6 4.0 %collective-permute-start.2 = (bf16[96,512]{1,0:T(8,128)(2,1)S(1)}, bf16[96,512]{1,0:T(8,128)(2,1)S(1)}, u32[]{:S(2)}, u32[]{:S(2)}) collective-permute-start(bf16[96,512]{1,0:T(8,128)(2,1)S(1)} %get-tuple-element.28), channel_id=1, source_target_pairs={{0,3},{1,0},{2,1},{3,2},{4,7},{5,4},{6,5},{7,6},{8,11},{9,8},{10,9... | collective-permute-start | bytes 294920 | tf_op jit(solution)/shard_map/ppermute | solution.py:17
  19.4 7.7 %collective-permute-start.3 = (bf16[1,96,512]{2,1,0:T(8,128)(2,1)S(1)}, bf16[1,96,512]{2,1,0:T(8,128)(2,1)S(1)}, u32[]{:S(2)}, u32[]{:S(2)}) collective-permute-start(bf16[1,96,512]{2,1,0:T(8,128)(2,1)S(1)} %get-tuple-element.26), channel_id=1, source_target_pairs={{0,4},{4,8},{8,12},{12,16},{16,20},{20,24},{24,28},{28,0},{1,5},{5... | collective-permute-start | bytes 294920 | tf_op jit(solution)/shard_map/ppermute | solution.py:17
  21.1 6.0 %collective-permute-start.7 = (bf16[1,96,512]{2,1,0:T(8,128)(2,1)S(1)}, bf16[1,96,512]{2,1,0:T(8,128)(2,1)S(1)}, u32[]{:S(2)}, u32[]{:S(2)}) collective-permute-start(bf16[1,96,512]{2,1,0:T(8,128)(2,1)S(1)} %get-tuple-element.26), channel_id=1, source_target_pairs={{0,28},{4,0},{8,4},{12,8},{16,12},{20,16},{24,20},{28,24},{1,29},{... | collective-permute-start | bytes 294920 | tf_op jit(solution)/shard_map/ppermute | solution.py:17
  27.1 4.7 %collective-permute-start.4 = (bf16[1,96,512]{2,1,0:T(8,128)(2,1)S(1)}, bf16[1,96,512]{2,1,0:T(8,128)(2,1)S(1)}, u32[]{:S(2)}, u32[]{:S(2)}) collective-permute-start(bf16[1,96,512]{2,1,0:T(8,128)(2,1)S(1)} %collective-permute-done.3), channel_id=1, source_target_pairs={{0,4},{4,8},{8,12},{12,16},{16,20},{20,24},{24,28},{28,0},{1,5},{5... | collective-permute-start | bytes 294920 | tf_op jit(solution)/shard_map/ppermute | solution.py:17
  27.1 4.7 %collective-permute-start.8 = (bf16[1,96,512]{2,1,0:T(8,128)(2,1)S(1)}, bf16[1,96,512]{2,1,0:T(8,128)(2,1)S(1)}, u32[]{:S(2)}, u32[]{:S(2)}) collective-permute-start(bf16[1,96,512]{2,1,0:T(8,128)(2,1)S(1)} %collective-permute-done.7), channel_id=1, source_target_pairs={{0,28},{4,0},{8,4},{12,8},{16,12},{20,16},{24,20},{28,24},{1,29},{... | collective-permute-start | bytes 294920 | tf_op jit(solution)/shard_map/ppermute | solution.py:17
  31.8 4.7 %collective-permute-start.5 = (bf16[1,96,512]{2,1,0:T(8,128)(2,1)S(1)}, bf16[1,96,512]{2,1,0:T(8,128)(2,1)S(1)}, u32[]{:S(2)}, u32[]{:S(2)}) collective-permute-start(bf16[1,96,512]{2,1,0:T(8,128)(2,1)S(1)} %collective-permute-done.4), channel_id=1, source_target_pairs={{0,4},{4,8},{8,12},{12,16},{16,20},{20,24},{24,28},{28,0},{1,5},{5... | collective-permute-start | bytes 294920 | tf_op jit(solution)/shard_map/ppermute | solution.py:17
  31.8 12.7 %collective-permute-start.9 = (bf16[1,96,512]{2,1,0:T(8,128)(2,1)S(1)}, bf16[1,96,512]{2,1,0:T(8,128)(2,1)S(1)}, u32[]{:S(2)}, u32[]{:S(2)}) collective-permute-start(bf16[1,96,512]{2,1,0:T(8,128)(2,1)S(1)} %collective-permute-done.8), channel_id=1, source_target_pairs={{0,28},{4,0},{8,4},{12,8},{16,12},{20,16},{24,20},{28,24},{1,29},{... | collective-permute-start | bytes 294920 | tf_op jit(solution)/shard_map/ppermute | solution.py:17
  36.4 8.1 %collective-permute-start.6 = (bf16[1,96,512]{2,1,0:T(8,128)(2,1)S(1)}, bf16[1,96,512]{2,1,0:T(8,128)(2,1)S(1)}, u32[]{:S(2)}, u32[]{:S(2)}) collective-permute-start(bf16[1,96,512]{2,1,0:T(8,128)(2,1)S(1)} %collective-permute-done.5), channel_id=1, source_target_pairs={{0,4},{4,8},{8,12},{12,16},{16,20},{20,24},{24,28},{28,0},{1,5},{5... | collective-permute-start | bytes 294920 | tf_op jit(solution)/shard_map/ppermute | solution.py:17
  44.6 12.6 %collective-permute-start.10 = (bf16[8,96,512]{2,1,0:T(8,128)(2,1)S(1)}, bf16[8,96,512]{2,1,0:T(8,128)(2,1)S(1)}, u32[]{:S(2)}, u32[]{:S(2)}) collective-permute-start(bf16[8,96,512]{2,1,0:T(8,128)(2,1)S(1)} %constant_dynamic-update-slice_fusion.9), channel_id=1, source_target_pairs={{0,1},{1,2},{2,3},{3,0},{4,5},{5,6},{6,7},{7,4},{8,9},{9,10},{10,1... | collective-permute-start | bytes 2359304 | tf_op jit(solution)/shard_map/ppermute | solution.py:17
  45.3 12.8 %collective-permute-start.12 = (bf16[8,96,512]{2,1,0:T(8,128)(2,1)S(1)}, bf16[8,96,512]{2,1,0:T(8,128)(2,1)S(1)}, u32[]{:S(2)}, u32[]{:S(2)}) collective-permute-start(bf16[8,96,512]{2,1,0:T(8,128)(2,1)S(1)} %constant_dynamic-update-slice_fusion.9), channel_id=1, source_target_pairs={{0,3},{1,0},{2,1},{3,2},{4,7},{5,4},{6,5},{7,6},{8,11},{9,8},{10,9... | collective-permute-start | bytes 2359304 | tf_op jit(solution)/shard_map/ppermute | solution.py:17
  58.1 11.7 %collective-permute-start.11 = (bf16[4,96,512]{2,1,0:T(8,128)(2,1)}, bf16[4,96,512]{2,1,0:T(8,128)(2,1)}, u32[]{:S(2)}, u32[]{:S(2)}) collective-permute-start(bf16[4,96,512]{2,1,0:T(8,128)(2,1)} %slice.74), channel_id=1, source_target_pairs={{0,1},{1,2},{2,3},{3,0},{4,5},{5,6},{6,7},{7,4},{8,9},{9,10},{10,1... | collective-permute-start | bytes 1179656 | tf_op jit(solution)/shard_map/ppermute | solution.py:17
  58.8 10.9 %collective-permute-start.13 = (bf16[4,96,512]{2,1,0:T(8,128)(2,1)}, bf16[4,96,512]{2,1,0:T(8,128)(2,1)}, u32[]{:S(2)}, u32[]{:S(2)}) collective-permute-start(bf16[4,96,512]{2,1,0:T(8,128)(2,1)} %slice.75), channel_id=1, source_target_pairs={{0,3},{1,0},{2,1},{3,2},{4,7},{5,4},{6,5},{7,6},{8,11},{9,8},{10,9... | collective-permute-start | bytes 1179656 | tf_op jit(solution)/shard_map/ppermute | solution.py:17
  85.1 13.3 %collective-permute-start.15 = (bf16[512,768]{1,0:T(8,128)(2,1)S(1)}, bf16[512,768]{1,0:T(8,128)(2,1)S(1)}, u32[]{:S(2)}, u32[]{:S(2)}) collective-permute-start(bf16[512,768]{1,0:T(8,128)(2,1)S(1)} %convolution_convert_fusion), channel_id=1, source_target_pairs={{0,32},{1,33},{2,34},{3,35},{4,36},{5,37},{6,38},{7,39},{8,40},{9,... | collective-permute-start | bytes 2359304 | tf_op jit(solution)/shard_map/ppermute | solution.py:85
  86.4 13.8 %collective-permute-start.14 = (bf16[512,768]{1,0:T(8,128)(2,1)}, bf16[512,768]{1,0:T(8,128)(2,1)S(1)}, u32[]{:S(2)}, u32[]{:S(2)}) collective-permute-start(bf16[512,768]{1,0:T(8,128)(2,1)} %convolution_convert_fusion.1), channel_id=1, source_target_pairs={{32,0},{33,1},{34,2},{35,3},{36,4},{37,5},{38,6},{39,7},{40,8},{41... | collective-permute-start | bytes 2359304 | tf_op jit(solution)/shard_map/ppermute | solution.py:85
  100.6 11.4 %collective-permute-start.18 = (bf16[128,768]{1,0:T(8,128)(2,1)S(1)}, bf16[128,768]{1,0:T(8,128)(2,1)S(1)}, u32[]{:S(2)}, u32[]{:S(2)}) collective-permute-start(bf16[128,768]{1,0:T(8,128)(2,1)S(1)} %get-tuple-element.14), channel_id=1, source_target_pairs={{0,64},{64,128},{128,192},{192,0},{1,65},{65,129},{129,193},{193,1... | collective-permute-start | bytes 589832 | tf_op jit(solution)/shard_map/ppermute | solution.py:17
  101.9 10.1 %collective-permute-start.19 = (bf16[128,768]{1,0:T(8,128)(2,1)S(1)}, bf16[128,768]{1,0:T(8,128)(2,1)S(1)}, u32[]{:S(2)}, u32[]{:S(2)}) collective-permute-start(bf16[128,768]{1,0:T(8,128)(2,1)S(1)} %get-tuple-element.15), channel_id=1, source_target_pairs={{0,192},{64,0},{128,64},{192,128},{1,193},{65,1},{129,65},{193,129... | collective-permute-start | bytes 589832 | tf_op jit(solution)/shard_map/ppermute | solution.py:17
  103.4 7.1 %collective-permute-start.16 = (bf16[64,768]{1,0:T(8,128)(2,1)S(1)}, bf16[64,768]{1,0:T(8,128)(2,1)S(1)}, u32[]{:S(2)}, u32[]{:S(2)}) collective-permute-start(bf16[64,768]{1,0:T(8,128)(2,1)S(1)} %get-tuple-element.12), channel_id=1, source_target_pairs={{0,128},{64,192},{128,0},{192,64},{1,129},{65,193},{129,1},{193,65... | collective-permute-start | bytes 294920 | tf_op jit(solution)/shard_map/ppermute | solution.py:17
  105.1 7.0 %collective-permute-start.17 = (bf16[64,768]{1,0:T(8,128)(2,1)S(1)}, bf16[64,768]{1,0:T(8,128)(2,1)S(1)}, u32[]{:S(2)}, u32[]{:S(2)}) collective-permute-start(bf16[64,768]{1,0:T(8,128)(2,1)S(1)} %get-tuple-element.13), channel_id=1, source_target_pairs={{0,128},{64,192},{128,0},{192,64},{1,129},{65,193},{129,1},{193,65... | collective-permute-start | bytes 294920 | tf_op jit(solution)/shard_map/ppermute | solution.py:17
  107.8 15.9 %collective-permute-start.25 = (bf16[768,512]{1,0:T(8,128)(2,1)S(1)}, bf16[768,512]{1,0:T(8,128)(2,1)S(1)}, u32[]{:S(2)}, u32[]{:S(2)}) collective-permute-start(bf16[768,512]{1,0:T(8,128)(2,1)S(1)} %broadcast_select_fusion), channel_id=1, source_target_pairs={{0,32},{32,0},{1,33},{33,1},{2,34},{34,2},{3,35},{35,3},{4,36},{36... | collective-permute-start | bytes 2359304 | tf_op jit(solution)/shard_map/ppermute | solution.py:145
  112.2 6.4 %collective-permute-start.21 = (bf16[128,768]{1,0:T(8,128)(2,1)S(1)}, bf16[128,768]{1,0:T(8,128)(2,1)S(1)}, u32[]{:S(2)}, u32[]{:S(2)}) collective-permute-start(bf16[128,768]{1,0:T(8,128)(2,1)S(1)} %fusion.11), channel_id=1, source_target_pairs={{64,0},{65,1},{66,2},{67,3},{68,4},{69,5},{70,6},{71,7},{136,72},{... | collective-permute-start | bytes 589832 | tf_op jit(solution)/shard_map/ppermute | solution.py:73
  113.5 10.2 %collective-permute-start.24 = (bf16[128,768]{1,0:T(8,128)(2,1)S(1)}, bf16[128,768]{1,0:T(8,128)(2,1)S(1)}, u32[]{:S(2)}, u32[]{:S(2)}) collective-permute-start(bf16[128,768]{1,0:T(8,128)(2,1)S(1)} %fusion.11), channel_id=1, source_target_pairs={{192,0},{193,1},{194,2},{195,3},{196,4},{197,5},{198,6},{199,7},{8... | collective-permute-start | bytes 589832 | tf_op jit(solution)/shard_map/ppermute | solution.py:73
  114.8 7.0 %collective-permute-start.22 = (bf16[64,768]{1,0:T(8,128)(2,1)S(1)}, bf16[64,768]{1,0:T(8,128)(2,1)S(1)}, u32[]{:S(2)}, u32[]{:S(2)}) collective-permute-start(bf16[64,768]{1,0:T(8,128)(2,1)S(1)} %get-tuple-element.25), channel_id=1, source_target_pairs={{128,0},{129,1},{130,2},{131,3},{132,4},{133,5},{134,6},{135,7},{2... | collective-permute-start | bytes 294920 | tf_op jit(solution)/shard_map/ppermute | solution.py:73
  116.1 6.9 %collective-permute-start.23 = (bf16[64,768]{1,0:T(8,128)(2,1)S(1)}, bf16[64,768]{1,0:T(8,128)(2,1)S(1)}, u32[]{:S(2)}, u32[]{:S(2)}) collective-permute-start(bf16[64,768]{1,0:T(8,128)(2,1)S(1)} %get-tuple-element.24), channel_id=1, source_target_pairs={{128,0},{129,1},{130,2},{131,3},{132,4},{133,5},{134,6},{135,7},{2... | collective-permute-start | bytes 294920 | tf_op jit(solution)/shard_map/ppermute | solution.py:73
  125.6 6.7 %collective-permute-start.26 = (bf16[128,512]{1,0:T(8,128)(2,1)S(1)}, bf16[128,512]{1,0:T(8,128)(2,1)S(1)}, u32[]{:S(2)}, u32[]{:S(2)}) collective-permute-start(bf16[128,512]{1,0:T(8,128)(2,1)S(1)} %get-tuple-element.18), channel_id=1, source_target_pairs={{0,64},{1,65},{2,66},{3,67},{4,68},{5,69},{6,70},{7,71},{72,136},{... | collective-permute-start | bytes 393224 | tf_op jit(solution)/shard_map/ppermute | solution.py:73
  127.1 5.2 %collective-permute-start.29 = (bf16[128,512]{1,0:T(8,128)(2,1)S(1)}, bf16[128,512]{1,0:T(8,128)(2,1)S(1)}, u32[]{:S(2)}, u32[]{:S(2)}) collective-permute-start(bf16[128,512]{1,0:T(8,128)(2,1)S(1)} %get-tuple-element.19), channel_id=1, source_target_pairs={{0,192},{1,193},{2,194},{3,195},{4,196},{5,197},{6,198},{7,199},{7... | collective-permute-start | bytes 393224 | tf_op jit(solution)/shard_map/ppermute | solution.py:73
  133.1 19.8 %all-to-all-start = ((bf16[32,4,512]{2,1,0:T(4,128)(2,1)}), bf16[32,4,512]{2,1,0:T(4,128)(2,1)S(1)}, u32[]{:S(2)}, u32[]{:S(2)}) async-start(bf16[32,4,512]{2,1,0:T(4,128)(2,1)} %reshape.76), calls=%async_computation | async-start | bytes 262144 | tf_op jit(solution)/shard_map/all_to_all | solution.py:103
  143.6 15.2 %collective-permute-start.20 = (bf16[64,768]{1,0:T(8,128)(2,1)S(1)}, bf16[64,768]{1,0:T(8,128)(2,1)S(1)}, u32[]{:S(2)}, u32[]{:S(2)}) collective-permute-start(bf16[64,768]{1,0:T(8,128)(2,1)S(1)} %dynamic-slice_bitcast_fusion.4), channel_id=1, source_target_pairs={{0,32},{32,0},{1,33},{33,1},{2,34},{34,2},{3,35},{35,3},{4,36},{36... | collective-permute-start | bytes 294920 | tf_op jit(solution)/shard_map/ppermute | solution.py:114
  153.7 14.5 %all-to-all-start.1 = ((bf16[32,4,512]{2,1,0:T(4,128)(2,1)}), bf16[32,4,512]{2,1,0:T(4,128)(2,1)S(1)}, u32[]{:S(2)}, u32[]{:S(2)}) async-start(bf16[32,4,512]{2,1,0:T(4,128)(2,1)} %broadcast_in_dim.44), calls=%async_computation.1 | async-start | bytes 262144 | tf_op jit(solution)/shard_map/all_to_all | solution.py:106
  168.2 6.9 %collective-permute-start.30 = (bf16[64,512]{1,0:T(8,128)(2,1)S(1)}, bf16[64,512]{1,0:T(8,128)(2,1)S(1)}, u32[]{:S(2)}, u32[]{:S(2)}) collective-permute-start(bf16[64,512]{1,0:T(8,128)(2,1)S(1)} %dynamic-slice_bitcast_fusion.5), channel_id=1, source_target_pairs={{0,32},{32,0},{1,33},{33,1},{2,34},{34,2},{3,35},{35,3},{4,36},{36... | collective-permute-start | bytes 196616 | tf_op jit(solution)/shard_map/ppermute | solution.py:114
  (12 other events, 107.0 us)
Sparse Core Ops, SparseCore 0:
  19.5 51.3 all-gather.1

commit v4 on v3

--- a/solution.py
+++ b/solution.py
@@ -53,30 +53,40 @@
     return lax.all_gather(part, "z", axis=0, tiled=True)
 
 
-def chunks_z_then_y(piece):
-    part = placed_by_owner(relay_ring(piece[None], "z", ZS, False), lax.axis_index("z"), 0)
-    return [g[:, None] for g in relay_ring(part, "y", YS, True)]
+def near_z_then_y(piece):
+    part = placed_by_owner(relay_ring(piece[None], "z", ZS, False), lax.axis_index("z"), 0)[:, None]
+    return [part, shift(part, "y", YS, 1), shift(part, "y", YS, -1)]
+
+
+def far_chunk(near):
+    half = near[0].shape[0] // 2
+    right = shift(near[1][:half], "y", YS, 1)
+    return jnp.concatenate([right, shift(near[2][half:], "y", YS, -1)], axis=0)
 
 
 def device(x, core, z, y):
     return ((x * CORES + core) * ZS + z) * YS + y
 
 
-def along_x(array, by, inward):
+def root_of(z):
+    return z // CORES
+
+
+def permuted(array, target):
     pairs = []
-    for core in range(CORES):
-        for z in range(ZS):
-            for y in range(YS):
-                root = device(z // CORES, core, z, y)
-                other = device((z // CORES + by) % XS, core, z, y)
-                pairs.append((other, root) if inward else (root, other))
+    for x in range(XS):
+        for core in range(CORES):
+            for z in range(ZS):
+                for y in range(YS):
+                    to = target(x, core, z, y)
+                    if to is not None:
+                        pairs.append((device(x, core, z, y), device(*to)))
     return lax.ppermute(array, ALL, pairs)
 
 
-def along_x_far(array, inward):
-    half = array.shape[0] // 2
-    return jnp.concatenate(
-        [along_x(array[:half], 2, inward), along_x(array[half:], -2, inward)], axis=0
+def to_root(array, by):
+    return permuted(
+        array, lambda x, c, z, y: (root_of(z), c, z, y) if x == (root_of(z) + by) % XS else None
     )
 
 
@@ -98,12 +108,47 @@
     return (tile(0).astype(F32) + opposite.astype(F32)) + near
 
 
-def summed_over_col(array):
-    shares = array.reshape(ZS * YS, -1, array.shape[1])
-    mine = lax.all_to_all(shares, COL, split_axis=0, concat_axis=0, tiled=True)
-    mine = mine.astype(F32).sum(axis=0).astype(BF16)
-    copies = jnp.broadcast_to(mine[None], shares.shape)
-    return lax.all_to_all(copies, COL, split_axis=0, concat_axis=0, tiled=True).reshape(array.shape)
+def exchanged(array, axis, size, by):
+    return lax.ppermute(array, axis, [(i, i ^ by) for i in range(size)])
+
+
+def total_of(parts):
+    parts = [p.astype(F32) for p in parts]
+    total = parts[0] + parts[1]
+    if len(parts) == 4:
+        total = total + (parts[2] + parts[3])
+    return lax.optimization_barrier(total.astype(BF16))
+
+
+def summed_at_roots(terms):
+    z, y = lax.axis_index("z"), lax.axis_index("y")
+    quarter = lambda k: lax.dynamic_index_in_dim(
+        terms, ((y ^ k) - root_of(z)) % XS, 0, keepdims=False
+    )
+    part = total_of([quarter(0)] + [exchanged(quarter(k), "y", YS, k) for k in range(1, YS)])
+    part = total_of([part, exchanged(part, "z", ZS, 1)])
+    return total_of(
+        [part]
+        + [
+            permuted(
+                part,
+                lambda x, c, z, y: (x ^ k, c, z ^ (CORES * k), y) if x == root_of(z) else None,
+            )
+            for k in range(1, XS)
+        ]
+    )
+
+
+def spread(quarter):
+    got = permuted(quarter, lambda x, c, z, y: (y, c, z, y) if x == root_of(z) else None)
+    got = lax.optimization_barrier(got)
+    return sum(
+        [
+            permuted(got, lambda x, c, z, y: (x, c, z, (y + by) % YS) if y == x else None)
+            for by in (1, 2, -1)
+        ],
+        got,
+    )
 
 
 def own_slab_of_both(array):
@@ -134,10 +179,12 @@
     def partial_of(panel):
         return jnp.einsum("qj,pq->jp", panel, inverse_block, preferred_element_type=F32).astype(BF16)
 
-    chunks = chunks_z_then_y(normed[1])
+    near = near_z_then_y(normed[1])
     panels = [panel_y_then_z(normed[0])]
+    panels[0], near = lax.optimization_barrier((panels[0], near))
+    far = far_chunk(near)
+    chunks = [near[0], near[1], far, near[2]]
     partial = [partial_of(panels[0])]
-    partial[0], chunks = lax.optimization_barrier((partial[0], chunks))
     panels.append(placed_by_owner(chunks, y, 1).reshape(panels[0].shape))
     partial.append(partial_of(panels[1]))
 
@@ -152,13 +199,12 @@
     col_keep = lax.dynamic_index_in_dim(keep_of(col * rows, rows), core, 0)
     offdiag = lax.optimization_barrier((-(product * col_keep)).astype(BF16))
 
-    tiles = [offdiag, along_x(offdiag, 1, True), along_x_far(offdiag, True), along_x(offdiag, -1, True)]
-    terms = -jnp.dot(jnp.concatenate(tiles, axis=0), factor_slab, preferred_element_type=F32)
+    half = offdiag.shape[0] // 2
+    far = jnp.concatenate([to_root(offdiag[:half], 2), to_root(offdiag[half:], -2)], axis=0)
+    tiles = jnp.concatenate([offdiag, to_root(offdiag, 1), far, to_root(offdiag, -1)], axis=0)
+    terms = -jnp.dot(tiles, factor_slab, preferred_element_type=F32)
     terms = lax.optimization_barrier(terms.astype(BF16)).reshape(XS, -1, width)
-    term = jnp.where(lax.axis_index("x") == z // CORES, terms[0], jnp.zeros((), BF16))
-    term = term + along_x(terms[1], 1, False) + along_x_far(terms[2], False)
-    term = term + along_x(terms[3], -1, False)
-    correction = own_slab_of_both(summed_over_col(term))
+    correction = own_slab_of_both(spread(summed_at_roots(terms)))
     return (
         own_slab_of_both(offdiag).transpose(0, 2, 1),
         diag_inv + correction.astype(F32).transpose(0, 2, 1),

time: 183 us -> 181 us (0.989)
  waiting for transfers between devices: 59.3 us -> 69.1 us
  local copies, waits for them, and re-layouts: 9.14 us -> 2.12 us
  starting transfers between devices: 81.4 us -> 75.2 us
    ppermute x8 -> x15, starting transfers between devices: 10.7 us -> 30.2 us  [the longest x11 25.8 us: permuted(): return lax.ppermute(array, ALL, pairs)]
    all_to_all x2 -> x0, starting transfers between devices: 15.6 us -> none  [the longest x1 10.5 us: summed_over_col(): mine = lax.all_to_all(shares, COL, split_axis=0, concat_axis=0, tiled=True)]
    ppermute x8 -> x15, waiting for transfers between devices: 7.34 us -> 22.6 us  [the longest x11 15.1 us: permuted(): return lax.ppermute(array, ALL, pairs)]
    all_gather x1, waiting for transfers between devices: 0.03 us -> 13.7 us  [panel_y_then_z(): return lax.all_gather(part, 'z', axis=0, tiled=True)]
    all_to_all x2 -> x0, waiting for transfers between devices: 13.7 us -> none  [the longest x1 9.3 us: summed_over_col(): lax.all_to_all(copies, COL, split_axis=0, concat_axis=0, tiled=True)]
    ppermute x1, starting transfers between devices: 11.7 us -> 4.33 us  [sum_over_row(): lax.ppermute(partial[0], 'core', [(1, 0)]).astype(F32)]
    ppermute x18, waiting for transfers between devices: 36.2 us -> 30 us  [shift(): lax.ppermute(array, axis, [(i, (i + by) % size) for i in range(size)])]
    unnamed x24 -> x20, local copies, waits for them, and re-layouts: 4.77 us -> 1.13 us
  transfers between devices with their start and end apart: 34 -> 39, of which waited for: 17 -> 22; matrix products, arithmetic and copies ran while one was open for 3% -> 7% of each run, Pallas kernels for 0% -> 0%
where the time goes in v4:
time: 181 us; the launch traced here: 180 us
  starting transfers between devices  75.2 us (42%)
  waiting for transfers between devices  69.1 us (38%)
  between operations  15 us (8%)
  matrix products  12.5 us (7%)
  other arithmetic  5.75 us (3%)
  local copies, waits for them, and re-layouts  2.12 us (1%)
    ppermute x18, waiting for transfers between devices, shift(): lax.ppermute(array, axis, [(i, (i + by) % size) for i in range(size)])  30 us
    ppermute x18, starting transfers between devices, shift(): lax.ppermute(array, axis, [(i, (i + by) % size) for i in range(size)])  28.7 us
    ppermute x11, starting transfers between devices, permuted(): return lax.ppermute(array, ALL, pairs)  25.8 us
    ppermute x11, waiting for transfers between devices, permuted(): return lax.ppermute(array, ALL, pairs)  15.1 us
    all_gather x1, waiting for transfers between devices, panel_y_then_z(): return lax.all_gather(part, 'z', axis=0, tiled=True)  13.7 us
    dot_general x2, matrix products, partial_of(): jnp.einsum('qj,pq->jp', panel, inverse_block, preferred_element_type=F32)  9.48 us
    ppermute x2, starting transfers between devices, own_slab_of_both(): got = lax.ppermute(given, 'core', [(0, 1), (1, 0)])  9.09 us
    ppermute x4, waiting for transfers between devices, exchanged(): return lax.ppermute(array, axis, [(i, i ^ by) for i in range(size)])  7.49 us
  transfers between devices with their start and end apart: 39, of which 22 were waited for; matrix products, arithmetic and copies ran while one was open for 7% of the time, Pallas kernels for 0%

profile of v4, /device:TPU:1, one launch (start us, length us, event | category | flops | bytes accessed | tf_op | source)
XLA Modules:
  0.0 179.7 jit_solution(9022600969273349605)
XLA Ops:
  9.7 2.2 %collective-permute-start = (bf16[96,512]{1,0:T(8,128)(2,1)S(1)}, bf16[96,512]{1,0:T(8,128)(2,1)S(1)}, u32[]{:S(2)}, u32[]{:S(2)}) collective-permute-start(bf16[96,512]{1,0:T(8,128)(2,1)S(1)} %get-tuple-element.24), channel_id=1, source_target_pairs={{0,1},{1,2},{2,3},{3,0},{4,5},{5,6},{6,7},{7,4},{8,9},{9,10},{10,1... | collective-permute-start | bytes 294920 | tf_op jit(solution)/shard_map/ppermute | solution.py:17
  11.9 2.6 %collective-permute-start.1 = (bf16[96,512]{1,0:T(8,128)(2,1)S(1)}, bf16[96,512]{1,0:T(8,128)(2,1)S(1)}, u32[]{:S(2)}, u32[]{:S(2)}) collective-permute-start(bf16[96,512]{1,0:T(8,128)(2,1)S(1)} %get-tuple-element.24), channel_id=1, source_target_pairs={{0,2},{1,3},{2,0},{3,1},{4,6},{5,7},{6,4},{7,5},{8,10},{9,11},{10,... | collective-permute-start | bytes 294920 | tf_op jit(solution)/shard_map/ppermute | solution.py:17
  15.7 2.8 %collective-permute-done.1 = bf16[96,512]{1,0:T(8,128)(2,1)S(1)} collective-permute-done((bf16[96,512]{1,0:T(8,128)(2,1)S(1)}, bf16[96,512]{1,0:T(8,128)(2,1)S(1)}, u32[]{:S(2)}, u32[]{:S(2)}) %collective-permute-start.1) | collective-permute-done | bytes 98336 | tf_op jit(solution)/shard_map/ppermute | solution.py:17
  21.0 4.0 %collective-permute-start.7 = (bf16[1,96,512]{2,1,0:T(8,128)(2,1)S(1)}, bf16[1,96,512]{2,1,0:T(8,128)(2,1)S(1)}, u32[]{:S(2)}, u32[]{:S(2)}) collective-permute-start(bf16[1,96,512]{2,1,0:T(8,128)(2,1)S(1)} %get-tuple-element.23), channel_id=1, source_target_pairs={{0,28},{4,0},{8,4},{12,8},{16,12},{20,16},{24,20},{28,24},{1,29},{... | collective-permute-start | bytes 294920 | tf_op jit(solution)/shard_map/ppermute | solution.py:17
  27.0 2.8 %collective-permute-start.8 = (bf16[1,96,512]{2,1,0:T(8,128)(2,1)S(1)}, bf16[1,96,512]{2,1,0:T(8,128)(2,1)S(1)}, u32[]{:S(2)}, u32[]{:S(2)}) collective-permute-start(bf16[1,96,512]{2,1,0:T(8,128)(2,1)S(1)} %collective-permute-done.7), channel_id=1, source_target_pairs={{0,28},{4,0},{8,4},{12,8},{16,12},{20,16},{24,20},{28,24},{1,29},{... | collective-permute-start | bytes 294920 | tf_op jit(solution)/shard_map/ppermute | solution.py:17
  29.8 1.9 %collective-permute-done.4 = bf16[1,96,512]{2,1,0:T(8,128)(2,1)S(1)} collective-permute-done((bf16[1,96,512]{2,1,0:T(8,128)(2,1)S(1)}, bf16[1,96,512]{2,1,0:T(8,128)(2,1)S(1)}, u32[]{:S(2)}, u32[]{:S(2)}) %collective-permute-start.4) | collective-permute-done | bytes 98336 | tf_op jit(solution)/shard_map/ppermute | solution.py:17
  31.7 2.8 %collective-permute-start.9 = (bf16[1,96,512]{2,1,0:T(8,128)(2,1)S(1)}, bf16[1,96,512]{2,1,0:T(8,128)(2,1)S(1)}, u32[]{:S(2)}, u32[]{:S(2)}) collective-permute-start(bf16[1,96,512]{2,1,0:T(8,128)(2,1)S(1)} %collective-permute-done.8), channel_id=1, source_target_pairs={{0,28},{4,0},{8,4},{12,8},{16,12},{20,16},{24,20},{28,24},{1,29},{... | collective-permute-start | bytes 294920 | tf_op jit(solution)/shard_map/ppermute | solution.py:17
  34.4 1.9 %collective-permute-done.5 = bf16[1,96,512]{2,1,0:T(8,128)(2,1)S(1)} collective-permute-done((bf16[1,96,512]{2,1,0:T(8,128)(2,1)S(1)}, bf16[1,96,512]{2,1,0:T(8,128)(2,1)S(1)}, u32[]{:S(2)}, u32[]{:S(2)}) %collective-permute-start.5) | collective-permute-done | bytes 98336 | tf_op jit(solution)/shard_map/ppermute | solution.py:17
  36.4 8.0 %collective-permute-done.6 = bf16[1,96,512]{2,1,0:T(8,128)(2,1)S(1)} collective-permute-done((bf16[1,96,512]{2,1,0:T(8,128)(2,1)S(1)}, bf16[1,96,512]{2,1,0:T(8,128)(2,1)S(1)}, u32[]{:S(2)}, u32[]{:S(2)}) %collective-permute-start.6) | collective-permute-done | bytes 98336 | tf_op jit(solution)/shard_map/ppermute | solution.py:17
  45.2 2.1 %collective-permute-start.11 = (bf16[8,1,96,512]{3,2,1,0:T(8,128)(2,1)S(1)}, bf16[8,1,96,512]{3,2,1,0:T(8,128)(2,1)S(1)}, u32[]{:S(2)}, u32[]{:S(2)}) collective-permute-start(bf16[8,1,96,512]{3,2,1,0:T(8,128)(2,1)S(1)} %bitcast_dynamic-update-slice_fusion), channel_id=1, source_target_pairs={{0,3},{1,0},{2,1},{3,2},{4,7},{5,4},{6,5},{7,6},{8,11},{9,8},{10,9... | collective-permute-start | bytes 2359304 | tf_op jit(solution)/shard_map/ppermute | solution.py:17
  47.2 9.9 %collective-permute-done.10 = bf16[8,1,96,512]{3,2,1,0:T(8,128)(2,1)S(1)} collective-permute-done((bf16[8,1,96,512]{3,2,1,0:T(8,128)(2,1)S(1)}, bf16[8,1,96,512]{3,2,1,0:T(8,128)(2,1)S(1)}, u32[]{:S(2)}, u32[]{:S(2)}) %collective-permute-start.10) | collective-permute-done | bytes 786464 | tf_op jit(solution)/shard_map/ppermute | solution.py:17
  57.1 13.7 %all-gather.2.cloned.1.call-done = bf16[3072,512]{1,0:T(8,128)(2,1)} async-done(((bf16[384,512]{1,0:T(8,128)(2,1)}), bf16[3072,512]{1,0:T(8,128)(2,1)}) %all-gather.2.cloned.1.call-update) | async-done | bytes 3145744 | tf_op jit(solution)/shard_map/all_gather | solution.py:53
  74.0 6.8 %convolution_convert_fusion.1 = bf16[512,768]{1,0:T(8,128)(2,1)} fusion(bf16[3072,512]{1,0:T(8,128)(2,1)} %all-gather.2.cloned.1.call-done, bf16[768,3072]{1,0:T(8,128)(2,1)} %param.8), kind=kOutput, calls=%fused_computation.2 | convolution fusion | flops 2416312320 | bytes 8650752 | tf_op jit(solution)/shard_map/qj,pq->jp/dot_general | solution.py:180
  80.8 4.3 %collective-permute-start.14 = (bf16[512,768]{1,0:T(8,128)(2,1)}, bf16[512,768]{1,0:T(8,128)(2,1)}, u32[]{:S(2)}, u32[]{:S(2)}) collective-permute-start(bf16[512,768]{1,0:T(8,128)(2,1)} %convolution_convert_fusion.1), channel_id=1, source_target_pairs={{32,0},{33,1},{34,2},{35,3},{36,4},{37,5},{38,6},{39,7},{40,8},{41... | collective-permute-start | bytes 2359304 | tf_op jit(solution)/shard_map/ppermute | solution.py:95
  85.8 2.7 %convolution_convert_fusion = bf16[512,768]{1,0:T(8,128)(2,1)S(1)} fusion(bf16[3072,512]{1,0:T(8,128)(2,1)S(1)} %bitcast.83, bf16[768,3072]{1,0:T(8,128)(2,1)S(1)} %bitcast.98), kind=kOutput, calls=%fused_computation.1 | convolution fusion | flops 2416312320 | bytes 8650752 | tf_op jit(solution)/shard_map/qj,pq->jp/dot_general | solution.py:180
  90.1 2.5 %collective-permute-done.15 = bf16[512,768]{1,0:T(8,128)(2,1)S(1)} collective-permute-done((bf16[512,768]{1,0:T(8,128)(2,1)S(1)}, bf16[512,768]{1,0:T(8,128)(2,1)S(1)}, u32[]{:S(2)}, u32[]{:S(2)}) %collective-permute-start.15) | collective-permute-done | bytes 786464 | tf_op jit(solution)/shard_map/ppermute | solution.py:95
  104.7 2.1 %collective-permute-done.17 = bf16[64,768]{1,0:T(8,128)(2,1)S(1)} collective-permute-done((bf16[64,768]{1,0:T(8,128)(2,1)S(1)}, bf16[64,768]{1,0:T(8,128)(2,1)S(1)}, u32[]{:S(2)}, u32[]{:S(2)}) %collective-permute-start.17) | collective-permute-done | bytes 98336 | tf_op jit(solution)/shard_map/ppermute | solution.py:17
  112.2 1.8 %collective-permute-done.21 = bf16[128,768]{1,0:T(8,128)(2,1)S(1)} collective-permute-done((bf16[128,768]{1,0:T(8,128)(2,1)S(1)}, bf16[128,768]{1,0:T(8,128)(2,1)S(1)}, u32[]{:S(2)}, u32[]{:S(2)}) %collective-permute-start.21) | collective-permute-done | bytes 196640 | tf_op jit(solution)/shard_map/ppermute | solution.py:84
  114.0 2.5 %collective-permute-done.22 = bf16[64,768]{1,0:T(8,128)(2,1)S(1)} collective-permute-done((bf16[64,768]{1,0:T(8,128)(2,1)S(1)}, bf16[64,768]{1,0:T(8,128)(2,1)S(1)}, u32[]{:S(2)}, u32[]{:S(2)}) %collective-permute-start.22) | collective-permute-done | bytes 98336 | tf_op jit(solution)/shard_map/ppermute | solution.py:84
  116.5 2.3 %collective-permute-done.23 = bf16[64,768]{1,0:T(8,128)(2,1)S(1)} collective-permute-done((bf16[64,768]{1,0:T(8,128)(2,1)S(1)}, bf16[64,768]{1,0:T(8,128)(2,1)S(1)}, u32[]{:S(2)}, u32[]{:S(2)}) %collective-permute-start.23) | collective-permute-done | bytes 98336 | tf_op jit(solution)/shard_map/ppermute | solution.py:84
  118.8 2.0 %collective-permute-done.24 = bf16[128,768]{1,0:T(8,128)(2,1)S(1)} collective-permute-done((bf16[128,768]{1,0:T(8,128)(2,1)S(1)}, bf16[128,768]{1,0:T(8,128)(2,1)S(1)}, u32[]{:S(2)}, u32[]{:S(2)}) %collective-permute-start.24) | collective-permute-done | bytes 196640 | tf_op jit(solution)/shard_map/ppermute | solution.py:84
  120.8 1.8 fusion
  123.1 2.0 %collective-permute-start.27 = (bf16[128,512]{1,0:T(8,128)(2,1)S(1)}, bf16[128,512]{1,0:T(8,128)(2,1)S(1)}, u32[]{:S(2)}, u32[]{:S(2)}) collective-permute-start(bf16[128,512]{1,0:T(8,128)(2,1)S(1)} %get-tuple-element.16), channel_id=1, source_target_pairs={{0,2},{1,3},{2,0},{3,1},{4,6},{5,7},{6,4},{7,5},{8,10},{9,11},{10,... | collective-permute-start | bytes 393224 | tf_op jit(solution)/shard_map/ppermute | solution.py:112
  126.6 2.5 %collective-permute-done.27 = bf16[128,512]{1,0:T(8,128)(2,1)S(1)} collective-permute-done((bf16[128,512]{1,0:T(8,128)(2,1)S(1)}, bf16[128,512]{1,0:T(8,128)(2,1)S(1)}, u32[]{:S(2)}, u32[]{:S(2)}) %collective-permute-start.27) | collective-permute-done | bytes 131104 | tf_op jit(solution)/shard_map/ppermute | solution.py:112
  131.2 3.4 %collective-permute-done.29 = bf16[128,512]{1,0:T(8,128)(2,1)S(1)} collective-permute-done((bf16[128,512]{1,0:T(8,128)(2,1)S(1)}, bf16[128,512]{1,0:T(8,128)(2,1)S(1)}, u32[]{:S(2)}, u32[]{:S(2)}) %collective-permute-start.29) | collective-permute-done | bytes 131104 | tf_op jit(solution)/shard_map/ppermute | solution.py:112
  134.7 1.9 %collective-permute-start.30 = (bf16[128,512]{1,0:T(8,128)(2,1)S(1)}, bf16[128,512]{1,0:T(8,128)(2,1)S(1)}, u32[]{:S(2)}, u32[]{:S(2)}) collective-permute-start(bf16[128,512]{1,0:T(8,128)(2,1)S(1)} %add_convert_fusion.2), channel_id=1, source_target_pairs={{0,72},{1,73},{2,74},{3,75},{4,76},{5,77},{6,78},{7,79},{32,104},{... | collective-permute-start | bytes 393224 | tf_op jit(solution)/shard_map/ppermute | solution.py:84
  136.6 4.9 %collective-permute-start.31 = (bf16[128,512]{1,0:T(8,128)(2,1)S(1)}, bf16[128,512]{1,0:T(8,128)(2,1)S(1)}, u32[]{:S(2)}, u32[]{:S(2)}) collective-permute-start(bf16[128,512]{1,0:T(8,128)(2,1)S(1)} %add_convert_fusion.2), channel_id=1, source_target_pairs={{0,144},{1,145},{2,146},{3,147},{4,148},{5,149},{6,150},{7,151},{3... | collective-permute-start | bytes 393224 | tf_op jit(solution)/shard_map/ppermute | solution.py:84
  141.5 7.6 %collective-permute-start.32 = (bf16[128,512]{1,0:T(8,128)(2,1)S(1)}, bf16[128,512]{1,0:T(8,128)(2,1)S(1)}, u32[]{:S(2)}, u32[]{:S(2)}) collective-permute-start(bf16[128,512]{1,0:T(8,128)(2,1)S(1)} %add_convert_fusion.2), channel_id=1, source_target_pairs={{0,216},{1,217},{2,218},{3,219},{4,220},{5,221},{6,222},{7,223},{3... | collective-permute-start | bytes 393224 | tf_op jit(solution)/shard_map/ppermute | solution.py:84
  150.1 3.7 %collective-permute-done.32 = bf16[128,512]{1,0:T(8,128)(2,1)S(1)} collective-permute-done((bf16[128,512]{1,0:T(8,128)(2,1)S(1)}, bf16[128,512]{1,0:T(8,128)(2,1)S(1)}, u32[]{:S(2)}, u32[]{:S(2)}) %collective-permute-start.32) | collective-permute-done | bytes 131104 | tf_op jit(solution)/shard_map/ppermute | solution.py:84
  154.5 5.8 %collective-permute-start.20 = (bf16[64,768]{1,0:T(8,128)(2,1)S(1)}, bf16[64,768]{1,0:T(8,128)(2,1)S(1)}, u32[]{:S(2)}, u32[]{:S(2)}) collective-permute-start(bf16[64,768]{1,0:T(8,128)(2,1)S(1)} %dynamic-slice_bitcast_fusion.7), channel_id=1, source_target_pairs={{0,32},{32,0},{1,33},{33,1},{2,34},{34,2},{3,35},{35,3},{4,36},{36... | collective-permute-start | bytes 294920 | tf_op jit(solution)/shard_map/ppermute | solution.py:159
  160.3 2.9 %collective-permute-start.34 = (bf16[128,512]{1,0:T(8,128)(2,1)S(1)}, bf16[128,512]{1,0:T(8,128)(2,1)S(1)}, u32[]{:S(2)}, u32[]{:S(2)}) collective-permute-start(bf16[128,512]{1,0:T(8,128)(2,1)S(1)} %collective-permute-done.33), channel_id=1, source_target_pairs={{0,1},{4,5},{8,9},{12,13},{16,17},{20,21},{24,25},{28,29},{32,33},... | collective-permute-start | bytes 393224 | tf_op jit(solution)/shard_map/ppermute | solution.py:84
  167.8 3.3 %collective-permute-start.37 = (bf16[64,512]{1,0:T(8,128)(2,1)S(1)}, bf16[64,512]{1,0:T(8,128)(2,1)S(1)}, u32[]{:S(2)}, u32[]{:S(2)}) collective-permute-start(bf16[64,512]{1,0:T(8,128)(2,1)S(1)} %dynamic-slice_bitcast_fusion.8), channel_id=1, source_target_pairs={{0,32},{32,0},{1,33},{33,1},{2,34},{34,2},{3,35},{35,3},{4,36},{36... | collective-permute-start | bytes 196616 | tf_op jit(solution)/shard_map/ppermute | solution.py:159
  (118 shorter events, 43.1 us)
Async XLA Ops:
  7.2 63.7 %all-gather.2.cloned.1.call-start = ((), (), s32[]{:S(2)}) async-start(), calls=%async_computation | async-start | bytes 3538944 | tf_op jit(solution)/shard_map/all_gather | solution.py:53
  9.7 6.0 %collective-permute-start = (bf16[96,512]{1,0:T(8,128)(2,1)S(1)}, bf16[96,512]{1,0:T(8,128)(2,1)S(1)}, u32[]{:S(2)}, u32[]{:S(2)}) collective-permute-start(bf16[96,512]{1,0:T(8,128)(2,1)S(1)} %get-tuple-element.24), channel_id=1, source_target_pairs={{0,1},{1,2},{2,3},{3,0},{4,5},{5,6},{6,7},{7,4},{8,9},{9,10},{10,1... | collective-permute-start | bytes 294920 | tf_op jit(solution)/shard_map/ppermute | solution.py:17
  11.9 6.6 %collective-permute-start.1 = (bf16[96,512]{1,0:T(8,128)(2,1)S(1)}, bf16[96,512]{1,0:T(8,128)(2,1)S(1)}, u32[]{:S(2)}, u32[]{:S(2)}) collective-permute-start(bf16[96,512]{1,0:T(8,128)(2,1)S(1)} %get-tuple-element.24), channel_id=1, source_target_pairs={{0,2},{1,3},{2,0},{3,1},{4,6},{5,7},{6,4},{7,5},{8,10},{9,11},{10,... | collective-permute-start | bytes 294920 | tf_op jit(solution)/shard_map/ppermute | solution.py:17
  19.3 7.7 %collective-permute-start.3 = (bf16[1,96,512]{2,1,0:T(8,128)(2,1)S(1)}, bf16[1,96,512]{2,1,0:T(8,128)(2,1)S(1)}, u32[]{:S(2)}, u32[]{:S(2)}) collective-permute-start(bf16[1,96,512]{2,1,0:T(8,128)(2,1)S(1)} %get-tuple-element.23), channel_id=1, source_target_pairs={{0,4},{4,8},{8,12},{12,16},{16,20},{20,24},{24,28},{28,0},{1,5},{5... | collective-permute-start | bytes 294920 | tf_op jit(solution)/shard_map/ppermute | solution.py:17
  21.0 6.0 %collective-permute-start.7 = (bf16[1,96,512]{2,1,0:T(8,128)(2,1)S(1)}, bf16[1,96,512]{2,1,0:T(8,128)(2,1)S(1)}, u32[]{:S(2)}, u32[]{:S(2)}) collective-permute-start(bf16[1,96,512]{2,1,0:T(8,128)(2,1)S(1)} %get-tuple-element.23), channel_id=1, source_target_pairs={{0,28},{4,0},{8,4},{12,8},{16,12},{20,16},{24,20},{28,24},{1,29},{... | collective-permute-start | bytes 294920 | tf_op jit(solution)/shard_map/ppermute | solution.py:17
  27.0 4.7 %collective-permute-start.4 = (bf16[1,96,512]{2,1,0:T(8,128)(2,1)S(1)}, bf16[1,96,512]{2,1,0:T(8,128)(2,1)S(1)}, u32[]{:S(2)}, u32[]{:S(2)}) collective-permute-start(bf16[1,96,512]{2,1,0:T(8,128)(2,1)S(1)} %collective-permute-done.3), channel_id=1, source_target_pairs={{0,4},{4,8},{8,12},{12,16},{16,20},{20,24},{24,28},{28,0},{1,5},{5... | collective-permute-start | bytes 294920 | tf_op jit(solution)/shard_map/ppermute | solution.py:17
  27.0 4.7 %collective-permute-start.8 = (bf16[1,96,512]{2,1,0:T(8,128)(2,1)S(1)}, bf16[1,96,512]{2,1,0:T(8,128)(2,1)S(1)}, u32[]{:S(2)}, u32[]{:S(2)}) collective-permute-start(bf16[1,96,512]{2,1,0:T(8,128)(2,1)S(1)} %collective-permute-done.7), channel_id=1, source_target_pairs={{0,28},{4,0},{8,4},{12,8},{16,12},{20,16},{24,20},{28,24},{1,29},{... | collective-permute-start | bytes 294920 | tf_op jit(solution)/shard_map/ppermute | solution.py:17
  31.7 4.7 %collective-permute-start.5 = (bf16[1,96,512]{2,1,0:T(8,128)(2,1)S(1)}, bf16[1,96,512]{2,1,0:T(8,128)(2,1)S(1)}, u32[]{:S(2)}, u32[]{:S(2)}) collective-permute-start(bf16[1,96,512]{2,1,0:T(8,128)(2,1)S(1)} %collective-permute-done.4), channel_id=1, source_target_pairs={{0,4},{4,8},{8,12},{12,16},{16,20},{20,24},{24,28},{28,0},{1,5},{5... | collective-permute-start | bytes 294920 | tf_op jit(solution)/shard_map/ppermute | solution.py:17
  31.7 12.7 %collective-permute-start.9 = (bf16[1,96,512]{2,1,0:T(8,128)(2,1)S(1)}, bf16[1,96,512]{2,1,0:T(8,128)(2,1)S(1)}, u32[]{:S(2)}, u32[]{:S(2)}) collective-permute-start(bf16[1,96,512]{2,1,0:T(8,128)(2,1)S(1)} %collective-permute-done.8), channel_id=1, source_target_pairs={{0,28},{4,0},{8,4},{12,8},{16,12},{20,16},{24,20},{28,24},{1,29},{... | collective-permute-start | bytes 294920 | tf_op jit(solution)/shard_map/ppermute | solution.py:17
  36.3 8.1 %collective-permute-start.6 = (bf16[1,96,512]{2,1,0:T(8,128)(2,1)S(1)}, bf16[1,96,512]{2,1,0:T(8,128)(2,1)S(1)}, u32[]{:S(2)}, u32[]{:S(2)}) collective-permute-start(bf16[1,96,512]{2,1,0:T(8,128)(2,1)S(1)} %collective-permute-done.5), channel_id=1, source_target_pairs={{0,4},{4,8},{8,12},{12,16},{16,20},{20,24},{24,28},{28,0},{1,5},{5... | collective-permute-start | bytes 294920 | tf_op jit(solution)/shard_map/ppermute | solution.py:17
  44.5 12.6 %collective-permute-start.10 = (bf16[8,1,96,512]{3,2,1,0:T(8,128)(2,1)S(1)}, bf16[8,1,96,512]{3,2,1,0:T(8,128)(2,1)S(1)}, u32[]{:S(2)}, u32[]{:S(2)}) collective-permute-start(bf16[8,1,96,512]{3,2,1,0:T(8,128)(2,1)S(1)} %bitcast_dynamic-update-slice_fusion), channel_id=1, source_target_pairs={{0,1},{1,2},{2,3},{3,0},{4,5},{5,6},{6,7},{7,4},{8,9},{9,10},{10,1... | collective-permute-start | bytes 2359304 | tf_op jit(solution)/shard_map/ppermute | solution.py:17
  45.2 12.0 %collective-permute-start.11 = (bf16[8,1,96,512]{3,2,1,0:T(8,128)(2,1)S(1)}, bf16[8,1,96,512]{3,2,1,0:T(8,128)(2,1)S(1)}, u32[]{:S(2)}, u32[]{:S(2)}) collective-permute-start(bf16[8,1,96,512]{3,2,1,0:T(8,128)(2,1)S(1)} %bitcast_dynamic-update-slice_fusion), channel_id=1, source_target_pairs={{0,3},{1,0},{2,1},{3,2},{4,7},{5,4},{6,5},{7,6},{8,11},{9,8},{10,9... | collective-permute-start | bytes 2359304 | tf_op jit(solution)/shard_map/ppermute | solution.py:17
  70.9 14.7 %collective-permute-start.12 = (bf16[4,1,96,512]{3,2,1,0:T(8,128)(2,1)S(1)}, bf16[4,1,96,512]{3,2,1,0:T(8,128)(2,1)S(1)}, u32[]{:S(2)}, u32[]{:S(2)}) collective-permute-start(bf16[4,1,96,512]{3,2,1,0:T(8,128)(2,1)S(1)} %slice.36), channel_id=1, source_target_pairs={{0,1},{1,2},{2,3},{3,0},{4,5},{5,6},{6,7},{7,4},{8,9},{9,10},{10,1... | collective-permute-start | bytes 1179656 | tf_op jit(solution)/shard_map/ppermute | solution.py:17
  72.2 13.4 %collective-permute-start.13 = (bf16[4,1,96,512]{3,2,1,0:T(8,128)(2,1)S(1)}, bf16[4,1,96,512]{3,2,1,0:T(8,128)(2,1)S(1)}, u32[]{:S(2)}, u32[]{:S(2)}) collective-permute-start(bf16[4,1,96,512]{3,2,1,0:T(8,128)(2,1)S(1)} %slice.37), channel_id=1, source_target_pairs={{0,3},{1,0},{2,1},{3,2},{4,7},{5,4},{6,5},{7,6},{8,11},{9,8},{10,9... | collective-permute-start | bytes 1179656 | tf_op jit(solution)/shard_map/ppermute | solution.py:17
  80.8 9.4 %collective-permute-start.14 = (bf16[512,768]{1,0:T(8,128)(2,1)}, bf16[512,768]{1,0:T(8,128)(2,1)}, u32[]{:S(2)}, u32[]{:S(2)}) collective-permute-start(bf16[512,768]{1,0:T(8,128)(2,1)} %convolution_convert_fusion.1), channel_id=1, source_target_pairs={{32,0},{33,1},{34,2},{35,3},{36,4},{37,5},{38,6},{39,7},{40,8},{41... | collective-permute-start | bytes 2359304 | tf_op jit(solution)/shard_map/ppermute | solution.py:95
  94.3 12.5 %collective-permute-start.18 = (bf16[128,768]{1,0:T(8,128)(2,1)S(1)}, bf16[128,768]{1,0:T(8,128)(2,1)S(1)}, u32[]{:S(2)}, u32[]{:S(2)}) collective-permute-start(bf16[128,768]{1,0:T(8,128)(2,1)S(1)} %get-tuple-element.12), channel_id=1, source_target_pairs={{0,64},{64,128},{128,192},{192,0},{1,65},{65,129},{129,193},{193,1... | collective-permute-start | bytes 589832 | tf_op jit(solution)/shard_map/ppermute | solution.py:17
  95.5 11.3 %collective-permute-start.19 = (bf16[128,768]{1,0:T(8,128)(2,1)S(1)}, bf16[128,768]{1,0:T(8,128)(2,1)S(1)}, u32[]{:S(2)}, u32[]{:S(2)}) collective-permute-start(bf16[128,768]{1,0:T(8,128)(2,1)S(1)} %get-tuple-element.13), channel_id=1, source_target_pairs={{0,192},{64,0},{128,64},{192,128},{1,193},{65,1},{129,65},{193,129... | collective-permute-start | bytes 589832 | tf_op jit(solution)/shard_map/ppermute | solution.py:17
  97.0 7.7 %collective-permute-start.16 = (bf16[64,768]{1,0:T(8,128)(2,1)S(1)}, bf16[64,768]{1,0:T(8,128)(2,1)S(1)}, u32[]{:S(2)}, u32[]{:S(2)}) collective-permute-start(bf16[64,768]{1,0:T(8,128)(2,1)S(1)} %get-tuple-element.10), channel_id=1, source_target_pairs={{0,128},{64,192},{128,0},{192,64},{1,129},{65,193},{129,1},{193,65... | collective-permute-start | bytes 294920 | tf_op jit(solution)/shard_map/ppermute | solution.py:17
  98.6 8.2 %collective-permute-start.17 = (bf16[64,768]{1,0:T(8,128)(2,1)S(1)}, bf16[64,768]{1,0:T(8,128)(2,1)S(1)}, u32[]{:S(2)}, u32[]{:S(2)}) collective-permute-start(bf16[64,768]{1,0:T(8,128)(2,1)S(1)} %get-tuple-element.11), channel_id=1, source_target_pairs={{0,128},{64,192},{128,0},{192,64},{1,129},{65,193},{129,1},{193,65... | collective-permute-start | bytes 294920 | tf_op jit(solution)/shard_map/ppermute | solution.py:17
  101.4 19.3 %collective-permute-start.25 = (bf16[768,512]{1,0:T(8,128)(2,1)S(1)}, bf16[768,512]{1,0:T(8,128)(2,1)S(1)}, u32[]{:S(2)}, u32[]{:S(2)}) collective-permute-start(bf16[768,512]{1,0:T(8,128)(2,1)S(1)} %broadcast_select_fusion), channel_id=1, source_target_pairs={{0,32},{32,0},{1,33},{33,1},{2,34},{34,2},{3,35},{35,3},{4,36},{36... | collective-permute-start | bytes 2359304 | tf_op jit(solution)/shard_map/ppermute | solution.py:192
  106.9 7.1 %collective-permute-start.21 = (bf16[128,768]{1,0:T(8,128)(2,1)S(1)}, bf16[128,768]{1,0:T(8,128)(2,1)S(1)}, u32[]{:S(2)}, u32[]{:S(2)}) collective-permute-start(bf16[128,768]{1,0:T(8,128)(2,1)S(1)} %fusion.11), channel_id=1, source_target_pairs={{24,216},{25,217},{26,218},{27,219},{28,220},{29,221},{30,222},{31... | collective-permute-start | bytes 589832 | tf_op jit(solution)/shard_map/ppermute | solution.py:84
  108.3 12.5 %collective-permute-start.24 = (bf16[128,768]{1,0:T(8,128)(2,1)S(1)}, bf16[128,768]{1,0:T(8,128)(2,1)S(1)}, u32[]{:S(2)}, u32[]{:S(2)}) collective-permute-start(bf16[128,768]{1,0:T(8,128)(2,1)S(1)} %fusion.11), channel_id=1, source_target_pairs={{8,72},{9,73},{10,74},{11,75},{12,76},{13,77},{14,78},{15,79},{40,... | collective-permute-start | bytes 589832 | tf_op jit(solution)/shard_map/ppermute | solution.py:84
  109.6 7.0 %collective-permute-start.22 = (bf16[64,768]{1,0:T(8,128)(2,1)S(1)}, bf16[64,768]{1,0:T(8,128)(2,1)S(1)}, u32[]{:S(2)}, u32[]{:S(2)}) collective-permute-start(bf16[64,768]{1,0:T(8,128)(2,1)S(1)} %get-tuple-element.22), channel_id=1, source_target_pairs={{16,144},{17,145},{18,146},{19,147},{20,148},{21,149},{22,150},{23... | collective-permute-start | bytes 294920 | tf_op jit(solution)/shard_map/ppermute | solution.py:84
  110.9 7.9 %collective-permute-start.23 = (bf16[64,768]{1,0:T(8,128)(2,1)S(1)}, bf16[64,768]{1,0:T(8,128)(2,1)S(1)}, u32[]{:S(2)}, u32[]{:S(2)}) collective-permute-start(bf16[64,768]{1,0:T(8,128)(2,1)S(1)} %get-tuple-element.21), channel_id=1, source_target_pairs={{16,144},{17,145},{18,146},{19,147},{20,148},{21,149},{22,150},{23... | collective-permute-start | bytes 294920 | tf_op jit(solution)/shard_map/ppermute | solution.py:84
  123.1 6.0 %collective-permute-start.27 = (bf16[128,512]{1,0:T(8,128)(2,1)S(1)}, bf16[128,512]{1,0:T(8,128)(2,1)S(1)}, u32[]{:S(2)}, u32[]{:S(2)}) collective-permute-start(bf16[128,512]{1,0:T(8,128)(2,1)S(1)} %get-tuple-element.16), channel_id=1, source_target_pairs={{0,2},{1,3},{2,0},{3,1},{4,6},{5,7},{6,4},{7,5},{8,10},{9,11},{10,... | collective-permute-start | bytes 393224 | tf_op jit(solution)/shard_map/ppermute | solution.py:112
  125.2 5.5 %collective-permute-start.28 = (bf16[128,512]{1,0:T(8,128)(2,1)S(1)}, bf16[128,512]{1,0:T(8,128)(2,1)S(1)}, u32[]{:S(2)}, u32[]{:S(2)}) collective-permute-start(bf16[128,512]{1,0:T(8,128)(2,1)S(1)} %get-tuple-element.15), channel_id=1, source_target_pairs={{0,3},{1,2},{2,1},{3,0},{4,7},{5,6},{6,5},{7,4},{8,11},{9,10},{10,... | collective-permute-start | bytes 393224 | tf_op jit(solution)/shard_map/ppermute | solution.py:112
  134.7 14.4 %collective-permute-start.30 = (bf16[128,512]{1,0:T(8,128)(2,1)S(1)}, bf16[128,512]{1,0:T(8,128)(2,1)S(1)}, u32[]{:S(2)}, u32[]{:S(2)}) collective-permute-start(bf16[128,512]{1,0:T(8,128)(2,1)S(1)} %add_convert_fusion.2), channel_id=1, source_target_pairs={{0,72},{1,73},{2,74},{3,75},{4,76},{5,77},{6,78},{7,79},{32,104},{... | collective-permute-start | bytes 393224 | tf_op jit(solution)/shard_map/ppermute | solution.py:84
  136.6 13.5 %collective-permute-start.31 = (bf16[128,512]{1,0:T(8,128)(2,1)S(1)}, bf16[128,512]{1,0:T(8,128)(2,1)S(1)}, u32[]{:S(2)}, u32[]{:S(2)}) collective-permute-start(bf16[128,512]{1,0:T(8,128)(2,1)S(1)} %add_convert_fusion.2), channel_id=1, source_target_pairs={{0,144},{1,145},{2,146},{3,147},{4,148},{5,149},{6,150},{7,151},{3... | collective-permute-start | bytes 393224 | tf_op jit(solution)/shard_map/ppermute | solution.py:84
  141.5 12.2 %collective-permute-start.32 = (bf16[128,512]{1,0:T(8,128)(2,1)S(1)}, bf16[128,512]{1,0:T(8,128)(2,1)S(1)}, u32[]{:S(2)}, u32[]{:S(2)}) collective-permute-start(bf16[128,512]{1,0:T(8,128)(2,1)S(1)} %add_convert_fusion.2), channel_id=1, source_target_pairs={{0,216},{1,217},{2,218},{3,219},{4,220},{5,221},{6,222},{7,223},{3... | collective-permute-start | bytes 393224 | tf_op jit(solution)/shard_map/ppermute | solution.py:84
  153.8 6.5 %collective-permute-start.33 = (bf16[128,512]{1,0:T(8,128)(2,1)S(1)}, bf16[128,512]{1,0:T(8,128)(2,1)S(1)}, u32[]{:S(2)}, u32[]{:S(2)}) collective-permute-start(bf16[128,512]{1,0:T(8,128)(2,1)S(1)} %add_convert_fusion.1), channel_id=1, source_target_pairs={{0,0},{1,65},{2,130},{3,195},{4,4},{5,69},{6,134},{7,199},{32,32},... | collective-permute-start | bytes 393224 | tf_op jit(solution)/shard_map/ppermute | solution.py:84
  154.5 11.3 %collective-permute-start.20 = (bf16[64,768]{1,0:T(8,128)(2,1)S(1)}, bf16[64,768]{1,0:T(8,128)(2,1)S(1)}, u32[]{:S(2)}, u32[]{:S(2)}) collective-permute-start(bf16[64,768]{1,0:T(8,128)(2,1)S(1)} %dynamic-slice_bitcast_fusion.7), channel_id=1, source_target_pairs={{0,32},{32,0},{1,33},{33,1},{2,34},{34,2},{3,35},{35,3},{4,36},{36... | collective-permute-start | bytes 294920 | tf_op jit(solution)/shard_map/ppermute | solution.py:159
  160.3 5.6 %collective-permute-start.34 = (bf16[128,512]{1,0:T(8,128)(2,1)S(1)}, bf16[128,512]{1,0:T(8,128)(2,1)S(1)}, u32[]{:S(2)}, u32[]{:S(2)}) collective-permute-start(bf16[128,512]{1,0:T(8,128)(2,1)S(1)} %collective-permute-done.33), channel_id=1, source_target_pairs={{0,1},{4,5},{8,9},{12,13},{16,17},{20,21},{24,25},{28,29},{32,33},... | collective-permute-start | bytes 393224 | tf_op jit(solution)/shard_map/ppermute | solution.py:84
  (15 other events, 122.5 us)
Sparse Core Ops, SparseCore 0:
  19.4 51.3 all-gather.1

commit v5 on v2

--- a/solution.py
+++ b/solution.py
@@ -53,46 +53,47 @@
     return lax.all_gather(part, "z", axis=0, tiled=True)
 
 
-def panel_z_then_y(piece):
-    part = placed_by_owner(direct_ring(piece[None], "z", ZS), lax.axis_index("z"), 0)
-    whole = placed_by_owner(
-        [g[:, None] for g in relay_ring(part, "y", YS, True)], lax.axis_index("y"), 1
-    )
-    return whole.reshape(-1, piece.shape[-1])
+def near_z_then_y(piece):
+    part = placed_by_owner(relay_ring(piece[None], "z", ZS, False), lax.axis_index("z"), 0)[:, None]
+    return [part, shift(part, "y", YS, 1), shift(part, "y", YS, -1)]
+
+
+def far_chunk(near):
+    half = near[0].shape[0] // 2
+    right = shift(near[1][:half], "y", YS, 1)
+    return jnp.concatenate([right, shift(near[2][half:], "y", YS, -1)], axis=0)
 
 
 def device(x, core, z, y):
     return ((x * CORES + core) * ZS + z) * YS + y
 
 
-def to_cores(own_slabs):
-    x, core, z = lax.axis_index("x"), lax.axis_index("core"), lax.axis_index("z")
-    home = (x == z // CORES) & (core == z % CORES)
-    total = jnp.where(home, jnp.where(core == 0, own_slabs[0], own_slabs[1]), jnp.zeros((), BF16))
-    across = jnp.where(core == 0, own_slabs[1], own_slabs[0])
-    pairs = lambda by, s: [
-        (device(r // CORES, r % CORES, r, y), device((r // CORES + by) % XS, s, r, y))
-        for r in range(ZS)
-        for y in range(YS)
-    ]
-    for s, shifts in ((0, (1, -1, 2)), (1, (1, -1, -2))):
-        for by in shifts:
-            total = total + lax.ppermute(own_slabs[s], ALL, pairs(by, s))
-    swapped = [
-        (device(r // CORES, r % CORES, r, y), device(r // CORES, 1 - r % CORES, r, y))
-        for r in range(ZS)
-        for y in range(YS)
-    ]
-    return total + lax.ppermute(across, ALL, swapped)
-
-
-def sum_over_row(partial):
-    x, core = lax.axis_index("x"), lax.axis_index("core")
-    moved = lax.ppermute(partial[0], "core", [(1, 0)]).astype(F32) + lax.ppermute(
-        partial[1], "core", [(0, 1)]
-    ).astype(F32)
-    pair = jnp.where(core == 0, partial[0], partial[1]).astype(F32) + moved
-    pair = lax.optimization_barrier(pair.astype(BF16))
+def root_of(z):
+    return z // CORES, z % CORES
+
+
+def from_root(array, target):
+    pairs = []
+    for z in range(ZS):
+        for y in range(YS):
+            x, core = root_of(z)
+            pairs.append((device(x, core, z, y), device(*target(x, core, z, y))))
+    return lax.ppermute(array, ALL, pairs)
+
+
+def along_x(slab, core, shifts):
+    return sum(from_root(slab, lambda x, c, z, y: ((x + by) % XS, core, z, y)) for by in shifts)
+
+
+def pair_sum(partial):
+    first = lax.axis_index("core") == 0
+    given = lax.ppermute(jnp.where(first, partial[1], partial[0]), "core", [(0, 1), (1, 0)])
+    pair = jnp.where(first, partial[0], partial[1]).astype(F32) + given.astype(F32)
+    return pair.astype(BF16)
+
+
+def sum_over_x(pair):
+    x = lax.axis_index("x")
     pair = pair.reshape(XS, -1, pair.shape[1])
     tile = lambda k: lax.dynamic_index_in_dim(pair, (x + k) % XS, 0, keepdims=False)
     far = tile(2)
@@ -112,13 +113,13 @@
     y = lax.axis_index("y")
     quarters = array.reshape(YS, -1, array.shape[1])
     own = lambda k: lax.dynamic_index_in_dim(quarters, y ^ k, 0, keepdims=False)
-    wide = [own(0)] + [exchanged(own(k), "y", YS, k) for k in range(1, YS)]
-    wide = [w.astype(F32) for w in wide]
-    part = lax.optimization_barrier(((wide[0] + wide[1]) + (wide[2] + wide[3])).astype(BF16))
-    wide = [part.astype(F32)] + [exchanged(part, "z", ZS, k).astype(F32) for k in range(1, 4)]
-    part = lax.optimization_barrier(((wide[0] + wide[1]) + (wide[2] + wide[3])).astype(BF16))
-    part = part.astype(F32) + exchanged(part, "z", ZS, 4).astype(F32)
+    part = own(0).astype(F32)
+    for k in range(1, YS):
+        part = part + exchanged(own(k), "y", YS, k).astype(F32)
     part = lax.optimization_barrier(part.astype(BF16))
+    copies = jnp.broadcast_to(part[None], (ZS, *part.shape))
+    part = lax.all_to_all(copies, "z", split_axis=0, concat_axis=0, tiled=True)
+    part = lax.optimization_barrier(part.astype(F32).sum(axis=0).astype(BF16))
     whole = jnp.zeros(quarters.shape, BF16)
     for k in range(YS):
         got = part if k == 0 else exchanged(part, "y", YS, k)
@@ -139,7 +140,7 @@
     piece_rows, width = pieces.shape[1:]
     row = lax.axis_index(ROW)
     col = lax.axis_index(COL)
-    core, y = lax.axis_index("core"), lax.axis_index("y")
+    core, z, y = lax.axis_index("core"), lax.axis_index("z"), lax.axis_index("y")
     chosen = listing[:, :NSEL]
 
     def keep_of(first, count):
@@ -149,17 +150,40 @@
     own_keep = keep_of((row * ZS * YS + col) * piece_rows, piece_rows)
     normed = jnp.einsum("srk,skj->srj", pieces, factor_inv, preferred_element_type=F32)
     normed = (normed * own_keep[:, :, None]).astype(BF16)
-    panels = [panel_y_then_z(normed[0]), panel_z_then_y(normed[1])]
-
     rows = inverse_block.shape[0]
-    partial = [
-        jnp.einsum("qj,pq->jp", panel, inverse_block, preferred_element_type=F32).astype(BF16)
-        for panel in panels
-    ]
-    factor_slab = to_cores(
-        [lax.dynamic_slice_in_dim(panel, y * rows, rows, 0) for panel in panels]
-    )
-    product = sum_over_row(partial)
+
+    def partial_of(panel):
+        return jnp.einsum("qj,pq->jp", panel, inverse_block, preferred_element_type=F32).astype(BF16)
+
+    first = core == 0
+    near = near_z_then_y(normed[1])
+
+    deep = rows // (piece_rows * YS)
+    of_slab = lambda part, lane: lax.dynamic_slice_in_dim(part, lane * deep, deep, 0)
+    far_part = from_root(
+        of_slab(near[0], (y + 2) % YS), lambda x, c, z, y: (x, c, z, (y + 2) % YS)
+    )
+    slab_parts = [of_slab(near[0], y), of_slab(near[1], y), far_part, of_slab(near[2], y)]
+    slab_1 = placed_by_owner(slab_parts, y, 1).reshape(rows, width)
+    sent_1 = along_x(slab_1, 1, (1, -1, -2))
+
+    panel_0 = panel_y_then_z(normed[0])
+    panel_0, near = lax.optimization_barrier((panel_0, near))
+    chunks = [near[0], near[1], far_chunk(near), near[2]]
+    slab_0 = lax.dynamic_slice_in_dim(panel_0, y * rows, rows, 0)
+    sent_0 = along_x(slab_0, 0, (1, -1, 2))
+    partial = [partial_of(panel_0)]
+
+    chunks, partial[0] = lax.optimization_barrier((chunks, partial[0]))
+    across = from_root(
+        jnp.where(first, slab_1, slab_0), lambda x, c, z, y: (x, 1 - c, z, y)
+    )
+    partial.append(partial_of(placed_by_owner(chunks, y, 1).reshape(panel_0.shape)))
+
+    home = row == z
+    factor_slab = jnp.where(home, jnp.where(first, slab_0, slab_1), sent_0 + sent_1 + across)
+    pair, factor_slab = lax.optimization_barrier((pair_sum(partial), factor_slab))
+    product = sum_over_x(pair)
     col_keep = lax.dynamic_index_in_dim(keep_of(col * rows, rows), core, 0)
     offdiag = lax.optimization_barrier((-(product * col_keep)).astype(BF16))
 

time: 205 us -> 168 us (0.82); the launches traced: 201 us -> 167 us
  starting transfers between devices: 98.1 us -> 79 us
  waiting for transfers between devices: 60.4 us -> 45 us
  matrix products: 14.2 us -> 11.2 us
  other arithmetic: 7.41 us -> 9.54 us
    ppermute x10 -> x6, starting transfers between devices: 41.3 us -> 7.12 us  [exchanged(): return lax.ppermute(array, axis, [(i, i ^ by) for i in range(size)])]
    ppermute x18, waiting for transfers between devices: 45.5 us -> 28.3 us  [shift(): lax.ppermute(array, axis, [(i, (i + by) % size) for i in range(size)])]
    ppermute x2, starting transfers between devices: 2.81 us -> 17.4 us  [own_slab_of_both(): got = lax.ppermute(given, 'core', [(0, 1), (1, 0)])]
    ppermute x10 -> x6, waiting for transfers between devices: 14.6 us -> 5.43 us  [exchanged(): return lax.ppermute(array, axis, [(i, i ^ by) for i in range(size)])]
    all_to_all x0 -> x1, starting transfers between devices: none -> 8.23 us  [summed_over_col(): part = lax.all_to_all(copies, 'z', split_axis=0, concat_axis=0, tiled=True)]
    all_gather x1, waiting for transfers between devices: 0.02 us -> 8.17 us  [panel_y_then_z(): return lax.all_gather(part, 'z', axis=0, tiled=True)]
    ppermute x18, starting transfers between devices: 33.4 us -> 27.1 us  [shift(): lax.ppermute(array, axis, [(i, (i + by) % size) for i in range(size)])]
    unnamed x16 -> x22, local copies, waits for them, and re-layouts: 4.9 us -> 1.09 us
  transfers between devices with their start and end apart: 40 -> 37, of which waited for: 18 -> 16; matrix products, arithmetic and copies ran while one was open for 8% -> 13% of each run, Pallas kernels for 0% -> 0%
where the time goes in v5:
time: 168 us; the launch traced here: 167 us
  starting transfers between devices  79 us (47%)
  waiting for transfers between devices  45 us (27%)
  between operations  14.8 us (9%)
  matrix products  11.2 us (7%)
  other arithmetic  9.54 us (6%)
  local copies, waits for them, and re-layouts  7.73 us (5%)
    ppermute x18, waiting for transfers between devices, shift(): lax.ppermute(array, axis, [(i, (i + by) % size) for i in range(size)])  28.3 us
    ppermute x18, starting transfers between devices, shift(): lax.ppermute(array, axis, [(i, (i + by) % size) for i in range(size)])  27.1 us
    ppermute x2, starting transfers between devices, own_slab_of_both(): got = lax.ppermute(given, 'core', [(0, 1), (1, 0)])  17.4 us
    ppermute x8, starting transfers between devices, from_root(): return lax.ppermute(array, ALL, pairs)  12 us
    dot_general x2, matrix products, partial_of(): jnp.einsum('qj,pq->jp', panel, inverse_block, preferred_element_type=F32)  9.74 us
    all_to_all x1, starting transfers between devices, summed_over_col(): part = lax.all_to_all(copies, 'z', split_axis=0, concat_axis=0, tiled=True)  8.23 us
    all_gather x1, waiting for transfers between devices, panel_y_then_z(): return lax.all_gather(part, 'z', axis=0, tiled=True)  8.17 us
    ppermute x1, starting transfers between devices, pair_sum(): lax.ppermute(jnp.where(first, partial[1], partial[0]), 'core', [(0, 1), (...  7.17 us
  transfers between devices with their start and end apart: 37, of which 16 were waited for; matrix products, arithmetic and copies ran while one was open for 13% of the time, Pallas kernels for 0%

profile of v5, /device:TPU:1, one launch (start us, length us, event | category | flops | bytes accessed | tf_op | source)
XLA Modules:
  0.0 167.4 jit_solution(10840667618164841803)
XLA Ops:
  9.7 3.8 %collective-permute-start.1 = (bf16[96,512]{1,0:T(8,128)(2,1)S(1)}, bf16[96,512]{1,0:T(8,128)(2,1)S(1)}, u32[]{:S(2)}, u32[]{:S(2)}) collective-permute-start(bf16[96,512]{1,0:T(8,128)(2,1)S(1)} %get-tuple-element.37), channel_id=1, source_target_pairs={{0,2},{1,3},{2,0},{3,1},{4,6},{5,7},{6,4},{7,5},{8,10},{9,11},{10,... | collective-permute-start | bytes 294920 | tf_op jit(solution)/shard_map/ppermute | solution.py:17
  13.9 2.3 %collective-permute-start.2 = (bf16[96,512]{1,0:T(8,128)(2,1)S(1)}, bf16[96,512]{1,0:T(8,128)(2,1)S(1)}, u32[]{:S(2)}, u32[]{:S(2)}) collective-permute-start(bf16[96,512]{1,0:T(8,128)(2,1)S(1)} %get-tuple-element.37), channel_id=1, source_target_pairs={{0,3},{1,0},{2,1},{3,2},{4,7},{5,4},{6,5},{7,6},{8,11},{9,8},{10,9... | collective-permute-start | bytes 294920 | tf_op jit(solution)/shard_map/ppermute | solution.py:17
  16.3 3.8 %collective-permute-done = bf16[96,512]{1,0:T(8,128)(2,1)S(1)} collective-permute-done((bf16[96,512]{1,0:T(8,128)(2,1)S(1)}, bf16[96,512]{1,0:T(8,128)(2,1)S(1)}, u32[]{:S(2)}, u32[]{:S(2)}) %collective-permute-start) | collective-permute-done | bytes 98336 | tf_op jit(solution)/shard_map/ppermute | solution.py:17
  21.1 3.8 %collective-permute-start.7 = (bf16[1,96,512]{2,1,0:T(8,128)(2,1)S(1)}, bf16[1,96,512]{2,1,0:T(8,128)(2,1)S(1)}, u32[]{:S(2)}, u32[]{:S(2)}) collective-permute-start(bf16[1,96,512]{2,1,0:T(8,128)(2,1)S(1)} %get-tuple-element.36), channel_id=1, source_target_pairs={{0,28},{4,0},{8,4},{12,8},{16,12},{20,16},{24,20},{28,24},{1,29},{... | collective-permute-start | bytes 294920 | tf_op jit(solution)/shard_map/ppermute | solution.py:17
  25.1 1.7 %collective-permute-done.3 = bf16[1,96,512]{2,1,0:T(8,128)(2,1)S(1)} collective-permute-done((bf16[1,96,512]{2,1,0:T(8,128)(2,1)S(1)}, bf16[1,96,512]{2,1,0:T(8,128)(2,1)S(1)}, u32[]{:S(2)}, u32[]{:S(2)}) %collective-permute-start.3) | collective-permute-done | bytes 98336 | tf_op jit(solution)/shard_map/ppermute | solution.py:17
  26.8 2.8 %collective-permute-start.8 = (bf16[1,96,512]{2,1,0:T(8,128)(2,1)S(1)}, bf16[1,96,512]{2,1,0:T(8,128)(2,1)S(1)}, u32[]{:S(2)}, u32[]{:S(2)}) collective-permute-start(bf16[1,96,512]{2,1,0:T(8,128)(2,1)S(1)} %collective-permute-done.7), channel_id=1, source_target_pairs={{0,28},{4,0},{8,4},{12,8},{16,12},{20,16},{24,20},{28,24},{1,29},{... | collective-permute-start | bytes 294920 | tf_op jit(solution)/shard_map/ppermute | solution.py:17
  29.6 1.9 %collective-permute-done.4 = bf16[1,96,512]{2,1,0:T(8,128)(2,1)S(1)} collective-permute-done((bf16[1,96,512]{2,1,0:T(8,128)(2,1)S(1)}, bf16[1,96,512]{2,1,0:T(8,128)(2,1)S(1)}, u32[]{:S(2)}, u32[]{:S(2)}) %collective-permute-start.4) | collective-permute-done | bytes 98336 | tf_op jit(solution)/shard_map/ppermute | solution.py:17
  31.5 2.8 %collective-permute-start.9 = (bf16[1,96,512]{2,1,0:T(8,128)(2,1)S(1)}, bf16[1,96,512]{2,1,0:T(8,128)(2,1)S(1)}, u32[]{:S(2)}, u32[]{:S(2)}) collective-permute-start(bf16[1,96,512]{2,1,0:T(8,128)(2,1)S(1)} %collective-permute-done.8), channel_id=1, source_target_pairs={{0,28},{4,0},{8,4},{12,8},{16,12},{20,16},{24,20},{28,24},{1,29},{... | collective-permute-start | bytes 294920 | tf_op jit(solution)/shard_map/ppermute | solution.py:17
  34.3 1.9 %collective-permute-done.5 = bf16[1,96,512]{2,1,0:T(8,128)(2,1)S(1)} collective-permute-done((bf16[1,96,512]{2,1,0:T(8,128)(2,1)S(1)}, bf16[1,96,512]{2,1,0:T(8,128)(2,1)S(1)}, u32[]{:S(2)}, u32[]{:S(2)}) %collective-permute-start.5) | collective-permute-done | bytes 98336 | tf_op jit(solution)/shard_map/ppermute | solution.py:17
  36.2 7.8 %collective-permute-done.6 = bf16[1,96,512]{2,1,0:T(8,128)(2,1)S(1)} collective-permute-done((bf16[1,96,512]{2,1,0:T(8,128)(2,1)S(1)}, bf16[1,96,512]{2,1,0:T(8,128)(2,1)S(1)}, u32[]{:S(2)}, u32[]{:S(2)}) %collective-permute-start.6) | collective-permute-done | bytes 98336 | tf_op jit(solution)/shard_map/ppermute | solution.py:17
  44.1 1.9 %collective-permute-start.10 = (bf16[8,1,96,512]{3,2,1,0:T(8,128)(2,1)S(1)}, bf16[8,1,96,512]{3,2,1,0:T(8,128)(2,1)}, u32[]{:S(2)}, u32[]{:S(2)}) collective-permute-start(bf16[8,1,96,512]{3,2,1,0:T(8,128)(2,1)S(1)} %bitcast_dynamic-update-slice_fusion), channel_id=1, source_target_pairs={{0,1},{1,2},{2,3},{3,0},{4,5},{5,6},{6,7},{7,4},{8,9},{9,10},{10,1... | collective-permute-start | bytes 2359304 | tf_op jit(solution)/shard_map/ppermute | solution.py:17
  49.3 7.6 %collective-permute-done.10 = bf16[8,1,96,512]{3,2,1,0:T(8,128)(2,1)} collective-permute-done((bf16[8,1,96,512]{3,2,1,0:T(8,128)(2,1)S(1)}, bf16[8,1,96,512]{3,2,1,0:T(8,128)(2,1)}, u32[]{:S(2)}, u32[]{:S(2)}) %collective-permute-start.10) | collective-permute-done | bytes 786464 | tf_op jit(solution)/shard_map/ppermute | solution.py:17
  60.4 1.6 collective-permute-start.19
  63.5 8.2 %all-gather.2.cloned.1.call-done = bf16[3072,512]{1,0:T(8,128)(2,1)} async-done(((bf16[384,512]{1,0:T(8,128)(2,1)}), bf16[3072,512]{1,0:T(8,128)(2,1)}) %all-gather.2.cloned.1.call-update) | async-done | bytes 3145744 | tf_op jit(solution)/shard_map/all_gather | solution.py:53
  72.8 2.3 %collective-permute-start.13 = (bf16[4,1,96,512]{3,2,1,0:T(8,128)(2,1)S(1)}, bf16[4,1,96,512]{3,2,1,0:T(8,128)(2,1)S(1)}, u32[]{:S(2)}, u32[]{:S(2)}) collective-permute-start(bf16[4,1,96,512]{3,2,1,0:T(8,128)(2,1)S(1)} %slice.31), channel_id=1, source_target_pairs={{0,3},{1,0},{2,1},{3,2},{4,7},{5,4},{6,5},{7,6},{8,11},{9,8},{10,9... | collective-permute-start | bytes 1179656 | tf_op jit(solution)/shard_map/ppermute | solution.py:17
  75.1 5.9 %convolution_convert_fusion.1 = bf16[512,768]{1,0:T(8,128)(2,1)S(1)} fusion(bf16[3072,512]{1,0:T(8,128)(2,1)} %all-gather.2.cloned.1.call-done, bf16[768,3072]{1,0:T(8,128)(2,1)} %param.8), kind=kOutput, calls=%fused_computation.2 | convolution fusion | flops 2416312320 | bytes 8650752 | tf_op jit(solution)/shard_map/qj,pq->jp/dot_general | solution.py:156
  81.1 2.6 %broadcast_select_fusion = (bf16[768,512]{1,0:T(8,128)(2,1)}, bf16[768,512]{1,0:T(8,128)(2,1)S(1)}) fusion(pred[]{:T(512)S(6)} %eq.63, bf16[2,4,96,512]{3,2,1,0:T(8,128)(2,1)S(1)} %dynamic-slice_dynamic-update-slice_fusion, bf16[3072,512]{1,0:T(8,128)(2,1)} %all-gather.2.cloned.1.call-done, s32[]{:T(128)S(6)} %select_n.299), kind=kLoop, calls=%fused_computation.9 | loop fusion | flops 393216 | bytes 3145733 | tf_op jit(solution)/shard_map/jit(_where)/select_n | solution.py:179
  83.7 1.6 collective-permute-start.18
  88.8 1.6 collective-permute-start.16
  91.7 3.8 %broadcast_select_fusion.1 = (bf16[512,768]{1,0:T(8,128)(2,1)}, bf16[512,768]{1,0:T(8,128)(2,1)}) fusion(bf16[512,768]{1,0:T(8,128)(2,1)S(1)} %convolution_convert_fusion.1, pred[]{:T(512)S(6)} %eq.63, bf16[3072,512]{1,0:T(8,128)(2,1)S(1)} %bitcast.98, bf16[768,3072]{1,0:T(8,128)(2,1)S(1)} %bitcast.111), kind=kOutput, calls=%fused_computation.10 | convolution fusion | flops 2416705536 | bytes 10223617 | tf_op jit(solution)/shard_map/qj,pq->jp/dot_general | solution.py:156
  95.5 7.2 %collective-permute-start.14 = (bf16[512,768]{1,0:T(8,128)(2,1)}, bf16[512,768]{1,0:T(8,128)(2,1)}, u32[]{:S(2)}, u32[]{:S(2)}) collective-permute-start(bf16[512,768]{1,0:T(8,128)(2,1)} %get-tuple-element.41), channel_id=1, source_target_pairs={{0,32},{32,0},{1,33},{33,1},{2,34},{34,2},{3,35},{35,3},{4,36},{36... | collective-permute-start | bytes 2359304 | tf_op jit(solution)/shard_map/ppermute | solution.py:90
  102.7 2.7 %add_select_fusion = bf16[768,512]{1,0:T(8,128)(2,1)S(1)} fusion(bf16[768,512]{1,0:T(8,128)(2,1)S(1)} %collective-permute-done.22, bf16[768,512]{1,0:T(8,128)(2,1)} %collective-permute-done.21, bf16[768,512]{1,0:T(8,128)(2,1)} %collective-permute-done.19, bf16[768,512]{1,0:T(8,128)(2,1)} %collective-permute-done.20, ...), kind=kLoop, calls=%fused_computation.8 | loop fusion | flops 3145728 | bytes 7864322 | tf_op jit(solution)/shard_map/jit(_where)/select_n | solution.py:184
  107.1 2.7 %collective-permute-start.26 = (bf16[128,768]{1,0:T(8,128)(2,1)S(1)}, bf16[128,768]{1,0:T(8,128)(2,1)S(1)}, u32[]{:S(2)}, u32[]{:S(2)}) collective-permute-start(bf16[128,768]{1,0:T(8,128)(2,1)S(1)} %get-tuple-element.29), channel_id=1, source_target_pairs={{0,192},{64,0},{128,64},{192,128},{1,193},{65,1},{129,65},{193,129... | collective-permute-start | bytes 589832 | tf_op jit(solution)/shard_map/ppermute | solution.py:17
  109.9 3.0 %collective-permute-start.24 = (bf16[64,768]{1,0:T(8,128)(2,1)S(1)}, bf16[64,768]{1,0:T(8,128)(2,1)S(1)}, u32[]{:S(2)}, u32[]{:S(2)}) collective-permute-start(bf16[64,768]{1,0:T(8,128)(2,1)S(1)} %get-tuple-element.27), channel_id=1, source_target_pairs={{0,128},{64,192},{128,0},{192,64},{1,129},{65,193},{129,1},{193,65... | collective-permute-start | bytes 294920 | tf_op jit(solution)/shard_map/ppermute | solution.py:17
  113.0 2.4 %collective-permute-done.23 = bf16[64,768]{1,0:T(8,128)(2,1)S(1)} collective-permute-done((bf16[64,768]{1,0:T(8,128)(2,1)S(1)}, bf16[64,768]{1,0:T(8,128)(2,1)S(1)}, u32[]{:S(2)}, u32[]{:S(2)}) %collective-permute-start.23) | collective-permute-done | bytes 98336 | tf_op jit(solution)/shard_map/ppermute | solution.py:17
  117.8 2.1 %collective-permute-start.30 = (bf16[32,512]{1,0:T(8,128)(2,1)S(1)}, bf16[32,512]{1,0:T(8,128)(2,1)S(1)}, u32[]{:S(2)}, u32[]{:S(2)}) collective-permute-start(bf16[32,512]{1,0:T(8,128)(2,1)S(1)} %get-tuple-element.39), channel_id=1, source_target_pairs={{0,3},{1,2},{2,1},{3,0},{4,7},{5,6},{6,5},{7,4},{8,11},{9,10},{10,... | collective-permute-start | bytes 98312 | tf_op jit(solution)/shard_map/ppermute | solution.py:109
  122.0 2.1 %collective-permute-done.29 = bf16[32,512]{1,0:T(8,128)(2,1)S(1)} collective-permute-done((bf16[32,512]{1,0:T(8,128)(2,1)S(1)}, bf16[32,512]{1,0:T(8,128)(2,1)S(1)}, u32[]{:S(2)}, u32[]{:S(2)}) %collective-permute-start.29) | collective-permute-done | bytes 32800 | tf_op jit(solution)/shard_map/ppermute | solution.py:109
  124.9 8.2 %all-to-all-start = ((bf16[8,32,512]{2,1,0:T(8,128)(2,1)}), bf16[8,32,512]{2,1,0:T(8,128)(2,1)S(1)}, u32[]{:S(2)}, u32[]{:S(2)}) async-start(bf16[8,32,512]{2,1,0:T(8,128)(2,1)} %broadcast_in_dim.68), calls=%async_computation | async-start | bytes 524288 | tf_op jit(solution)/shard_map/all_to_all | solution.py:121
  133.1 6.5 %collective-permute-start.27 = (bf16[64,768]{1,0:T(8,128)(2,1)S(1)}, bf16[64,768]{1,0:T(8,128)(2,1)S(1)}, u32[]{:S(2)}, u32[]{:S(2)}) collective-permute-start(bf16[64,768]{1,0:T(8,128)(2,1)S(1)} %dynamic-slice_bitcast_fusion.4), channel_id=1, source_target_pairs={{0,32},{32,0},{1,33},{33,1},{2,34},{34,2},{3,35},{35,3},{4,36},{36... | collective-permute-start | bytes 294920 | tf_op jit(solution)/shard_map/ppermute | solution.py:135
  140.5 1.9 %all-to-all-done = bf16[8,32,512]{2,1,0:T(8,128)(2,1)S(1)} async-done(((bf16[8,32,512]{2,1,0:T(8,128)(2,1)}), bf16[8,32,512]{2,1,0:T(8,128)(2,1)S(1)}, u32[]{:S(2)}, u32[]{:S(2)}) %all-to-all-start) | async-done | bytes 262176 | tf_op jit(solution)/shard_map/all_to_all | solution.py:121
  145.8 2.0 %collective-permute-done.31 = bf16[32,512]{1,0:T(8,128)(2,1)S(1)} collective-permute-done((bf16[32,512]{1,0:T(8,128)(2,1)S(1)}, bf16[32,512]{1,0:T(8,128)(2,1)S(1)}, u32[]{:S(2)}, u32[]{:S(2)}) %collective-permute-start.31) | collective-permute-done | bytes 32800 | tf_op jit(solution)/shard_map/ppermute | solution.py:109
  147.9 10.9 %collective-permute-start.34 = (bf16[64,512]{1,0:T(8,128)(2,1)S(1)}, bf16[64,512]{1,0:T(8,128)(2,1)S(1)}, u32[]{:S(2)}, u32[]{:S(2)}) collective-permute-start(bf16[64,512]{1,0:T(8,128)(2,1)S(1)} %dynamic-slice_bitcast_fusion.5), channel_id=1, source_target_pairs={{0,32},{32,0},{1,33},{33,1},{2,34},{34,2},{3,35},{35,3},{4,36},{36... | collective-permute-start | bytes 196616 | tf_op jit(solution)/shard_map/ppermute | solution.py:135
  (125 shorter events, 31.2 us)
Async XLA Ops:
  7.2 64.5 %all-gather.2.cloned.1.call-start = ((), (), s32[]{:S(2)}) async-start(), calls=%async_computation.1 | async-start | bytes 3538944 | tf_op jit(solution)/shard_map/all_gather | solution.py:53
  9.7 10.5 %collective-permute-start.1 = (bf16[96,512]{1,0:T(8,128)(2,1)S(1)}, bf16[96,512]{1,0:T(8,128)(2,1)S(1)}, u32[]{:S(2)}, u32[]{:S(2)}) collective-permute-start(bf16[96,512]{1,0:T(8,128)(2,1)S(1)} %get-tuple-element.37), channel_id=1, source_target_pairs={{0,2},{1,3},{2,0},{3,1},{4,6},{5,7},{6,4},{7,5},{8,10},{9,11},{10,... | collective-permute-start | bytes 294920 | tf_op jit(solution)/shard_map/ppermute | solution.py:17
  13.5 6.6 %collective-permute-start = (bf16[96,512]{1,0:T(8,128)(2,1)S(1)}, bf16[96,512]{1,0:T(8,128)(2,1)S(1)}, u32[]{:S(2)}, u32[]{:S(2)}) collective-permute-start(bf16[96,512]{1,0:T(8,128)(2,1)S(1)} %get-tuple-element.37), channel_id=1, source_target_pairs={{0,1},{1,2},{2,3},{3,0},{4,5},{5,6},{6,7},{7,4},{8,9},{9,10},{10,1... | collective-permute-start | bytes 294920 | tf_op jit(solution)/shard_map/ppermute | solution.py:17
  13.9 6.3 %collective-permute-start.2 = (bf16[96,512]{1,0:T(8,128)(2,1)S(1)}, bf16[96,512]{1,0:T(8,128)(2,1)S(1)}, u32[]{:S(2)}, u32[]{:S(2)}) collective-permute-start(bf16[96,512]{1,0:T(8,128)(2,1)S(1)} %get-tuple-element.37), channel_id=1, source_target_pairs={{0,3},{1,0},{2,1},{3,2},{4,7},{5,4},{6,5},{7,6},{8,11},{9,8},{10,9... | collective-permute-start | bytes 294920 | tf_op jit(solution)/shard_map/ppermute | solution.py:17
  21.0 5.9 %collective-permute-start.3 = (bf16[1,96,512]{2,1,0:T(8,128)(2,1)S(1)}, bf16[1,96,512]{2,1,0:T(8,128)(2,1)S(1)}, u32[]{:S(2)}, u32[]{:S(2)}) collective-permute-start(bf16[1,96,512]{2,1,0:T(8,128)(2,1)S(1)} %get-tuple-element.36), channel_id=1, source_target_pairs={{0,4},{4,8},{8,12},{12,16},{16,20},{20,24},{24,28},{28,0},{1,5},{5... | collective-permute-start | bytes 294920 | tf_op jit(solution)/shard_map/ppermute | solution.py:17
  21.1 5.8 %collective-permute-start.7 = (bf16[1,96,512]{2,1,0:T(8,128)(2,1)S(1)}, bf16[1,96,512]{2,1,0:T(8,128)(2,1)S(1)}, u32[]{:S(2)}, u32[]{:S(2)}) collective-permute-start(bf16[1,96,512]{2,1,0:T(8,128)(2,1)S(1)} %get-tuple-element.36), channel_id=1, source_target_pairs={{0,28},{4,0},{8,4},{12,8},{16,12},{20,16},{24,20},{28,24},{1,29},{... | collective-permute-start | bytes 294920 | tf_op jit(solution)/shard_map/ppermute | solution.py:17
  26.8 4.7 %collective-permute-start.4 = (bf16[1,96,512]{2,1,0:T(8,128)(2,1)S(1)}, bf16[1,96,512]{2,1,0:T(8,128)(2,1)S(1)}, u32[]{:S(2)}, u32[]{:S(2)}) collective-permute-start(bf16[1,96,512]{2,1,0:T(8,128)(2,1)S(1)} %collective-permute-done.3), channel_id=1, source_target_pairs={{0,4},{4,8},{8,12},{12,16},{16,20},{20,24},{24,28},{28,0},{1,5},{5... | collective-permute-start | bytes 294920 | tf_op jit(solution)/shard_map/ppermute | solution.py:17
  26.8 4.7 %collective-permute-start.8 = (bf16[1,96,512]{2,1,0:T(8,128)(2,1)S(1)}, bf16[1,96,512]{2,1,0:T(8,128)(2,1)S(1)}, u32[]{:S(2)}, u32[]{:S(2)}) collective-permute-start(bf16[1,96,512]{2,1,0:T(8,128)(2,1)S(1)} %collective-permute-done.7), channel_id=1, source_target_pairs={{0,28},{4,0},{8,4},{12,8},{16,12},{20,16},{24,20},{28,24},{1,29},{... | collective-permute-start | bytes 294920 | tf_op jit(solution)/shard_map/ppermute | solution.py:17
  31.5 4.7 %collective-permute-start.5 = (bf16[1,96,512]{2,1,0:T(8,128)(2,1)S(1)}, bf16[1,96,512]{2,1,0:T(8,128)(2,1)S(1)}, u32[]{:S(2)}, u32[]{:S(2)}) collective-permute-start(bf16[1,96,512]{2,1,0:T(8,128)(2,1)S(1)} %collective-permute-done.4), channel_id=1, source_target_pairs={{0,4},{4,8},{8,12},{12,16},{16,20},{20,24},{24,28},{28,0},{1,5},{5... | collective-permute-start | bytes 294920 | tf_op jit(solution)/shard_map/ppermute | solution.py:17
  31.5 12.6 %collective-permute-start.9 = (bf16[1,96,512]{2,1,0:T(8,128)(2,1)S(1)}, bf16[1,96,512]{2,1,0:T(8,128)(2,1)S(1)}, u32[]{:S(2)}, u32[]{:S(2)}) collective-permute-start(bf16[1,96,512]{2,1,0:T(8,128)(2,1)S(1)} %collective-permute-done.8), channel_id=1, source_target_pairs={{0,28},{4,0},{8,4},{12,8},{16,12},{20,16},{24,20},{28,24},{1,29},{... | collective-permute-start | bytes 294920 | tf_op jit(solution)/shard_map/ppermute | solution.py:17
  36.2 7.9 %collective-permute-start.6 = (bf16[1,96,512]{2,1,0:T(8,128)(2,1)S(1)}, bf16[1,96,512]{2,1,0:T(8,128)(2,1)S(1)}, u32[]{:S(2)}, u32[]{:S(2)}) collective-permute-start(bf16[1,96,512]{2,1,0:T(8,128)(2,1)S(1)} %collective-permute-done.5), channel_id=1, source_target_pairs={{0,4},{4,8},{8,12},{12,16},{16,20},{20,24},{24,28},{28,0},{1,5},{5... | collective-permute-start | bytes 294920 | tf_op jit(solution)/shard_map/ppermute | solution.py:17
  44.1 12.7 %collective-permute-start.10 = (bf16[8,1,96,512]{3,2,1,0:T(8,128)(2,1)S(1)}, bf16[8,1,96,512]{3,2,1,0:T(8,128)(2,1)}, u32[]{:S(2)}, u32[]{:S(2)}) collective-permute-start(bf16[8,1,96,512]{3,2,1,0:T(8,128)(2,1)S(1)} %bitcast_dynamic-update-slice_fusion), channel_id=1, source_target_pairs={{0,1},{1,2},{2,3},{3,0},{4,5},{5,6},{6,7},{7,4},{8,9},{9,10},{10,1... | collective-permute-start | bytes 2359304 | tf_op jit(solution)/shard_map/ppermute | solution.py:17
  46.0 12.8 %collective-permute-start.11 = (bf16[8,1,96,512]{3,2,1,0:T(8,128)(2,1)S(1)}, bf16[8,1,96,512]{3,2,1,0:T(8,128)(2,1)S(1)}, u32[]{:S(2)}, u32[]{:S(2)}) collective-permute-start(bf16[8,1,96,512]{3,2,1,0:T(8,128)(2,1)S(1)} %bitcast_dynamic-update-slice_fusion), channel_id=1, source_target_pairs={{0,3},{1,0},{2,1},{3,2},{4,7},{5,4},{6,5},{7,6},{8,11},{9,8},{10,9... | collective-permute-start | bytes 2359304 | tf_op jit(solution)/shard_map/ppermute | solution.py:17
  48.0 9.9 %collective-permute-start.15 = (bf16[2,1,96,512]{3,2,1,0:T(8,128)(2,1)}, bf16[2,1,96,512]{3,2,1,0:T(8,128)(2,1)}, u32[]{:S(2)}, u32[]{:S(2)}) collective-permute-start(bf16[2,1,96,512]{3,2,1,0:T(8,128)(2,1)} %get-tuple-element.30), channel_id=1, source_target_pairs={{0,2},{1,3},{2,0},{3,1},{36,38},{37,39},{38,36},{39,37},{72,74},{7... | collective-permute-start | bytes 589832 | tf_op jit(solution)/shard_map/ppermute | solution.py:81
  58.9 29.9 %collective-permute-start.20 = (bf16[768,512]{1,0:T(8,128)(2,1)S(1)}, bf16[768,512]{1,0:T(8,128)(2,1)}, u32[]{:S(2)}, u32[]{:S(2)}) collective-permute-start(bf16[768,512]{1,0:T(8,128)(2,1)S(1)} %bitcast.95), channel_id=1, source_target_pairs={{0,224},{1,225},{2,226},{3,227},{36,228},{37,229},{38,230},{39,231... | collective-permute-start | bytes 2359304 | tf_op jit(solution)/shard_map/ppermute | solution.py:81
  60.4 30.0 %collective-permute-start.19 = (bf16[768,512]{1,0:T(8,128)(2,1)S(1)}, bf16[768,512]{1,0:T(8,128)(2,1)}, u32[]{:S(2)}, u32[]{:S(2)}) collective-permute-start(bf16[768,512]{1,0:T(8,128)(2,1)S(1)} %bitcast.96), channel_id=1, source_target_pairs={{0,96},{1,97},{2,98},{3,99},{36,100},{37,101},{38,102},{39,103},{7... | collective-permute-start | bytes 2359304 | tf_op jit(solution)/shard_map/ppermute | solution.py:81
  62.0 33.5 %collective-permute-start.21 = (bf16[768,512]{1,0:T(8,128)(2,1)S(1)}, bf16[768,512]{1,0:T(8,128)(2,1)}, u32[]{:S(2)}, u32[]{:S(2)}) collective-permute-start(bf16[768,512]{1,0:T(8,128)(2,1)S(1)} %bitcast.97), channel_id=1, source_target_pairs={{0,160},{1,161},{2,162},{3,163},{36,164},{37,165},{38,166},{39,167... | collective-permute-start | bytes 2359304 | tf_op jit(solution)/shard_map/ppermute | solution.py:81
  72.8 10.9 %collective-permute-start.13 = (bf16[4,1,96,512]{3,2,1,0:T(8,128)(2,1)S(1)}, bf16[4,1,96,512]{3,2,1,0:T(8,128)(2,1)S(1)}, u32[]{:S(2)}, u32[]{:S(2)}) collective-permute-start(bf16[4,1,96,512]{3,2,1,0:T(8,128)(2,1)S(1)} %slice.31), channel_id=1, source_target_pairs={{0,3},{1,0},{2,1},{3,2},{4,7},{5,4},{6,5},{7,6},{8,11},{9,8},{10,9... | collective-permute-start | bytes 1179656 | tf_op jit(solution)/shard_map/ppermute | solution.py:17
  75.1 10.2 %collective-permute-start.12 = (bf16[4,1,96,512]{3,2,1,0:T(8,128)(2,1)S(1)}, bf16[4,1,96,512]{3,2,1,0:T(8,128)(2,1)S(1)}, u32[]{:S(2)}, u32[]{:S(2)}) collective-permute-start(bf16[4,1,96,512]{3,2,1,0:T(8,128)(2,1)S(1)} %slice.30), channel_id=1, source_target_pairs={{0,1},{1,2},{2,3},{3,0},{4,5},{5,6},{6,7},{7,4},{8,9},{9,10},{10,1... | collective-permute-start | bytes 1179656 | tf_op jit(solution)/shard_map/ppermute | solution.py:17
  83.7 19.0 %collective-permute-start.18 = (bf16[768,512]{1,0:T(8,128)(2,1)S(1)}, bf16[768,512]{1,0:T(8,128)(2,1)}, u32[]{:S(2)}, u32[]{:S(2)}) collective-permute-start(bf16[768,512]{1,0:T(8,128)(2,1)S(1)} %get-tuple-element.25), channel_id=1, source_target_pairs={{0,128},{1,129},{2,130},{3,131},{36,132},{37,133},{38,134},{39,135... | collective-permute-start | bytes 2359304 | tf_op jit(solution)/shard_map/ppermute | solution.py:81
  85.3 17.5 %collective-permute-start.17 = (bf16[768,512]{1,0:T(8,128)(2,1)S(1)}, bf16[768,512]{1,0:T(8,128)(2,1)}, u32[]{:S(2)}, u32[]{:S(2)}) collective-permute-start(bf16[768,512]{1,0:T(8,128)(2,1)S(1)} %get-tuple-element.25), channel_id=1, source_target_pairs={{0,192},{1,193},{2,194},{3,195},{36,196},{37,197},{38,198},{39,199... | collective-permute-start | bytes 2359304 | tf_op jit(solution)/shard_map/ppermute | solution.py:81
  88.8 14.0 %collective-permute-start.16 = (bf16[768,512]{1,0:T(8,128)(2,1)S(1)}, bf16[768,512]{1,0:T(8,128)(2,1)}, u32[]{:S(2)}, u32[]{:S(2)}) collective-permute-start(bf16[768,512]{1,0:T(8,128)(2,1)S(1)} %get-tuple-element.25), channel_id=1, source_target_pairs={{0,64},{1,65},{2,66},{3,67},{36,68},{37,69},{38,70},{39,71},{72,13... | collective-permute-start | bytes 2359304 | tf_op jit(solution)/shard_map/ppermute | solution.py:81
  90.4 12.3 %collective-permute-start.22 = (bf16[768,512]{1,0:T(8,128)(2,1)}, bf16[768,512]{1,0:T(8,128)(2,1)S(1)}, u32[]{:S(2)}, u32[]{:S(2)}) collective-permute-start(bf16[768,512]{1,0:T(8,128)(2,1)} %get-tuple-element.24), channel_id=1, source_target_pairs={{0,32},{1,33},{2,34},{3,35},{36,4},{37,5},{38,6},{39,7},{72,104},{... | collective-permute-start | bytes 2359304 | tf_op jit(solution)/shard_map/ppermute | solution.py:81
  95.5 10.0 %collective-permute-start.14 = (bf16[512,768]{1,0:T(8,128)(2,1)}, bf16[512,768]{1,0:T(8,128)(2,1)}, u32[]{:S(2)}, u32[]{:S(2)}) collective-permute-start(bf16[512,768]{1,0:T(8,128)(2,1)} %get-tuple-element.41), channel_id=1, source_target_pairs={{0,32},{32,0},{1,33},{33,1},{2,34},{34,2},{3,35},{35,3},{4,36},{36... | collective-permute-start | bytes 2359304 | tf_op jit(solution)/shard_map/ppermute | solution.py:90
  107.0 9.5 %collective-permute-start.25 = (bf16[128,768]{1,0:T(8,128)(2,1)S(1)}, bf16[128,768]{1,0:T(8,128)(2,1)S(1)}, u32[]{:S(2)}, u32[]{:S(2)}) collective-permute-start(bf16[128,768]{1,0:T(8,128)(2,1)S(1)} %get-tuple-element.28), channel_id=1, source_target_pairs={{0,64},{64,128},{128,192},{192,0},{1,65},{65,129},{129,193},{193,1... | collective-permute-start | bytes 589832 | tf_op jit(solution)/shard_map/ppermute | solution.py:17
  107.1 9.4 %collective-permute-start.26 = (bf16[128,768]{1,0:T(8,128)(2,1)S(1)}, bf16[128,768]{1,0:T(8,128)(2,1)S(1)}, u32[]{:S(2)}, u32[]{:S(2)}) collective-permute-start(bf16[128,768]{1,0:T(8,128)(2,1)S(1)} %get-tuple-element.29), channel_id=1, source_target_pairs={{0,192},{64,0},{128,64},{192,128},{1,193},{65,1},{129,65},{193,129... | collective-permute-start | bytes 589832 | tf_op jit(solution)/shard_map/ppermute | solution.py:17
  109.8 5.6 %collective-permute-start.23 = (bf16[64,768]{1,0:T(8,128)(2,1)S(1)}, bf16[64,768]{1,0:T(8,128)(2,1)S(1)}, u32[]{:S(2)}, u32[]{:S(2)}) collective-permute-start(bf16[64,768]{1,0:T(8,128)(2,1)S(1)} %get-tuple-element.26), channel_id=1, source_target_pairs={{0,128},{64,192},{128,0},{192,64},{1,129},{65,193},{129,1},{193,65... | collective-permute-start | bytes 294920 | tf_op jit(solution)/shard_map/ppermute | solution.py:17
  109.9 6.6 %collective-permute-start.24 = (bf16[64,768]{1,0:T(8,128)(2,1)S(1)}, bf16[64,768]{1,0:T(8,128)(2,1)S(1)}, u32[]{:S(2)}, u32[]{:S(2)}) collective-permute-start(bf16[64,768]{1,0:T(8,128)(2,1)S(1)} %get-tuple-element.27), channel_id=1, source_target_pairs={{0,128},{64,192},{128,0},{192,64},{1,129},{65,193},{129,1},{193,65... | collective-permute-start | bytes 294920 | tf_op jit(solution)/shard_map/ppermute | solution.py:17
  124.9 17.6 %all-to-all-start = ((bf16[8,32,512]{2,1,0:T(8,128)(2,1)}), bf16[8,32,512]{2,1,0:T(8,128)(2,1)S(1)}, u32[]{:S(2)}, u32[]{:S(2)}) async-start(bf16[8,32,512]{2,1,0:T(8,128)(2,1)} %broadcast_in_dim.68), calls=%async_computation | async-start | bytes 524288 | tf_op jit(solution)/shard_map/all_to_all | solution.py:121
  133.1 7.4 %collective-permute-start.27 = (bf16[64,768]{1,0:T(8,128)(2,1)S(1)}, bf16[64,768]{1,0:T(8,128)(2,1)S(1)}, u32[]{:S(2)}, u32[]{:S(2)}) collective-permute-start(bf16[64,768]{1,0:T(8,128)(2,1)S(1)} %dynamic-slice_bitcast_fusion.4), channel_id=1, source_target_pairs={{0,32},{32,0},{1,33},{33,1},{2,34},{34,2},{3,35},{35,3},{4,36},{36... | collective-permute-start | bytes 294920 | tf_op jit(solution)/shard_map/ppermute | solution.py:135
  142.5 5.4 %collective-permute-start.33 = (bf16[32,512]{1,0:T(8,128)(2,1)S(1)}, bf16[32,512]{1,0:T(8,128)(2,1)S(1)}, u32[]{:S(2)}, u32[]{:S(2)}) collective-permute-start(bf16[32,512]{1,0:T(8,128)(2,1)S(1)} %reduce_sum.12), channel_id=1, source_target_pairs={{0,3},{1,2},{2,1},{3,0},{4,7},{5,6},{6,5},{7,4},{8,11},{9,10},{10,... | collective-permute-start | bytes 98312 | tf_op jit(solution)/shard_map/ppermute | solution.py:109
  147.9 11.8 %collective-permute-start.34 = (bf16[64,512]{1,0:T(8,128)(2,1)S(1)}, bf16[64,512]{1,0:T(8,128)(2,1)S(1)}, u32[]{:S(2)}, u32[]{:S(2)}) collective-permute-start(bf16[64,512]{1,0:T(8,128)(2,1)S(1)} %dynamic-slice_bitcast_fusion.5), channel_id=1, source_target_pairs={{0,32},{32,0},{1,33},{33,1},{2,34},{34,2},{3,35},{35,3},{4,36},{36... | collective-permute-start | bytes 196616 | tf_op jit(solution)/shard_map/ppermute | solution.py:135
  (16 other events, 153.6 us)
Sparse Core Ops, SparseCore 0:
  21.1 50.5 all-gather.1

commit v6 on v5

--- a/solution.py
+++ b/solution.py
@@ -21,20 +21,14 @@
     return [array] + [shift(array, axis, size, d if d <= size // 2 else d - size) for d in range(1, size)]
 
 
-def relay_ring(array, axis, size, halved):
+def relay_ring(array, axis, size):
     got = [array] + [None] * (size - 1)
     right = left = array
     for step in range(1, size // 2):
         right = shift(right, axis, size, 1)
         left = shift(left, axis, size, -1)
         got[step], got[size - step] = right, left
-    if halved:
-        half = array.shape[0] // 2
-        got[size // 2] = jnp.concatenate(
-            [shift(right[:half], axis, size, 1), shift(left[half:], axis, size, -1)], axis=0
-        )
-    else:
-        got[size // 2] = shift(right, axis, size, 1)
+    got[size // 2] = shift(right, axis, size, 1)
     return got
 
 
@@ -53,8 +47,7 @@
     return lax.all_gather(part, "z", axis=0, tiled=True)
 
 
-def near_z_then_y(piece):
-    part = placed_by_owner(relay_ring(piece[None], "z", ZS, False), lax.axis_index("z"), 0)[:, None]
+def near_of(part):
     return [part, shift(part, "y", YS, 1), shift(part, "y", YS, -1)]
 
 
@@ -77,19 +70,15 @@
     for z in range(ZS):
         for y in range(YS):
             x, core = root_of(z)
-            pairs.append((device(x, core, z, y), device(*target(x, core, z, y))))
+            to = target(x, core, z, y)
+            if to is not None:
+                pairs.append((device(x, core, z, y), device(*to)))
     return lax.ppermute(array, ALL, pairs)
 
 
 def along_x(slab, core, shifts):
-    return sum(from_root(slab, lambda x, c, z, y: ((x + by) % XS, core, z, y)) for by in shifts)
-
-
-def pair_sum(partial):
-    first = lax.axis_index("core") == 0
-    given = lax.ppermute(jnp.where(first, partial[1], partial[0]), "core", [(0, 1), (1, 0)])
-    pair = jnp.where(first, partial[0], partial[1]).astype(F32) + given.astype(F32)
-    return pair.astype(BF16)
+    sent = [from_root(slab, lambda x, c, z, y: ((x + by) % XS, core, z, y)) for by in shifts]
+    return sent + [from_root(slab, lambda x, c, z, y: (x, core, z, y) if c != core else None)]
 
 
 def sum_over_x(pair):
@@ -155,9 +144,12 @@
     def partial_of(panel):
         return jnp.einsum("qj,pq->jp", panel, inverse_block, preferred_element_type=F32).astype(BF16)
 
-    first = core == 0
-    near = near_z_then_y(normed[1])
+    ring = relay_ring(normed[1][None], "z", ZS)
+    normed_0, ring[1], ring[ZS - 1] = lax.optimization_barrier((normed[0], ring[1], ring[ZS - 1]))
+    panel_0 = panel_y_then_z(normed_0)
 
+    near = near_of(placed_by_owner(ring, z, 0)[:, None])
+    chunks = [near[0], near[1], far_chunk(near), near[2]]
     deep = rows // (piece_rows * YS)
     of_slab = lambda part, lane: lax.dynamic_slice_in_dim(part, lane * deep, deep, 0)
     far_part = from_root(
@@ -165,24 +157,24 @@
     )
     slab_parts = [of_slab(near[0], y), of_slab(near[1], y), far_part, of_slab(near[2], y)]
     slab_1 = placed_by_owner(slab_parts, y, 1).reshape(rows, width)
-    sent_1 = along_x(slab_1, 1, (1, -1, -2))
+    zero = jnp.zeros((), BF16)
+    home = row == z
+    factor_slab = sum(along_x(slab_1, 1, (1, -1, -2)), jnp.where(home & (core == 1), slab_1, zero))
+    partial_1 = partial_of(placed_by_owner(chunks, y, 1).reshape(panel_0.shape))
+    given_1 = lax.ppermute(partial_1, "core", [(0, 1)])
 
-    panel_0 = panel_y_then_z(normed[0])
-    panel_0, near = lax.optimization_barrier((panel_0, near))
-    chunks = [near[0], near[1], far_chunk(near), near[2]]
+    panel_0, factor_slab, given_1 = lax.optimization_barrier((panel_0, factor_slab, given_1))
     slab_0 = lax.dynamic_slice_in_dim(panel_0, y * rows, rows, 0)
     sent_0 = along_x(slab_0, 0, (1, -1, 2))
-    partial = [partial_of(panel_0)]
+    partial_0 = partial_of(panel_0)
+    near_0, far_0 = [*sent_0[:2], sent_0[3]], sent_0[2]
+    partial_0, near_0 = lax.optimization_barrier((partial_0, near_0))
+    given_0 = lax.ppermute(partial_0, "core", [(1, 0)])
 
-    chunks, partial[0] = lax.optimization_barrier((chunks, partial[0]))
-    across = from_root(
-        jnp.where(first, slab_1, slab_0), lambda x, c, z, y: (x, 1 - c, z, y)
-    )
-    partial.append(partial_of(placed_by_owner(chunks, y, 1).reshape(panel_0.shape)))
-
-    home = row == z
-    factor_slab = jnp.where(home, jnp.where(first, slab_0, slab_1), sent_0 + sent_1 + across)
-    pair, factor_slab = lax.optimization_barrier((pair_sum(partial), factor_slab))
+    pair = jnp.where(core == 0, partial_0, partial_1).astype(F32)
+    pair = (pair + (given_0.astype(F32) + given_1.astype(F32))).astype(BF16)
+    pair, far_0 = lax.optimization_barrier((pair, far_0))
+    factor_slab = sum([*near_0, far_0], factor_slab + jnp.where(home & (core == 0), slab_0, zero))
     product = sum_over_x(pair)
     col_keep = lax.dynamic_index_in_dim(keep_of(col * rows, rows), core, 0)
     offdiag = lax.optimization_barrier((-(product * col_keep)).astype(BF16))

time: 168 us -> 182 us (1.083)
  starting transfers between devices: 79 us -> 89.1 us
  matrix products: 11.2 us -> 14.7 us
  waiting for transfers between devices: 45 us -> 48.3 us
  other arithmetic: 9.54 us -> 6.66 us
    all_gather x1, waiting for transfers between devices: 8.17 us -> 0.01 us  [panel_y_then_z(): return lax.all_gather(part, 'z', axis=0, tiled=True)]
    ppermute x8 -> x9, waiting for transfers between devices: 0.02 us -> 7.46 us  [from_root(): return lax.ppermute(array, ALL, pairs)]
    ppermute x2, starting transfers between devices: 17.4 us -> 22.9 us  [own_slab_of_both(): got = lax.ppermute(given, 'core', [(0, 1), (1, 0)])]
    select_n x2 -> x0, other arithmetic: 5.39 us -> none  [the longest x1 2.74 us: body(): jnp.where(home, jnp.where(first, slab_0, slab_1), sent_0 + sent_1 + across)]
    ppermute x1 -> x2, waiting for transfers between devices: 0.01 us -> 5.35 us  [the longest x1 5.34 us: body(): given_1 = lax.ppermute(partial_1, 'core', [(0, 1)])]
    dot_general x2, matrix products: 9.74 us -> 11.9 us  [partial_of(): jnp.einsum('qj,pq->jp', panel, inverse_block, preferred_element_type=F32)]
    ppermute x18, starting transfers between devices: 27.1 us -> 29.2 us  [shift(): lax.ppermute(array, axis, [(i, (i + by) % size) for i in range(size)])]
    add x0 -> x1, other arithmetic: none -> 2.03 us  [body(): sum(along_x(slab_1, 1, (1, -1, -2)), jnp.where(home & (core == 1), slab_1...]
  transfers between devices with their start and end apart: 37 -> 39, of which waited for: 16 -> 18; matrix products, arithmetic and copies ran while one was open for 13% -> 12% of each run, Pallas kernels for 0% -> 0%
where the time goes in v6:
time: 182 us
  starting transfers between devices  89.1 us (49%)
  waiting for transfers between devices  48.3 us (27%)
  between operations  14.8 us (8%)
  matrix products  14.7 us (8%)
  local copies, waits for them, and re-layouts  8.03 us (4%)
  other arithmetic  6.66 us (4%)
    ppermute x18, starting transfers between devices, shift(): lax.ppermute(array, axis, [(i, (i + by) % size) for i in range(size)])  29.2 us
    ppermute x18, waiting for transfers between devices, shift(): lax.ppermute(array, axis, [(i, (i + by) % size) for i in range(size)])  27.8 us
    ppermute x2, starting transfers between devices, own_slab_of_both(): got = lax.ppermute(given, 'core', [(0, 1), (1, 0)])  22.9 us
    dot_general x2, matrix products, partial_of(): jnp.einsum('qj,pq->jp', panel, inverse_block, preferred_element_type=F32)  11.9 us
    ppermute x9, starting transfers between devices, from_root(): return lax.ppermute(array, ALL, pairs)  10.5 us
    all_to_all x1, starting transfers between devices, summed_over_col(): part = lax.all_to_all(copies, 'z', split_axis=0, concat_axis=0, tiled=True)  9.23 us
    ppermute x6, starting transfers between devices, exchanged(): return lax.ppermute(array, axis, [(i, i ^ by) for i in range(size)])  8.14 us
    ppermute x1, starting transfers between devices, body(): given_0 = lax.ppermute(partial_0, 'core', [(1, 0)])  7.84 us
  transfers between devices with their start and end apart: 39, of which 18 were waited for; matrix products, arithmetic and copies ran while one was open for 12% of the time, Pallas kernels for 0%

profile of v6, /device:TPU:1, one launch (start us, length us, event | category | flops | bytes accessed | tf_op | source)
XLA Modules:
  0.0 181.6 jit_solution(17265953657589374623)
XLA Ops:
  9.7 2.5 %collective-permute-start = (bf16[1,96,512]{2,1,0:T(8,128)(2,1)S(1)}, bf16[1,96,512]{2,1,0:T(8,128)(2,1)S(1)}, u32[]{:S(2)}, u32[]{:S(2)}) collective-permute-start(bf16[1,96,512]{2,1,0:T(8,128)(2,1)S(1)} %get-tuple-element.36), channel_id=1, source_target_pairs={{0,4},{4,8},{8,12},{12,16},{16,20},{20,24},{24,28},{28,0},{1,5},{5... | collective-permute-start | bytes 294920 | tf_op jit(solution)/shard_map/ppermute | solution.py:17
  12.2 4.0 %collective-permute-start.1 = (bf16[1,96,512]{2,1,0:T(8,128)(2,1)S(1)}, bf16[1,96,512]{2,1,0:T(8,128)(2,1)S(1)}, u32[]{:S(2)}, u32[]{:S(2)}) collective-permute-start(bf16[1,96,512]{2,1,0:T(8,128)(2,1)S(1)} %get-tuple-element.36), channel_id=1, source_target_pairs={{0,28},{4,0},{8,4},{12,8},{16,12},{20,16},{24,20},{28,24},{1,29},{... | collective-permute-start | bytes 294920 | tf_op jit(solution)/shard_map/ppermute | solution.py:17
  16.2 2.4 %collective-permute-done = bf16[1,96,512]{2,1,0:T(8,128)(2,1)S(1)} collective-permute-done((bf16[1,96,512]{2,1,0:T(8,128)(2,1)S(1)}, bf16[1,96,512]{2,1,0:T(8,128)(2,1)S(1)}, u32[]{:S(2)}, u32[]{:S(2)}) %collective-permute-start) | collective-permute-done | bytes 98336 | tf_op jit(solution)/shard_map/ppermute | solution.py:17
  20.0 2.6 %collective-permute-start.3 = (bf16[96,512]{1,0:T(8,128)(2,1)S(1)}, bf16[96,512]{1,0:T(8,128)(2,1)S(1)}, u32[]{:S(2)}, u32[]{:S(2)}) collective-permute-start(bf16[96,512]{1,0:T(8,128)(2,1)S(1)} %get-tuple-element.14), channel_id=1, source_target_pairs={{0,2},{1,3},{2,0},{3,1},{4,6},{5,7},{6,4},{7,5},{8,10},{9,11},{10,... | collective-permute-start | bytes 294920 | tf_op jit(solution)/shard_map/ppermute | solution.py:17
  23.7 2.3 %collective-permute-done.3 = bf16[96,512]{1,0:T(8,128)(2,1)S(1)} collective-permute-done((bf16[96,512]{1,0:T(8,128)(2,1)S(1)}, bf16[96,512]{1,0:T(8,128)(2,1)S(1)}, u32[]{:S(2)}, u32[]{:S(2)}) %collective-permute-start.3) | collective-permute-done | bytes 98336 | tf_op jit(solution)/shard_map/ppermute | solution.py:17
  28.4 2.7 %collective-permute-start.8 = (bf16[1,96,512]{2,1,0:T(8,128)(2,1)S(1)}, bf16[1,96,512]{2,1,0:T(8,128)(2,1)S(1)}, u32[]{:S(2)}, u32[]{:S(2)}) collective-permute-start(bf16[1,96,512]{2,1,0:T(8,128)(2,1)S(1)} %collective-permute-done.1), channel_id=1, source_target_pairs={{0,28},{4,0},{8,4},{12,8},{16,12},{20,16},{24,20},{28,24},{1,29},{... | collective-permute-start | bytes 294920 | tf_op jit(solution)/shard_map/ppermute | solution.py:17
  31.0 2.0 %collective-permute-done.5 = bf16[1,96,512]{2,1,0:T(8,128)(2,1)S(1)} collective-permute-done((bf16[1,96,512]{2,1,0:T(8,128)(2,1)S(1)}, bf16[1,96,512]{2,1,0:T(8,128)(2,1)S(1)}, u32[]{:S(2)}, u32[]{:S(2)}) %collective-permute-start.5) | collective-permute-done | bytes 98336 | tf_op jit(solution)/shard_map/ppermute | solution.py:17
  33.0 2.7 %collective-permute-start.9 = (bf16[1,96,512]{2,1,0:T(8,128)(2,1)S(1)}, bf16[1,96,512]{2,1,0:T(8,128)(2,1)S(1)}, u32[]{:S(2)}, u32[]{:S(2)}) collective-permute-start(bf16[1,96,512]{2,1,0:T(8,128)(2,1)S(1)} %collective-permute-done.8), channel_id=1, source_target_pairs={{0,28},{4,0},{8,4},{12,8},{16,12},{20,16},{24,20},{28,24},{1,29},{... | collective-permute-start | bytes 294920 | tf_op jit(solution)/shard_map/ppermute | solution.py:17
  35.7 2.0 %collective-permute-done.6 = bf16[1,96,512]{2,1,0:T(8,128)(2,1)S(1)} collective-permute-done((bf16[1,96,512]{2,1,0:T(8,128)(2,1)S(1)}, bf16[1,96,512]{2,1,0:T(8,128)(2,1)S(1)}, u32[]{:S(2)}, u32[]{:S(2)}) %collective-permute-start.6) | collective-permute-done | bytes 98336 | tf_op jit(solution)/shard_map/ppermute | solution.py:17
  37.7 4.7 %collective-permute-done.7 = bf16[1,96,512]{2,1,0:T(8,128)(2,1)S(1)} collective-permute-done((bf16[1,96,512]{2,1,0:T(8,128)(2,1)S(1)}, bf16[1,96,512]{2,1,0:T(8,128)(2,1)S(1)}, u32[]{:S(2)}, u32[]{:S(2)}) %collective-permute-start.7) | collective-permute-done | bytes 98336 | tf_op jit(solution)/shard_map/ppermute | solution.py:17
  42.8 2.5 %collective-permute-start.12 = (bf16[8,1,96,512]{3,2,1,0:T(8,128)(2,1)S(1)}, bf16[8,1,96,512]{3,2,1,0:T(8,128)(2,1)S(1)}, u32[]{:S(2)}, u32[]{:S(2)}) collective-permute-start(bf16[8,1,96,512]{3,2,1,0:T(8,128)(2,1)S(1)} %bitcast_dynamic-update-slice_fusion), channel_id=1, source_target_pairs={{0,3},{1,0},{2,1},{3,2},{4,7},{5,4},{6,5},{7,6},{8,11},{9,8},{10,9... | collective-permute-start | bytes 2359304 | tf_op jit(solution)/shard_map/ppermute | solution.py:17
  46.5 9.3 %collective-permute-done.10 = bf16[8,1,96,512]{3,2,1,0:T(8,128)(2,1)} collective-permute-done((bf16[8,1,96,512]{3,2,1,0:T(8,128)(2,1)S(1)}, bf16[8,1,96,512]{3,2,1,0:T(8,128)(2,1)}, u32[]{:S(2)}, u32[]{:S(2)}) %collective-permute-start.10) | collective-permute-done | bytes 786464 | tf_op jit(solution)/shard_map/ppermute | solution.py:17
  56.9 2.7 %collective-permute-start.18 = (bf16[4,1,96,512]{3,2,1,0:T(8,128)(2,1)S(1)}, bf16[4,1,96,512]{3,2,1,0:T(8,128)(2,1)S(1)}, u32[]{:S(2)}, u32[]{:S(2)}) collective-permute-start(bf16[4,1,96,512]{3,2,1,0:T(8,128)(2,1)S(1)} %slice.39), channel_id=1, source_target_pairs={{0,3},{1,0},{2,1},{3,2},{4,7},{5,4},{6,5},{7,6},{8,11},{9,8},{10,9... | collective-permute-start | bytes 1179656 | tf_op jit(solution)/shard_map/ppermute | solution.py:17
  63.8 1.7 collective-permute-start.15
  69.1 5.1 %convolution_convert_fusion.1 = bf16[512,768]{1,0:T(8,128)(2,1)S(1)} fusion(bf16[3072,512]{1,0:T(8,128)(2,1)S(1)} %bitcast.98, bf16[768,3072]{1,0:T(8,128)(2,1)} %param.8), kind=kOutput, calls=%fused_computation.2 | convolution fusion | flops 2416312320 | bytes 8650752 | tf_op jit(solution)/shard_map/qj,pq->jp/dot_general | solution.py:145
  75.5 7.4 %collective-permute-done.16 = bf16[768,512]{1,0:T(8,128)(2,1)} collective-permute-done((bf16[768,512]{1,0:T(8,128)(2,1)S(1)}, bf16[768,512]{1,0:T(8,128)(2,1)}, u32[]{:S(2)}, u32[]{:S(2)}) %collective-permute-start.16) | collective-permute-done | bytes 786464 | tf_op jit(solution)/shard_map/ppermute | solution.py:76
  83.0 2.0 %add_add_fusion = bf16[768,512]{1,0:T(8,128)(2,1)S(1)} fusion(bf16[768,512]{1,0:T(8,128)(2,1)} %collective-permute-done.16, bf16[768,512]{1,0:T(8,128)(2,1)} %collective-permute-done.15, bf16[768,512]{1,0:T(8,128)(2,1)} %collective-permute-done.14, bf16[768,512]{1,0:T(8,128)(2,1)} %collective-permute-done.13, pred[]{:T(512)S(6)} %and.118, ...), kind=kLoop, calls=%fused_computation.14 | loop fusion | flops 1966080 | bytes 4718593 | tf_op jit(solution)/shard_map/add | solution.py:162
  85.0 5.3 %collective-permute-done.19 = bf16[512,768]{1,0:T(8,128)(2,1)} collective-permute-done((bf16[512,768]{1,0:T(8,128)(2,1)S(1)}, bf16[512,768]{1,0:T(8,128)(2,1)}, u32[]{:S(2)}, u32[]{:S(2)}) %collective-permute-start.19) | collective-permute-done | bytes 786464 | tf_op jit(solution)/shard_map/ppermute | solution.py:164
  93.7 6.8 %convolution_convert_fusion = bf16[512,768]{1,0:T(8,128)(2,1)} fusion(bf16[3072,512]{1,0:T(8,128)(2,1)} %all-gather.2.cloned.1.call-done, bf16[768,3072]{1,0:T(8,128)(2,1)} %param.8), kind=kOutput, calls=%fused_computation.1 | convolution fusion | flops 2416312320 | bytes 8650752 | tf_op jit(solution)/shard_map/qj,pq->jp/dot_general | solution.py:145
  101.5 7.8 %collective-permute-start.23 = (bf16[512,768]{1,0:T(8,128)(2,1)}, bf16[512,768]{1,0:T(8,128)(2,1)}, u32[]{:S(2)}, u32[]{:S(2)}) collective-permute-start(bf16[512,768]{1,0:T(8,128)(2,1)} %convolution_convert_fusion), channel_id=1, source_target_pairs={{32,0},{33,1},{34,2},{35,3},{36,4},{37,5},{38,6},{39,7},{40,8},{41... | collective-permute-start | bytes 2359304 | tf_op jit(solution)/shard_map/ppermute | solution.py:172
  110.9 1.9 %add_convert_fusion = bf16[512,768]{1,0:T(8,128)(2,1)S(1)} fusion(bf16[512,768]{1,0:T(8,128)(2,1)} %collective-permute-done.19, bf16[512,768]{1,0:T(8,128)(2,1)} %collective-permute-done.23, bf16[512,768]{1,0:T(8,128)(2,1)} %convolution_convert_fusion, bf16[512,768]{1,0:T(8,128)(2,1)S(1)} %convolution_convert_fusion.1, pred[]{:T(512)S(6)} %eq.66), kind=kLoop, calls=%fused_computation | loop fusion | flops 2752512 | bytes 3932161 | tf_op jit(solution)/shard_map/convert_element_type | solution.py:175
  112.8 1.8 collective-permute-start.27
  114.6 1.8 collective-permute-start.28
  117.6 1.9 %collective-permute-start.26 = (bf16[64,768]{1,0:T(8,128)(2,1)S(1)}, bf16[64,768]{1,0:T(8,128)(2,1)S(1)}, u32[]{:S(2)}, u32[]{:S(2)}) collective-permute-start(bf16[64,768]{1,0:T(8,128)(2,1)S(1)} %get-tuple-element.27), channel_id=1, source_target_pairs={{0,128},{64,192},{128,0},{192,64},{1,129},{65,193},{129,1},{193,65... | collective-permute-start | bytes 294920 | tf_op jit(solution)/shard_map/ppermute | solution.py:17
  119.6 2.0 %collective-permute-done.25 = bf16[64,768]{1,0:T(8,128)(2,1)S(1)} collective-permute-done((bf16[64,768]{1,0:T(8,128)(2,1)S(1)}, bf16[64,768]{1,0:T(8,128)(2,1)S(1)}, u32[]{:S(2)}, u32[]{:S(2)}) %collective-permute-start.25) | collective-permute-done | bytes 98336 | tf_op jit(solution)/shard_map/ppermute | solution.py:17
  124.6 2.2 %collective-permute-start.31 = (bf16[32,512]{1,0:T(8,128)(2,1)S(1)}, bf16[32,512]{1,0:T(8,128)(2,1)S(1)}, u32[]{:S(2)}, u32[]{:S(2)}) collective-permute-start(bf16[32,512]{1,0:T(8,128)(2,1)S(1)} %get-tuple-element.40), channel_id=1, source_target_pairs={{0,2},{1,3},{2,0},{3,1},{4,6},{5,7},{6,4},{7,5},{8,10},{9,11},{10,... | collective-permute-start | bytes 98312 | tf_op jit(solution)/shard_map/ppermute | solution.py:98
  128.9 1.8 collective-permute-done.32
  131.5 9.2 %all-to-all-start = ((bf16[8,32,512]{2,1,0:T(8,128)(2,1)}), bf16[8,32,512]{2,1,0:T(8,128)(2,1)S(1)}, u32[]{:S(2)}, u32[]{:S(2)}) async-start(bf16[8,32,512]{2,1,0:T(8,128)(2,1)} %broadcast_in_dim.74), calls=%async_computation | async-start | bytes 524288 | tf_op jit(solution)/shard_map/all_to_all | solution.py:110
  140.7 12.0 %collective-permute-start.29 = (bf16[64,768]{1,0:T(8,128)(2,1)S(1)}, bf16[64,768]{1,0:T(8,128)(2,1)S(1)}, u32[]{:S(2)}, u32[]{:S(2)}) collective-permute-start(bf16[64,768]{1,0:T(8,128)(2,1)S(1)} %dynamic-slice_bitcast_fusion.4), channel_id=1, source_target_pairs={{0,32},{32,0},{1,33},{33,1},{2,34},{34,2},{3,35},{35,3},{4,36},{36... | collective-permute-start | bytes 294920 | tf_op jit(solution)/shard_map/ppermute | solution.py:124
  154.3 3.6 %collective-permute-start.34 = (bf16[32,512]{1,0:T(8,128)(2,1)S(1)}, bf16[32,512]{1,0:T(8,128)(2,1)S(1)}, u32[]{:S(2)}, u32[]{:S(2)}) collective-permute-start(bf16[32,512]{1,0:T(8,128)(2,1)S(1)} %reduce_sum.12), channel_id=1, source_target_pairs={{0,2},{1,3},{2,0},{3,1},{4,6},{5,7},{6,4},{7,5},{8,10},{9,11},{10,... | collective-permute-start | bytes 98312 | tf_op jit(solution)/shard_map/ppermute | solution.py:98
  159.6 2.6 %collective-permute-done.35 = bf16[32,512]{1,0:T(8,128)(2,1)S(1)} collective-permute-done((bf16[32,512]{1,0:T(8,128)(2,1)S(1)}, bf16[32,512]{1,0:T(8,128)(2,1)S(1)}, u32[]{:S(2)}, u32[]{:S(2)}) %collective-permute-start.35) | collective-permute-done | bytes 32800 | tf_op jit(solution)/shard_map/ppermute | solution.py:98
  162.2 10.9 %collective-permute-start.36 = (bf16[64,512]{1,0:T(8,128)(2,1)S(1)}, bf16[64,512]{1,0:T(8,128)(2,1)S(1)}, u32[]{:S(2)}, u32[]{:S(2)}) collective-permute-start(bf16[64,512]{1,0:T(8,128)(2,1)S(1)} %dynamic-slice_bitcast_fusion.5), channel_id=1, source_target_pairs={{0,32},{32,0},{1,33},{33,1},{2,34},{34,2},{3,35},{35,3},{4,36},{36... | collective-permute-start | bytes 196616 | tf_op jit(solution)/shard_map/ppermute | solution.py:124
  (125 shorter events, 36.6 us)
Async XLA Ops:
  7.2 83.2 %all-gather.2.cloned.1.call-start = ((), (), s32[]{:S(2)}) async-start(), calls=%async_computation.1 | async-start | bytes 3538944 | tf_op jit(solution)/shard_map/all_gather | solution.py:47
  9.7 9.0 %collective-permute-start = (bf16[1,96,512]{2,1,0:T(8,128)(2,1)S(1)}, bf16[1,96,512]{2,1,0:T(8,128)(2,1)S(1)}, u32[]{:S(2)}, u32[]{:S(2)}) collective-permute-start(bf16[1,96,512]{2,1,0:T(8,128)(2,1)S(1)} %get-tuple-element.36), channel_id=1, source_target_pairs={{0,4},{4,8},{8,12},{12,16},{16,20},{20,24},{24,28},{28,0},{1,5},{5... | collective-permute-start | bytes 294920 | tf_op jit(solution)/shard_map/ppermute | solution.py:17
  12.2 6.5 %collective-permute-start.1 = (bf16[1,96,512]{2,1,0:T(8,128)(2,1)S(1)}, bf16[1,96,512]{2,1,0:T(8,128)(2,1)S(1)}, u32[]{:S(2)}, u32[]{:S(2)}) collective-permute-start(bf16[1,96,512]{2,1,0:T(8,128)(2,1)S(1)} %get-tuple-element.36), channel_id=1, source_target_pairs={{0,28},{4,0},{8,4},{12,8},{16,12},{20,16},{24,20},{28,24},{1,29},{... | collective-permute-start | bytes 294920 | tf_op jit(solution)/shard_map/ppermute | solution.py:17
  18.7 5.1 %collective-permute-start.2 = (bf16[96,512]{1,0:T(8,128)(2,1)S(1)}, bf16[96,512]{1,0:T(8,128)(2,1)S(1)}, u32[]{:S(2)}, u32[]{:S(2)}) collective-permute-start(bf16[96,512]{1,0:T(8,128)(2,1)S(1)} %get-tuple-element.14), channel_id=1, source_target_pairs={{0,1},{1,2},{2,3},{3,0},{4,5},{5,6},{6,7},{7,4},{8,9},{9,10},{10,1... | collective-permute-start | bytes 294920 | tf_op jit(solution)/shard_map/ppermute | solution.py:17
  20.0 6.0 %collective-permute-start.3 = (bf16[96,512]{1,0:T(8,128)(2,1)S(1)}, bf16[96,512]{1,0:T(8,128)(2,1)S(1)}, u32[]{:S(2)}, u32[]{:S(2)}) collective-permute-start(bf16[96,512]{1,0:T(8,128)(2,1)S(1)} %get-tuple-element.14), channel_id=1, source_target_pairs={{0,2},{1,3},{2,0},{3,1},{4,6},{5,7},{6,4},{7,5},{8,10},{9,11},{10,... | collective-permute-start | bytes 294920 | tf_op jit(solution)/shard_map/ppermute | solution.py:17
  28.3 4.8 %collective-permute-start.5 = (bf16[1,96,512]{2,1,0:T(8,128)(2,1)S(1)}, bf16[1,96,512]{2,1,0:T(8,128)(2,1)S(1)}, u32[]{:S(2)}, u32[]{:S(2)}) collective-permute-start(bf16[1,96,512]{2,1,0:T(8,128)(2,1)S(1)} %collective-permute-done), channel_id=1, source_target_pairs={{0,4},{4,8},{8,12},{12,16},{16,20},{20,24},{24,28},{28,0},{1,5},{5... | collective-permute-start | bytes 294920 | tf_op jit(solution)/shard_map/ppermute | solution.py:17
  28.4 4.7 %collective-permute-start.8 = (bf16[1,96,512]{2,1,0:T(8,128)(2,1)S(1)}, bf16[1,96,512]{2,1,0:T(8,128)(2,1)S(1)}, u32[]{:S(2)}, u32[]{:S(2)}) collective-permute-start(bf16[1,96,512]{2,1,0:T(8,128)(2,1)S(1)} %collective-permute-done.1), channel_id=1, source_target_pairs={{0,28},{4,0},{8,4},{12,8},{16,12},{20,16},{24,20},{28,24},{1,29},{... | collective-permute-start | bytes 294920 | tf_op jit(solution)/shard_map/ppermute | solution.py:17
  33.0 4.7 %collective-permute-start.6 = (bf16[1,96,512]{2,1,0:T(8,128)(2,1)S(1)}, bf16[1,96,512]{2,1,0:T(8,128)(2,1)S(1)}, u32[]{:S(2)}, u32[]{:S(2)}) collective-permute-start(bf16[1,96,512]{2,1,0:T(8,128)(2,1)S(1)} %collective-permute-done.5), channel_id=1, source_target_pairs={{0,4},{4,8},{8,12},{12,16},{16,20},{20,24},{24,28},{28,0},{1,5},{5... | collective-permute-start | bytes 294920 | tf_op jit(solution)/shard_map/ppermute | solution.py:17
  33.0 9.4 %collective-permute-start.9 = (bf16[1,96,512]{2,1,0:T(8,128)(2,1)S(1)}, bf16[1,96,512]{2,1,0:T(8,128)(2,1)S(1)}, u32[]{:S(2)}, u32[]{:S(2)}) collective-permute-start(bf16[1,96,512]{2,1,0:T(8,128)(2,1)S(1)} %collective-permute-done.8), channel_id=1, source_target_pairs={{0,28},{4,0},{8,4},{12,8},{16,12},{20,16},{24,20},{28,24},{1,29},{... | collective-permute-start | bytes 294920 | tf_op jit(solution)/shard_map/ppermute | solution.py:17
  37.7 4.7 %collective-permute-start.7 = (bf16[1,96,512]{2,1,0:T(8,128)(2,1)S(1)}, bf16[1,96,512]{2,1,0:T(8,128)(2,1)S(1)}, u32[]{:S(2)}, u32[]{:S(2)}) collective-permute-start(bf16[1,96,512]{2,1,0:T(8,128)(2,1)S(1)} %collective-permute-done.6), channel_id=1, source_target_pairs={{0,4},{4,8},{8,12},{12,16},{16,20},{20,24},{24,28},{28,0},{1,5},{5... | collective-permute-start | bytes 294920 | tf_op jit(solution)/shard_map/ppermute | solution.py:17
  42.5 13.2 %collective-permute-start.10 = (bf16[8,1,96,512]{3,2,1,0:T(8,128)(2,1)S(1)}, bf16[8,1,96,512]{3,2,1,0:T(8,128)(2,1)}, u32[]{:S(2)}, u32[]{:S(2)}) collective-permute-start(bf16[8,1,96,512]{3,2,1,0:T(8,128)(2,1)S(1)} %bitcast_dynamic-update-slice_fusion), channel_id=1, source_target_pairs={{0,1},{1,2},{2,3},{3,0},{4,5},{5,6},{6,7},{7,4},{8,9},{9,10},{10,1... | collective-permute-start | bytes 2359304 | tf_op jit(solution)/shard_map/ppermute | solution.py:17
  42.8 14.1 %collective-permute-start.12 = (bf16[8,1,96,512]{3,2,1,0:T(8,128)(2,1)S(1)}, bf16[8,1,96,512]{3,2,1,0:T(8,128)(2,1)S(1)}, u32[]{:S(2)}, u32[]{:S(2)}) collective-permute-start(bf16[8,1,96,512]{3,2,1,0:T(8,128)(2,1)S(1)} %bitcast_dynamic-update-slice_fusion), channel_id=1, source_target_pairs={{0,3},{1,0},{2,1},{3,2},{4,7},{5,4},{6,5},{7,6},{8,11},{9,8},{10,9... | collective-permute-start | bytes 2359304 | tf_op jit(solution)/shard_map/ppermute | solution.py:17
  45.3 15.2 %collective-permute-start.11 = (bf16[2,1,96,512]{3,2,1,0:T(8,128)(2,1)S(1)}, bf16[2,1,96,512]{3,2,1,0:T(8,128)(2,1)S(1)}, u32[]{:S(2)}, u32[]{:S(2)}) collective-permute-start(bf16[2,1,96,512]{3,2,1,0:T(8,128)(2,1)S(1)} %get-tuple-element.30), channel_id=1, source_target_pairs={{0,2},{1,3},{2,0},{3,1},{36,38},{37,39},{38,36},{39,37},{72,74},{7... | collective-permute-start | bytes 589832 | tf_op jit(solution)/shard_map/ppermute | solution.py:76
  56.8 10.9 %collective-permute-start.17 = (bf16[4,1,96,512]{3,2,1,0:T(8,128)(2,1)S(1)}, bf16[4,1,96,512]{3,2,1,0:T(8,128)(2,1)S(1)}, u32[]{:S(2)}, u32[]{:S(2)}) collective-permute-start(bf16[4,1,96,512]{3,2,1,0:T(8,128)(2,1)S(1)} %slice.38), channel_id=1, source_target_pairs={{0,1},{1,2},{2,3},{3,0},{4,5},{5,6},{6,7},{7,4},{8,9},{9,10},{10,1... | collective-permute-start | bytes 1179656 | tf_op jit(solution)/shard_map/ppermute | solution.py:17
  56.9 12.1 %collective-permute-start.18 = (bf16[4,1,96,512]{3,2,1,0:T(8,128)(2,1)S(1)}, bf16[4,1,96,512]{3,2,1,0:T(8,128)(2,1)S(1)}, u32[]{:S(2)}, u32[]{:S(2)}) collective-permute-start(bf16[4,1,96,512]{3,2,1,0:T(8,128)(2,1)S(1)} %slice.39), channel_id=1, source_target_pairs={{0,3},{1,0},{2,1},{3,2},{4,7},{5,4},{6,5},{7,6},{8,11},{9,8},{10,9... | collective-permute-start | bytes 1179656 | tf_op jit(solution)/shard_map/ppermute | solution.py:17
  60.6 14.9 %collective-permute-start.13 = (bf16[768,512]{1,0:T(8,128)(2,1)S(1)}, bf16[768,512]{1,0:T(8,128)(2,1)}, u32[]{:S(2)}, u32[]{:S(2)}) collective-permute-start(bf16[768,512]{1,0:T(8,128)(2,1)S(1)} %bitcast.94), channel_id=1, source_target_pairs={{0,96},{1,97},{2,98},{3,99},{36,100},{37,101},{38,102},{39,103},{7... | collective-permute-start | bytes 2359304 | tf_op jit(solution)/shard_map/ppermute | solution.py:76
  62.2 13.3 %collective-permute-start.14 = (bf16[768,512]{1,0:T(8,128)(2,1)S(1)}, bf16[768,512]{1,0:T(8,128)(2,1)}, u32[]{:S(2)}, u32[]{:S(2)}) collective-permute-start(bf16[768,512]{1,0:T(8,128)(2,1)S(1)} %bitcast.95), channel_id=1, source_target_pairs={{0,224},{1,225},{2,226},{3,227},{36,228},{37,229},{38,230},{39,231... | collective-permute-start | bytes 2359304 | tf_op jit(solution)/shard_map/ppermute | solution.py:76
  63.8 11.7 %collective-permute-start.15 = (bf16[768,512]{1,0:T(8,128)(2,1)S(1)}, bf16[768,512]{1,0:T(8,128)(2,1)}, u32[]{:S(2)}, u32[]{:S(2)}) collective-permute-start(bf16[768,512]{1,0:T(8,128)(2,1)S(1)} %bitcast.96), channel_id=1, source_target_pairs={{0,160},{1,161},{2,162},{3,163},{36,164},{37,165},{38,166},{39,167... | collective-permute-start | bytes 2359304 | tf_op jit(solution)/shard_map/ppermute | solution.py:76
  67.6 15.3 %collective-permute-start.16 = (bf16[768,512]{1,0:T(8,128)(2,1)S(1)}, bf16[768,512]{1,0:T(8,128)(2,1)}, u32[]{:S(2)}, u32[]{:S(2)}) collective-permute-start(bf16[768,512]{1,0:T(8,128)(2,1)S(1)} %bitcast.97), channel_id=1, source_target_pairs={{0,32},{1,33},{2,34},{3,35},{72,104},{73,105},{74,106},{75,107},{1... | collective-permute-start | bytes 2359304 | tf_op jit(solution)/shard_map/ppermute | solution.py:76
  74.2 16.2 %collective-permute-start.19 = (bf16[512,768]{1,0:T(8,128)(2,1)S(1)}, bf16[512,768]{1,0:T(8,128)(2,1)}, u32[]{:S(2)}, u32[]{:S(2)}) collective-permute-start(bf16[512,768]{1,0:T(8,128)(2,1)S(1)} %convolution_convert_fusion.1), channel_id=1, source_target_pairs={{0,32},{1,33},{2,34},{3,35},{4,36},{5,37},{6,38},{7,39},{8,40},{9,... | collective-permute-start | bytes 2359304 | tf_op jit(solution)/shard_map/ppermute | solution.py:164
  91.5 9.0 %collective-permute-start.20 = (bf16[768,512]{1,0:T(8,128)(2,1)S(1)}, bf16[768,512]{1,0:T(8,128)(2,1)S(1)}, u32[]{:S(2)}, u32[]{:S(2)}) collective-permute-start(bf16[768,512]{1,0:T(8,128)(2,1)S(1)} %constant_dynamic-slice_fusion), channel_id=1, source_target_pairs={{0,64},{1,65},{2,66},{3,67},{36,68},{37,69},{38,70},{39,71},{72,13... | collective-permute-start | bytes 2359304 | tf_op jit(solution)/shard_map/ppermute | solution.py:76
  92.3 8.3 %collective-permute-start.21 = (bf16[768,512]{1,0:T(8,128)(2,1)S(1)}, bf16[768,512]{1,0:T(8,128)(2,1)S(1)}, u32[]{:S(2)}, u32[]{:S(2)}) collective-permute-start(bf16[768,512]{1,0:T(8,128)(2,1)S(1)} %constant_dynamic-slice_fusion), channel_id=1, source_target_pairs={{0,192},{1,193},{2,194},{3,195},{36,196},{37,197},{38,198},{39,199... | collective-permute-start | bytes 2359304 | tf_op jit(solution)/shard_map/ppermute | solution.py:76
  93.0 7.6 %collective-permute-start.22 = (bf16[768,512]{1,0:T(8,128)(2,1)S(1)}, bf16[768,512]{1,0:T(8,128)(2,1)S(1)}, u32[]{:S(2)}, u32[]{:S(2)}) collective-permute-start(bf16[768,512]{1,0:T(8,128)(2,1)S(1)} %constant_dynamic-slice_fusion), channel_id=1, source_target_pairs={{36,4},{37,5},{38,6},{39,7},{108,76},{109,77},{110,78},{111,79},{1... | collective-permute-start | bytes 2359304 | tf_op jit(solution)/shard_map/ppermute | solution.py:76
  101.5 9.4 %collective-permute-start.23 = (bf16[512,768]{1,0:T(8,128)(2,1)}, bf16[512,768]{1,0:T(8,128)(2,1)}, u32[]{:S(2)}, u32[]{:S(2)}) collective-permute-start(bf16[512,768]{1,0:T(8,128)(2,1)} %convolution_convert_fusion), channel_id=1, source_target_pairs={{32,0},{33,1},{34,2},{35,3},{36,4},{37,5},{38,6},{39,7},{40,8},{41... | collective-permute-start | bytes 2359304 | tf_op jit(solution)/shard_map/ppermute | solution.py:172
  112.8 9.8 %collective-permute-start.27 = (bf16[128,768]{1,0:T(8,128)(2,1)S(1)}, bf16[128,768]{1,0:T(8,128)(2,1)S(1)}, u32[]{:S(2)}, u32[]{:S(2)}) collective-permute-start(bf16[128,768]{1,0:T(8,128)(2,1)S(1)} %get-tuple-element.28), channel_id=1, source_target_pairs={{0,64},{64,128},{128,192},{192,0},{1,65},{65,129},{129,193},{193,1... | collective-permute-start | bytes 589832 | tf_op jit(solution)/shard_map/ppermute | solution.py:17
  114.6 8.0 %collective-permute-start.28 = (bf16[128,768]{1,0:T(8,128)(2,1)S(1)}, bf16[128,768]{1,0:T(8,128)(2,1)S(1)}, u32[]{:S(2)}, u32[]{:S(2)}) collective-permute-start(bf16[128,768]{1,0:T(8,128)(2,1)S(1)} %get-tuple-element.29), channel_id=1, source_target_pairs={{0,192},{64,0},{128,64},{192,128},{1,193},{65,1},{129,65},{193,129... | collective-permute-start | bytes 589832 | tf_op jit(solution)/shard_map/ppermute | solution.py:17
  116.4 5.2 %collective-permute-start.25 = (bf16[64,768]{1,0:T(8,128)(2,1)S(1)}, bf16[64,768]{1,0:T(8,128)(2,1)S(1)}, u32[]{:S(2)}, u32[]{:S(2)}) collective-permute-start(bf16[64,768]{1,0:T(8,128)(2,1)S(1)} %get-tuple-element.26), channel_id=1, source_target_pairs={{0,128},{64,192},{128,0},{192,64},{1,129},{65,193},{129,1},{193,65... | collective-permute-start | bytes 294920 | tf_op jit(solution)/shard_map/ppermute | solution.py:17
  117.6 5.1 %collective-permute-start.26 = (bf16[64,768]{1,0:T(8,128)(2,1)S(1)}, bf16[64,768]{1,0:T(8,128)(2,1)S(1)}, u32[]{:S(2)}, u32[]{:S(2)}) collective-permute-start(bf16[64,768]{1,0:T(8,128)(2,1)S(1)} %get-tuple-element.27), channel_id=1, source_target_pairs={{0,128},{64,192},{128,0},{192,64},{1,129},{65,193},{129,1},{193,65... | collective-permute-start | bytes 294920 | tf_op jit(solution)/shard_map/ppermute | solution.py:17
  131.5 22.2 %all-to-all-start = ((bf16[8,32,512]{2,1,0:T(8,128)(2,1)}), bf16[8,32,512]{2,1,0:T(8,128)(2,1)S(1)}, u32[]{:S(2)}, u32[]{:S(2)}) async-start(bf16[8,32,512]{2,1,0:T(8,128)(2,1)} %broadcast_in_dim.74), calls=%async_computation | async-start | bytes 524288 | tf_op jit(solution)/shard_map/all_to_all | solution.py:110
  140.7 12.9 %collective-permute-start.29 = (bf16[64,768]{1,0:T(8,128)(2,1)S(1)}, bf16[64,768]{1,0:T(8,128)(2,1)S(1)}, u32[]{:S(2)}, u32[]{:S(2)}) collective-permute-start(bf16[64,768]{1,0:T(8,128)(2,1)S(1)} %dynamic-slice_bitcast_fusion.4), channel_id=1, source_target_pairs={{0,32},{32,0},{1,33},{33,1},{2,34},{34,2},{3,35},{35,3},{4,36},{36... | collective-permute-start | bytes 294920 | tf_op jit(solution)/shard_map/ppermute | solution.py:124
  154.3 5.2 %collective-permute-start.34 = (bf16[32,512]{1,0:T(8,128)(2,1)S(1)}, bf16[32,512]{1,0:T(8,128)(2,1)S(1)}, u32[]{:S(2)}, u32[]{:S(2)}) collective-permute-start(bf16[32,512]{1,0:T(8,128)(2,1)S(1)} %reduce_sum.12), channel_id=1, source_target_pairs={{0,2},{1,3},{2,0},{3,1},{4,6},{5,7},{6,4},{7,5},{8,10},{9,11},{10,... | collective-permute-start | bytes 98312 | tf_op jit(solution)/shard_map/ppermute | solution.py:98
  162.2 11.8 %collective-permute-start.36 = (bf16[64,512]{1,0:T(8,128)(2,1)S(1)}, bf16[64,512]{1,0:T(8,128)(2,1)S(1)}, u32[]{:S(2)}, u32[]{:S(2)}) collective-permute-start(bf16[64,512]{1,0:T(8,128)(2,1)S(1)} %dynamic-slice_bitcast_fusion.5), channel_id=1, source_target_pairs={{0,32},{32,0},{1,33},{33,1},{2,34},{34,2},{3,35},{35,3},{4,36},{36... | collective-permute-start | bytes 196616 | tf_op jit(solution)/shard_map/ppermute | solution.py:124
  (17 other events, 154.5 us)
Sparse Core Ops, SparseCore 0:
  28.1 46.9 all-gather.1

commit v7 on v6

--- a/solution.py
+++ b/solution.py
@@ -21,17 +21,6 @@
     return [array] + [shift(array, axis, size, d if d <= size // 2 else d - size) for d in range(1, size)]
 
 
-def relay_ring(array, axis, size):
-    got = [array] + [None] * (size - 1)
-    right = left = array
-    for step in range(1, size // 2):
-        right = shift(right, axis, size, 1)
-        left = shift(left, axis, size, -1)
-        got[step], got[size - step] = right, left
-    got[size // 2] = shift(right, axis, size, 1)
-    return got
-
-
 def placed_by_owner(got, own, axis):
     size, width = len(got), got[0].shape[axis]
     dims = list(got[0].shape)
@@ -42,9 +31,9 @@
     return whole
 
 
-def panel_y_then_z(piece):
-    part = placed_by_owner(direct_ring(piece, "y", YS), lax.axis_index("y"), 0)
-    return lax.all_gather(part, "z", axis=0, tiled=True)
+def copies_to(array, axis, size):
+    copies = jnp.broadcast_to(array[None], (size, *array.shape))
+    return lax.all_to_all(copies, axis, split_axis=0, concat_axis=0, tiled=True)
 
 
 def near_of(part):
@@ -74,6 +63,15 @@
             if to is not None:
                 pairs.append((device(x, core, z, y), device(*to)))
     return lax.ppermute(array, ALL, pairs)
+
+
+def moved_home(part, half):
+    pairs = []
+    for z in range(ZS):
+        for y in range(YS):
+            x, core = root_of(z)
+            pairs.append((device(x, core, 2 * y + half, y), device(x, core, z, y)))
+    return lax.ppermute(part, ALL, pairs)
 
 
 def along_x(slab, core, shifts):
@@ -144,11 +142,15 @@
     def partial_of(panel):
         return jnp.einsum("qj,pq->jp", panel, inverse_block, preferred_element_type=F32).astype(BF16)
 
-    ring = relay_ring(normed[1][None], "z", ZS)
-    normed_0, ring[1], ring[ZS - 1] = lax.optimization_barrier((normed[0], ring[1], ring[ZS - 1]))
-    panel_0 = panel_y_then_z(normed_0)
+    zero = jnp.zeros((), BF16)
+    home = row == z
+    part_0 = placed_by_owner(direct_ring(normed[0], "y", YS), y, 0)
+    panel_0 = lax.all_gather(part_0, "z", axis=0, tiled=True)
+    near = near_of(copies_to(normed[1], "z", ZS)[:, None])
 
-    near = near_of(placed_by_owner(ring, z, 0)[:, None])
+    slab_0 = jnp.concatenate([moved_home(part_0, half) for half in range(2)], axis=0)
+    factor_slab = sum(along_x(slab_0, 0, (1, -1, 2)), jnp.where(home & (core == 0), slab_0, zero))
+    near, factor_slab = lax.optimization_barrier((near, factor_slab))
     chunks = [near[0], near[1], far_chunk(near), near[2]]
     deep = rows // (piece_rows * YS)
     of_slab = lambda part, lane: lax.dynamic_slice_in_dim(part, lane * deep, deep, 0)
@@ -157,24 +159,19 @@
     )
     slab_parts = [of_slab(near[0], y), of_slab(near[1], y), far_part, of_slab(near[2], y)]
     slab_1 = placed_by_owner(slab_parts, y, 1).reshape(rows, width)
-    zero = jnp.zeros((), BF16)
-    home = row == z
-    factor_slab = sum(along_x(slab_1, 1, (1, -1, -2)), jnp.where(home & (core == 1), slab_1, zero))
-    partial_1 = partial_of(placed_by_owner(chunks, y, 1).reshape(panel_0.shape))
+    factor_slab = sum(
+        along_x(slab_1, 1, (1, -1, -2)),
+        factor_slab + jnp.where(home & (core == 1), slab_1, zero),
+    )
+    partial_1 = partial_of(placed_by_owner(chunks, y, 1).reshape((-1, width)))
     given_1 = lax.ppermute(partial_1, "core", [(0, 1)])
 
     panel_0, factor_slab, given_1 = lax.optimization_barrier((panel_0, factor_slab, given_1))
-    slab_0 = lax.dynamic_slice_in_dim(panel_0, y * rows, rows, 0)
-    sent_0 = along_x(slab_0, 0, (1, -1, 2))
     partial_0 = partial_of(panel_0)
-    near_0, far_0 = [*sent_0[:2], sent_0[3]], sent_0[2]
-    partial_0, near_0 = lax.optimization_barrier((partial_0, near_0))
     given_0 = lax.ppermute(partial_0, "core", [(1, 0)])
-
     pair = jnp.where(core == 0, partial_0, partial_1).astype(F32)
     pair = (pair + (given_0.astype(F32) + given_1.astype(F32))).astype(BF16)
-    pair, far_0 = lax.optimization_barrier((pair, far_0))
-    factor_slab = sum([*near_0, far_0], factor_slab + jnp.where(home & (core == 0), slab_0, zero))
+    pair = lax.optimization_barrier(pair)
     product = sum_over_x(pair)
     col_keep = lax.dynamic_index_in_dim(keep_of(col * rows, rows), core, 0)
     offdiag = lax.optimization_barrier((-(product * col_keep)).astype(BF16))

time: 182 us -> 207 us (1.14)
  waiting for transfers between devices: 48.3 us -> 88.8 us
  starting transfers between devices: 89.1 us -> 74.8 us
  matrix products: 14.7 us -> 11 us
  other arithmetic: 6.66 us -> 8.78 us
    ppermute x9, waiting for transfers between devices: 7.46 us -> 32.7 us  [from_root(): return lax.ppermute(array, ALL, pairs)]
    all_to_all x0 -> x1, waiting for transfers between devices: none -> 20.2 us  [copies_to(): return lax.all_to_all(copies, axis, split_axis=0, concat_axis=0, tiled=True)]
    ppermute x2, starting transfers between devices: 22.9 us -> 8.63 us  [own_slab_of_both(): got = lax.ppermute(given, 'core', [(0, 1), (1, 0)])]
    ppermute x18 -> x11, starting transfers between devices: 29.2 us -> 17.2 us  [shift(): lax.ppermute(array, axis, [(i, (i + by) % size) for i in range(size)])]
    ppermute x18 -> x11, waiting for transfers between devices: 27.8 us -> 17 us  [shift(): lax.ppermute(array, axis, [(i, (i + by) % size) for i in range(size)])]
    all_to_all x1, waiting for transfers between devices: 0.01 us -> 5.38 us  [summed_over_col(): part = lax.all_to_all(copies, 'z', split_axis=0, concat_axis=0, tiled=True)]
    all_to_all x0 -> x1, starting transfers between devices: none -> 5.31 us  [copies_to(): return lax.all_to_all(copies, axis, split_axis=0, concat_axis=0, tiled=True)]
    ppermute x0 -> x2, starting transfers between devices: none -> 4.24 us  [moved_home(): return lax.ppermute(part, ALL, pairs)]
  transfers between devices with their start and end apart: 39 -> 35, of which waited for: 18 -> 16; matrix products, arithmetic and copies ran while one was open for 12% -> 7% of each run, Pallas kernels for 0% -> 0%
where the time goes in v7:
time: 207 us; the launch traced here: 206 us
  waiting for transfers between devices  88.8 us (43%)
  starting transfers between devices  74.8 us (36%)
  between operations  14.8 us (7%)
  matrix products  11 us (5%)
  other arithmetic  8.78 us (4%)
  local copies, waits for them, and re-layouts  8.05 us (4%)
    ppermute x9, waiting for transfers between devices, from_root(): return lax.ppermute(array, ALL, pairs)  32.7 us
    all_to_all x1, waiting for transfers between devices, copies_to(): return lax.all_to_all(copies, axis, split_axis=0, concat_axis=0, tiled=True)  20.2 us
    ppermute x11, starting transfers between devices, shift(): lax.ppermute(array, axis, [(i, (i + by) % size) for i in range(size)])  17.2 us
    ppermute x11, waiting for transfers between devices, shift(): lax.ppermute(array, axis, [(i, (i + by) % size) for i in range(size)])  17 us
    ppermute x9, starting transfers between devices, from_root(): return lax.ppermute(array, ALL, pairs)  12.1 us
    all_to_all x1, starting transfers between devices, summed_over_col(): part = lax.all_to_all(copies, 'z', split_axis=0, concat_axis=0, tiled=True)  9.65 us
    dot_general x2, matrix products, partial_of(): jnp.einsum('qj,pq->jp', panel, inverse_block, preferred_element_type=F32)  9.49 us
    ppermute x2, starting transfers between devices, own_slab_of_both(): got = lax.ppermute(given, 'core', [(0, 1), (1, 0)])  8.63 us
  transfers between devices with their start and end apart: 35, of which 16 were waited for; matrix products, arithmetic and copies ran while one was open for 7% of the time, Pallas kernels for 0%

profile of v7, /device:TPU:1, one launch (start us, length us, event | category | flops | bytes accessed | tf_op | source)
XLA Modules:
  0.0 206.1 jit_solution(14669511812366781249)
XLA Ops:
  9.7 2.2 %collective-permute-start = (bf16[96,512]{1,0:T(8,128)(2,1)S(1)}, bf16[96,512]{1,0:T(8,128)(2,1)S(1)}, u32[]{:S(2)}, u32[]{:S(2)}) collective-permute-start(bf16[96,512]{1,0:T(8,128)(2,1)S(1)} %get-tuple-element.27), channel_id=1, source_target_pairs={{0,1},{1,2},{2,3},{3,0},{4,5},{5,6},{6,7},{7,4},{8,9},{9,10},{10,1... | collective-permute-start | bytes 294920 | tf_op jit(solution)/shard_map/ppermute | solution.py:17
  11.9 2.6 %collective-permute-start.1 = (bf16[96,512]{1,0:T(8,128)(2,1)S(1)}, bf16[96,512]{1,0:T(8,128)(2,1)S(1)}, u32[]{:S(2)}, u32[]{:S(2)}) collective-permute-start(bf16[96,512]{1,0:T(8,128)(2,1)S(1)} %get-tuple-element.27), channel_id=1, source_target_pairs={{0,2},{1,3},{2,0},{3,1},{4,6},{5,7},{6,4},{7,5},{8,10},{9,11},{10,... | collective-permute-start | bytes 294920 | tf_op jit(solution)/shard_map/ppermute | solution.py:17
  15.7 2.8 %collective-permute-done.1 = bf16[96,512]{1,0:T(8,128)(2,1)S(1)} collective-permute-done((bf16[96,512]{1,0:T(8,128)(2,1)S(1)}, bf16[96,512]{1,0:T(8,128)(2,1)S(1)}, u32[]{:S(2)}, u32[]{:S(2)}) %collective-permute-start.1) | collective-permute-done | bytes 98336 | tf_op jit(solution)/shard_map/ppermute | solution.py:17
  19.3 3.6 %collective-permute-start.5 = (bf16[384,512]{1,0:T(8,128)(2,1)}, bf16[384,512]{1,0:T(8,128)(2,1)S(1)}, u32[]{:S(2)}, u32[]{:S(2)}) collective-permute-start(bf16[384,512]{1,0:T(8,128)(2,1)} %copy-done.4), channel_id=1, source_target_pairs={{0,0},{9,1},{18,2},{27,3},{32,36},{41,37},{50,38},{59,39},{64,72},... | collective-permute-start | bytes 1179656 | tf_op jit(solution)/shard_map/ppermute | solution.py:74
  23.9 5.3 %all-to-all-start = ((bf16[8,96,512]{2,1,0:T(8,128)(2,1)}), bf16[8,96,512]{2,1,0:T(8,128)(2,1)S(1)}, u32[]{:S(2)}, u32[]{:S(2)}) async-start(bf16[8,96,512]{2,1,0:T(8,128)(2,1)} %broadcast_in_dim.52), calls=%async_computation | async-start | bytes 1572864 | tf_op jit(solution)/shard_map/all_to_all | solution.py:36
  29.9 1.6 collective-permute-start.10
  34.6 1.6 collective-permute-start.9
  36.2 20.2 %all-to-all-done = bf16[8,96,512]{2,1,0:T(8,128)(2,1)S(1)} async-done(((bf16[8,96,512]{2,1,0:T(8,128)(2,1)}), bf16[8,96,512]{2,1,0:T(8,128)(2,1)S(1)}, u32[]{:S(2)}, u32[]{:S(2)}) %all-to-all-start) | async-done | bytes 786464 | tf_op jit(solution)/shard_map/all_to_all | solution.py:36
  56.3 2.7 %collective-permute-start.4 = (bf16[8,1,96,512]{3,2,1,0:T(8,128)(2,1)S(1)}, bf16[8,1,96,512]{3,2,1,0:T(8,128)(2,1)S(1)}, u32[]{:S(2)}, u32[]{:S(2)}) collective-permute-start(bf16[8,1,96,512]{3,2,1,0:T(8,128)(2,1)S(1)} %bitcast.82), channel_id=1, source_target_pairs={{0,3},{1,0},{2,1},{3,2},{4,7},{5,4},{6,5},{7,6},{8,11},{9,8},{10,9... | collective-permute-start | bytes 2359304 | tf_op jit(solution)/shard_map/ppermute | solution.py:17
  59.0 2.2 %add_add_fusion.1 = bf16[768,512]{1,0:T(8,128)(2,1)S(1)} fusion(bf16[768,512]{1,0:T(8,128)(2,1)} %collective-permute-done.10, bf16[768,512]{1,0:T(8,128)(2,1)} %collective-permute-done.9, bf16[768,512]{1,0:T(8,128)(2,1)} %collective-permute-done.8, bf16[768,512]{1,0:T(8,128)(2,1)} %collective-permute-done.7, bf16[768,512]{1,0:T(8,128)(2,1)} %copy-done.3, ...), kind=kLoop, calls=%fused_computation.9 | loop fusion | flops 1966080 | bytes 4718593 | tf_op jit(solution)/shard_map/add | solution.py:152
  61.2 7.5 %collective-permute-done.3 = bf16[8,1,96,512]{3,2,1,0:T(8,128)(2,1)} collective-permute-done((bf16[8,1,96,512]{3,2,1,0:T(8,128)(2,1)S(1)}, bf16[8,1,96,512]{3,2,1,0:T(8,128)(2,1)}, u32[]{:S(2)}, u32[]{:S(2)}) %collective-permute-start.3) | collective-permute-done | bytes 786464 | tf_op jit(solution)/shard_map/ppermute | solution.py:17
  82.5 3.5 %convolution_convert_fusion.1 = bf16[512,768]{1,0:T(8,128)(2,1)} fusion(bf16[3072,512]{1,0:T(8,128)(2,1)S(1)} %bitcast.88, bf16[768,3072]{1,0:T(8,128)(2,1)S(1)} %bitcast.102), kind=kOutput, calls=%fused_computation.2 | convolution fusion | flops 2416312320 | bytes 8650752 | tf_op jit(solution)/shard_map/qj,pq->jp/dot_general | solution.py:143
  88.5 32.7 %collective-permute-done.15 = bf16[768,512]{1,0:T(8,128)(2,1)} collective-permute-done((bf16[768,512]{1,0:T(8,128)(2,1)S(1)}, bf16[768,512]{1,0:T(8,128)(2,1)}, u32[]{:S(2)}, u32[]{:S(2)}) %collective-permute-start.15) | collective-permute-done | bytes 786464 | tf_op jit(solution)/shard_map/ppermute | solution.py:65
  121.2 2.1 add_add_fusion
  123.3 4.1 %collective-permute-done.18 = bf16[512,768]{1,0:T(8,128)(2,1)} collective-permute-done((bf16[512,768]{1,0:T(8,128)(2,1)}, bf16[512,768]{1,0:T(8,128)(2,1)}, u32[]{:S(2)}, u32[]{:S(2)}) %collective-permute-start.18) | collective-permute-done | bytes 786464 | tf_op jit(solution)/shard_map/ppermute | solution.py:167
  127.4 6.0 %convolution_convert_fusion = bf16[512,768]{1,0:T(8,128)(2,1)S(1)} fusion(bf16[3072,512]{1,0:T(8,128)(2,1)} %all-gather.2.cloned.1.call-done, bf16[768,3072]{1,0:T(8,128)(2,1)} %param.8), kind=kOutput, calls=%fused_computation.1 | convolution fusion | flops 2416312320 | bytes 8650752 | tf_op jit(solution)/shard_map/qj,pq->jp/dot_general | solution.py:143
  133.3 8.3 %collective-permute-start.19 = (bf16[512,768]{1,0:T(8,128)(2,1)S(1)}, bf16[512,768]{1,0:T(8,128)(2,1)S(1)}, u32[]{:S(2)}, u32[]{:S(2)}) collective-permute-start(bf16[512,768]{1,0:T(8,128)(2,1)S(1)} %convolution_convert_fusion), channel_id=1, source_target_pairs={{32,0},{33,1},{34,2},{35,3},{36,4},{37,5},{38,6},{39,7},{40,8},{41... | collective-permute-start | bytes 2359304 | tf_op jit(solution)/shard_map/ppermute | solution.py:171
  141.7 1.8 collective-permute-done.19
  143.4 1.8 add_convert_fusion
  145.4 2.7 %collective-permute-start.23 = (bf16[128,768]{1,0:T(8,128)(2,1)S(1)}, bf16[128,768]{1,0:T(8,128)(2,1)S(1)}, u32[]{:S(2)}, u32[]{:S(2)}) collective-permute-start(bf16[128,768]{1,0:T(8,128)(2,1)S(1)} %get-tuple-element.19), channel_id=1, source_target_pairs={{0,192},{64,0},{128,64},{192,128},{1,193},{65,1},{129,65},{193,129... | collective-permute-start | bytes 589832 | tf_op jit(solution)/shard_map/ppermute | solution.py:17
  149.5 1.7 collective-permute-start.21
  151.3 3.9 %collective-permute-done.20 = bf16[64,768]{1,0:T(8,128)(2,1)S(1)} collective-permute-done((bf16[64,768]{1,0:T(8,128)(2,1)S(1)}, bf16[64,768]{1,0:T(8,128)(2,1)S(1)}, u32[]{:S(2)}, u32[]{:S(2)}) %collective-permute-start.20) | collective-permute-done | bytes 98336 | tf_op jit(solution)/shard_map/ppermute | solution.py:17
  155.2 2.1 %collective-permute-done.21 = bf16[64,768]{1,0:T(8,128)(2,1)S(1)} collective-permute-done((bf16[64,768]{1,0:T(8,128)(2,1)S(1)}, bf16[64,768]{1,0:T(8,128)(2,1)S(1)}, u32[]{:S(2)}, u32[]{:S(2)}) %collective-permute-start.21) | collective-permute-done | bytes 98336 | tf_op jit(solution)/shard_map/ppermute | solution.py:17
  158.9 1.8 collective-permute-start.26
  161.7 1.7 collective-permute-done.26
  163.4 1.6 collective-permute-done.27
  165.8 9.6 %all-to-all-start.1 = ((bf16[8,32,512]{2,1,0:T(8,128)(2,1)}), bf16[8,32,512]{2,1,0:T(8,128)(2,1)S(1)}, u32[]{:S(2)}, u32[]{:S(2)}) async-start(bf16[8,32,512]{2,1,0:T(8,128)(2,1)} %broadcast_in_dim.58), calls=%async_computation.1 | async-start | bytes 524288 | tf_op jit(solution)/shard_map/all_to_all | solution.py:108
  175.5 3.0 %collective-permute-start.24 = (bf16[64,768]{1,0:T(8,128)(2,1)S(1)}, bf16[64,768]{1,0:T(8,128)(2,1)S(1)}, u32[]{:S(2)}, u32[]{:S(2)}) collective-permute-start(bf16[64,768]{1,0:T(8,128)(2,1)S(1)} %dynamic-slice_bitcast_fusion.4), channel_id=1, source_target_pairs={{0,32},{32,0},{1,33},{33,1},{2,34},{34,2},{3,35},{35,3},{4,36},{36... | collective-permute-start | bytes 294920 | tf_op jit(solution)/shard_map/ppermute | solution.py:122
  179.5 5.4 %all-to-all-done.1 = bf16[8,32,512]{2,1,0:T(8,128)(2,1)S(1)} async-done(((bf16[8,32,512]{2,1,0:T(8,128)(2,1)}), bf16[8,32,512]{2,1,0:T(8,128)(2,1)S(1)}, u32[]{:S(2)}, u32[]{:S(2)}) %all-to-all-start.1) | async-done | bytes 262176 | tf_op jit(solution)/shard_map/all_to_all | solution.py:108
  185.0 3.0 %collective-permute-start.29 = (bf16[32,512]{1,0:T(8,128)(2,1)S(1)}, bf16[32,512]{1,0:T(8,128)(2,1)S(1)}, u32[]{:S(2)}, u32[]{:S(2)}) collective-permute-start(bf16[32,512]{1,0:T(8,128)(2,1)S(1)} %reduce_sum.12), channel_id=1, source_target_pairs={{0,2},{1,3},{2,0},{3,1},{4,6},{5,7},{6,4},{7,5},{8,10},{9,11},{10,... | collective-permute-start | bytes 98312 | tf_op jit(solution)/shard_map/ppermute | solution.py:96
  189.7 2.3 %collective-permute-done.30 = bf16[32,512]{1,0:T(8,128)(2,1)S(1)} collective-permute-done((bf16[32,512]{1,0:T(8,128)(2,1)S(1)}, bf16[32,512]{1,0:T(8,128)(2,1)S(1)}, u32[]{:S(2)}, u32[]{:S(2)}) %collective-permute-start.30) | collective-permute-done | bytes 32800 | tf_op jit(solution)/shard_map/ppermute | solution.py:96
  192.0 5.6 %collective-permute-start.31 = (bf16[64,512]{1,0:T(8,128)(2,1)S(1)}, bf16[64,512]{1,0:T(8,128)(2,1)S(1)}, u32[]{:S(2)}, u32[]{:S(2)}) collective-permute-start(bf16[64,512]{1,0:T(8,128)(2,1)S(1)} %dynamic-slice_bitcast_fusion.5), channel_id=1, source_target_pairs={{0,32},{32,0},{1,33},{33,1},{2,34},{34,2},{3,35},{35,3},{4,36},{36... | collective-permute-start | bytes 196616 | tf_op jit(solution)/shard_map/ppermute | solution.py:122
  (112 shorter events, 34.5 us)
Async XLA Ops:
  7.2 120.2 %all-gather.2.cloned.1.call-start = ((), (), s32[]{:S(2)}) async-start(), calls=%async_computation.2 | async-start | bytes 3538944 | tf_op jit(solution)/shard_map/all_gather | solution.py:148
  9.7 6.0 %collective-permute-start = (bf16[96,512]{1,0:T(8,128)(2,1)S(1)}, bf16[96,512]{1,0:T(8,128)(2,1)S(1)}, u32[]{:S(2)}, u32[]{:S(2)}) collective-permute-start(bf16[96,512]{1,0:T(8,128)(2,1)S(1)} %get-tuple-element.27), channel_id=1, source_target_pairs={{0,1},{1,2},{2,3},{3,0},{4,5},{5,6},{6,7},{7,4},{8,9},{9,10},{10,1... | collective-permute-start | bytes 294920 | tf_op jit(solution)/shard_map/ppermute | solution.py:17
  11.9 6.6 %collective-permute-start.1 = (bf16[96,512]{1,0:T(8,128)(2,1)S(1)}, bf16[96,512]{1,0:T(8,128)(2,1)S(1)}, u32[]{:S(2)}, u32[]{:S(2)}) collective-permute-start(bf16[96,512]{1,0:T(8,128)(2,1)S(1)} %get-tuple-element.27), channel_id=1, source_target_pairs={{0,2},{1,3},{2,0},{3,1},{4,6},{5,7},{6,4},{7,5},{8,10},{9,11},{10,... | collective-permute-start | bytes 294920 | tf_op jit(solution)/shard_map/ppermute | solution.py:17
  14.5 4.0 %collective-permute-start.2 = (bf16[96,512]{1,0:T(8,128)(2,1)S(1)}, bf16[96,512]{1,0:T(8,128)(2,1)S(1)}, u32[]{:S(2)}, u32[]{:S(2)}) collective-permute-start(bf16[96,512]{1,0:T(8,128)(2,1)S(1)} %get-tuple-element.27), channel_id=1, source_target_pairs={{0,3},{1,0},{2,1},{3,2},{4,7},{5,4},{6,5},{7,6},{8,11},{9,8},{10,9... | collective-permute-start | bytes 294920 | tf_op jit(solution)/shard_map/ppermute | solution.py:17
  19.3 10.5 %collective-permute-start.5 = (bf16[384,512]{1,0:T(8,128)(2,1)}, bf16[384,512]{1,0:T(8,128)(2,1)S(1)}, u32[]{:S(2)}, u32[]{:S(2)}) collective-permute-start(bf16[384,512]{1,0:T(8,128)(2,1)} %copy-done.4), channel_id=1, source_target_pairs={{0,0},{9,1},{18,2},{27,3},{32,36},{41,37},{50,38},{59,39},{64,72},... | collective-permute-start | bytes 1179656 | tf_op jit(solution)/shard_map/ppermute | solution.py:74
  23.9 32.5 %all-to-all-start = ((bf16[8,96,512]{2,1,0:T(8,128)(2,1)}), bf16[8,96,512]{2,1,0:T(8,128)(2,1)S(1)}, u32[]{:S(2)}, u32[]{:S(2)}) async-start(bf16[8,96,512]{2,1,0:T(8,128)(2,1)} %broadcast_in_dim.52), calls=%async_computation | async-start | bytes 1572864 | tf_op jit(solution)/shard_map/all_to_all | solution.py:36
  29.9 26.4 %collective-permute-start.10 = (bf16[768,512]{1,0:T(8,128)(2,1)S(1)}, bf16[768,512]{1,0:T(8,128)(2,1)}, u32[]{:S(2)}, u32[]{:S(2)}) collective-permute-start(bf16[768,512]{1,0:T(8,128)(2,1)S(1)} %constant_dynamic-update-slice_fusion.8), channel_id=1, source_target_pairs={{36,4},{37,5},{38,6},{39,7},{108,76},{109,77},{110,78},{111,79},{1... | collective-permute-start | bytes 2359304 | tf_op jit(solution)/shard_map/ppermute | solution.py:65
  31.5 27.5 %collective-permute-start.7 = (bf16[768,512]{1,0:T(8,128)(2,1)S(1)}, bf16[768,512]{1,0:T(8,128)(2,1)}, u32[]{:S(2)}, u32[]{:S(2)}) collective-permute-start(bf16[768,512]{1,0:T(8,128)(2,1)S(1)} %constant_dynamic-update-slice_fusion.8), channel_id=1, source_target_pairs={{0,64},{1,65},{2,66},{3,67},{36,68},{37,69},{38,70},{39,71},{72,13... | collective-permute-start | bytes 2359304 | tf_op jit(solution)/shard_map/ppermute | solution.py:65
  33.0 26.0 %collective-permute-start.8 = (bf16[768,512]{1,0:T(8,128)(2,1)S(1)}, bf16[768,512]{1,0:T(8,128)(2,1)}, u32[]{:S(2)}, u32[]{:S(2)}) collective-permute-start(bf16[768,512]{1,0:T(8,128)(2,1)S(1)} %constant_dynamic-update-slice_fusion.8), channel_id=1, source_target_pairs={{0,192},{1,193},{2,194},{3,195},{36,196},{37,197},{38,198},{39,199... | collective-permute-start | bytes 2359304 | tf_op jit(solution)/shard_map/ppermute | solution.py:65
  34.6 24.4 %collective-permute-start.9 = (bf16[768,512]{1,0:T(8,128)(2,1)S(1)}, bf16[768,512]{1,0:T(8,128)(2,1)}, u32[]{:S(2)}, u32[]{:S(2)}) collective-permute-start(bf16[768,512]{1,0:T(8,128)(2,1)S(1)} %constant_dynamic-update-slice_fusion.8), channel_id=1, source_target_pairs={{0,128},{1,129},{2,130},{3,131},{36,132},{37,133},{38,134},{39,135... | collective-permute-start | bytes 2359304 | tf_op jit(solution)/shard_map/ppermute | solution.py:65
  56.3 12.5 %collective-permute-start.3 = (bf16[8,1,96,512]{3,2,1,0:T(8,128)(2,1)S(1)}, bf16[8,1,96,512]{3,2,1,0:T(8,128)(2,1)}, u32[]{:S(2)}, u32[]{:S(2)}) collective-permute-start(bf16[8,1,96,512]{3,2,1,0:T(8,128)(2,1)S(1)} %bitcast.81), channel_id=1, source_target_pairs={{0,1},{1,2},{2,3},{3,0},{4,5},{5,6},{6,7},{7,4},{8,9},{9,10},{10,1... | collective-permute-start | bytes 2359304 | tf_op jit(solution)/shard_map/ppermute | solution.py:17
  56.3 13.1 %collective-permute-start.4 = (bf16[8,1,96,512]{3,2,1,0:T(8,128)(2,1)S(1)}, bf16[8,1,96,512]{3,2,1,0:T(8,128)(2,1)S(1)}, u32[]{:S(2)}, u32[]{:S(2)}) collective-permute-start(bf16[8,1,96,512]{3,2,1,0:T(8,128)(2,1)S(1)} %bitcast.82), channel_id=1, source_target_pairs={{0,3},{1,0},{2,1},{3,2},{4,7},{5,4},{6,5},{7,6},{8,11},{9,8},{10,9... | collective-permute-start | bytes 2359304 | tf_op jit(solution)/shard_map/ppermute | solution.py:17
  70.8 10.3 %collective-permute-start.16 = (bf16[4,1,96,512]{3,2,1,0:T(8,128)(2,1)S(1)}, bf16[4,1,96,512]{3,2,1,0:T(8,128)(2,1)S(1)}, u32[]{:S(2)}, u32[]{:S(2)}) collective-permute-start(bf16[4,1,96,512]{3,2,1,0:T(8,128)(2,1)S(1)} %slice.30), channel_id=1, source_target_pairs={{0,1},{1,2},{2,3},{3,0},{4,5},{5,6},{6,7},{7,4},{8,9},{9,10},{10,1... | collective-permute-start | bytes 1179656 | tf_op jit(solution)/shard_map/ppermute | solution.py:17
  72.3 10.0 %collective-permute-start.17 = (bf16[4,1,96,512]{3,2,1,0:T(8,128)(2,1)S(1)}, bf16[4,1,96,512]{3,2,1,0:T(8,128)(2,1)S(1)}, u32[]{:S(2)}, u32[]{:S(2)}) collective-permute-start(bf16[4,1,96,512]{3,2,1,0:T(8,128)(2,1)S(1)} %slice.31), channel_id=1, source_target_pairs={{0,3},{1,0},{2,1},{3,2},{4,7},{5,4},{6,5},{7,6},{8,11},{9,8},{10,9... | collective-permute-start | bytes 1179656 | tf_op jit(solution)/shard_map/ppermute | solution.py:17
  77.3 10.3 %collective-permute-start.12 = (bf16[768,512]{1,0:T(8,128)(2,1)S(1)}, bf16[768,512]{1,0:T(8,128)(2,1)S(1)}, u32[]{:S(2)}, u32[]{:S(2)}) collective-permute-start(bf16[768,512]{1,0:T(8,128)(2,1)S(1)} %bitcast.89), channel_id=1, source_target_pairs={{0,96},{1,97},{2,98},{3,99},{36,100},{37,101},{38,102},{39,103},{7... | collective-permute-start | bytes 2359304 | tf_op jit(solution)/shard_map/ppermute | solution.py:65
  78.0 9.6 %collective-permute-start.13 = (bf16[768,512]{1,0:T(8,128)(2,1)S(1)}, bf16[768,512]{1,0:T(8,128)(2,1)}, u32[]{:S(2)}, u32[]{:S(2)}) collective-permute-start(bf16[768,512]{1,0:T(8,128)(2,1)S(1)} %bitcast.90), channel_id=1, source_target_pairs={{0,224},{1,225},{2,226},{3,227},{36,228},{37,229},{38,230},{39,231... | collective-permute-start | bytes 2359304 | tf_op jit(solution)/shard_map/ppermute | solution.py:65
  79.5 8.1 %collective-permute-start.14 = (bf16[768,512]{1,0:T(8,128)(2,1)S(1)}, bf16[768,512]{1,0:T(8,128)(2,1)}, u32[]{:S(2)}, u32[]{:S(2)}) collective-permute-start(bf16[768,512]{1,0:T(8,128)(2,1)S(1)} %bitcast.91), channel_id=1, source_target_pairs={{0,160},{1,161},{2,162},{3,163},{36,164},{37,165},{38,166},{39,167... | collective-permute-start | bytes 2359304 | tf_op jit(solution)/shard_map/ppermute | solution.py:65
  81.1 40.1 %collective-permute-start.15 = (bf16[768,512]{1,0:T(8,128)(2,1)S(1)}, bf16[768,512]{1,0:T(8,128)(2,1)}, u32[]{:S(2)}, u32[]{:S(2)}) collective-permute-start(bf16[768,512]{1,0:T(8,128)(2,1)S(1)} %bitcast.92), channel_id=1, source_target_pairs={{0,32},{1,33},{2,34},{3,35},{72,104},{73,105},{74,106},{75,107},{1... | collective-permute-start | bytes 2359304 | tf_op jit(solution)/shard_map/ppermute | solution.py:65
  86.1 41.3 %collective-permute-start.18 = (bf16[512,768]{1,0:T(8,128)(2,1)}, bf16[512,768]{1,0:T(8,128)(2,1)}, u32[]{:S(2)}, u32[]{:S(2)}) collective-permute-start(bf16[512,768]{1,0:T(8,128)(2,1)} %convolution_convert_fusion.1), channel_id=1, source_target_pairs={{0,32},{1,33},{2,34},{3,35},{4,36},{5,37},{6,38},{7,39},{8,40},{9,... | collective-permute-start | bytes 2359304 | tf_op jit(solution)/shard_map/ppermute | solution.py:167
  133.3 10.1 %collective-permute-start.19 = (bf16[512,768]{1,0:T(8,128)(2,1)S(1)}, bf16[512,768]{1,0:T(8,128)(2,1)S(1)}, u32[]{:S(2)}, u32[]{:S(2)}) collective-permute-start(bf16[512,768]{1,0:T(8,128)(2,1)S(1)} %convolution_convert_fusion), channel_id=1, source_target_pairs={{32,0},{33,1},{34,2},{35,3},{36,4},{37,5},{38,6},{39,7},{40,8},{41... | collective-permute-start | bytes 2359304 | tf_op jit(solution)/shard_map/ppermute | solution.py:171
  145.3 12.0 %collective-permute-start.22 = (bf16[128,768]{1,0:T(8,128)(2,1)S(1)}, bf16[128,768]{1,0:T(8,128)(2,1)S(1)}, u32[]{:S(2)}, u32[]{:S(2)}) collective-permute-start(bf16[128,768]{1,0:T(8,128)(2,1)S(1)} %get-tuple-element.18), channel_id=1, source_target_pairs={{0,64},{64,128},{128,192},{192,0},{1,65},{65,129},{129,193},{193,1... | collective-permute-start | bytes 589832 | tf_op jit(solution)/shard_map/ppermute | solution.py:17
  145.4 11.9 %collective-permute-start.23 = (bf16[128,768]{1,0:T(8,128)(2,1)S(1)}, bf16[128,768]{1,0:T(8,128)(2,1)S(1)}, u32[]{:S(2)}, u32[]{:S(2)}) collective-permute-start(bf16[128,768]{1,0:T(8,128)(2,1)S(1)} %get-tuple-element.19), channel_id=1, source_target_pairs={{0,192},{64,0},{128,64},{192,128},{1,193},{65,1},{129,65},{193,129... | collective-permute-start | bytes 589832 | tf_op jit(solution)/shard_map/ppermute | solution.py:17
  148.1 7.1 %collective-permute-start.20 = (bf16[64,768]{1,0:T(8,128)(2,1)S(1)}, bf16[64,768]{1,0:T(8,128)(2,1)S(1)}, u32[]{:S(2)}, u32[]{:S(2)}) collective-permute-start(bf16[64,768]{1,0:T(8,128)(2,1)S(1)} %get-tuple-element.16), channel_id=1, source_target_pairs={{0,128},{64,192},{128,0},{192,64},{1,129},{65,193},{129,1},{193,65... | collective-permute-start | bytes 294920 | tf_op jit(solution)/shard_map/ppermute | solution.py:17
  149.5 7.8 %collective-permute-start.21 = (bf16[64,768]{1,0:T(8,128)(2,1)S(1)}, bf16[64,768]{1,0:T(8,128)(2,1)S(1)}, u32[]{:S(2)}, u32[]{:S(2)}) collective-permute-start(bf16[64,768]{1,0:T(8,128)(2,1)S(1)} %get-tuple-element.17), channel_id=1, source_target_pairs={{0,128},{64,192},{128,0},{192,64},{1,129},{65,193},{129,1},{193,65... | collective-permute-start | bytes 294920 | tf_op jit(solution)/shard_map/ppermute | solution.py:17
  158.9 4.5 %collective-permute-start.26 = (bf16[32,512]{1,0:T(8,128)(2,1)S(1)}, bf16[32,512]{1,0:T(8,128)(2,1)S(1)}, u32[]{:S(2)}, u32[]{:S(2)}) collective-permute-start(bf16[32,512]{1,0:T(8,128)(2,1)S(1)} %get-tuple-element.30), channel_id=1, source_target_pairs={{0,2},{1,3},{2,0},{3,1},{4,6},{5,7},{6,4},{7,5},{8,10},{9,11},{10,... | collective-permute-start | bytes 98312 | tf_op jit(solution)/shard_map/ppermute | solution.py:96
  160.7 4.3 %collective-permute-start.27 = (bf16[32,512]{1,0:T(8,128)(2,1)S(1)}, bf16[32,512]{1,0:T(8,128)(2,1)S(1)}, u32[]{:S(2)}, u32[]{:S(2)}) collective-permute-start(bf16[32,512]{1,0:T(8,128)(2,1)S(1)} %get-tuple-element.29), channel_id=1, source_target_pairs={{0,3},{1,2},{2,1},{3,0},{4,7},{5,6},{6,5},{7,4},{8,11},{9,10},{10,... | collective-permute-start | bytes 98312 | tf_op jit(solution)/shard_map/ppermute | solution.py:96
  165.8 19.0 %all-to-all-start.1 = ((bf16[8,32,512]{2,1,0:T(8,128)(2,1)}), bf16[8,32,512]{2,1,0:T(8,128)(2,1)S(1)}, u32[]{:S(2)}, u32[]{:S(2)}) async-start(bf16[8,32,512]{2,1,0:T(8,128)(2,1)} %broadcast_in_dim.58), calls=%async_computation.1 | async-start | bytes 524288 | tf_op jit(solution)/shard_map/all_to_all | solution.py:108
  175.5 4.0 %collective-permute-start.24 = (bf16[64,768]{1,0:T(8,128)(2,1)S(1)}, bf16[64,768]{1,0:T(8,128)(2,1)S(1)}, u32[]{:S(2)}, u32[]{:S(2)}) collective-permute-start(bf16[64,768]{1,0:T(8,128)(2,1)S(1)} %dynamic-slice_bitcast_fusion.4), channel_id=1, source_target_pairs={{0,32},{32,0},{1,33},{33,1},{2,34},{34,2},{3,35},{35,3},{4,36},{36... | collective-permute-start | bytes 294920 | tf_op jit(solution)/shard_map/ppermute | solution.py:122
  184.9 4.0 %collective-permute-start.28 = (bf16[32,512]{1,0:T(8,128)(2,1)S(1)}, bf16[32,512]{1,0:T(8,128)(2,1)S(1)}, u32[]{:S(2)}, u32[]{:S(2)}) collective-permute-start(bf16[32,512]{1,0:T(8,128)(2,1)S(1)} %reduce_sum.12), channel_id=1, source_target_pairs={{0,1},{1,0},{2,3},{3,2},{4,5},{5,4},{6,7},{7,6},{8,9},{9,8},{10,11... | collective-permute-start | bytes 98312 | tf_op jit(solution)/shard_map/ppermute | solution.py:96
  185.0 4.7 %collective-permute-start.29 = (bf16[32,512]{1,0:T(8,128)(2,1)S(1)}, bf16[32,512]{1,0:T(8,128)(2,1)S(1)}, u32[]{:S(2)}, u32[]{:S(2)}) collective-permute-start(bf16[32,512]{1,0:T(8,128)(2,1)S(1)} %reduce_sum.12), channel_id=1, source_target_pairs={{0,2},{1,3},{2,0},{3,1},{4,6},{5,7},{6,4},{7,5},{8,10},{9,11},{10,... | collective-permute-start | bytes 98312 | tf_op jit(solution)/shard_map/ppermute | solution.py:96
  188.0 4.0 %collective-permute-start.30 = (bf16[32,512]{1,0:T(8,128)(2,1)S(1)}, bf16[32,512]{1,0:T(8,128)(2,1)S(1)}, u32[]{:S(2)}, u32[]{:S(2)}) collective-permute-start(bf16[32,512]{1,0:T(8,128)(2,1)S(1)} %reduce_sum.12), channel_id=1, source_target_pairs={{0,3},{1,2},{2,1},{3,0},{4,7},{5,6},{6,5},{7,4},{8,11},{9,10},{10,... | collective-permute-start | bytes 98312 | tf_op jit(solution)/shard_map/ppermute | solution.py:96
  192.0 6.5 %collective-permute-start.31 = (bf16[64,512]{1,0:T(8,128)(2,1)S(1)}, bf16[64,512]{1,0:T(8,128)(2,1)S(1)}, u32[]{:S(2)}, u32[]{:S(2)}) collective-permute-start(bf16[64,512]{1,0:T(8,128)(2,1)S(1)} %dynamic-slice_bitcast_fusion.5), channel_id=1, source_target_pairs={{0,32},{32,0},{1,33},{33,1},{2,34},{34,2},{3,35},{35,3},{4,36},{36... | collective-permute-start | bytes 196616 | tf_op jit(solution)/shard_map/ppermute | solution.py:122
  (13 other events, 149.8 us)
Sparse Core Ops, SparseCore 0:
  19.5 63.6 all-gather.1

commit v8 on v5

--- a/solution.py
+++ b/solution.py
@@ -82,7 +82,7 @@
 
 
 def along_x(slab, core, shifts):
-    return sum(from_root(slab, lambda x, c, z, y: ((x + by) % XS, core, z, y)) for by in shifts)
+    return [from_root(slab, lambda x, c, z, y: ((x + by) % XS, core, z, y)) for by in shifts]
 
 
 def pair_sum(partial):
@@ -96,11 +96,7 @@
     x = lax.axis_index("x")
     pair = pair.reshape(XS, -1, pair.shape[1])
     tile = lambda k: lax.dynamic_index_in_dim(pair, (x + k) % XS, 0, keepdims=False)
-    far = tile(2)
-    half = far.shape[0] // 2
-    opposite = jnp.concatenate(
-        [shift(far[:half], "x", XS, 2), shift(far[half:], "x", XS, -2)], axis=0
-    )
+    opposite = shift(tile(2), "x", XS, 2)
     near = shift(tile(1), "x", XS, 1).astype(F32) + shift(tile(3), "x", XS, -1).astype(F32)
     return (tile(0).astype(F32) + opposite.astype(F32)) + near
 
@@ -174,15 +170,18 @@
     sent_0 = along_x(slab_0, 0, (1, -1, 2))
     partial = [partial_of(panel_0)]
 
-    chunks, partial[0] = lax.optimization_barrier((chunks, partial[0]))
+    chunks, partial[0], sent_1 = lax.optimization_barrier((chunks, partial[0], sent_1))
     across = from_root(
         jnp.where(first, slab_1, slab_0), lambda x, c, z, y: (x, 1 - c, z, y)
     )
     partial.append(partial_of(placed_by_owner(chunks, y, 1).reshape(panel_0.shape)))
 
+    partial[1], sent_0[:2] = lax.optimization_barrier((partial[1], sent_0[:2]))
+    pair = lax.optimization_barrier(pair_sum(partial))
+    sent = [*sent_1, *sent_0, across]
     home = row == z
-    factor_slab = jnp.where(home, jnp.where(first, slab_0, slab_1), sent_0 + sent_1 + across)
-    pair, factor_slab = lax.optimization_barrier((pair_sum(partial), factor_slab))
+    slab = jnp.where(first, slab_0, slab_1)
+    factor_slab = sum(sent, jnp.where(home, slab, jnp.zeros((), BF16)))
     product = sum_over_x(pair)
     col_keep = lax.dynamic_index_in_dim(keep_of(col * rows, rows), core, 0)
     offdiag = lax.optimization_barrier((-(product * col_keep)).astype(BF16))

time: 168 us -> 170 us (1.012)
  waiting for transfers between devices: 45 us -> 50.1 us
  starting transfers between devices: 79 us -> 76.1 us
  other arithmetic: 9.54 us -> 7.55 us
    ppermute x18 -> x17, waiting for transfers between devices: 28.3 us -> 33.8 us  [shift(): lax.ppermute(array, axis, [(i, (i + by) % size) for i in range(size)])]
    ppermute x2, starting transfers between devices: 17.4 us -> 12.5 us  [own_slab_of_both(): got = lax.ppermute(given, 'core', [(0, 1), (1, 0)])]
    ppermute x1, starting transfers between devices: 7.17 us -> 11.5 us  [pair_sum(): lax.ppermute(jnp.where(first, partial[1], partial[0]), 'core', [(0, 1), (...]
    ppermute x8, starting transfers between devices: 12 us -> 9.58 us  [from_root(): return lax.ppermute(array, ALL, pairs)]
    dot_general x1, matrix products: 0.27 us -> 2.26 us  [body(): term = -jnp.dot(offdiag, factor_slab, preferred_element_type=F32)]
    all_to_all x1, waiting for transfers between devices: 1.87 us -> 3.59 us  [summed_over_col(): part = lax.all_to_all(copies, 'z', split_axis=0, concat_axis=0, tiled=True)]
    ppermute x18 -> x17, starting transfers between devices: 27.1 us -> 27.5 us  [shift(): lax.ppermute(array, axis, [(i, (i + by) % size) for i in range(size)])]
  transfers between devices with their start and end apart: 37 -> 36, of which waited for: 16 -> 17; matrix products, arithmetic and copies ran while one was open for 13% -> 11% of each run, Pallas kernels for 0% -> 0%
where the time goes in v8:
time: 170 us
  starting transfers between devices  76.1 us (45%)
  waiting for transfers between devices  50.1 us (29%)
  between operations  14.9 us (9%)
  matrix products  12.1 us (7%)
  local copies, waits for them, and re-layouts  8.84 us (5%)
  other arithmetic  7.55 us (4%)
    ppermute x17, waiting for transfers between devices, shift(): lax.ppermute(array, axis, [(i, (i + by) % size) for i in range(size)])  33.8 us
    ppermute x17, starting transfers between devices, shift(): lax.ppermute(array, axis, [(i, (i + by) % size) for i in range(size)])  27.5 us
    ppermute x2, starting transfers between devices, own_slab_of_both(): got = lax.ppermute(given, 'core', [(0, 1), (1, 0)])  12.5 us
    ppermute x1, starting transfers between devices, pair_sum(): lax.ppermute(jnp.where(first, partial[1], partial[0]), 'core', [(0, 1), (...  11.5 us
    ppermute x8, starting transfers between devices, from_root(): return lax.ppermute(array, ALL, pairs)  9.58 us
    dot_general x2, matrix products, partial_of(): jnp.einsum('qj,pq->jp', panel, inverse_block, preferred_element_type=F32)  8.66 us
    all_to_all x1, starting transfers between devices, summed_over_col(): part = lax.all_to_all(copies, 'z', split_axis=0, concat_axis=0, tiled=True)  7.74 us
    ppermute x6, starting transfers between devices, exchanged(): return lax.ppermute(array, axis, [(i, i ^ by) for i in range(size)])  7.28 us
  transfers between devices with their start and end apart: 36, of which 17 were waited for; matrix products, arithmetic and copies ran while one was open for 11% of the time, Pallas kernels for 0%

profile of v8, /device:TPU:1, one launch (start us, length us, event | category | flops | bytes accessed | tf_op | source)
XLA Modules:
  0.0 169.6 jit_solution(6620000460310528611)
XLA Ops:
  9.7 2.2 %collective-permute-start = (bf16[96,512]{1,0:T(8,128)(2,1)S(1)}, bf16[96,512]{1,0:T(8,128)(2,1)S(1)}, u32[]{:S(2)}, u32[]{:S(2)}) collective-permute-start(bf16[96,512]{1,0:T(8,128)(2,1)S(1)} %get-tuple-element.44), channel_id=1, source_target_pairs={{0,1},{1,2},{2,3},{3,0},{4,5},{5,6},{6,7},{7,4},{8,9},{9,10},{10,1... | collective-permute-start | bytes 294920 | tf_op jit(solution)/shard_map/ppermute | solution.py:17
  11.9 2.6 %collective-permute-start.1 = (bf16[96,512]{1,0:T(8,128)(2,1)S(1)}, bf16[96,512]{1,0:T(8,128)(2,1)S(1)}, u32[]{:S(2)}, u32[]{:S(2)}) collective-permute-start(bf16[96,512]{1,0:T(8,128)(2,1)S(1)} %get-tuple-element.44), channel_id=1, source_target_pairs={{0,2},{1,3},{2,0},{3,1},{4,6},{5,7},{6,4},{7,5},{8,10},{9,11},{10,... | collective-permute-start | bytes 294920 | tf_op jit(solution)/shard_map/ppermute | solution.py:17
  15.7 2.8 %collective-permute-done.1 = bf16[96,512]{1,0:T(8,128)(2,1)S(1)} collective-permute-done((bf16[96,512]{1,0:T(8,128)(2,1)S(1)}, bf16[96,512]{1,0:T(8,128)(2,1)S(1)}, u32[]{:S(2)}, u32[]{:S(2)}) %collective-permute-start.1) | collective-permute-done | bytes 98336 | tf_op jit(solution)/shard_map/ppermute | solution.py:17
  19.3 1.7 %collective-permute-start.3 = (bf16[1,96,512]{2,1,0:T(8,128)(2,1)S(1)}, bf16[1,96,512]{2,1,0:T(8,128)(2,1)S(1)}, u32[]{:S(2)}, u32[]{:S(2)}) collective-permute-start(bf16[1,96,512]{2,1,0:T(8,128)(2,1)S(1)} %get-tuple-element.43), channel_id=1, source_target_pairs={{0,4},{4,8},{8,12},{12,16},{16,20},{20,24},{24,28},{28,0},{1,5},{5... | collective-permute-start | bytes 294920 | tf_op jit(solution)/shard_map/ppermute | solution.py:17
  21.0 4.0 %collective-permute-start.7 = (bf16[1,96,512]{2,1,0:T(8,128)(2,1)S(1)}, bf16[1,96,512]{2,1,0:T(8,128)(2,1)S(1)}, u32[]{:S(2)}, u32[]{:S(2)}) collective-permute-start(bf16[1,96,512]{2,1,0:T(8,128)(2,1)S(1)} %get-tuple-element.43), channel_id=1, source_target_pairs={{0,28},{4,0},{8,4},{12,8},{16,12},{20,16},{24,20},{28,24},{1,29},{... | collective-permute-start | bytes 294920 | tf_op jit(solution)/shard_map/ppermute | solution.py:17
  25.3 1.7 collective-permute-done.3
  27.0 2.8 %collective-permute-start.8 = (bf16[1,96,512]{2,1,0:T(8,128)(2,1)S(1)}, bf16[1,96,512]{2,1,0:T(8,128)(2,1)S(1)}, u32[]{:S(2)}, u32[]{:S(2)}) collective-permute-start(bf16[1,96,512]{2,1,0:T(8,128)(2,1)S(1)} %collective-permute-done.7), channel_id=1, source_target_pairs={{0,28},{4,0},{8,4},{12,8},{16,12},{20,16},{24,20},{28,24},{1,29},{... | collective-permute-start | bytes 294920 | tf_op jit(solution)/shard_map/ppermute | solution.py:17
  29.8 1.9 %collective-permute-done.4 = bf16[1,96,512]{2,1,0:T(8,128)(2,1)S(1)} collective-permute-done((bf16[1,96,512]{2,1,0:T(8,128)(2,1)S(1)}, bf16[1,96,512]{2,1,0:T(8,128)(2,1)S(1)}, u32[]{:S(2)}, u32[]{:S(2)}) %collective-permute-start.4) | collective-permute-done | bytes 98336 | tf_op jit(solution)/shard_map/ppermute | solution.py:17
  31.7 2.8 %collective-permute-start.9 = (bf16[1,96,512]{2,1,0:T(8,128)(2,1)S(1)}, bf16[1,96,512]{2,1,0:T(8,128)(2,1)S(1)}, u32[]{:S(2)}, u32[]{:S(2)}) collective-permute-start(bf16[1,96,512]{2,1,0:T(8,128)(2,1)S(1)} %collective-permute-done.8), channel_id=1, source_target_pairs={{0,28},{4,0},{8,4},{12,8},{16,12},{20,16},{24,20},{28,24},{1,29},{... | collective-permute-start | bytes 294920 | tf_op jit(solution)/shard_map/ppermute | solution.py:17
  34.4 1.9 %collective-permute-done.5 = bf16[1,96,512]{2,1,0:T(8,128)(2,1)S(1)} collective-permute-done((bf16[1,96,512]{2,1,0:T(8,128)(2,1)S(1)}, bf16[1,96,512]{2,1,0:T(8,128)(2,1)S(1)}, u32[]{:S(2)}, u32[]{:S(2)}) %collective-permute-start.5) | collective-permute-done | bytes 98336 | tf_op jit(solution)/shard_map/ppermute | solution.py:17
  36.4 8.0 %collective-permute-done.6 = bf16[1,96,512]{2,1,0:T(8,128)(2,1)S(1)} collective-permute-done((bf16[1,96,512]{2,1,0:T(8,128)(2,1)S(1)}, bf16[1,96,512]{2,1,0:T(8,128)(2,1)S(1)}, u32[]{:S(2)}, u32[]{:S(2)}) %collective-permute-start.6) | collective-permute-done | bytes 98336 | tf_op jit(solution)/shard_map/ppermute | solution.py:17
  45.2 2.1 %collective-permute-start.11 = (bf16[8,1,96,512]{3,2,1,0:T(8,128)(2,1)S(1)}, bf16[8,1,96,512]{3,2,1,0:T(8,128)(2,1)S(1)}, u32[]{:S(2)}, u32[]{:S(2)}) collective-permute-start(bf16[8,1,96,512]{3,2,1,0:T(8,128)(2,1)S(1)} %bitcast_dynamic-update-slice_fusion), channel_id=1, source_target_pairs={{0,3},{1,0},{2,1},{3,2},{4,7},{5,4},{6,5},{7,6},{8,11},{9,8},{10,9... | collective-permute-start | bytes 2359304 | tf_op jit(solution)/shard_map/ppermute | solution.py:17
  49.4 7.7 %collective-permute-done.10 = bf16[8,1,96,512]{3,2,1,0:T(8,128)(2,1)} collective-permute-done((bf16[8,1,96,512]{3,2,1,0:T(8,128)(2,1)S(1)}, bf16[8,1,96,512]{3,2,1,0:T(8,128)(2,1)}, u32[]{:S(2)}, u32[]{:S(2)}) %collective-permute-start.10) | collective-permute-done | bytes 786464 | tf_op jit(solution)/shard_map/ppermute | solution.py:17
  59.1 1.6 collective-permute-start.15
  63.8 7.1 %all-gather.2.cloned.1.call-done = bf16[3072,512]{1,0:T(8,128)(2,1)} async-done(((bf16[384,512]{1,0:T(8,128)(2,1)}), bf16[3072,512]{1,0:T(8,128)(2,1)}) %all-gather.2.cloned.1.call-update) | async-done | bytes 3145744 | tf_op jit(solution)/shard_map/all_gather | solution.py:53
  70.9 2.5 %collective-permute-start.13 = (bf16[4,1,96,512]{3,2,1,0:T(8,128)(2,1)S(1)}, bf16[4,1,96,512]{3,2,1,0:T(8,128)(2,1)S(1)}, u32[]{:S(2)}, u32[]{:S(2)}) collective-permute-start(bf16[4,1,96,512]{3,2,1,0:T(8,128)(2,1)S(1)} %slice.19), channel_id=1, source_target_pairs={{0,3},{1,0},{2,1},{3,2},{4,7},{5,4},{6,5},{7,6},{8,11},{9,8},{10,9... | collective-permute-start | bytes 1179656 | tf_op jit(solution)/shard_map/ppermute | solution.py:17
  74.9 6.0 %convolution_convert_fusion.1 = bf16[512,768]{1,0:T(8,128)(2,1)S(1)} fusion(bf16[3072,512]{1,0:T(8,128)(2,1)} %all-gather.2.cloned.1.call-done, bf16[768,3072]{1,0:T(8,128)(2,1)} %param.8), kind=kOutput, calls=%fused_computation.2 | convolution fusion | flops 2416312320 | bytes 8650752 | tf_op jit(solution)/shard_map/qj,pq->jp/dot_general | solution.py:152
  80.9 2.3 %broadcast_select_fusion = (bf16[768,512]{1,0:T(8,128)(2,1)}, bf16[768,512]{1,0:T(8,128)(2,1)S(1)}) fusion(pred[]{:T(512)S(6)} %eq.63, bf16[2,4,96,512]{3,2,1,0:T(8,128)(2,1)S(1)} %dynamic-slice_dynamic-update-slice_fusion, bf16[3072,512]{1,0:T(8,128)(2,1)} %all-gather.2.cloned.1.call-done, s32[]{:T(128)S(6)} %select_n.300), kind=kLoop, calls=%fused_computation.17 | loop fusion | flops 393216 | bytes 3145733 | tf_op jit(solution)/shard_map/jit(_where)/select_n | solution.py:175
  86.7 2.7 %convolution_convert_fusion = bf16[512,768]{1,0:T(8,128)(2,1)S(1)} fusion(bf16[3072,512]{1,0:T(8,128)(2,1)S(1)} %bitcast.91, bf16[768,3072]{1,0:T(8,128)(2,1)S(1)} %bitcast.107), kind=kOutput, calls=%fused_computation.1 | convolution fusion | flops 2416312320 | bytes 8650752 | tf_op jit(solution)/shard_map/qj,pq->jp/dot_general | solution.py:152
  91.4 11.5 %collective-permute-start.20 = (bf16[512,768]{1,0:T(8,128)(2,1)}, bf16[512,768]{1,0:T(8,128)(2,1)}, u32[]{:S(2)}, u32[]{:S(2)}) collective-permute-start(bf16[512,768]{1,0:T(8,128)(2,1)} %broadcast_select_fusion.1), channel_id=1, source_target_pairs={{0,32},{32,0},{1,33},{33,1},{2,34},{34,2},{3,35},{35,3},{4,36},{36... | collective-permute-start | bytes 2359304 | tf_op jit(solution)/shard_map/ppermute | solution.py:90
  106.6 3.5 %collective-permute-start.23 = (bf16[128,768]{1,0:T(8,128)(2,1)S(1)}, bf16[128,768]{1,0:T(8,128)(2,1)S(1)}, u32[]{:S(2)}, u32[]{:S(2)}) collective-permute-start(bf16[128,768]{1,0:T(8,128)(2,1)S(1)} %get-tuple-element.35), channel_id=1, source_target_pairs={{0,192},{64,0},{128,64},{192,128},{1,193},{65,1},{129,65},{193,129... | collective-permute-start | bytes 589832 | tf_op jit(solution)/shard_map/ppermute | solution.py:17
  111.6 2.3 %collective-permute-done.23 = bf16[128,768]{1,0:T(8,128)(2,1)S(1)} collective-permute-done((bf16[128,768]{1,0:T(8,128)(2,1)S(1)}, bf16[128,768]{1,0:T(8,128)(2,1)S(1)}, u32[]{:S(2)}, u32[]{:S(2)}) %collective-permute-start.23) | collective-permute-done | bytes 196640 | tf_op jit(solution)/shard_map/ppermute | solution.py:17
  113.9 7.4 %collective-permute-done.22 = bf16[128,768]{1,0:T(8,128)(2,1)S(1)} collective-permute-done((bf16[128,768]{1,0:T(8,128)(2,1)S(1)}, bf16[128,768]{1,0:T(8,128)(2,1)S(1)}, u32[]{:S(2)}, u32[]{:S(2)}) %collective-permute-start.22) | collective-permute-done | bytes 196640 | tf_op jit(solution)/shard_map/ppermute | solution.py:17
  121.5 2.3 %fusion.1 = bf16[128,512]{1,0:T(8,128)(2,1)S(1)} fusion(bf16[128,768]{1,0:T(8,128)(2,1)S(1)} %fusion.16, bf16[768,512]{1,0:T(8,128)(2,1)S(1)} %collective-permute-done.26, bf16[768,512]{1,0:T(8,128)(2,1)S(1)} %collective-permute-done.25, bf16[768,512]{1,0:T(8,128)(2,1)S(1)} %copy-done.11, bf16[768,512]{1,0:T(8,128)(2,1)S(1)} %copy-done.9, ...), kind=kOutput, calls=%fused_computation.6 | convolution fusion | flops 104333312 | bytes 7405570 | tf_op jit(solution)/shard_map/dot_general | solution.py:189
  125.3 1.9 %collective-permute-start.27 = (bf16[32,512]{1,0:T(8,128)(2,1)S(1)}, bf16[32,512]{1,0:T(8,128)(2,1)S(1)}, u32[]{:S(2)}, u32[]{:S(2)}) collective-permute-start(bf16[32,512]{1,0:T(8,128)(2,1)S(1)} %get-tuple-element.45), channel_id=1, source_target_pairs={{0,1},{1,0},{2,3},{3,2},{4,5},{5,4},{6,7},{7,6},{8,9},{9,8},{10,11... | collective-permute-start | bytes 98312 | tf_op jit(solution)/shard_map/ppermute | solution.py:105
  127.9 1.7 collective-permute-done.28
  130.3 7.7 %all-to-all-start = ((bf16[8,32,512]{2,1,0:T(8,128)(2,1)}), bf16[8,32,512]{2,1,0:T(8,128)(2,1)S(1)}, u32[]{:S(2)}, u32[]{:S(2)}) async-start(bf16[8,32,512]{2,1,0:T(8,128)(2,1)} %broadcast_in_dim.73), calls=%async_computation | async-start | bytes 524288 | tf_op jit(solution)/shard_map/all_to_all | solution.py:117
  138.1 4.9 %collective-permute-start.24 = (bf16[64,768]{1,0:T(8,128)(2,1)S(1)}, bf16[64,768]{1,0:T(8,128)(2,1)S(1)}, u32[]{:S(2)}, u32[]{:S(2)}) collective-permute-start(bf16[64,768]{1,0:T(8,128)(2,1)S(1)} %dynamic-slice_bitcast_fusion.3), channel_id=1, source_target_pairs={{0,32},{32,0},{1,33},{33,1},{2,34},{34,2},{3,35},{35,3},{4,36},{36... | collective-permute-start | bytes 294920 | tf_op jit(solution)/shard_map/ppermute | solution.py:131
  143.9 3.6 %all-to-all-done = bf16[8,32,512]{2,1,0:T(8,128)(2,1)S(1)} async-done(((bf16[8,32,512]{2,1,0:T(8,128)(2,1)}), bf16[8,32,512]{2,1,0:T(8,128)(2,1)S(1)}, u32[]{:S(2)}, u32[]{:S(2)}) %all-to-all-start) | async-done | bytes 262176 | tf_op jit(solution)/shard_map/all_to_all | solution.py:117
  147.6 1.8 %collective-permute-start.31 = (bf16[32,512]{1,0:T(8,128)(2,1)S(1)}, bf16[32,512]{1,0:T(8,128)(2,1)S(1)}, u32[]{:S(2)}, u32[]{:S(2)}) collective-permute-start(bf16[32,512]{1,0:T(8,128)(2,1)S(1)} %reduce_sum.12), channel_id=1, source_target_pairs={{0,2},{1,3},{2,0},{3,1},{4,6},{5,7},{6,4},{7,5},{8,10},{9,11},{10,... | collective-permute-start | bytes 98312 | tf_op jit(solution)/shard_map/ppermute | solution.py:105
  149.4 2.0 %collective-permute-start.32 = (bf16[32,512]{1,0:T(8,128)(2,1)S(1)}, bf16[32,512]{1,0:T(8,128)(2,1)S(1)}, u32[]{:S(2)}, u32[]{:S(2)}) collective-permute-start(bf16[32,512]{1,0:T(8,128)(2,1)S(1)} %reduce_sum.12), channel_id=1, source_target_pairs={{0,3},{1,2},{2,1},{3,0},{4,7},{5,6},{6,5},{7,4},{8,11},{9,10},{10,... | collective-permute-start | bytes 98312 | tf_op jit(solution)/shard_map/ppermute | solution.py:105
  153.4 7.6 %collective-permute-start.33 = (bf16[64,512]{1,0:T(8,128)(2,1)S(1)}, bf16[64,512]{1,0:T(8,128)(2,1)S(1)}, u32[]{:S(2)}, u32[]{:S(2)}) collective-permute-start(bf16[64,512]{1,0:T(8,128)(2,1)S(1)} %dynamic-slice_bitcast_fusion.4), channel_id=1, source_target_pairs={{0,32},{32,0},{1,33},{33,1},{2,34},{34,2},{3,35},{35,3},{4,36},{36... | collective-permute-start | bytes 196616 | tf_op jit(solution)/shard_map/ppermute | solution.py:131
  (128 shorter events, 32.1 us)
Async XLA Ops:
  7.2 63.7 %all-gather.2.cloned.1.call-start = ((), (), s32[]{:S(2)}) async-start(), calls=%async_computation.1 | async-start | bytes 3538944 | tf_op jit(solution)/shard_map/all_gather | solution.py:53
  9.7 6.0 %collective-permute-start = (bf16[96,512]{1,0:T(8,128)(2,1)S(1)}, bf16[96,512]{1,0:T(8,128)(2,1)S(1)}, u32[]{:S(2)}, u32[]{:S(2)}) collective-permute-start(bf16[96,512]{1,0:T(8,128)(2,1)S(1)} %get-tuple-element.44), channel_id=1, source_target_pairs={{0,1},{1,2},{2,3},{3,0},{4,5},{5,6},{6,7},{7,4},{8,9},{9,10},{10,1... | collective-permute-start | bytes 294920 | tf_op jit(solution)/shard_map/ppermute | solution.py:17
  11.9 6.6 %collective-permute-start.1 = (bf16[96,512]{1,0:T(8,128)(2,1)S(1)}, bf16[96,512]{1,0:T(8,128)(2,1)S(1)}, u32[]{:S(2)}, u32[]{:S(2)}) collective-permute-start(bf16[96,512]{1,0:T(8,128)(2,1)S(1)} %get-tuple-element.44), channel_id=1, source_target_pairs={{0,2},{1,3},{2,0},{3,1},{4,6},{5,7},{6,4},{7,5},{8,10},{9,11},{10,... | collective-permute-start | bytes 294920 | tf_op jit(solution)/shard_map/ppermute | solution.py:17
  19.3 7.7 %collective-permute-start.3 = (bf16[1,96,512]{2,1,0:T(8,128)(2,1)S(1)}, bf16[1,96,512]{2,1,0:T(8,128)(2,1)S(1)}, u32[]{:S(2)}, u32[]{:S(2)}) collective-permute-start(bf16[1,96,512]{2,1,0:T(8,128)(2,1)S(1)} %get-tuple-element.43), channel_id=1, source_target_pairs={{0,4},{4,8},{8,12},{12,16},{16,20},{20,24},{24,28},{28,0},{1,5},{5... | collective-permute-start | bytes 294920 | tf_op jit(solution)/shard_map/ppermute | solution.py:17
  21.0 6.0 %collective-permute-start.7 = (bf16[1,96,512]{2,1,0:T(8,128)(2,1)S(1)}, bf16[1,96,512]{2,1,0:T(8,128)(2,1)S(1)}, u32[]{:S(2)}, u32[]{:S(2)}) collective-permute-start(bf16[1,96,512]{2,1,0:T(8,128)(2,1)S(1)} %get-tuple-element.43), channel_id=1, source_target_pairs={{0,28},{4,0},{8,4},{12,8},{16,12},{20,16},{24,20},{28,24},{1,29},{... | collective-permute-start | bytes 294920 | tf_op jit(solution)/shard_map/ppermute | solution.py:17
  27.0 4.7 %collective-permute-start.4 = (bf16[1,96,512]{2,1,0:T(8,128)(2,1)S(1)}, bf16[1,96,512]{2,1,0:T(8,128)(2,1)S(1)}, u32[]{:S(2)}, u32[]{:S(2)}) collective-permute-start(bf16[1,96,512]{2,1,0:T(8,128)(2,1)S(1)} %collective-permute-done.3), channel_id=1, source_target_pairs={{0,4},{4,8},{8,12},{12,16},{16,20},{20,24},{24,28},{28,0},{1,5},{5... | collective-permute-start | bytes 294920 | tf_op jit(solution)/shard_map/ppermute | solution.py:17
  27.0 4.7 %collective-permute-start.8 = (bf16[1,96,512]{2,1,0:T(8,128)(2,1)S(1)}, bf16[1,96,512]{2,1,0:T(8,128)(2,1)S(1)}, u32[]{:S(2)}, u32[]{:S(2)}) collective-permute-start(bf16[1,96,512]{2,1,0:T(8,128)(2,1)S(1)} %collective-permute-done.7), channel_id=1, source_target_pairs={{0,28},{4,0},{8,4},{12,8},{16,12},{20,16},{24,20},{28,24},{1,29},{... | collective-permute-start | bytes 294920 | tf_op jit(solution)/shard_map/ppermute | solution.py:17
  31.7 4.7 %collective-permute-start.5 = (bf16[1,96,512]{2,1,0:T(8,128)(2,1)S(1)}, bf16[1,96,512]{2,1,0:T(8,128)(2,1)S(1)}, u32[]{:S(2)}, u32[]{:S(2)}) collective-permute-start(bf16[1,96,512]{2,1,0:T(8,128)(2,1)S(1)} %collective-permute-done.4), channel_id=1, source_target_pairs={{0,4},{4,8},{8,12},{12,16},{16,20},{20,24},{24,28},{28,0},{1,5},{5... | collective-permute-start | bytes 294920 | tf_op jit(solution)/shard_map/ppermute | solution.py:17
  31.7 12.7 %collective-permute-start.9 = (bf16[1,96,512]{2,1,0:T(8,128)(2,1)S(1)}, bf16[1,96,512]{2,1,0:T(8,128)(2,1)S(1)}, u32[]{:S(2)}, u32[]{:S(2)}) collective-permute-start(bf16[1,96,512]{2,1,0:T(8,128)(2,1)S(1)} %collective-permute-done.8), channel_id=1, source_target_pairs={{0,28},{4,0},{8,4},{12,8},{16,12},{20,16},{24,20},{28,24},{1,29},{... | collective-permute-start | bytes 294920 | tf_op jit(solution)/shard_map/ppermute | solution.py:17
  36.4 8.1 %collective-permute-start.6 = (bf16[1,96,512]{2,1,0:T(8,128)(2,1)S(1)}, bf16[1,96,512]{2,1,0:T(8,128)(2,1)S(1)}, u32[]{:S(2)}, u32[]{:S(2)}) collective-permute-start(bf16[1,96,512]{2,1,0:T(8,128)(2,1)S(1)} %collective-permute-done.5), channel_id=1, source_target_pairs={{0,4},{4,8},{8,12},{12,16},{16,20},{20,24},{24,28},{28,0},{1,5},{5... | collective-permute-start | bytes 294920 | tf_op jit(solution)/shard_map/ppermute | solution.py:17
  44.5 12.6 %collective-permute-start.10 = (bf16[8,1,96,512]{3,2,1,0:T(8,128)(2,1)S(1)}, bf16[8,1,96,512]{3,2,1,0:T(8,128)(2,1)}, u32[]{:S(2)}, u32[]{:S(2)}) collective-permute-start(bf16[8,1,96,512]{3,2,1,0:T(8,128)(2,1)S(1)} %bitcast_dynamic-update-slice_fusion), channel_id=1, source_target_pairs={{0,1},{1,2},{2,3},{3,0},{4,5},{5,6},{6,7},{7,4},{8,9},{9,10},{10,1... | collective-permute-start | bytes 2359304 | tf_op jit(solution)/shard_map/ppermute | solution.py:17
  45.2 13.9 %collective-permute-start.11 = (bf16[8,1,96,512]{3,2,1,0:T(8,128)(2,1)S(1)}, bf16[8,1,96,512]{3,2,1,0:T(8,128)(2,1)S(1)}, u32[]{:S(2)}, u32[]{:S(2)}) collective-permute-start(bf16[8,1,96,512]{3,2,1,0:T(8,128)(2,1)S(1)} %bitcast_dynamic-update-slice_fusion), channel_id=1, source_target_pairs={{0,3},{1,0},{2,1},{3,2},{4,7},{5,4},{6,5},{7,6},{8,11},{9,8},{10,9... | collective-permute-start | bytes 2359304 | tf_op jit(solution)/shard_map/ppermute | solution.py:17
  48.0 10.0 %collective-permute-start.14 = (bf16[2,1,96,512]{3,2,1,0:T(8,128)(2,1)}, bf16[2,1,96,512]{3,2,1,0:T(8,128)(2,1)}, u32[]{:S(2)}, u32[]{:S(2)}) collective-permute-start(bf16[2,1,96,512]{3,2,1,0:T(8,128)(2,1)} %get-tuple-element.37), channel_id=1, source_target_pairs={{0,2},{1,3},{2,0},{3,1},{36,38},{37,39},{38,36},{39,37},{72,74},{7... | collective-permute-start | bytes 589832 | tf_op jit(solution)/shard_map/ppermute | solution.py:81
  59.1 25.7 %collective-permute-start.15 = (bf16[768,512]{1,0:T(8,128)(2,1)S(1)}, bf16[768,512]{1,0:T(8,128)(2,1)}, u32[]{:S(2)}, u32[]{:S(2)}) collective-permute-start(bf16[768,512]{1,0:T(8,128)(2,1)S(1)} %bitcast.94), channel_id=1, source_target_pairs={{0,96},{1,97},{2,98},{3,99},{36,100},{37,101},{38,102},{39,103},{7... | collective-permute-start | bytes 2359304 | tf_op jit(solution)/shard_map/ppermute | solution.py:81
  60.7 24.1 %collective-permute-start.16 = (bf16[768,512]{1,0:T(8,128)(2,1)S(1)}, bf16[768,512]{1,0:T(8,128)(2,1)}, u32[]{:S(2)}, u32[]{:S(2)}) collective-permute-start(bf16[768,512]{1,0:T(8,128)(2,1)S(1)} %bitcast.95), channel_id=1, source_target_pairs={{0,224},{1,225},{2,226},{3,227},{36,228},{37,229},{38,230},{39,231... | collective-permute-start | bytes 2359304 | tf_op jit(solution)/shard_map/ppermute | solution.py:81
  62.2 22.5 %collective-permute-start.17 = (bf16[768,512]{1,0:T(8,128)(2,1)S(1)}, bf16[768,512]{1,0:T(8,128)(2,1)}, u32[]{:S(2)}, u32[]{:S(2)}) collective-permute-start(bf16[768,512]{1,0:T(8,128)(2,1)S(1)} %bitcast.96), channel_id=1, source_target_pairs={{0,160},{1,161},{2,162},{3,163},{36,164},{37,165},{38,166},{39,167... | collective-permute-start | bytes 2359304 | tf_op jit(solution)/shard_map/ppermute | solution.py:81
  70.9 12.3 %collective-permute-start.13 = (bf16[4,1,96,512]{3,2,1,0:T(8,128)(2,1)S(1)}, bf16[4,1,96,512]{3,2,1,0:T(8,128)(2,1)S(1)}, u32[]{:S(2)}, u32[]{:S(2)}) collective-permute-start(bf16[4,1,96,512]{3,2,1,0:T(8,128)(2,1)S(1)} %slice.19), channel_id=1, source_target_pairs={{0,3},{1,0},{2,1},{3,2},{4,7},{5,4},{6,5},{7,6},{8,11},{9,8},{10,9... | collective-permute-start | bytes 1179656 | tf_op jit(solution)/shard_map/ppermute | solution.py:17
  74.6 9.3 %collective-permute-start.12 = (bf16[4,1,96,512]{3,2,1,0:T(8,128)(2,1)S(1)}, bf16[4,1,96,512]{3,2,1,0:T(8,128)(2,1)S(1)}, u32[]{:S(2)}, u32[]{:S(2)}) collective-permute-start(bf16[4,1,96,512]{3,2,1,0:T(8,128)(2,1)S(1)} %slice.18), channel_id=1, source_target_pairs={{0,1},{1,2},{2,3},{3,0},{4,5},{5,6},{6,7},{7,4},{8,9},{9,10},{10,1... | collective-permute-start | bytes 1179656 | tf_op jit(solution)/shard_map/ppermute | solution.py:17
  83.2 6.1 %collective-permute-start.18 = (bf16[768,512]{1,0:T(8,128)(2,1)S(1)}, bf16[768,512]{1,0:T(8,128)(2,1)S(1)}, u32[]{:S(2)}, u32[]{:S(2)}) collective-permute-start(bf16[768,512]{1,0:T(8,128)(2,1)S(1)} %get-tuple-element.33), channel_id=1, source_target_pairs={{0,64},{1,65},{2,66},{3,67},{36,68},{37,69},{38,70},{39,71},{72,13... | collective-permute-start | bytes 2359304 | tf_op jit(solution)/shard_map/ppermute | solution.py:81
  84.0 5.4 %collective-permute-start.19 = (bf16[768,512]{1,0:T(8,128)(2,1)S(1)}, bf16[768,512]{1,0:T(8,128)(2,1)S(1)}, u32[]{:S(2)}, u32[]{:S(2)}) collective-permute-start(bf16[768,512]{1,0:T(8,128)(2,1)S(1)} %get-tuple-element.33), channel_id=1, source_target_pairs={{0,192},{1,193},{2,194},{3,195},{36,196},{37,197},{38,198},{39,199... | collective-permute-start | bytes 2359304 | tf_op jit(solution)/shard_map/ppermute | solution.py:81
  91.4 13.7 %collective-permute-start.20 = (bf16[512,768]{1,0:T(8,128)(2,1)}, bf16[512,768]{1,0:T(8,128)(2,1)}, u32[]{:S(2)}, u32[]{:S(2)}) collective-permute-start(bf16[512,768]{1,0:T(8,128)(2,1)} %broadcast_select_fusion.1), channel_id=1, source_target_pairs={{0,32},{32,0},{1,33},{33,1},{2,34},{34,2},{3,35},{35,3},{4,36},{36... | collective-permute-start | bytes 2359304 | tf_op jit(solution)/shard_map/ppermute | solution.py:90
  102.9 18.6 %collective-permute-start.25 = (bf16[768,512]{1,0:T(8,128)(2,1)}, bf16[768,512]{1,0:T(8,128)(2,1)S(1)}, u32[]{:S(2)}, u32[]{:S(2)}) collective-permute-start(bf16[768,512]{1,0:T(8,128)(2,1)} %copy-done.4), channel_id=1, source_target_pairs={{0,128},{1,129},{2,130},{3,131},{36,132},{37,133},{38,134},{39,135... | collective-permute-start | bytes 2359304 | tf_op jit(solution)/shard_map/ppermute | solution.py:81
  103.7 17.8 %collective-permute-start.26 = (bf16[768,512]{1,0:T(8,128)(2,1)}, bf16[768,512]{1,0:T(8,128)(2,1)S(1)}, u32[]{:S(2)}, u32[]{:S(2)}) collective-permute-start(bf16[768,512]{1,0:T(8,128)(2,1)} %get-tuple-element.32), channel_id=1, source_target_pairs={{0,32},{1,33},{2,34},{3,35},{36,4},{37,5},{38,6},{39,7},{72,104},{... | collective-permute-start | bytes 2359304 | tf_op jit(solution)/shard_map/ppermute | solution.py:81
  106.6 7.3 %collective-permute-start.23 = (bf16[128,768]{1,0:T(8,128)(2,1)S(1)}, bf16[128,768]{1,0:T(8,128)(2,1)S(1)}, u32[]{:S(2)}, u32[]{:S(2)}) collective-permute-start(bf16[128,768]{1,0:T(8,128)(2,1)S(1)} %get-tuple-element.35), channel_id=1, source_target_pairs={{0,192},{64,0},{128,64},{192,128},{1,193},{65,1},{129,65},{193,129... | collective-permute-start | bytes 589832 | tf_op jit(solution)/shard_map/ppermute | solution.py:17
  110.1 11.2 %collective-permute-start.22 = (bf16[128,768]{1,0:T(8,128)(2,1)S(1)}, bf16[128,768]{1,0:T(8,128)(2,1)S(1)}, u32[]{:S(2)}, u32[]{:S(2)}) collective-permute-start(bf16[128,768]{1,0:T(8,128)(2,1)S(1)} %get-tuple-element.36), channel_id=1, source_target_pairs={{0,64},{64,128},{128,192},{192,0},{1,65},{65,129},{129,193},{193,1... | collective-permute-start | bytes 589832 | tf_op jit(solution)/shard_map/ppermute | solution.py:17
  110.1 11.2 %collective-permute-start.21 = (bf16[128,768]{1,0:T(8,128)(2,1)S(1)}, bf16[128,768]{1,0:T(8,128)(2,1)S(1)}, u32[]{:S(2)}, u32[]{:S(2)}) collective-permute-start(bf16[128,768]{1,0:T(8,128)(2,1)S(1)} %get-tuple-element.34), channel_id=1, source_target_pairs={{0,128},{64,192},{128,0},{192,64},{1,129},{65,193},{129,1},{193,65... | collective-permute-start | bytes 589832 | tf_op jit(solution)/shard_map/ppermute | solution.py:17
  125.3 4.3 %collective-permute-start.28 = (bf16[32,512]{1,0:T(8,128)(2,1)S(1)}, bf16[32,512]{1,0:T(8,128)(2,1)S(1)}, u32[]{:S(2)}, u32[]{:S(2)}) collective-permute-start(bf16[32,512]{1,0:T(8,128)(2,1)S(1)} %get-tuple-element.47), channel_id=1, source_target_pairs={{0,2},{1,3},{2,0},{3,1},{4,6},{5,7},{6,4},{7,5},{8,10},{9,11},{10,... | collective-permute-start | bytes 98312 | tf_op jit(solution)/shard_map/ppermute | solution.py:105
  125.3 4.3 %collective-permute-start.27 = (bf16[32,512]{1,0:T(8,128)(2,1)S(1)}, bf16[32,512]{1,0:T(8,128)(2,1)S(1)}, u32[]{:S(2)}, u32[]{:S(2)}) collective-permute-start(bf16[32,512]{1,0:T(8,128)(2,1)S(1)} %get-tuple-element.45), channel_id=1, source_target_pairs={{0,1},{1,0},{2,3},{3,2},{4,5},{5,4},{6,7},{7,6},{8,9},{9,8},{10,11... | collective-permute-start | bytes 98312 | tf_op jit(solution)/shard_map/ppermute | solution.py:105
  130.3 17.2 %all-to-all-start = ((bf16[8,32,512]{2,1,0:T(8,128)(2,1)}), bf16[8,32,512]{2,1,0:T(8,128)(2,1)S(1)}, u32[]{:S(2)}, u32[]{:S(2)}) async-start(bf16[8,32,512]{2,1,0:T(8,128)(2,1)} %broadcast_in_dim.73), calls=%async_computation | async-start | bytes 524288 | tf_op jit(solution)/shard_map/all_to_all | solution.py:117
  138.1 5.8 %collective-permute-start.24 = (bf16[64,768]{1,0:T(8,128)(2,1)S(1)}, bf16[64,768]{1,0:T(8,128)(2,1)S(1)}, u32[]{:S(2)}, u32[]{:S(2)}) collective-permute-start(bf16[64,768]{1,0:T(8,128)(2,1)S(1)} %dynamic-slice_bitcast_fusion.3), channel_id=1, source_target_pairs={{0,32},{32,0},{1,33},{33,1},{2,34},{34,2},{3,35},{35,3},{4,36},{36... | collective-permute-start | bytes 294920 | tf_op jit(solution)/shard_map/ppermute | solution.py:131
  147.6 4.7 %collective-permute-start.31 = (bf16[32,512]{1,0:T(8,128)(2,1)S(1)}, bf16[32,512]{1,0:T(8,128)(2,1)S(1)}, u32[]{:S(2)}, u32[]{:S(2)}) collective-permute-start(bf16[32,512]{1,0:T(8,128)(2,1)S(1)} %reduce_sum.12), channel_id=1, source_target_pairs={{0,2},{1,3},{2,0},{3,1},{4,6},{5,7},{6,4},{7,5},{8,10},{9,11},{10,... | collective-permute-start | bytes 98312 | tf_op jit(solution)/shard_map/ppermute | solution.py:105
  153.4 8.5 %collective-permute-start.33 = (bf16[64,512]{1,0:T(8,128)(2,1)S(1)}, bf16[64,512]{1,0:T(8,128)(2,1)S(1)}, u32[]{:S(2)}, u32[]{:S(2)}) collective-permute-start(bf16[64,512]{1,0:T(8,128)(2,1)S(1)} %dynamic-slice_bitcast_fusion.4), channel_id=1, source_target_pairs={{0,32},{32,0},{1,33},{33,1},{2,34},{34,2},{3,35},{35,3},{4,36},{36... | collective-permute-start | bytes 196616 | tf_op jit(solution)/shard_map/ppermute | solution.py:131
  (18 other events, 180.5 us)
Sparse Core Ops, SparseCore 0:
  19.4 51.3 all-gather.1

commit v9 on v8

--- a/solution.py
+++ b/solution.py
@@ -81,8 +81,10 @@
     return lax.ppermute(array, ALL, pairs)
 
 
-def along_x(slab, core, shifts):
-    return [from_root(slab, lambda x, c, z, y: ((x + by) % XS, core, z, y)) for by in shifts]
+def to_ring(tiles, core):
+    return [
+        from_root(tiles[by], lambda x, c, z, y: ((x + by) % XS, core, z, y)) for by in (1, 2, 3)
+    ]
 
 
 def pair_sum(partial):
@@ -149,7 +151,7 @@
     rows = inverse_block.shape[0]
 
     def partial_of(panel):
-        return jnp.einsum("qj,pq->jp", panel, inverse_block, preferred_element_type=F32).astype(BF16)
+        return jnp.dot(inverse_block, panel, preferred_element_type=F32).astype(BF16)
 
     first = core == 0
     near = near_z_then_y(normed[1])
@@ -161,33 +163,42 @@
     )
     slab_parts = [of_slab(near[0], y), of_slab(near[1], y), far_part, of_slab(near[2], y)]
     slab_1 = placed_by_owner(slab_parts, y, 1).reshape(rows, width)
-    sent_1 = along_x(slab_1, 1, (1, -1, -2))
-
+    x = lax.axis_index("x")
+    share = rows // XS
+    chip = lambda by: (z // CORES + by) % XS
+    tiles_1 = [lax.dynamic_slice_in_dim(slab_1, chip(by) * share, share, 0) for by in range(XS)]
     panel_0 = panel_y_then_z(normed[0])
-    panel_0, near = lax.optimization_barrier((panel_0, near))
+    panel_0, near, tiles_1 = lax.optimization_barrier((panel_0, near, tiles_1))
     chunks = [near[0], near[1], far_chunk(near), near[2]]
-    slab_0 = lax.dynamic_slice_in_dim(panel_0, y * rows, rows, 0)
-    sent_0 = along_x(slab_0, 0, (1, -1, 2))
+    tiles_0 = [
+        lax.dynamic_slice_in_dim(panel_0, y * rows + chip(by) * share, share, 0) for by in range(XS)
+    ]
+    sent_1, sent_0 = to_ring(tiles_1, 1), to_ring(tiles_0, 0)
+    across = from_root(
+        jnp.where(first, tiles_1[0], tiles_0[0]), lambda x, c, z, y: (x, 1 - c, z, y)
+    )
     partial = [partial_of(panel_0)]
 
     chunks, partial[0], sent_1 = lax.optimization_barrier((chunks, partial[0], sent_1))
-    across = from_root(
-        jnp.where(first, slab_1, slab_0), lambda x, c, z, y: (x, 1 - c, z, y)
-    )
     partial.append(partial_of(placed_by_owner(chunks, y, 1).reshape(panel_0.shape)))
 
-    partial[1], sent_0[:2] = lax.optimization_barrier((partial[1], sent_0[:2]))
-    pair = lax.optimization_barrier(pair_sum(partial))
     sent = [*sent_1, *sent_0, across]
-    home = row == z
-    slab = jnp.where(first, slab_0, slab_1)
-    factor_slab = sum(sent, jnp.where(home, slab, jnp.zeros((), BF16)))
+    pair, sent = lax.optimization_barrier((pair_sum(partial), sent))
     product = sum_over_x(pair)
-    col_keep = lax.dynamic_index_in_dim(keep_of(col * rows, rows), core, 0)
-    offdiag = lax.optimization_barrier((-(product * col_keep)).astype(BF16))
-
-    term = -jnp.dot(offdiag, factor_slab, preferred_element_type=F32)
+    own_tile = jnp.where(first, tiles_0[0], tiles_1[0])
+    factor_tile = sum(sent, jnp.where(row == z, own_tile, jnp.zeros((), BF16)))
+    tile_keep = lax.dynamic_index_in_dim(keep_of(col * rows + x * share, share), core, 0)
+    offdiag_tile = lax.optimization_barrier((-(product * tile_keep.T)).astype(BF16))
+
+    term = -jnp.einsum("pk,pj->kj", offdiag_tile, factor_tile, preferred_element_type=F32)
+    term = sum_over_x(lax.optimization_barrier(term.astype(BF16)))
     correction = own_slab_of_both(summed_over_col(term.astype(BF16)))
+
+    sent_to = lambda by: lax.dynamic_slice_in_dim(
+        offdiag_tile, (x + by) % XS * (width // XS), width // XS, 1
+    )
+    got = [sent_to(0)] + [shift(sent_to(by), "x", XS, by) for by in range(1, XS)]
+    offdiag = placed_by_owner(got, x, 0).T
     return (
         own_slab_of_both(offdiag).transpose(0, 2, 1),
         diag_inv + correction.astype(F32).transpose(0, 2, 1),

time: 170 us -> 172 us (1.012)
  starting transfers between devices: 76.1 us -> 70 us
  local copies, waits for them, and re-layouts: 8.84 us -> 14.6 us
  waiting for transfers between devices: 50.1 us -> 53.4 us
  other arithmetic: 7.55 us -> 5.5 us
    ppermute x1, starting transfers between devices: 11.5 us -> 2.7 us  [pair_sum(): lax.ppermute(jnp.where(first, partial[1], partial[0]), 'core', [(0, 1), (...]
    all_to_all x1, starting transfers between devices: 7.74 us -> 12.6 us  [summed_over_col(): part = lax.all_to_all(copies, 'z', split_axis=0, concat_axis=0, tiled=True)]
    all_gather x1, waiting for transfers between devices: 7.09 us -> 10.9 us  [panel_y_then_z(): return lax.all_gather(part, 'z', axis=0, tiled=True)]
    ppermute x17 -> x23, starting transfers between devices: 27.5 us -> 30.9 us  [shift(): lax.ppermute(array, axis, [(i, (i + by) % size) for i in range(size)])]
    ppermute x2, starting transfers between devices: 12.5 us -> 9.56 us  [own_slab_of_both(): got = lax.ppermute(given, 'core', [(0, 1), (1, 0)])]
    ppermute x6, waiting for transfers between devices: 4.27 us -> 1.39 us  [exchanged(): return lax.ppermute(array, axis, [(i, i ^ by) for i in range(size)])]
    ppermute x17 -> x23, waiting for transfers between devices: 33.8 us -> 36.7 us  [shift(): lax.ppermute(array, axis, [(i, (i + by) % size) for i in range(size)])]
    dynamic_update_slice x19 -> x23, local copies, waits for them, and re-layouts: 3.51 us -> 6.27 us  [placed_by_owner(): lax.dynamic_update_slice_in_dim(whole, chunk, (own - d) % size * width, a...]
  transfers between devices with their start and end apart: 36 -> 42, of which waited for: 17 -> 18; matrix products, arithmetic and copies ran while one was open for 11% -> 11% of each run, Pallas kernels for 0% -> 0%
where the time goes in v9:
time: 172 us; the launch traced here: 171 us
  starting transfers between devices  70 us (41%)
  waiting for transfers between devices  53.4 us (31%)
  between operations  15 us (9%)
  local copies, waits for them, and re-layouts  14.6 us (8%)
  matrix products  12.6 us (7%)
  other arithmetic  5.5 us (3%)
    ppermute x23, waiting for transfers between devices, shift(): lax.ppermute(array, axis, [(i, (i + by) % size) for i in range(size)])  36.7 us
    ppermute x23, starting transfers between devices, shift(): lax.ppermute(array, axis, [(i, (i + by) % size) for i in range(size)])  30.9 us
    all_to_all x1, starting transfers between devices, summed_over_col(): part = lax.all_to_all(copies, 'z', split_axis=0, concat_axis=0, tiled=True)  12.6 us
    all_gather x1, waiting for transfers between devices, panel_y_then_z(): return lax.all_gather(part, 'z', axis=0, tiled=True)  10.9 us
    ppermute x2, starting transfers between devices, own_slab_of_both(): got = lax.ppermute(given, 'core', [(0, 1), (1, 0)])  9.56 us
    dot_general x2, matrix products, partial_of(): jnp.dot(inverse_block, panel, preferred_element_type=F32).astype(BF16)  9.49 us
    ppermute x6, starting transfers between devices, exchanged(): return lax.ppermute(array, axis, [(i, i ^ by) for i in range(size)])  7.28 us
    ppermute x8, starting transfers between devices, from_root(): return lax.ppermute(array, ALL, pairs)  6.98 us
  transfers between devices with their start and end apart: 42, of which 18 were waited for; matrix products, arithmetic and copies ran while one was open for 11% of the time, Pallas kernels for 0%

profile of v9, /device:TPU:1, one launch (start us, length us, event | category | flops | bytes accessed | tf_op | source)
XLA Modules:
  0.0 171.1 jit_solution(8261972689355625268)
XLA Ops:
  9.7 2.2 %collective-permute-start = (bf16[96,512]{1,0:T(8,128)(2,1)S(1)}, bf16[96,512]{1,0:T(8,128)(2,1)S(1)}, u32[]{:S(2)}, u32[]{:S(2)}) collective-permute-start(bf16[96,512]{1,0:T(8,128)(2,1)S(1)} %get-tuple-element.75), channel_id=1, source_target_pairs={{0,1},{1,2},{2,3},{3,0},{4,5},{5,6},{6,7},{7,4},{8,9},{9,10},{10,1... | collective-permute-start | bytes 294920 | tf_op jit(solution)/shard_map/ppermute | solution.py:17
  11.9 2.6 %collective-permute-start.1 = (bf16[96,512]{1,0:T(8,128)(2,1)S(1)}, bf16[96,512]{1,0:T(8,128)(2,1)S(1)}, u32[]{:S(2)}, u32[]{:S(2)}) collective-permute-start(bf16[96,512]{1,0:T(8,128)(2,1)S(1)} %get-tuple-element.75), channel_id=1, source_target_pairs={{0,2},{1,3},{2,0},{3,1},{4,6},{5,7},{6,4},{7,5},{8,10},{9,11},{10,... | collective-permute-start | bytes 294920 | tf_op jit(solution)/shard_map/ppermute | solution.py:17
  15.7 2.8 %collective-permute-done.1 = bf16[96,512]{1,0:T(8,128)(2,1)S(1)} collective-permute-done((bf16[96,512]{1,0:T(8,128)(2,1)S(1)}, bf16[96,512]{1,0:T(8,128)(2,1)S(1)}, u32[]{:S(2)}, u32[]{:S(2)}) %collective-permute-start.1) | collective-permute-done | bytes 98336 | tf_op jit(solution)/shard_map/ppermute | solution.py:17
  19.3 1.7 %collective-permute-start.3 = (bf16[1,96,512]{2,1,0:T(8,128)(2,1)S(1)}, bf16[1,96,512]{2,1,0:T(8,128)(2,1)S(1)}, u32[]{:S(2)}, u32[]{:S(2)}) collective-permute-start(bf16[1,96,512]{2,1,0:T(8,128)(2,1)S(1)} %get-tuple-element.74), channel_id=1, source_target_pairs={{0,4},{4,8},{8,12},{12,16},{16,20},{20,24},{24,28},{28,0},{1,5},{5... | collective-permute-start | bytes 294920 | tf_op jit(solution)/shard_map/ppermute | solution.py:17
  21.0 4.0 %collective-permute-start.7 = (bf16[1,96,512]{2,1,0:T(8,128)(2,1)S(1)}, bf16[1,96,512]{2,1,0:T(8,128)(2,1)S(1)}, u32[]{:S(2)}, u32[]{:S(2)}) collective-permute-start(bf16[1,96,512]{2,1,0:T(8,128)(2,1)S(1)} %get-tuple-element.74), channel_id=1, source_target_pairs={{0,28},{4,0},{8,4},{12,8},{16,12},{20,16},{24,20},{28,24},{1,29},{... | collective-permute-start | bytes 294920 | tf_op jit(solution)/shard_map/ppermute | solution.py:17
  25.3 1.7 collective-permute-done.3
  27.0 2.8 %collective-permute-start.8 = (bf16[1,96,512]{2,1,0:T(8,128)(2,1)S(1)}, bf16[1,96,512]{2,1,0:T(8,128)(2,1)S(1)}, u32[]{:S(2)}, u32[]{:S(2)}) collective-permute-start(bf16[1,96,512]{2,1,0:T(8,128)(2,1)S(1)} %collective-permute-done.7), channel_id=1, source_target_pairs={{0,28},{4,0},{8,4},{12,8},{16,12},{20,16},{24,20},{28,24},{1,29},{... | collective-permute-start | bytes 294920 | tf_op jit(solution)/shard_map/ppermute | solution.py:17
  29.8 1.9 %collective-permute-done.4 = bf16[1,96,512]{2,1,0:T(8,128)(2,1)S(1)} collective-permute-done((bf16[1,96,512]{2,1,0:T(8,128)(2,1)S(1)}, bf16[1,96,512]{2,1,0:T(8,128)(2,1)S(1)}, u32[]{:S(2)}, u32[]{:S(2)}) %collective-permute-start.4) | collective-permute-done | bytes 98336 | tf_op jit(solution)/shard_map/ppermute | solution.py:17
  31.7 2.8 %collective-permute-start.9 = (bf16[1,96,512]{2,1,0:T(8,128)(2,1)S(1)}, bf16[1,96,512]{2,1,0:T(8,128)(2,1)S(1)}, u32[]{:S(2)}, u32[]{:S(2)}) collective-permute-start(bf16[1,96,512]{2,1,0:T(8,128)(2,1)S(1)} %collective-permute-done.8), channel_id=1, source_target_pairs={{0,28},{4,0},{8,4},{12,8},{16,12},{20,16},{24,20},{28,24},{1,29},{... | collective-permute-start | bytes 294920 | tf_op jit(solution)/shard_map/ppermute | solution.py:17
  34.4 1.9 %collective-permute-done.5 = bf16[1,96,512]{2,1,0:T(8,128)(2,1)S(1)} collective-permute-done((bf16[1,96,512]{2,1,0:T(8,128)(2,1)S(1)}, bf16[1,96,512]{2,1,0:T(8,128)(2,1)S(1)}, u32[]{:S(2)}, u32[]{:S(2)}) %collective-permute-start.5) | collective-permute-done | bytes 98336 | tf_op jit(solution)/shard_map/ppermute | solution.py:17
  36.4 8.0 %collective-permute-done.6 = bf16[1,96,512]{2,1,0:T(8,128)(2,1)S(1)} collective-permute-done((bf16[1,96,512]{2,1,0:T(8,128)(2,1)S(1)}, bf16[1,96,512]{2,1,0:T(8,128)(2,1)S(1)}, u32[]{:S(2)}, u32[]{:S(2)}) %collective-permute-start.6) | collective-permute-done | bytes 98336 | tf_op jit(solution)/shard_map/ppermute | solution.py:17
  45.2 2.1 %collective-permute-start.11 = (bf16[8,1,96,512]{3,2,1,0:T(8,128)(2,1)S(1)}, bf16[8,1,96,512]{3,2,1,0:T(8,128)(2,1)S(1)}, u32[]{:S(2)}, u32[]{:S(2)}) collective-permute-start(bf16[8,1,96,512]{3,2,1,0:T(8,128)(2,1)S(1)} %bitcast_dynamic-update-slice_fusion), channel_id=1, source_target_pairs={{0,3},{1,0},{2,1},{3,2},{4,7},{5,4},{6,5},{7,6},{8,11},{9,8},{10,9... | collective-permute-start | bytes 2359304 | tf_op jit(solution)/shard_map/ppermute | solution.py:17
  49.4 7.8 %collective-permute-done.10 = bf16[8,1,96,512]{3,2,1,0:T(8,128)(2,1)} collective-permute-done((bf16[8,1,96,512]{3,2,1,0:T(8,128)(2,1)S(1)}, bf16[8,1,96,512]{3,2,1,0:T(8,128)(2,1)}, u32[]{:S(2)}, u32[]{:S(2)}) %collective-permute-start.10) | collective-permute-done | bytes 786464 | tf_op jit(solution)/shard_map/ppermute | solution.py:17
  60.0 10.9 %all-gather.2.cloned.1.call-done = bf16[3072,512]{1,0:T(8,128)(2,1)} async-done(((bf16[384,512]{1,0:T(8,128)(2,1)}), bf16[3072,512]{1,0:T(8,128)(2,1)}) %all-gather.2.cloned.1.call-update) | async-done | bytes 3145744 | tf_op jit(solution)/shard_map/all_gather | solution.py:53
  70.9 2.5 %collective-permute-start.14 = (bf16[4,1,96,512]{3,2,1,0:T(8,128)(2,1)S(1)}, bf16[4,1,96,512]{3,2,1,0:T(8,128)(2,1)S(1)}, u32[]{:S(2)}, u32[]{:S(2)}) collective-permute-start(bf16[4,1,96,512]{3,2,1,0:T(8,128)(2,1)S(1)} %slice.19), channel_id=1, source_target_pairs={{0,3},{1,0},{2,1},{3,2},{4,7},{5,4},{6,5},{7,6},{8,11},{9,8},{10,9... | collective-permute-start | bytes 1179656 | tf_op jit(solution)/shard_map/ppermute | solution.py:17
  77.1 6.0 %fusion = bf16[768,512]{0,1:T(8,128)(2,1)S(1)} fusion(bf16[3072,512]{1,0:T(8,128)(2,1)} %all-gather.2.cloned.1.call-done, bf16[768,3072]{1,0:T(8,128)(2,1)} %param.8), kind=kOutput, calls=%fused_computation.4 | convolution fusion | flops 2416312320 | bytes 8650752 | tf_op jit(solution)/shard_map/dot_general | solution.py:154
  83.1 2.3 %collective-permute-done.13 = bf16[4,1,96,512]{3,2,1,0:T(8,128)(2,1)S(1)} collective-permute-done((bf16[4,1,96,512]{3,2,1,0:T(8,128)(2,1)S(1)}, bf16[4,1,96,512]{3,2,1,0:T(8,128)(2,1)S(1)}, u32[]{:S(2)}, u32[]{:S(2)}) %collective-permute-start.13) | collective-permute-done | bytes 393248 | tf_op jit(solution)/shard_map/ppermute | solution.py:17
  87.3 3.5 %broadcast_select_fusion = (bf16[768,512]{0,1:T(8,128)(2,1)}, bf16[768,512]{0,1:T(8,128)(2,1)S(1)}) fusion(bf16[768,512]{0,1:T(8,128)(2,1)S(1)} %fusion, pred[]{:T(512)S(6)} %eq.83, bf16[3072,512]{1,0:T(8,128)(2,1)S(1)} %bitcast.110, bf16[768,3072]{1,0:T(8,128)(2,1)S(1)} %bitcast.123), kind=kOutput, calls=%fused_computation.10 | convolution fusion | flops 2416705536 | bytes 10223617 | tf_op jit(solution)/shard_map/dot_general | solution.py:154
  90.8 2.7 %collective-permute-start.18 = (bf16[768,512]{0,1:T(8,128)(2,1)}, bf16[768,512]{0,1:T(8,128)(2,1)S(1)}, u32[]{:S(2)}, u32[]{:S(2)}) collective-permute-start(bf16[768,512]{0,1:T(8,128)(2,1)} %get-tuple-element.79), channel_id=1, source_target_pairs={{0,32},{32,0},{1,33},{33,1},{2,34},{34,2},{3,35},{35,3},{4,36},{36... | collective-permute-start | bytes 2359304 | tf_op jit(solution)/shard_map/ppermute | solution.py:92
  102.0 1.6 collective-permute-done.22
  106.1 2.3 %collective-permute-done.25 = bf16[192,512]{1,0:T(8,128)(2,1)S(1)} collective-permute-done((bf16[192,512]{1,0:T(8,128)(2,1)S(1)}, bf16[192,512]{1,0:T(8,128)(2,1)S(1)}, u32[]{:S(2)}, u32[]{:S(2)}) %collective-permute-start.25) | collective-permute-done | bytes 196640 | tf_op jit(solution)/shard_map/ppermute | solution.py:17
  108.5 3.6 %collective-permute-done.24 = bf16[192,512]{1,0:T(8,128)(2,1)S(1)} collective-permute-done((bf16[192,512]{1,0:T(8,128)(2,1)S(1)}, bf16[192,512]{1,0:T(8,128)(2,1)S(1)}, u32[]{:S(2)}, u32[]{:S(2)}) %collective-permute-start.24) | collective-permute-done | bytes 196640 | tf_op jit(solution)/shard_map/ppermute | solution.py:17
  112.2 1.9 %fusion.2 = bf16[512,512]{1,0:T(8,128)(2,1)S(1)} fusion(bf16[192,512]{1,0:T(8,128)(2,1)S(1)} %fusion.7, bf16[192,512]{1,0:T(8,128)(2,1)} %collective-permute-done.22, bf16[192,512]{1,0:T(8,128)(2,1)} %copy-done.10, bf16[192,512]{1,0:T(8,128)(2,1)} %copy-done.9, bf16[192,512]{1,0:T(8,128)(2,1)} %copy-done.8, bf16[192,512]{1,0:T(8,128)(2,1)} %copy-done.7, ...), kind=kOutput, calls=%fused_computation.6 | convolution fusion | flops 102957056 | bytes 2490374 | tf_op jit(solution)/shard_map/pk,pj->kj/dot_general | solution.py:193
  115.7 1.6 collective-permute-start.30
  118.1 3.6 %collective-permute-done.31 = bf16[128,512]{1,0:T(8,128)(2,1)S(1)} collective-permute-done((bf16[128,512]{1,0:T(8,128)(2,1)S(1)}, bf16[128,512]{1,0:T(8,128)(2,1)S(1)}, u32[]{:S(2)}, u32[]{:S(2)}) %collective-permute-start.31) | collective-permute-done | bytes 131104 | tf_op jit(solution)/shard_map/ppermute | solution.py:17
  121.7 1.9 %collective-permute-start.35 = (bf16[32,512]{1,0:T(8,128)(2,1)S(1)}, bf16[32,512]{1,0:T(8,128)(2,1)S(1)}, u32[]{:S(2)}, u32[]{:S(2)}) collective-permute-start(bf16[32,512]{1,0:T(8,128)(2,1)S(1)} %get-tuple-element.77), channel_id=1, source_target_pairs={{0,3},{1,2},{2,1},{3,0},{4,7},{5,6},{6,5},{7,4},{8,11},{9,10},{10,... | collective-permute-start | bytes 98312 | tf_op jit(solution)/shard_map/ppermute | solution.py:107
  125.2 2.7 %collective-permute-start.27 = (bf16[192,128]{1,0:T(8,128)(2,1)S(1)}, bf16[192,128]{1,0:T(8,128)(2,1)S(1)}, u32[]{:S(2)}, u32[]{:S(2)}) collective-permute-start(bf16[192,128]{1,0:T(8,128)(2,1)S(1)} %get-tuple-element.71), channel_id=1, source_target_pairs={{0,128},{64,192},{128,0},{192,64},{1,129},{65,193},{129,1},{193,65... | collective-permute-start | bytes 147464 | tf_op jit(solution)/shard_map/ppermute | solution.py:17
  129.0 12.6 %all-to-all-start = ((bf16[8,32,512]{2,1,0:T(8,128)(2,1)}), bf16[8,32,512]{2,1,0:T(8,128)(2,1)S(1)}, u32[]{:S(2)}, u32[]{:S(2)}) async-start(bf16[8,32,512]{2,1,0:T(8,128)(2,1)} %broadcast_in_dim.77), calls=%async_computation | async-start | bytes 524288 | tf_op jit(solution)/shard_map/all_to_all | solution.py:119
  144.9 3.4 %collective-permute-start.29 = (bf16[64,768]{1,0:T(8,128)(2,1)S(1)}, bf16[64,768]{1,0:T(8,128)(2,1)S(1)}, u32[]{:S(2)}, u32[]{:S(2)}) collective-permute-start(bf16[64,768]{1,0:T(8,128)(2,1)S(1)} %dynamic-slice_bitcast_fusion.6), channel_id=1, source_target_pairs={{0,32},{32,0},{1,33},{33,1},{2,34},{34,2},{3,35},{35,3},{4,36},{36... | collective-permute-start | bytes 294920 | tf_op jit(solution)/shard_map/ppermute | solution.py:133
  149.3 1.7 all-to-all-done
  152.4 2.5 %collective-permute-start.38 = (bf16[32,512]{1,0:T(8,128)(2,1)S(1)}, bf16[32,512]{1,0:T(8,128)(2,1)S(1)}, u32[]{:S(2)}, u32[]{:S(2)}) collective-permute-start(bf16[32,512]{1,0:T(8,128)(2,1)S(1)} %reduce_sum.12), channel_id=1, source_target_pairs={{0,3},{1,2},{2,1},{3,0},{4,7},{5,6},{6,5},{7,4},{8,11},{9,10},{10,... | collective-permute-start | bytes 98312 | tf_op jit(solution)/shard_map/ppermute | solution.py:107
  156.4 6.2 %collective-permute-start.39 = (bf16[64,512]{1,0:T(8,128)(2,1)S(1)}, bf16[64,512]{1,0:T(8,128)(2,1)S(1)}, u32[]{:S(2)}, u32[]{:S(2)}) collective-permute-start(bf16[64,512]{1,0:T(8,128)(2,1)S(1)} %dynamic-slice_bitcast_fusion.7), channel_id=1, source_target_pairs={{0,32},{32,0},{1,33},{33,1},{2,34},{34,2},{3,35},{35,3},{4,36},{36... | collective-permute-start | bytes 196616 | tf_op jit(solution)/shard_map/ppermute | solution.py:133
  (151 shorter events, 40.5 us)
Async XLA Ops:
  7.2 63.7 %all-gather.2.cloned.1.call-start = ((), (), s32[]{:S(2)}) async-start(), calls=%async_computation.1 | async-start | bytes 3538944 | tf_op jit(solution)/shard_map/all_gather | solution.py:53
  9.7 6.0 %collective-permute-start = (bf16[96,512]{1,0:T(8,128)(2,1)S(1)}, bf16[96,512]{1,0:T(8,128)(2,1)S(1)}, u32[]{:S(2)}, u32[]{:S(2)}) collective-permute-start(bf16[96,512]{1,0:T(8,128)(2,1)S(1)} %get-tuple-element.75), channel_id=1, source_target_pairs={{0,1},{1,2},{2,3},{3,0},{4,5},{5,6},{6,7},{7,4},{8,9},{9,10},{10,1... | collective-permute-start | bytes 294920 | tf_op jit(solution)/shard_map/ppermute | solution.py:17
  11.9 6.6 %collective-permute-start.1 = (bf16[96,512]{1,0:T(8,128)(2,1)S(1)}, bf16[96,512]{1,0:T(8,128)(2,1)S(1)}, u32[]{:S(2)}, u32[]{:S(2)}) collective-permute-start(bf16[96,512]{1,0:T(8,128)(2,1)S(1)} %get-tuple-element.75), channel_id=1, source_target_pairs={{0,2},{1,3},{2,0},{3,1},{4,6},{5,7},{6,4},{7,5},{8,10},{9,11},{10,... | collective-permute-start | bytes 294920 | tf_op jit(solution)/shard_map/ppermute | solution.py:17
  19.3 7.7 %collective-permute-start.3 = (bf16[1,96,512]{2,1,0:T(8,128)(2,1)S(1)}, bf16[1,96,512]{2,1,0:T(8,128)(2,1)S(1)}, u32[]{:S(2)}, u32[]{:S(2)}) collective-permute-start(bf16[1,96,512]{2,1,0:T(8,128)(2,1)S(1)} %get-tuple-element.74), channel_id=1, source_target_pairs={{0,4},{4,8},{8,12},{12,16},{16,20},{20,24},{24,28},{28,0},{1,5},{5... | collective-permute-start | bytes 294920 | tf_op jit(solution)/shard_map/ppermute | solution.py:17
  21.0 6.0 %collective-permute-start.7 = (bf16[1,96,512]{2,1,0:T(8,128)(2,1)S(1)}, bf16[1,96,512]{2,1,0:T(8,128)(2,1)S(1)}, u32[]{:S(2)}, u32[]{:S(2)}) collective-permute-start(bf16[1,96,512]{2,1,0:T(8,128)(2,1)S(1)} %get-tuple-element.74), channel_id=1, source_target_pairs={{0,28},{4,0},{8,4},{12,8},{16,12},{20,16},{24,20},{28,24},{1,29},{... | collective-permute-start | bytes 294920 | tf_op jit(solution)/shard_map/ppermute | solution.py:17
  27.0 4.7 %collective-permute-start.4 = (bf16[1,96,512]{2,1,0:T(8,128)(2,1)S(1)}, bf16[1,96,512]{2,1,0:T(8,128)(2,1)S(1)}, u32[]{:S(2)}, u32[]{:S(2)}) collective-permute-start(bf16[1,96,512]{2,1,0:T(8,128)(2,1)S(1)} %collective-permute-done.3), channel_id=1, source_target_pairs={{0,4},{4,8},{8,12},{12,16},{16,20},{20,24},{24,28},{28,0},{1,5},{5... | collective-permute-start | bytes 294920 | tf_op jit(solution)/shard_map/ppermute | solution.py:17
  27.0 4.7 %collective-permute-start.8 = (bf16[1,96,512]{2,1,0:T(8,128)(2,1)S(1)}, bf16[1,96,512]{2,1,0:T(8,128)(2,1)S(1)}, u32[]{:S(2)}, u32[]{:S(2)}) collective-permute-start(bf16[1,96,512]{2,1,0:T(8,128)(2,1)S(1)} %collective-permute-done.7), channel_id=1, source_target_pairs={{0,28},{4,0},{8,4},{12,8},{16,12},{20,16},{24,20},{28,24},{1,29},{... | collective-permute-start | bytes 294920 | tf_op jit(solution)/shard_map/ppermute | solution.py:17
  31.7 4.7 %collective-permute-start.5 = (bf16[1,96,512]{2,1,0:T(8,128)(2,1)S(1)}, bf16[1,96,512]{2,1,0:T(8,128)(2,1)S(1)}, u32[]{:S(2)}, u32[]{:S(2)}) collective-permute-start(bf16[1,96,512]{2,1,0:T(8,128)(2,1)S(1)} %collective-permute-done.4), channel_id=1, source_target_pairs={{0,4},{4,8},{8,12},{12,16},{16,20},{20,24},{24,28},{28,0},{1,5},{5... | collective-permute-start | bytes 294920 | tf_op jit(solution)/shard_map/ppermute | solution.py:17
  31.7 12.7 %collective-permute-start.9 = (bf16[1,96,512]{2,1,0:T(8,128)(2,1)S(1)}, bf16[1,96,512]{2,1,0:T(8,128)(2,1)S(1)}, u32[]{:S(2)}, u32[]{:S(2)}) collective-permute-start(bf16[1,96,512]{2,1,0:T(8,128)(2,1)S(1)} %collective-permute-done.8), channel_id=1, source_target_pairs={{0,28},{4,0},{8,4},{12,8},{16,12},{20,16},{24,20},{28,24},{1,29},{... | collective-permute-start | bytes 294920 | tf_op jit(solution)/shard_map/ppermute | solution.py:17
  36.3 8.1 %collective-permute-start.6 = (bf16[1,96,512]{2,1,0:T(8,128)(2,1)S(1)}, bf16[1,96,512]{2,1,0:T(8,128)(2,1)S(1)}, u32[]{:S(2)}, u32[]{:S(2)}) collective-permute-start(bf16[1,96,512]{2,1,0:T(8,128)(2,1)S(1)} %collective-permute-done.5), channel_id=1, source_target_pairs={{0,4},{4,8},{8,12},{12,16},{16,20},{20,24},{24,28},{28,0},{1,5},{5... | collective-permute-start | bytes 294920 | tf_op jit(solution)/shard_map/ppermute | solution.py:17
  44.5 12.6 %collective-permute-start.10 = (bf16[8,1,96,512]{3,2,1,0:T(8,128)(2,1)S(1)}, bf16[8,1,96,512]{3,2,1,0:T(8,128)(2,1)}, u32[]{:S(2)}, u32[]{:S(2)}) collective-permute-start(bf16[8,1,96,512]{3,2,1,0:T(8,128)(2,1)S(1)} %bitcast_dynamic-update-slice_fusion), channel_id=1, source_target_pairs={{0,1},{1,2},{2,3},{3,0},{4,5},{5,6},{6,7},{7,4},{8,9},{9,10},{10,1... | collective-permute-start | bytes 2359304 | tf_op jit(solution)/shard_map/ppermute | solution.py:17
  45.2 13.9 %collective-permute-start.11 = (bf16[8,1,96,512]{3,2,1,0:T(8,128)(2,1)S(1)}, bf16[8,1,96,512]{3,2,1,0:T(8,128)(2,1)S(1)}, u32[]{:S(2)}, u32[]{:S(2)}) collective-permute-start(bf16[8,1,96,512]{3,2,1,0:T(8,128)(2,1)S(1)} %bitcast_dynamic-update-slice_fusion), channel_id=1, source_target_pairs={{0,3},{1,0},{2,1},{3,2},{4,7},{5,4},{6,5},{7,6},{8,11},{9,8},{10,9... | collective-permute-start | bytes 2359304 | tf_op jit(solution)/shard_map/ppermute | solution.py:17
  48.0 10.0 %collective-permute-start.12 = (bf16[2,1,96,512]{3,2,1,0:T(8,128)(2,1)}, bf16[2,1,96,512]{3,2,1,0:T(8,128)(2,1)}, u32[]{:S(2)}, u32[]{:S(2)}) collective-permute-start(bf16[2,1,96,512]{3,2,1,0:T(8,128)(2,1)} %get-tuple-element.61), channel_id=1, source_target_pairs={{0,2},{1,3},{2,0},{3,1},{36,38},{37,39},{38,36},{39,37},{72,74},{7... | collective-permute-start | bytes 589832 | tf_op jit(solution)/shard_map/ppermute | solution.py:81
  70.9 12.1 %collective-permute-start.14 = (bf16[4,1,96,512]{3,2,1,0:T(8,128)(2,1)S(1)}, bf16[4,1,96,512]{3,2,1,0:T(8,128)(2,1)S(1)}, u32[]{:S(2)}, u32[]{:S(2)}) collective-permute-start(bf16[4,1,96,512]{3,2,1,0:T(8,128)(2,1)S(1)} %slice.19), channel_id=1, source_target_pairs={{0,3},{1,0},{2,1},{3,2},{4,7},{5,4},{6,5},{7,6},{8,11},{9,8},{10,9... | collective-permute-start | bytes 1179656 | tf_op jit(solution)/shard_map/ppermute | solution.py:17
  74.6 10.7 %collective-permute-start.13 = (bf16[4,1,96,512]{3,2,1,0:T(8,128)(2,1)S(1)}, bf16[4,1,96,512]{3,2,1,0:T(8,128)(2,1)S(1)}, u32[]{:S(2)}, u32[]{:S(2)}) collective-permute-start(bf16[4,1,96,512]{3,2,1,0:T(8,128)(2,1)S(1)} %slice.18), channel_id=1, source_target_pairs={{0,1},{1,2},{2,3},{3,0},{4,5},{5,6},{6,7},{7,4},{8,9},{9,10},{10,1... | collective-permute-start | bytes 1179656 | tf_op jit(solution)/shard_map/ppermute | solution.py:17
  74.7 10.7 %collective-permute-start.15 = (bf16[192,512]{1,0:T(8,128)(2,1)}, bf16[192,512]{1,0:T(8,128)(2,1)S(1)}, u32[]{:S(2)}, u32[]{:S(2)}) collective-permute-start(bf16[192,512]{1,0:T(8,128)(2,1)} %get-tuple-element.30), channel_id=1, source_target_pairs={{0,96},{1,97},{2,98},{3,99},{36,100},{37,101},{38,102},{39,103},{7... | collective-permute-start | bytes 589832 | tf_op jit(solution)/shard_map/ppermute | solution.py:81
  75.5 9.9 %collective-permute-start.16 = (bf16[192,512]{1,0:T(8,128)(2,1)}, bf16[192,512]{1,0:T(8,128)(2,1)S(1)}, u32[]{:S(2)}, u32[]{:S(2)}) collective-permute-start(bf16[192,512]{1,0:T(8,128)(2,1)} %get-tuple-element.31), channel_id=1, source_target_pairs={{0,160},{1,161},{2,162},{3,163},{36,164},{37,165},{38,166},{39,167... | collective-permute-start | bytes 589832 | tf_op jit(solution)/shard_map/ppermute | solution.py:81
  76.2 9.2 %collective-permute-start.17 = (bf16[192,512]{1,0:T(8,128)(2,1)}, bf16[192,512]{1,0:T(8,128)(2,1)S(1)}, u32[]{:S(2)}, u32[]{:S(2)}) collective-permute-start(bf16[192,512]{1,0:T(8,128)(2,1)} %get-tuple-element.32), channel_id=1, source_target_pairs={{0,224},{1,225},{2,226},{3,227},{36,228},{37,229},{38,230},{39,231... | collective-permute-start | bytes 589832 | tf_op jit(solution)/shard_map/ppermute | solution.py:81
  90.8 7.4 %collective-permute-start.18 = (bf16[768,512]{0,1:T(8,128)(2,1)}, bf16[768,512]{0,1:T(8,128)(2,1)S(1)}, u32[]{:S(2)}, u32[]{:S(2)}) collective-permute-start(bf16[768,512]{0,1:T(8,128)(2,1)} %get-tuple-element.79), channel_id=1, source_target_pairs={{0,32},{32,0},{1,33},{33,1},{2,34},{34,2},{3,35},{35,3},{4,36},{36... | collective-permute-start | bytes 2359304 | tf_op jit(solution)/shard_map/ppermute | solution.py:92
  94.9 5.7 %collective-permute-start.19 = (bf16[192,512]{1,0:T(8,128)(2,1)S(1)}, bf16[192,512]{1,0:T(8,128)(2,1)S(1)}, u32[]{:S(2)}, u32[]{:S(2)}) collective-permute-start(bf16[192,512]{1,0:T(8,128)(2,1)S(1)} %get-tuple-element.53), channel_id=1, source_target_pairs={{0,64},{1,65},{2,66},{3,67},{36,68},{37,69},{38,70},{39,71},{72,13... | collective-permute-start | bytes 589832 | tf_op jit(solution)/shard_map/ppermute | solution.py:81
  95.5 5.0 %collective-permute-start.20 = (bf16[192,512]{1,0:T(8,128)(2,1)S(1)}, bf16[192,512]{1,0:T(8,128)(2,1)S(1)}, u32[]{:S(2)}, u32[]{:S(2)}) collective-permute-start(bf16[192,512]{1,0:T(8,128)(2,1)S(1)} %get-tuple-element.52), channel_id=1, source_target_pairs={{0,128},{1,129},{2,130},{3,131},{36,132},{37,133},{38,134},{39,135... | collective-permute-start | bytes 589832 | tf_op jit(solution)/shard_map/ppermute | solution.py:81
  96.9 6.6 %collective-permute-start.22 = (bf16[192,512]{1,0:T(8,128)(2,1)S(1)}, bf16[192,512]{1,0:T(8,128)(2,1)}, u32[]{:S(2)}, u32[]{:S(2)}) collective-permute-start(bf16[192,512]{1,0:T(8,128)(2,1)S(1)} %get-tuple-element.50), channel_id=1, source_target_pairs={{0,32},{1,33},{2,34},{3,35},{36,4},{37,5},{38,6},{39,7},{72,104},{... | collective-permute-start | bytes 589832 | tf_op jit(solution)/shard_map/ppermute | solution.py:81
  104.2 7.8 %collective-permute-start.24 = (bf16[192,512]{1,0:T(8,128)(2,1)S(1)}, bf16[192,512]{1,0:T(8,128)(2,1)S(1)}, u32[]{:S(2)}, u32[]{:S(2)}) collective-permute-start(bf16[192,512]{1,0:T(8,128)(2,1)S(1)} %get-tuple-element.56), channel_id=1, source_target_pairs={{0,64},{64,128},{128,192},{192,0},{1,65},{65,129},{129,193},{193,1... | collective-permute-start | bytes 589832 | tf_op jit(solution)/shard_map/ppermute | solution.py:17
  105.4 6.7 %collective-permute-start.23 = (bf16[192,512]{1,0:T(8,128)(2,1)S(1)}, bf16[192,512]{1,0:T(8,128)(2,1)S(1)}, u32[]{:S(2)}, u32[]{:S(2)}) collective-permute-start(bf16[192,512]{1,0:T(8,128)(2,1)S(1)} %get-tuple-element.54), channel_id=1, source_target_pairs={{0,128},{64,192},{128,0},{192,64},{1,129},{65,193},{129,1},{193,65... | collective-permute-start | bytes 589832 | tf_op jit(solution)/shard_map/ppermute | solution.py:17
  115.2 6.4 %collective-permute-start.31 = (bf16[128,512]{1,0:T(8,128)(2,1)S(1)}, bf16[128,512]{1,0:T(8,128)(2,1)S(1)}, u32[]{:S(2)}, u32[]{:S(2)}) collective-permute-start(bf16[128,512]{1,0:T(8,128)(2,1)S(1)} %get-tuple-element.65), channel_id=1, source_target_pairs={{0,64},{64,128},{128,192},{192,0},{1,65},{65,129},{129,193},{193,1... | collective-permute-start | bytes 393224 | tf_op jit(solution)/shard_map/ppermute | solution.py:17
  115.7 5.9 %collective-permute-start.30 = (bf16[128,512]{1,0:T(8,128)(2,1)S(1)}, bf16[128,512]{1,0:T(8,128)(2,1)S(1)}, u32[]{:S(2)}, u32[]{:S(2)}) collective-permute-start(bf16[128,512]{1,0:T(8,128)(2,1)S(1)} %get-tuple-element.63), channel_id=1, source_target_pairs={{0,128},{64,192},{128,0},{192,64},{1,129},{65,193},{129,1},{193,65... | collective-permute-start | bytes 393224 | tf_op jit(solution)/shard_map/ppermute | solution.py:17
  121.7 6.2 %collective-permute-start.35 = (bf16[32,512]{1,0:T(8,128)(2,1)S(1)}, bf16[32,512]{1,0:T(8,128)(2,1)S(1)}, u32[]{:S(2)}, u32[]{:S(2)}) collective-permute-start(bf16[32,512]{1,0:T(8,128)(2,1)S(1)} %get-tuple-element.77), channel_id=1, source_target_pairs={{0,3},{1,2},{2,1},{3,0},{4,7},{5,6},{6,5},{7,4},{8,11},{9,10},{10,... | collective-permute-start | bytes 98312 | tf_op jit(solution)/shard_map/ppermute | solution.py:107
  125.1 17.3 %collective-permute-start.26 = (bf16[192,128]{1,0:T(8,128)(2,1)S(1)}, bf16[192,128]{1,0:T(8,128)(2,1)S(1)}, u32[]{:S(2)}, u32[]{:S(2)}) collective-permute-start(bf16[192,128]{1,0:T(8,128)(2,1)S(1)} %get-tuple-element.72), channel_id=1, source_target_pairs={{0,64},{64,128},{128,192},{192,0},{1,65},{65,129},{129,193},{193,1... | collective-permute-start | bytes 147464 | tf_op jit(solution)/shard_map/ppermute | solution.py:17
  125.2 18.0 %collective-permute-start.27 = (bf16[192,128]{1,0:T(8,128)(2,1)S(1)}, bf16[192,128]{1,0:T(8,128)(2,1)S(1)}, u32[]{:S(2)}, u32[]{:S(2)}) collective-permute-start(bf16[192,128]{1,0:T(8,128)(2,1)S(1)} %get-tuple-element.71), channel_id=1, source_target_pairs={{0,128},{64,192},{128,0},{192,64},{1,129},{65,193},{129,1},{193,65... | collective-permute-start | bytes 147464 | tf_op jit(solution)/shard_map/ppermute | solution.py:17
  127.9 15.9 %collective-permute-start.28 = (bf16[192,128]{1,0:T(8,128)(2,1)S(1)}, bf16[192,128]{1,0:T(8,128)(2,1)S(1)}, u32[]{:S(2)}, u32[]{:S(2)}) collective-permute-start(bf16[192,128]{1,0:T(8,128)(2,1)S(1)} %get-tuple-element.70), channel_id=1, source_target_pairs={{0,192},{64,0},{128,64},{192,128},{1,193},{65,1},{129,65},{193,129... | collective-permute-start | bytes 147464 | tf_op jit(solution)/shard_map/ppermute | solution.py:17
  129.0 22.0 %all-to-all-start = ((bf16[8,32,512]{2,1,0:T(8,128)(2,1)}), bf16[8,32,512]{2,1,0:T(8,128)(2,1)S(1)}, u32[]{:S(2)}, u32[]{:S(2)}) async-start(bf16[8,32,512]{2,1,0:T(8,128)(2,1)} %broadcast_in_dim.77), calls=%async_computation | async-start | bytes 524288 | tf_op jit(solution)/shard_map/all_to_all | solution.py:119
  156.4 7.1 %collective-permute-start.39 = (bf16[64,512]{1,0:T(8,128)(2,1)S(1)}, bf16[64,512]{1,0:T(8,128)(2,1)S(1)}, u32[]{:S(2)}, u32[]{:S(2)}) collective-permute-start(bf16[64,512]{1,0:T(8,128)(2,1)S(1)} %dynamic-slice_bitcast_fusion.7), channel_id=1, source_target_pairs={{0,32},{32,0},{1,33},{33,1},{2,34},{34,2},{3,35},{35,3},{4,36},{36... | collective-permute-start | bytes 196616 | tf_op jit(solution)/shard_map/ppermute | solution.py:133
  (23 other events, 146.8 us)
Sparse Core Ops, SparseCore 0:
  19.4 51.3 all-gather.1

commit v10 on v9

--- a/solution.py
+++ b/solution.py
@@ -38,13 +38,13 @@
     return got
 
 
-def placed_by_owner(got, own, axis):
+def placed_by_owner(got, own, axis, order=None):
     size, width = len(got), got[0].shape[axis]
     dims = list(got[0].shape)
     dims[axis] *= size
     whole = jnp.zeros(dims, got[0].dtype)
-    for d, chunk in enumerate(got):
-        whole = lax.dynamic_update_slice_in_dim(whole, chunk, (own - d) % size * width, axis)
+    for d in order or range(size):
+        whole = lax.dynamic_update_slice_in_dim(whole, got[d], (own - d) % size * width, axis)
     return whole
 
 
@@ -168,8 +168,8 @@
     chip = lambda by: (z // CORES + by) % XS
     tiles_1 = [lax.dynamic_slice_in_dim(slab_1, chip(by) * share, share, 0) for by in range(XS)]
     panel_0 = panel_y_then_z(normed[0])
-    panel_0, near, tiles_1 = lax.optimization_barrier((panel_0, near, tiles_1))
-    chunks = [near[0], near[1], far_chunk(near), near[2]]
+    panel_0, tiles_1 = lax.optimization_barrier((panel_0, tiles_1))
+    far = far_chunk(near)
     tiles_0 = [
         lax.dynamic_slice_in_dim(panel_0, y * rows + chip(by) * share, share, 0) for by in range(XS)
     ]
@@ -179,8 +179,9 @@
     )
     partial = [partial_of(panel_0)]
 
-    chunks, partial[0], sent_1 = lax.optimization_barrier((chunks, partial[0], sent_1))
-    partial.append(partial_of(placed_by_owner(chunks, y, 1).reshape(panel_0.shape)))
+    near, partial[0], sent_1 = lax.optimization_barrier((near, partial[0], sent_1))
+    panel_1 = placed_by_owner([near[0], near[1], far, near[2]], y, 1, (0, 1, 3, 2))
+    partial.append(partial_of(panel_1.reshape(panel_0.shape)))
 
     sent = [*sent_1, *sent_0, across]
     pair, sent = lax.optimization_barrier((pair_sum(partial), sent))

time: 172 us -> 177 us (1.029)
  starting transfers between devices: 70 us -> 77.8 us
  waiting for transfers between devices: 53.4 us -> 46 us
  matrix products: 12.6 us -> 15 us
    ppermute x1, starting transfers between devices: 2.7 us -> 7.89 us  [pair_sum(): lax.ppermute(jnp.where(first, partial[1], partial[0]), 'core', [(0, 1), (...]
    all_gather x1, waiting for transfers between devices: 10.9 us -> 6.33 us  [panel_y_then_z(): return lax.all_gather(part, 'z', axis=0, tiled=True)]
    ppermute x2, starting transfers between devices: 9.56 us -> 12.7 us  [own_slab_of_both(): got = lax.ppermute(given, 'core', [(0, 1), (1, 0)])]
    ppermute x6, waiting for transfers between devices: 1.39 us -> 4.3 us  [exchanged(): return lax.ppermute(array, axis, [(i, i ^ by) for i in range(size)])]
    ppermute x23, waiting for transfers between devices: 36.7 us -> 33.9 us  [shift(): lax.ppermute(array, axis, [(i, (i + by) % size) for i in range(size)])]
    dot_general x2, matrix products: 9.49 us -> 11.9 us  [partial_of(): jnp.dot(inverse_block, panel, preferred_element_type=F32).astype(BF16)]
    dynamic_update_slice x23 -> x22, local copies, waits for them, and re-layouts: 6.27 us -> 6.21 us  [placed_by_owner(): lax.dynamic_update_slice_in_dim(whole, got[d], (own - d) % size * width,...]
  transfers between devices with their start and end apart: 42 -> 42, of which waited for: 18 -> 17; matrix products, arithmetic and copies ran while one was open for 11% -> 12% of each run, Pallas kernels for 0% -> 0%
where the time goes in v10:
time: 177 us; the launch traced here: 176 us
  starting transfers between devices  77.8 us (44%)
  waiting for transfers between devices  46 us (26%)
  local copies, waits for them, and re-layouts  15.9 us (9%)
  matrix products  15 us (8%)
  between operations  15 us (8%)
  other arithmetic  6.6 us (4%)
    ppermute x23, waiting for transfers between devices, shift(): lax.ppermute(array, axis, [(i, (i + by) % size) for i in range(size)])  33.9 us
    ppermute x23, starting transfers between devices, shift(): lax.ppermute(array, axis, [(i, (i + by) % size) for i in range(size)])  30.8 us
    ppermute x2, starting transfers between devices, own_slab_of_both(): got = lax.ppermute(given, 'core', [(0, 1), (1, 0)])  12.7 us
    dot_general x2, matrix products, partial_of(): jnp.dot(inverse_block, panel, preferred_element_type=F32).astype(BF16)  11.9 us
    all_to_all x1, starting transfers between devices, summed_over_col(): part = lax.all_to_all(copies, 'z', split_axis=0, concat_axis=0, tiled=True)  11.8 us
    ppermute x1, starting transfers between devices, pair_sum(): lax.ppermute(jnp.where(first, partial[1], partial[0]), 'core', [(0, 1), (...  7.89 us
    ppermute x6, starting transfers between devices, exchanged(): return lax.ppermute(array, axis, [(i, i ^ by) for i in range(size)])  7.66 us
    ppermute x8, starting transfers between devices, from_root(): return lax.ppermute(array, ALL, pairs)  6.83 us
  transfers between devices with their start and end apart: 42, of which 17 were waited for; matrix products, arithmetic and copies ran while one was open for 12% of the time, Pallas kernels for 0%

profile of v10, /device:TPU:1, one launch (start us, length us, event | category | flops | bytes accessed | tf_op | source)
XLA Modules:
  0.0 176.3 jit_solution(10717751229909150898)
XLA Ops:
  9.7 2.2 %collective-permute-start.9 = (bf16[96,512]{1,0:T(8,128)(2,1)S(1)}, bf16[96,512]{1,0:T(8,128)(2,1)S(1)}, u32[]{:S(2)}, u32[]{:S(2)}) collective-permute-start(bf16[96,512]{1,0:T(8,128)(2,1)S(1)} %get-tuple-element.66), channel_id=1, source_target_pairs={{0,1},{1,2},{2,3},{3,0},{4,5},{5,6},{6,7},{7,4},{8,9},{9,10},{10,1... | collective-permute-start | bytes 294920 | tf_op jit(solution)/shard_map/ppermute | solution.py:17
  11.9 2.6 %collective-permute-start.10 = (bf16[96,512]{1,0:T(8,128)(2,1)S(1)}, bf16[96,512]{1,0:T(8,128)(2,1)S(1)}, u32[]{:S(2)}, u32[]{:S(2)}) collective-permute-start(bf16[96,512]{1,0:T(8,128)(2,1)S(1)} %get-tuple-element.66), channel_id=1, source_target_pairs={{0,2},{1,3},{2,0},{3,1},{4,6},{5,7},{6,4},{7,5},{8,10},{9,11},{10,... | collective-permute-start | bytes 294920 | tf_op jit(solution)/shard_map/ppermute | solution.py:17
  15.7 2.8 %collective-permute-done.10 = bf16[96,512]{1,0:T(8,128)(2,1)S(1)} collective-permute-done((bf16[96,512]{1,0:T(8,128)(2,1)S(1)}, bf16[96,512]{1,0:T(8,128)(2,1)S(1)}, u32[]{:S(2)}, u32[]{:S(2)}) %collective-permute-start.10) | collective-permute-done | bytes 98336 | tf_op jit(solution)/shard_map/ppermute | solution.py:17
  19.3 1.7 collective-permute-start
  21.1 4.0 %collective-permute-start.4 = (bf16[1,96,512]{2,1,0:T(8,128)(2,1)S(1)}, bf16[1,96,512]{2,1,0:T(8,128)(2,1)S(1)}, u32[]{:S(2)}, u32[]{:S(2)}) collective-permute-start(bf16[1,96,512]{2,1,0:T(8,128)(2,1)S(1)} %get-tuple-element.67), channel_id=1, source_target_pairs={{0,28},{4,0},{8,4},{12,8},{16,12},{20,16},{24,20},{28,24},{1,29},{... | collective-permute-start | bytes 294920 | tf_op jit(solution)/shard_map/ppermute | solution.py:17
  25.3 1.7 collective-permute-done
  27.0 2.8 %collective-permute-start.5 = (bf16[1,96,512]{2,1,0:T(8,128)(2,1)S(1)}, bf16[1,96,512]{2,1,0:T(8,128)(2,1)S(1)}, u32[]{:S(2)}, u32[]{:S(2)}) collective-permute-start(bf16[1,96,512]{2,1,0:T(8,128)(2,1)S(1)} %collective-permute-done.4), channel_id=1, source_target_pairs={{0,28},{4,0},{8,4},{12,8},{16,12},{20,16},{24,20},{28,24},{1,29},{... | collective-permute-start | bytes 294920 | tf_op jit(solution)/shard_map/ppermute | solution.py:17
  29.8 1.9 %collective-permute-done.1 = bf16[1,96,512]{2,1,0:T(8,128)(2,1)S(1)} collective-permute-done((bf16[1,96,512]{2,1,0:T(8,128)(2,1)S(1)}, bf16[1,96,512]{2,1,0:T(8,128)(2,1)S(1)}, u32[]{:S(2)}, u32[]{:S(2)}) %collective-permute-start.1) | collective-permute-done | bytes 98336 | tf_op jit(solution)/shard_map/ppermute | solution.py:17
  31.7 2.8 %collective-permute-start.6 = (bf16[1,96,512]{2,1,0:T(8,128)(2,1)S(1)}, bf16[1,96,512]{2,1,0:T(8,128)(2,1)S(1)}, u32[]{:S(2)}, u32[]{:S(2)}) collective-permute-start(bf16[1,96,512]{2,1,0:T(8,128)(2,1)S(1)} %collective-permute-done.5), channel_id=1, source_target_pairs={{0,28},{4,0},{8,4},{12,8},{16,12},{20,16},{24,20},{28,24},{1,29},{... | collective-permute-start | bytes 294920 | tf_op jit(solution)/shard_map/ppermute | solution.py:17
  34.5 1.9 %collective-permute-done.2 = bf16[1,96,512]{2,1,0:T(8,128)(2,1)S(1)} collective-permute-done((bf16[1,96,512]{2,1,0:T(8,128)(2,1)S(1)}, bf16[1,96,512]{2,1,0:T(8,128)(2,1)S(1)}, u32[]{:S(2)}, u32[]{:S(2)}) %collective-permute-start.2) | collective-permute-done | bytes 98336 | tf_op jit(solution)/shard_map/ppermute | solution.py:17
  36.4 8.0 %collective-permute-done.3 = bf16[1,96,512]{2,1,0:T(8,128)(2,1)S(1)} collective-permute-done((bf16[1,96,512]{2,1,0:T(8,128)(2,1)S(1)}, bf16[1,96,512]{2,1,0:T(8,128)(2,1)S(1)}, u32[]{:S(2)}, u32[]{:S(2)}) %collective-permute-start.3) | collective-permute-done | bytes 98336 | tf_op jit(solution)/shard_map/ppermute | solution.py:17
  44.5 2.2 %collective-permute-start.8 = (bf16[8,1,96,512]{3,2,1,0:T(8,128)(2,1)S(1)}, bf16[8,1,96,512]{3,2,1,0:T(8,128)(2,1)S(1)}, u32[]{:S(2)}, u32[]{:S(2)}) collective-permute-start(bf16[8,1,96,512]{3,2,1,0:T(8,128)(2,1)S(1)} %bitcast_dynamic-update-slice_fusion), channel_id=1, source_target_pairs={{0,3},{1,0},{2,1},{3,2},{4,7},{5,4},{6,5},{7,6},{8,11},{9,8},{10,9... | collective-permute-start | bytes 2359304 | tf_op jit(solution)/shard_map/ppermute | solution.py:17
  48.8 7.1 %collective-permute-done.8 = bf16[8,1,96,512]{3,2,1,0:T(8,128)(2,1)S(1)} collective-permute-done((bf16[8,1,96,512]{3,2,1,0:T(8,128)(2,1)S(1)}, bf16[8,1,96,512]{3,2,1,0:T(8,128)(2,1)S(1)}, u32[]{:S(2)}, u32[]{:S(2)}) %collective-permute-start.8) | collective-permute-done | bytes 786464 | tf_op jit(solution)/shard_map/ppermute | solution.py:17
  56.7 3.2 %collective-permute-start.17 = (bf16[4,1,96,512]{3,2,1,0:T(8,128)(2,1)}, bf16[4,1,96,512]{3,2,1,0:T(8,128)(2,1)}, u32[]{:S(2)}, u32[]{:S(2)}) collective-permute-start(bf16[4,1,96,512]{3,2,1,0:T(8,128)(2,1)} %slice.23), channel_id=1, source_target_pairs={{0,3},{1,0},{2,1},{3,2},{4,7},{5,4},{6,5},{7,6},{8,11},{9,8},{10,9... | collective-permute-start | bytes 1179656 | tf_op jit(solution)/shard_map/ppermute | solution.py:17
  59.9 1.8 %slice.22 = bf16[4,1,96,512]{3,2,1,0:T(8,128)(2,1)} slice(bf16[8,1,96,512]{3,2,1,0:T(8,128)(2,1)} %collective-permute-done.7), slice={[0:4], [0:1], [0:96], [0:512]} | slice | bytes 786432 | tf_op jit(solution)/shard_map/slice | solution.py:63
  64.6 6.3 %all-gather.2.cloned.1.call-done = bf16[3072,512]{1,0:T(8,128)(2,1)} async-done(((bf16[384,512]{1,0:T(8,128)(2,1)}), bf16[3072,512]{1,0:T(8,128)(2,1)}) %all-gather.2.cloned.1.call-update) | async-done | bytes 3145744 | tf_op jit(solution)/shard_map/all_gather | solution.py:53
  73.1 6.0 %fusion = bf16[768,512]{0,1:T(8,128)(2,1)S(1)} fusion(bf16[3072,512]{1,0:T(8,128)(2,1)} %all-gather.2.cloned.1.call-done, bf16[768,3072]{1,0:T(8,128)(2,1)} %param.8), kind=kOutput, calls=%fused_computation.4 | convolution fusion | flops 2416312320 | bytes 8650752 | tf_op jit(solution)/shard_map/dot_general | solution.py:154
  82.1 6.0 %broadcast_select_fusion = (bf16[768,512]{0,1:T(8,128)(2,1)}, bf16[768,512]{0,1:T(8,128)(2,1)S(1)}) fusion(bf16[768,512]{0,1:T(8,128)(2,1)S(1)} %fusion, pred[]{:T(512)S(6)} %eq.83, bf16[3072,512]{1,0:T(8,128)(2,1)S(1)} %bitcast.110, bf16[768,3072]{1,0:T(8,128)(2,1)} %param.8), kind=kOutput, calls=%fused_computation.10 | convolution fusion | flops 2416705536 | bytes 10223617 | tf_op jit(solution)/shard_map/dot_general | solution.py:154
  88.0 7.9 %collective-permute-start.18 = (bf16[768,512]{0,1:T(8,128)(2,1)}, bf16[768,512]{0,1:T(8,128)(2,1)S(1)}, u32[]{:S(2)}, u32[]{:S(2)}) collective-permute-start(bf16[768,512]{0,1:T(8,128)(2,1)} %get-tuple-element.71), channel_id=1, source_target_pairs={{0,32},{32,0},{1,33},{33,1},{2,34},{34,2},{3,35},{35,3},{4,36},{36... | collective-permute-start | bytes 2359304 | tf_op jit(solution)/shard_map/ppermute | solution.py:92
  107.3 2.3 %collective-permute-done.25 = bf16[192,512]{1,0:T(8,128)(2,1)S(1)} collective-permute-done((bf16[192,512]{1,0:T(8,128)(2,1)S(1)}, bf16[192,512]{1,0:T(8,128)(2,1)S(1)}, u32[]{:S(2)}, u32[]{:S(2)}) %collective-permute-start.25) | collective-permute-done | bytes 196640 | tf_op jit(solution)/shard_map/ppermute | solution.py:17
  109.6 3.7 %collective-permute-done.24 = bf16[192,512]{1,0:T(8,128)(2,1)S(1)} collective-permute-done((bf16[192,512]{1,0:T(8,128)(2,1)S(1)}, bf16[192,512]{1,0:T(8,128)(2,1)S(1)}, u32[]{:S(2)}, u32[]{:S(2)}) %collective-permute-start.24) | collective-permute-done | bytes 196640 | tf_op jit(solution)/shard_map/ppermute | solution.py:17
  113.4 1.9 %fusion.2 = bf16[512,512]{1,0:T(8,128)(2,1)S(1)} fusion(bf16[192,512]{1,0:T(8,128)(2,1)S(1)} %fusion.7, bf16[192,512]{1,0:T(8,128)(2,1)} %collective-permute-done.22, bf16[192,512]{1,0:T(8,128)(2,1)} %copy-done.10, bf16[192,512]{1,0:T(8,128)(2,1)} %copy-done.9, bf16[192,512]{1,0:T(8,128)(2,1)} %copy-done.8, bf16[192,512]{1,0:T(8,128)(2,1)} %copy-done.7, ...), kind=kOutput, calls=%fused_computation.6 | convolution fusion | flops 102957056 | bytes 2490374 | tf_op jit(solution)/shard_map/pk,pj->kj/dot_general | solution.py:194
  116.9 1.5 collective-permute-start.30
  119.2 3.6 %collective-permute-done.31 = bf16[128,512]{1,0:T(8,128)(2,1)S(1)} collective-permute-done((bf16[128,512]{1,0:T(8,128)(2,1)S(1)}, bf16[128,512]{1,0:T(8,128)(2,1)S(1)}, u32[]{:S(2)}, u32[]{:S(2)}) %collective-permute-start.31) | collective-permute-done | bytes 131104 | tf_op jit(solution)/shard_map/ppermute | solution.py:17
  122.9 3.0 %collective-permute-start.35 = (bf16[32,512]{1,0:T(8,128)(2,1)S(1)}, bf16[32,512]{1,0:T(8,128)(2,1)S(1)}, u32[]{:S(2)}, u32[]{:S(2)}) collective-permute-start(bf16[32,512]{1,0:T(8,128)(2,1)S(1)} %get-tuple-element.69), channel_id=1, source_target_pairs={{0,3},{1,2},{2,1},{3,0},{4,7},{5,6},{6,5},{7,4},{8,11},{9,10},{10,... | collective-permute-start | bytes 98312 | tf_op jit(solution)/shard_map/ppermute | solution.py:107
  126.8 2.7 %collective-permute-start.27 = (bf16[192,128]{1,0:T(8,128)(2,1)S(1)}, bf16[192,128]{1,0:T(8,128)(2,1)S(1)}, u32[]{:S(2)}, u32[]{:S(2)}) collective-permute-start(bf16[192,128]{1,0:T(8,128)(2,1)S(1)} %get-tuple-element.63), channel_id=1, source_target_pairs={{0,128},{64,192},{128,0},{192,64},{1,129},{65,193},{129,1},{193,65... | collective-permute-start | bytes 147464 | tf_op jit(solution)/shard_map/ppermute | solution.py:17
  131.0 11.8 %all-to-all-start = ((bf16[8,32,512]{2,1,0:T(8,128)(2,1)}), bf16[8,32,512]{2,1,0:T(8,128)(2,1)S(1)}, u32[]{:S(2)}, u32[]{:S(2)}) async-start(bf16[8,32,512]{2,1,0:T(8,128)(2,1)} %broadcast_in_dim.77), calls=%async_computation | async-start | bytes 524288 | tf_op jit(solution)/shard_map/all_to_all | solution.py:119
  146.1 5.0 %collective-permute-start.29 = (bf16[64,768]{1,0:T(8,128)(2,1)S(1)}, bf16[64,768]{1,0:T(8,128)(2,1)S(1)}, u32[]{:S(2)}, u32[]{:S(2)}) collective-permute-start(bf16[64,768]{1,0:T(8,128)(2,1)S(1)} %dynamic-slice_bitcast_fusion.6), channel_id=1, source_target_pairs={{0,32},{32,0},{1,33},{33,1},{2,34},{34,2},{3,35},{35,3},{4,36},{36... | collective-permute-start | bytes 294920 | tf_op jit(solution)/shard_map/ppermute | solution.py:133
  153.1 2.9 %collective-permute-start.37 = (bf16[32,512]{1,0:T(8,128)(2,1)S(1)}, bf16[32,512]{1,0:T(8,128)(2,1)S(1)}, u32[]{:S(2)}, u32[]{:S(2)}) collective-permute-start(bf16[32,512]{1,0:T(8,128)(2,1)S(1)} %reduce_sum.12), channel_id=1, source_target_pairs={{0,2},{1,3},{2,0},{3,1},{4,6},{5,7},{6,4},{7,5},{8,10},{9,11},{10,... | collective-permute-start | bytes 98312 | tf_op jit(solution)/shard_map/ppermute | solution.py:107
  156.1 1.6 collective-permute-done.37
  157.7 2.2 %collective-permute-done.38 = bf16[32,512]{1,0:T(8,128)(2,1)S(1)} collective-permute-done((bf16[32,512]{1,0:T(8,128)(2,1)S(1)}, bf16[32,512]{1,0:T(8,128)(2,1)S(1)}, u32[]{:S(2)}, u32[]{:S(2)}) %collective-permute-start.38) | collective-permute-done | bytes 32800 | tf_op jit(solution)/shard_map/ppermute | solution.py:107
  160.0 7.8 %collective-permute-start.39 = (bf16[64,512]{1,0:T(8,128)(2,1)S(1)}, bf16[64,512]{1,0:T(8,128)(2,1)S(1)}, u32[]{:S(2)}, u32[]{:S(2)}) collective-permute-start(bf16[64,512]{1,0:T(8,128)(2,1)S(1)} %dynamic-slice_bitcast_fusion.7), channel_id=1, source_target_pairs={{0,32},{32,0},{1,33},{33,1},{2,34},{34,2},{3,35},{35,3},{4,36},{36... | collective-permute-start | bytes 196616 | tf_op jit(solution)/shard_map/ppermute | solution.py:133
  (145 shorter events, 38.5 us)
Async XLA Ops:
  7.2 63.7 %all-gather.2.cloned.1.call-start = ((), (), s32[]{:S(2)}) async-start(), calls=%async_computation.1 | async-start | bytes 3538944 | tf_op jit(solution)/shard_map/all_gather | solution.py:53
  9.7 6.0 %collective-permute-start.9 = (bf16[96,512]{1,0:T(8,128)(2,1)S(1)}, bf16[96,512]{1,0:T(8,128)(2,1)S(1)}, u32[]{:S(2)}, u32[]{:S(2)}) collective-permute-start(bf16[96,512]{1,0:T(8,128)(2,1)S(1)} %get-tuple-element.66), channel_id=1, source_target_pairs={{0,1},{1,2},{2,3},{3,0},{4,5},{5,6},{6,7},{7,4},{8,9},{9,10},{10,1... | collective-permute-start | bytes 294920 | tf_op jit(solution)/shard_map/ppermute | solution.py:17
  11.9 6.6 %collective-permute-start.10 = (bf16[96,512]{1,0:T(8,128)(2,1)S(1)}, bf16[96,512]{1,0:T(8,128)(2,1)S(1)}, u32[]{:S(2)}, u32[]{:S(2)}) collective-permute-start(bf16[96,512]{1,0:T(8,128)(2,1)S(1)} %get-tuple-element.66), channel_id=1, source_target_pairs={{0,2},{1,3},{2,0},{3,1},{4,6},{5,7},{6,4},{7,5},{8,10},{9,11},{10,... | collective-permute-start | bytes 294920 | tf_op jit(solution)/shard_map/ppermute | solution.py:17
  19.3 7.7 %collective-permute-start = (bf16[1,96,512]{2,1,0:T(8,128)(2,1)S(1)}, bf16[1,96,512]{2,1,0:T(8,128)(2,1)S(1)}, u32[]{:S(2)}, u32[]{:S(2)}) collective-permute-start(bf16[1,96,512]{2,1,0:T(8,128)(2,1)S(1)} %get-tuple-element.67), channel_id=1, source_target_pairs={{0,4},{4,8},{8,12},{12,16},{16,20},{20,24},{24,28},{28,0},{1,5},{5... | collective-permute-start | bytes 294920 | tf_op jit(solution)/shard_map/ppermute | solution.py:17
  21.1 6.0 %collective-permute-start.4 = (bf16[1,96,512]{2,1,0:T(8,128)(2,1)S(1)}, bf16[1,96,512]{2,1,0:T(8,128)(2,1)S(1)}, u32[]{:S(2)}, u32[]{:S(2)}) collective-permute-start(bf16[1,96,512]{2,1,0:T(8,128)(2,1)S(1)} %get-tuple-element.67), channel_id=1, source_target_pairs={{0,28},{4,0},{8,4},{12,8},{16,12},{20,16},{24,20},{28,24},{1,29},{... | collective-permute-start | bytes 294920 | tf_op jit(solution)/shard_map/ppermute | solution.py:17
  27.0 4.7 %collective-permute-start.1 = (bf16[1,96,512]{2,1,0:T(8,128)(2,1)S(1)}, bf16[1,96,512]{2,1,0:T(8,128)(2,1)S(1)}, u32[]{:S(2)}, u32[]{:S(2)}) collective-permute-start(bf16[1,96,512]{2,1,0:T(8,128)(2,1)S(1)} %collective-permute-done), channel_id=1, source_target_pairs={{0,4},{4,8},{8,12},{12,16},{16,20},{20,24},{24,28},{28,0},{1,5},{5... | collective-permute-start | bytes 294920 | tf_op jit(solution)/shard_map/ppermute | solution.py:17
  27.0 4.7 %collective-permute-start.5 = (bf16[1,96,512]{2,1,0:T(8,128)(2,1)S(1)}, bf16[1,96,512]{2,1,0:T(8,128)(2,1)S(1)}, u32[]{:S(2)}, u32[]{:S(2)}) collective-permute-start(bf16[1,96,512]{2,1,0:T(8,128)(2,1)S(1)} %collective-permute-done.4), channel_id=1, source_target_pairs={{0,28},{4,0},{8,4},{12,8},{16,12},{20,16},{24,20},{28,24},{1,29},{... | collective-permute-start | bytes 294920 | tf_op jit(solution)/shard_map/ppermute | solution.py:17
  31.7 12.7 %collective-permute-start.6 = (bf16[1,96,512]{2,1,0:T(8,128)(2,1)S(1)}, bf16[1,96,512]{2,1,0:T(8,128)(2,1)S(1)}, u32[]{:S(2)}, u32[]{:S(2)}) collective-permute-start(bf16[1,96,512]{2,1,0:T(8,128)(2,1)S(1)} %collective-permute-done.5), channel_id=1, source_target_pairs={{0,28},{4,0},{8,4},{12,8},{16,12},{20,16},{24,20},{28,24},{1,29},{... | collective-permute-start | bytes 294920 | tf_op jit(solution)/shard_map/ppermute | solution.py:17
  36.4 8.1 %collective-permute-start.3 = (bf16[1,96,512]{2,1,0:T(8,128)(2,1)S(1)}, bf16[1,96,512]{2,1,0:T(8,128)(2,1)S(1)}, u32[]{:S(2)}, u32[]{:S(2)}) collective-permute-start(bf16[1,96,512]{2,1,0:T(8,128)(2,1)S(1)} %collective-permute-done.2), channel_id=1, source_target_pairs={{0,4},{4,8},{8,12},{12,16},{16,20},{20,24},{24,28},{28,0},{1,5},{5... | collective-permute-start | bytes 294920 | tf_op jit(solution)/shard_map/ppermute | solution.py:17
  44.5 11.4 %collective-permute-start.8 = (bf16[8,1,96,512]{3,2,1,0:T(8,128)(2,1)S(1)}, bf16[8,1,96,512]{3,2,1,0:T(8,128)(2,1)S(1)}, u32[]{:S(2)}, u32[]{:S(2)}) collective-permute-start(bf16[8,1,96,512]{3,2,1,0:T(8,128)(2,1)S(1)} %bitcast_dynamic-update-slice_fusion), channel_id=1, source_target_pairs={{0,3},{1,0},{2,1},{3,2},{4,7},{5,4},{6,5},{7,6},{8,11},{9,8},{10,9... | collective-permute-start | bytes 2359304 | tf_op jit(solution)/shard_map/ppermute | solution.py:17
  46.7 13.2 %collective-permute-start.7 = (bf16[8,1,96,512]{3,2,1,0:T(8,128)(2,1)S(1)}, bf16[8,1,96,512]{3,2,1,0:T(8,128)(2,1)}, u32[]{:S(2)}, u32[]{:S(2)}) collective-permute-start(bf16[8,1,96,512]{3,2,1,0:T(8,128)(2,1)S(1)} %bitcast_dynamic-update-slice_fusion), channel_id=1, source_target_pairs={{0,1},{1,2},{2,3},{3,0},{4,5},{5,6},{6,7},{7,4},{8,9},{9,10},{10,1... | collective-permute-start | bytes 2359304 | tf_op jit(solution)/shard_map/ppermute | solution.py:17
  47.5 15.2 %collective-permute-start.12 = (bf16[2,1,96,512]{3,2,1,0:T(8,128)(2,1)}, bf16[2,1,96,512]{3,2,1,0:T(8,128)(2,1)}, u32[]{:S(2)}, u32[]{:S(2)}) collective-permute-start(bf16[2,1,96,512]{3,2,1,0:T(8,128)(2,1)} %get-tuple-element.53), channel_id=1, source_target_pairs={{0,2},{1,3},{2,0},{3,1},{36,38},{37,39},{38,36},{39,37},{72,74},{7... | collective-permute-start | bytes 589832 | tf_op jit(solution)/shard_map/ppermute | solution.py:81
  56.7 24.1 %collective-permute-start.17 = (bf16[4,1,96,512]{3,2,1,0:T(8,128)(2,1)}, bf16[4,1,96,512]{3,2,1,0:T(8,128)(2,1)}, u32[]{:S(2)}, u32[]{:S(2)}) collective-permute-start(bf16[4,1,96,512]{3,2,1,0:T(8,128)(2,1)} %slice.23), channel_id=1, source_target_pairs={{0,3},{1,0},{2,1},{3,2},{4,7},{5,4},{6,5},{7,6},{8,11},{9,8},{10,9... | collective-permute-start | bytes 1179656 | tf_op jit(solution)/shard_map/ppermute | solution.py:17
  61.7 19.1 %collective-permute-start.16 = (bf16[4,1,96,512]{3,2,1,0:T(8,128)(2,1)}, bf16[4,1,96,512]{3,2,1,0:T(8,128)(2,1)}, u32[]{:S(2)}, u32[]{:S(2)}) collective-permute-start(bf16[4,1,96,512]{3,2,1,0:T(8,128)(2,1)} %slice.22), channel_id=1, source_target_pairs={{0,1},{1,2},{2,3},{3,0},{4,5},{5,6},{6,7},{7,4},{8,9},{9,10},{10,1... | collective-permute-start | bytes 1179656 | tf_op jit(solution)/shard_map/ppermute | solution.py:17
  70.9 8.2 %collective-permute-start.13 = (bf16[192,512]{1,0:T(8,128)(2,1)}, bf16[192,512]{1,0:T(8,128)(2,1)S(1)}, u32[]{:S(2)}, u32[]{:S(2)}) collective-permute-start(bf16[192,512]{1,0:T(8,128)(2,1)} %get-tuple-element.23), channel_id=1, source_target_pairs={{0,96},{1,97},{2,98},{3,99},{36,100},{37,101},{38,102},{39,103},{7... | collective-permute-start | bytes 589832 | tf_op jit(solution)/shard_map/ppermute | solution.py:81
  71.6 7.5 %collective-permute-start.14 = (bf16[192,512]{1,0:T(8,128)(2,1)}, bf16[192,512]{1,0:T(8,128)(2,1)S(1)}, u32[]{:S(2)}, u32[]{:S(2)}) collective-permute-start(bf16[192,512]{1,0:T(8,128)(2,1)} %get-tuple-element.24), channel_id=1, source_target_pairs={{0,160},{1,161},{2,162},{3,163},{36,164},{37,165},{38,166},{39,167... | collective-permute-start | bytes 589832 | tf_op jit(solution)/shard_map/ppermute | solution.py:81
  72.2 6.9 %collective-permute-start.15 = (bf16[192,512]{1,0:T(8,128)(2,1)}, bf16[192,512]{1,0:T(8,128)(2,1)S(1)}, u32[]{:S(2)}, u32[]{:S(2)}) collective-permute-start(bf16[192,512]{1,0:T(8,128)(2,1)} %get-tuple-element.25), channel_id=1, source_target_pairs={{0,224},{1,225},{2,226},{3,227},{36,228},{37,229},{38,230},{39,231... | collective-permute-start | bytes 589832 | tf_op jit(solution)/shard_map/ppermute | solution.py:81
  88.0 12.6 %collective-permute-start.18 = (bf16[768,512]{0,1:T(8,128)(2,1)}, bf16[768,512]{0,1:T(8,128)(2,1)S(1)}, u32[]{:S(2)}, u32[]{:S(2)}) collective-permute-start(bf16[768,512]{0,1:T(8,128)(2,1)} %get-tuple-element.71), channel_id=1, source_target_pairs={{0,32},{32,0},{1,33},{33,1},{2,34},{34,2},{3,35},{35,3},{4,36},{36... | collective-permute-start | bytes 2359304 | tf_op jit(solution)/shard_map/ppermute | solution.py:92
  97.3 5.7 %collective-permute-start.19 = (bf16[192,512]{1,0:T(8,128)(2,1)S(1)}, bf16[192,512]{1,0:T(8,128)(2,1)S(1)}, u32[]{:S(2)}, u32[]{:S(2)}) collective-permute-start(bf16[192,512]{1,0:T(8,128)(2,1)S(1)} %get-tuple-element.45), channel_id=1, source_target_pairs={{0,64},{1,65},{2,66},{3,67},{36,68},{37,69},{38,70},{39,71},{72,13... | collective-permute-start | bytes 589832 | tf_op jit(solution)/shard_map/ppermute | solution.py:81
  97.9 5.0 %collective-permute-start.20 = (bf16[192,512]{1,0:T(8,128)(2,1)S(1)}, bf16[192,512]{1,0:T(8,128)(2,1)S(1)}, u32[]{:S(2)}, u32[]{:S(2)}) collective-permute-start(bf16[192,512]{1,0:T(8,128)(2,1)S(1)} %get-tuple-element.44), channel_id=1, source_target_pairs={{0,128},{1,129},{2,130},{3,131},{36,132},{37,133},{38,134},{39,135... | collective-permute-start | bytes 589832 | tf_op jit(solution)/shard_map/ppermute | solution.py:81
  99.3 5.4 %collective-permute-start.22 = (bf16[192,512]{1,0:T(8,128)(2,1)S(1)}, bf16[192,512]{1,0:T(8,128)(2,1)}, u32[]{:S(2)}, u32[]{:S(2)}) collective-permute-start(bf16[192,512]{1,0:T(8,128)(2,1)S(1)} %get-tuple-element.42), channel_id=1, source_target_pairs={{0,32},{1,33},{2,34},{3,35},{36,4},{37,5},{38,6},{39,7},{72,104},{... | collective-permute-start | bytes 589832 | tf_op jit(solution)/shard_map/ppermute | solution.py:81
  105.4 7.8 %collective-permute-start.24 = (bf16[192,512]{1,0:T(8,128)(2,1)S(1)}, bf16[192,512]{1,0:T(8,128)(2,1)S(1)}, u32[]{:S(2)}, u32[]{:S(2)}) collective-permute-start(bf16[192,512]{1,0:T(8,128)(2,1)S(1)} %get-tuple-element.48), channel_id=1, source_target_pairs={{0,64},{64,128},{128,192},{192,0},{1,65},{65,129},{129,193},{193,1... | collective-permute-start | bytes 589832 | tf_op jit(solution)/shard_map/ppermute | solution.py:17
  106.6 6.7 %collective-permute-start.23 = (bf16[192,512]{1,0:T(8,128)(2,1)S(1)}, bf16[192,512]{1,0:T(8,128)(2,1)S(1)}, u32[]{:S(2)}, u32[]{:S(2)}) collective-permute-start(bf16[192,512]{1,0:T(8,128)(2,1)S(1)} %get-tuple-element.46), channel_id=1, source_target_pairs={{0,128},{64,192},{128,0},{192,64},{1,129},{65,193},{129,1},{193,65... | collective-permute-start | bytes 589832 | tf_op jit(solution)/shard_map/ppermute | solution.py:17
  116.4 6.4 %collective-permute-start.31 = (bf16[128,512]{1,0:T(8,128)(2,1)S(1)}, bf16[128,512]{1,0:T(8,128)(2,1)S(1)}, u32[]{:S(2)}, u32[]{:S(2)}) collective-permute-start(bf16[128,512]{1,0:T(8,128)(2,1)S(1)} %get-tuple-element.57), channel_id=1, source_target_pairs={{0,64},{64,128},{128,192},{192,0},{1,65},{65,129},{129,193},{193,1... | collective-permute-start | bytes 393224 | tf_op jit(solution)/shard_map/ppermute | solution.py:17
  116.9 5.9 %collective-permute-start.30 = (bf16[128,512]{1,0:T(8,128)(2,1)S(1)}, bf16[128,512]{1,0:T(8,128)(2,1)S(1)}, u32[]{:S(2)}, u32[]{:S(2)}) collective-permute-start(bf16[128,512]{1,0:T(8,128)(2,1)S(1)} %get-tuple-element.55), channel_id=1, source_target_pairs={{0,128},{64,192},{128,0},{192,64},{1,129},{65,193},{129,1},{193,65... | collective-permute-start | bytes 393224 | tf_op jit(solution)/shard_map/ppermute | solution.py:17
  122.9 6.6 %collective-permute-start.35 = (bf16[32,512]{1,0:T(8,128)(2,1)S(1)}, bf16[32,512]{1,0:T(8,128)(2,1)S(1)}, u32[]{:S(2)}, u32[]{:S(2)}) collective-permute-start(bf16[32,512]{1,0:T(8,128)(2,1)S(1)} %get-tuple-element.69), channel_id=1, source_target_pairs={{0,3},{1,2},{2,1},{3,0},{4,7},{5,6},{6,5},{7,4},{8,11},{9,10},{10,... | collective-permute-start | bytes 98312 | tf_op jit(solution)/shard_map/ppermute | solution.py:107
  126.7 16.9 %collective-permute-start.26 = (bf16[192,128]{1,0:T(8,128)(2,1)S(1)}, bf16[192,128]{1,0:T(8,128)(2,1)S(1)}, u32[]{:S(2)}, u32[]{:S(2)}) collective-permute-start(bf16[192,128]{1,0:T(8,128)(2,1)S(1)} %get-tuple-element.64), channel_id=1, source_target_pairs={{0,64},{64,128},{128,192},{192,0},{1,65},{65,129},{129,193},{193,1... | collective-permute-start | bytes 147464 | tf_op jit(solution)/shard_map/ppermute | solution.py:17
  126.8 17.7 %collective-permute-start.27 = (bf16[192,128]{1,0:T(8,128)(2,1)S(1)}, bf16[192,128]{1,0:T(8,128)(2,1)S(1)}, u32[]{:S(2)}, u32[]{:S(2)}) collective-permute-start(bf16[192,128]{1,0:T(8,128)(2,1)S(1)} %get-tuple-element.63), channel_id=1, source_target_pairs={{0,128},{64,192},{128,0},{192,64},{1,129},{65,193},{129,1},{193,65... | collective-permute-start | bytes 147464 | tf_op jit(solution)/shard_map/ppermute | solution.py:17
  129.5 15.5 %collective-permute-start.28 = (bf16[192,128]{1,0:T(8,128)(2,1)S(1)}, bf16[192,128]{1,0:T(8,128)(2,1)S(1)}, u32[]{:S(2)}, u32[]{:S(2)}) collective-permute-start(bf16[192,128]{1,0:T(8,128)(2,1)S(1)} %get-tuple-element.62), channel_id=1, source_target_pairs={{0,192},{64,0},{128,64},{192,128},{1,193},{65,1},{129,65},{193,129... | collective-permute-start | bytes 147464 | tf_op jit(solution)/shard_map/ppermute | solution.py:17
  131.0 21.1 %all-to-all-start = ((bf16[8,32,512]{2,1,0:T(8,128)(2,1)}), bf16[8,32,512]{2,1,0:T(8,128)(2,1)S(1)}, u32[]{:S(2)}, u32[]{:S(2)}) async-start(bf16[8,32,512]{2,1,0:T(8,128)(2,1)} %broadcast_in_dim.77), calls=%async_computation | async-start | bytes 524288 | tf_op jit(solution)/shard_map/all_to_all | solution.py:119
  146.1 5.9 %collective-permute-start.29 = (bf16[64,768]{1,0:T(8,128)(2,1)S(1)}, bf16[64,768]{1,0:T(8,128)(2,1)S(1)}, u32[]{:S(2)}, u32[]{:S(2)}) collective-permute-start(bf16[64,768]{1,0:T(8,128)(2,1)S(1)} %dynamic-slice_bitcast_fusion.6), channel_id=1, source_target_pairs={{0,32},{32,0},{1,33},{33,1},{2,34},{34,2},{3,35},{35,3},{4,36},{36... | collective-permute-start | bytes 294920 | tf_op jit(solution)/shard_map/ppermute | solution.py:133
  160.0 8.7 %collective-permute-start.39 = (bf16[64,512]{1,0:T(8,128)(2,1)S(1)}, bf16[64,512]{1,0:T(8,128)(2,1)S(1)}, u32[]{:S(2)}, u32[]{:S(2)}) collective-permute-start(bf16[64,512]{1,0:T(8,128)(2,1)S(1)} %dynamic-slice_bitcast_fusion.7), channel_id=1, source_target_pairs={{0,32},{32,0},{1,33},{33,1},{2,34},{34,2},{3,35},{35,3},{4,36},{36... | collective-permute-start | bytes 196616 | tf_op jit(solution)/shard_map/ppermute | solution.py:133
  (21 other events, 129.4 us)
Sparse Core Ops, SparseCore 0:
  19.5 51.3 all-gather.1

commit v11 on v5

--- a/solution.py
+++ b/solution.py
@@ -96,11 +96,7 @@
     x = lax.axis_index("x")
     pair = pair.reshape(XS, -1, pair.shape[1])
     tile = lambda k: lax.dynamic_index_in_dim(pair, (x + k) % XS, 0, keepdims=False)
-    far = tile(2)
-    half = far.shape[0] // 2
-    opposite = jnp.concatenate(
-        [shift(far[:half], "x", XS, 2), shift(far[half:], "x", XS, -2)], axis=0
-    )
+    opposite = shift(tile(2), "x", XS, 2)
     near = shift(tile(1), "x", XS, 1).astype(F32) + shift(tile(3), "x", XS, -1).astype(F32)
     return (tile(0).astype(F32) + opposite.astype(F32)) + near
 

time: 168 us -> 167 us (level)
  starting transfers between devices: 79 us -> 73.3 us
  waiting for transfers between devices: 45 us -> 50 us
    ppermute x2, starting transfers between devices: 17.4 us -> 12.6 us  [own_slab_of_both(): got = lax.ppermute(given, 'core', [(0, 1), (1, 0)])]
    ppermute x18 -> x17, starting transfers between devices: 27.1 us -> 22.9 us  [shift(): lax.ppermute(array, axis, [(i, (i + by) % size) for i in range(size)])]
    all_to_all x1, starting transfers between devices: 8.23 us -> 11.4 us  [summed_over_col(): part = lax.all_to_all(copies, 'z', split_axis=0, concat_axis=0, tiled=True)]
    ppermute x18 -> x17, waiting for transfers between devices: 28.3 us -> 31.2 us  [shift(): lax.ppermute(array, axis, [(i, (i + by) % size) for i in range(size)])]
    all_to_all x1, waiting for transfers between devices: 1.87 us -> 4.34 us  [summed_over_col(): part = lax.all_to_all(copies, 'z', split_axis=0, concat_axis=0, tiled=True)]
  transfers between devices with their start and end apart: 37 -> 36, of which waited for: 16 -> 16; matrix products, arithmetic and copies ran while one was open for 13% -> 13% of each run, Pallas kernels for 0% -> 0%
where the time goes in v11:
time: 167 us
  starting transfers between devices  73.3 us (44%)
  waiting for transfers between devices  50 us (30%)
  between operations  14.8 us (9%)
  matrix products  11.2 us (7%)
  other arithmetic  9.54 us (6%)
  local copies, waits for them, and re-layouts  7.73 us (5%)
    ppermute x17, waiting for transfers between devices, shift(): lax.ppermute(array, axis, [(i, (i + by) % size) for i in range(size)])  31.2 us
    ppermute x17, starting transfers between devices, shift(): lax.ppermute(array, axis, [(i, (i + by) % size) for i in range(size)])  22.9 us
    ppermute x2, starting transfers between devices, own_slab_of_both(): got = lax.ppermute(given, 'core', [(0, 1), (1, 0)])  12.6 us
    ppermute x8, starting transfers between devices, from_root(): return lax.ppermute(array, ALL, pairs)  12.1 us
    all_to_all x1, starting transfers between devices, summed_over_col(): part = lax.all_to_all(copies, 'z', split_axis=0, concat_axis=0, tiled=True)  11.4 us
    dot_general x2, matrix products, partial_of(): jnp.einsum('qj,pq->jp', panel, inverse_block, preferred_element_type=F32)  9.75 us
    all_gather x1, waiting for transfers between devices, panel_y_then_z(): return lax.all_gather(part, 'z', axis=0, tiled=True)  8.13 us
    ppermute x1, starting transfers between devices, pair_sum(): lax.ppermute(jnp.where(first, partial[1], partial[0]), 'core', [(0, 1), (...  7.18 us
  transfers between devices with their start and end apart: 36, of which 16 were waited for; matrix products, arithmetic and copies ran while one was open for 13% of the time, Pallas kernels for 0%

profile of v11, /device:TPU:1, one launch (start us, length us, event | category | flops | bytes accessed | tf_op | source)
XLA Modules:
  0.0 166.6 jit_solution(9911630012255583256)
XLA Ops:
  9.7 3.8 %collective-permute-start.1 = (bf16[96,512]{1,0:T(8,128)(2,1)S(1)}, bf16[96,512]{1,0:T(8,128)(2,1)S(1)}, u32[]{:S(2)}, u32[]{:S(2)}) collective-permute-start(bf16[96,512]{1,0:T(8,128)(2,1)S(1)} %get-tuple-element.36), channel_id=1, source_target_pairs={{0,2},{1,3},{2,0},{3,1},{4,6},{5,7},{6,4},{7,5},{8,10},{9,11},{10,... | collective-permute-start | bytes 294920 | tf_op jit(solution)/shard_map/ppermute | solution.py:17
  13.9 2.3 %collective-permute-start.2 = (bf16[96,512]{1,0:T(8,128)(2,1)S(1)}, bf16[96,512]{1,0:T(8,128)(2,1)S(1)}, u32[]{:S(2)}, u32[]{:S(2)}) collective-permute-start(bf16[96,512]{1,0:T(8,128)(2,1)S(1)} %get-tuple-element.36), channel_id=1, source_target_pairs={{0,3},{1,0},{2,1},{3,2},{4,7},{5,4},{6,5},{7,6},{8,11},{9,8},{10,9... | collective-permute-start | bytes 294920 | tf_op jit(solution)/shard_map/ppermute | solution.py:17
  16.3 3.8 %collective-permute-done = bf16[96,512]{1,0:T(8,128)(2,1)S(1)} collective-permute-done((bf16[96,512]{1,0:T(8,128)(2,1)S(1)}, bf16[96,512]{1,0:T(8,128)(2,1)S(1)}, u32[]{:S(2)}, u32[]{:S(2)}) %collective-permute-start) | collective-permute-done | bytes 98336 | tf_op jit(solution)/shard_map/ppermute | solution.py:17
  21.1 3.8 %collective-permute-start.7 = (bf16[1,96,512]{2,1,0:T(8,128)(2,1)S(1)}, bf16[1,96,512]{2,1,0:T(8,128)(2,1)S(1)}, u32[]{:S(2)}, u32[]{:S(2)}) collective-permute-start(bf16[1,96,512]{2,1,0:T(8,128)(2,1)S(1)} %get-tuple-element.35), channel_id=1, source_target_pairs={{0,28},{4,0},{8,4},{12,8},{16,12},{20,16},{24,20},{28,24},{1,29},{... | collective-permute-start | bytes 294920 | tf_op jit(solution)/shard_map/ppermute | solution.py:17
  25.1 1.7 %collective-permute-done.3 = bf16[1,96,512]{2,1,0:T(8,128)(2,1)S(1)} collective-permute-done((bf16[1,96,512]{2,1,0:T(8,128)(2,1)S(1)}, bf16[1,96,512]{2,1,0:T(8,128)(2,1)S(1)}, u32[]{:S(2)}, u32[]{:S(2)}) %collective-permute-start.3) | collective-permute-done | bytes 98336 | tf_op jit(solution)/shard_map/ppermute | solution.py:17
  26.8 2.8 %collective-permute-start.8 = (bf16[1,96,512]{2,1,0:T(8,128)(2,1)S(1)}, bf16[1,96,512]{2,1,0:T(8,128)(2,1)S(1)}, u32[]{:S(2)}, u32[]{:S(2)}) collective-permute-start(bf16[1,96,512]{2,1,0:T(8,128)(2,1)S(1)} %collective-permute-done.7), channel_id=1, source_target_pairs={{0,28},{4,0},{8,4},{12,8},{16,12},{20,16},{24,20},{28,24},{1,29},{... | collective-permute-start | bytes 294920 | tf_op jit(solution)/shard_map/ppermute | solution.py:17
  29.6 1.9 %collective-permute-done.4 = bf16[1,96,512]{2,1,0:T(8,128)(2,1)S(1)} collective-permute-done((bf16[1,96,512]{2,1,0:T(8,128)(2,1)S(1)}, bf16[1,96,512]{2,1,0:T(8,128)(2,1)S(1)}, u32[]{:S(2)}, u32[]{:S(2)}) %collective-permute-start.4) | collective-permute-done | bytes 98336 | tf_op jit(solution)/shard_map/ppermute | solution.py:17
  31.5 2.8 %collective-permute-start.9 = (bf16[1,96,512]{2,1,0:T(8,128)(2,1)S(1)}, bf16[1,96,512]{2,1,0:T(8,128)(2,1)S(1)}, u32[]{:S(2)}, u32[]{:S(2)}) collective-permute-start(bf16[1,96,512]{2,1,0:T(8,128)(2,1)S(1)} %collective-permute-done.8), channel_id=1, source_target_pairs={{0,28},{4,0},{8,4},{12,8},{16,12},{20,16},{24,20},{28,24},{1,29},{... | collective-permute-start | bytes 294920 | tf_op jit(solution)/shard_map/ppermute | solution.py:17
  34.3 1.9 %collective-permute-done.5 = bf16[1,96,512]{2,1,0:T(8,128)(2,1)S(1)} collective-permute-done((bf16[1,96,512]{2,1,0:T(8,128)(2,1)S(1)}, bf16[1,96,512]{2,1,0:T(8,128)(2,1)S(1)}, u32[]{:S(2)}, u32[]{:S(2)}) %collective-permute-start.5) | collective-permute-done | bytes 98336 | tf_op jit(solution)/shard_map/ppermute | solution.py:17
  36.2 7.8 %collective-permute-done.6 = bf16[1,96,512]{2,1,0:T(8,128)(2,1)S(1)} collective-permute-done((bf16[1,96,512]{2,1,0:T(8,128)(2,1)S(1)}, bf16[1,96,512]{2,1,0:T(8,128)(2,1)S(1)}, u32[]{:S(2)}, u32[]{:S(2)}) %collective-permute-start.6) | collective-permute-done | bytes 98336 | tf_op jit(solution)/shard_map/ppermute | solution.py:17
  44.1 1.9 %collective-permute-start.10 = (bf16[8,1,96,512]{3,2,1,0:T(8,128)(2,1)S(1)}, bf16[8,1,96,512]{3,2,1,0:T(8,128)(2,1)}, u32[]{:S(2)}, u32[]{:S(2)}) collective-permute-start(bf16[8,1,96,512]{3,2,1,0:T(8,128)(2,1)S(1)} %bitcast_dynamic-update-slice_fusion), channel_id=1, source_target_pairs={{0,1},{1,2},{2,3},{3,0},{4,5},{5,6},{6,7},{7,4},{8,9},{9,10},{10,1... | collective-permute-start | bytes 2359304 | tf_op jit(solution)/shard_map/ppermute | solution.py:17
  49.3 7.6 %collective-permute-done.10 = bf16[8,1,96,512]{3,2,1,0:T(8,128)(2,1)} collective-permute-done((bf16[8,1,96,512]{3,2,1,0:T(8,128)(2,1)S(1)}, bf16[8,1,96,512]{3,2,1,0:T(8,128)(2,1)}, u32[]{:S(2)}, u32[]{:S(2)}) %collective-permute-start.10) | collective-permute-done | bytes 786464 | tf_op jit(solution)/shard_map/ppermute | solution.py:17
  60.4 1.6 collective-permute-start.19
  62.0 1.6 collective-permute-start.21
  63.6 8.1 %all-gather.2.cloned.1.call-done = bf16[3072,512]{1,0:T(8,128)(2,1)} async-done(((bf16[384,512]{1,0:T(8,128)(2,1)}), bf16[3072,512]{1,0:T(8,128)(2,1)}) %all-gather.2.cloned.1.call-update) | async-done | bytes 3145744 | tf_op jit(solution)/shard_map/all_gather | solution.py:53
  72.8 2.3 %collective-permute-start.13 = (bf16[4,1,96,512]{3,2,1,0:T(8,128)(2,1)S(1)}, bf16[4,1,96,512]{3,2,1,0:T(8,128)(2,1)S(1)}, u32[]{:S(2)}, u32[]{:S(2)}) collective-permute-start(bf16[4,1,96,512]{3,2,1,0:T(8,128)(2,1)S(1)} %slice.19), channel_id=1, source_target_pairs={{0,3},{1,0},{2,1},{3,2},{4,7},{5,4},{6,5},{7,6},{8,11},{9,8},{10,9... | collective-permute-start | bytes 1179656 | tf_op jit(solution)/shard_map/ppermute | solution.py:17
  75.1 5.9 %convolution_convert_fusion.1 = bf16[512,768]{1,0:T(8,128)(2,1)S(1)} fusion(bf16[3072,512]{1,0:T(8,128)(2,1)} %all-gather.2.cloned.1.call-done, bf16[768,3072]{1,0:T(8,128)(2,1)} %param.8), kind=kOutput, calls=%fused_computation.2 | convolution fusion | flops 2416312320 | bytes 8650752 | tf_op jit(solution)/shard_map/qj,pq->jp/dot_general | solution.py:152
  81.1 2.6 %broadcast_select_fusion = (bf16[768,512]{1,0:T(8,128)(2,1)}, bf16[768,512]{1,0:T(8,128)(2,1)S(1)}) fusion(pred[]{:T(512)S(6)} %eq.63, bf16[2,4,96,512]{3,2,1,0:T(8,128)(2,1)S(1)} %dynamic-slice_dynamic-update-slice_fusion, bf16[3072,512]{1,0:T(8,128)(2,1)} %all-gather.2.cloned.1.call-done, s32[]{:T(128)S(6)} %select_n.299), kind=kLoop, calls=%fused_computation.9 | loop fusion | flops 393216 | bytes 3145733 | tf_op jit(solution)/shard_map/jit(_where)/select_n | solution.py:175
  88.8 1.6 collective-permute-start.16
  91.7 3.8 %broadcast_select_fusion.1 = (bf16[512,768]{1,0:T(8,128)(2,1)}, bf16[512,768]{1,0:T(8,128)(2,1)}) fusion(bf16[512,768]{1,0:T(8,128)(2,1)S(1)} %convolution_convert_fusion.1, pred[]{:T(512)S(6)} %eq.63, bf16[3072,512]{1,0:T(8,128)(2,1)S(1)} %bitcast.96, bf16[768,3072]{1,0:T(8,128)(2,1)S(1)} %bitcast.108), kind=kOutput, calls=%fused_computation.10 | convolution fusion | flops 2416705536 | bytes 10223617 | tf_op jit(solution)/shard_map/qj,pq->jp/dot_general | solution.py:152
  95.5 7.2 %collective-permute-start.14 = (bf16[512,768]{1,0:T(8,128)(2,1)}, bf16[512,768]{1,0:T(8,128)(2,1)}, u32[]{:S(2)}, u32[]{:S(2)}) collective-permute-start(bf16[512,768]{1,0:T(8,128)(2,1)} %get-tuple-element.40), channel_id=1, source_target_pairs={{0,32},{32,0},{1,33},{33,1},{2,34},{34,2},{3,35},{35,3},{4,36},{36... | collective-permute-start | bytes 2359304 | tf_op jit(solution)/shard_map/ppermute | solution.py:90
  102.7 2.7 %add_select_fusion = bf16[768,512]{1,0:T(8,128)(2,1)S(1)} fusion(bf16[768,512]{1,0:T(8,128)(2,1)S(1)} %collective-permute-done.22, bf16[768,512]{1,0:T(8,128)(2,1)} %collective-permute-done.21, bf16[768,512]{1,0:T(8,128)(2,1)} %collective-permute-done.19, bf16[768,512]{1,0:T(8,128)(2,1)} %collective-permute-done.20, ...), kind=kLoop, calls=%fused_computation.8 | loop fusion | flops 3145728 | bytes 7864322 | tf_op jit(solution)/shard_map/jit(_where)/select_n | solution.py:180
  108.8 4.4 %collective-permute-done.23 = bf16[128,768]{1,0:T(8,128)(2,1)S(1)} collective-permute-done((bf16[128,768]{1,0:T(8,128)(2,1)S(1)}, bf16[128,768]{1,0:T(8,128)(2,1)S(1)}, u32[]{:S(2)}, u32[]{:S(2)}) %collective-permute-start.23) | collective-permute-done | bytes 196640 | tf_op jit(solution)/shard_map/ppermute | solution.py:17
  113.2 2.0 %collective-permute-done.24 = bf16[128,768]{1,0:T(8,128)(2,1)S(1)} collective-permute-done((bf16[128,768]{1,0:T(8,128)(2,1)S(1)}, bf16[128,768]{1,0:T(8,128)(2,1)S(1)}, u32[]{:S(2)}, u32[]{:S(2)}) %collective-permute-start.24) | collective-permute-done | bytes 196640 | tf_op jit(solution)/shard_map/ppermute | solution.py:17
  116.6 1.8 %collective-permute-start.29 = (bf16[32,512]{1,0:T(8,128)(2,1)S(1)}, bf16[32,512]{1,0:T(8,128)(2,1)S(1)}, u32[]{:S(2)}, u32[]{:S(2)}) collective-permute-start(bf16[32,512]{1,0:T(8,128)(2,1)S(1)} %get-tuple-element.38), channel_id=1, source_target_pairs={{0,3},{1,2},{2,1},{3,0},{4,7},{5,6},{6,5},{7,4},{8,11},{9,10},{10,... | collective-permute-start | bytes 98312 | tf_op jit(solution)/shard_map/ppermute | solution.py:105
  120.5 2.1 %collective-permute-done.28 = bf16[32,512]{1,0:T(8,128)(2,1)S(1)} collective-permute-done((bf16[32,512]{1,0:T(8,128)(2,1)S(1)}, bf16[32,512]{1,0:T(8,128)(2,1)S(1)}, u32[]{:S(2)}, u32[]{:S(2)}) %collective-permute-start.28) | collective-permute-done | bytes 32800 | tf_op jit(solution)/shard_map/ppermute | solution.py:105
  123.4 11.4 %all-to-all-start = ((bf16[8,32,512]{2,1,0:T(8,128)(2,1)}), bf16[8,32,512]{2,1,0:T(8,128)(2,1)S(1)}, u32[]{:S(2)}, u32[]{:S(2)}) async-start(bf16[8,32,512]{2,1,0:T(8,128)(2,1)} %broadcast_in_dim.68), calls=%async_computation | async-start | bytes 524288 | tf_op jit(solution)/shard_map/all_to_all | solution.py:117
  134.8 4.1 %collective-permute-start.26 = (bf16[64,768]{1,0:T(8,128)(2,1)S(1)}, bf16[64,768]{1,0:T(8,128)(2,1)S(1)}, u32[]{:S(2)}, u32[]{:S(2)}) collective-permute-start(bf16[64,768]{1,0:T(8,128)(2,1)S(1)} %dynamic-slice_bitcast_fusion.3), channel_id=1, source_target_pairs={{0,32},{32,0},{1,33},{33,1},{2,34},{34,2},{3,35},{35,3},{4,36},{36... | collective-permute-start | bytes 294920 | tf_op jit(solution)/shard_map/ppermute | solution.py:131
  139.8 4.3 %all-to-all-done = bf16[8,32,512]{2,1,0:T(8,128)(2,1)S(1)} async-done(((bf16[8,32,512]{2,1,0:T(8,128)(2,1)}), bf16[8,32,512]{2,1,0:T(8,128)(2,1)S(1)}, u32[]{:S(2)}, u32[]{:S(2)}) %all-to-all-start) | async-done | bytes 262176 | tf_op jit(solution)/shard_map/all_to_all | solution.py:117
  144.5 2.2 %collective-permute-start.31 = (bf16[32,512]{1,0:T(8,128)(2,1)S(1)}, bf16[32,512]{1,0:T(8,128)(2,1)S(1)}, u32[]{:S(2)}, u32[]{:S(2)}) collective-permute-start(bf16[32,512]{1,0:T(8,128)(2,1)S(1)} %reduce_sum.12), channel_id=1, source_target_pairs={{0,2},{1,3},{2,0},{3,1},{4,6},{5,7},{6,4},{7,5},{8,10},{9,11},{10,... | collective-permute-start | bytes 98312 | tf_op jit(solution)/shard_map/ppermute | solution.py:105
  147.6 1.9 %collective-permute-done.30 = bf16[32,512]{1,0:T(8,128)(2,1)S(1)} collective-permute-done((bf16[32,512]{1,0:T(8,128)(2,1)S(1)}, bf16[32,512]{1,0:T(8,128)(2,1)S(1)}, u32[]{:S(2)}, u32[]{:S(2)}) %collective-permute-start.30) | collective-permute-done | bytes 32800 | tf_op jit(solution)/shard_map/ppermute | solution.py:105
  149.6 8.5 %collective-permute-start.33 = (bf16[64,512]{1,0:T(8,128)(2,1)S(1)}, bf16[64,512]{1,0:T(8,128)(2,1)S(1)}, u32[]{:S(2)}, u32[]{:S(2)}) collective-permute-start(bf16[64,512]{1,0:T(8,128)(2,1)S(1)} %dynamic-slice_bitcast_fusion.4), channel_id=1, source_target_pairs={{0,32},{32,0},{1,33},{33,1},{2,34},{34,2},{3,35},{35,3},{4,36},{36... | collective-permute-start | bytes 196616 | tf_op jit(solution)/shard_map/ppermute | solution.py:131
  (122 shorter events, 29.4 us)
Async XLA Ops:
  7.2 64.5 %all-gather.2.cloned.1.call-start = ((), (), s32[]{:S(2)}) async-start(), calls=%async_computation.1 | async-start | bytes 3538944 | tf_op jit(solution)/shard_map/all_gather | solution.py:53
  9.7 10.5 %collective-permute-start.1 = (bf16[96,512]{1,0:T(8,128)(2,1)S(1)}, bf16[96,512]{1,0:T(8,128)(2,1)S(1)}, u32[]{:S(2)}, u32[]{:S(2)}) collective-permute-start(bf16[96,512]{1,0:T(8,128)(2,1)S(1)} %get-tuple-element.36), channel_id=1, source_target_pairs={{0,2},{1,3},{2,0},{3,1},{4,6},{5,7},{6,4},{7,5},{8,10},{9,11},{10,... | collective-permute-start | bytes 294920 | tf_op jit(solution)/shard_map/ppermute | solution.py:17
  13.5 6.6 %collective-permute-start = (bf16[96,512]{1,0:T(8,128)(2,1)S(1)}, bf16[96,512]{1,0:T(8,128)(2,1)S(1)}, u32[]{:S(2)}, u32[]{:S(2)}) collective-permute-start(bf16[96,512]{1,0:T(8,128)(2,1)S(1)} %get-tuple-element.36), channel_id=1, source_target_pairs={{0,1},{1,2},{2,3},{3,0},{4,5},{5,6},{6,7},{7,4},{8,9},{9,10},{10,1... | collective-permute-start | bytes 294920 | tf_op jit(solution)/shard_map/ppermute | solution.py:17
  13.9 6.3 %collective-permute-start.2 = (bf16[96,512]{1,0:T(8,128)(2,1)S(1)}, bf16[96,512]{1,0:T(8,128)(2,1)S(1)}, u32[]{:S(2)}, u32[]{:S(2)}) collective-permute-start(bf16[96,512]{1,0:T(8,128)(2,1)S(1)} %get-tuple-element.36), channel_id=1, source_target_pairs={{0,3},{1,0},{2,1},{3,2},{4,7},{5,4},{6,5},{7,6},{8,11},{9,8},{10,9... | collective-permute-start | bytes 294920 | tf_op jit(solution)/shard_map/ppermute | solution.py:17
  21.0 5.9 %collective-permute-start.3 = (bf16[1,96,512]{2,1,0:T(8,128)(2,1)S(1)}, bf16[1,96,512]{2,1,0:T(8,128)(2,1)S(1)}, u32[]{:S(2)}, u32[]{:S(2)}) collective-permute-start(bf16[1,96,512]{2,1,0:T(8,128)(2,1)S(1)} %get-tuple-element.35), channel_id=1, source_target_pairs={{0,4},{4,8},{8,12},{12,16},{16,20},{20,24},{24,28},{28,0},{1,5},{5... | collective-permute-start | bytes 294920 | tf_op jit(solution)/shard_map/ppermute | solution.py:17
  21.1 5.8 %collective-permute-start.7 = (bf16[1,96,512]{2,1,0:T(8,128)(2,1)S(1)}, bf16[1,96,512]{2,1,0:T(8,128)(2,1)S(1)}, u32[]{:S(2)}, u32[]{:S(2)}) collective-permute-start(bf16[1,96,512]{2,1,0:T(8,128)(2,1)S(1)} %get-tuple-element.35), channel_id=1, source_target_pairs={{0,28},{4,0},{8,4},{12,8},{16,12},{20,16},{24,20},{28,24},{1,29},{... | collective-permute-start | bytes 294920 | tf_op jit(solution)/shard_map/ppermute | solution.py:17
  26.8 4.7 %collective-permute-start.4 = (bf16[1,96,512]{2,1,0:T(8,128)(2,1)S(1)}, bf16[1,96,512]{2,1,0:T(8,128)(2,1)S(1)}, u32[]{:S(2)}, u32[]{:S(2)}) collective-permute-start(bf16[1,96,512]{2,1,0:T(8,128)(2,1)S(1)} %collective-permute-done.3), channel_id=1, source_target_pairs={{0,4},{4,8},{8,12},{12,16},{16,20},{20,24},{24,28},{28,0},{1,5},{5... | collective-permute-start | bytes 294920 | tf_op jit(solution)/shard_map/ppermute | solution.py:17
  26.8 4.7 %collective-permute-start.8 = (bf16[1,96,512]{2,1,0:T(8,128)(2,1)S(1)}, bf16[1,96,512]{2,1,0:T(8,128)(2,1)S(1)}, u32[]{:S(2)}, u32[]{:S(2)}) collective-permute-start(bf16[1,96,512]{2,1,0:T(8,128)(2,1)S(1)} %collective-permute-done.7), channel_id=1, source_target_pairs={{0,28},{4,0},{8,4},{12,8},{16,12},{20,16},{24,20},{28,24},{1,29},{... | collective-permute-start | bytes 294920 | tf_op jit(solution)/shard_map/ppermute | solution.py:17
  31.5 4.7 %collective-permute-start.5 = (bf16[1,96,512]{2,1,0:T(8,128)(2,1)S(1)}, bf16[1,96,512]{2,1,0:T(8,128)(2,1)S(1)}, u32[]{:S(2)}, u32[]{:S(2)}) collective-permute-start(bf16[1,96,512]{2,1,0:T(8,128)(2,1)S(1)} %collective-permute-done.4), channel_id=1, source_target_pairs={{0,4},{4,8},{8,12},{12,16},{16,20},{20,24},{24,28},{28,0},{1,5},{5... | collective-permute-start | bytes 294920 | tf_op jit(solution)/shard_map/ppermute | solution.py:17
  31.5 12.6 %collective-permute-start.9 = (bf16[1,96,512]{2,1,0:T(8,128)(2,1)S(1)}, bf16[1,96,512]{2,1,0:T(8,128)(2,1)S(1)}, u32[]{:S(2)}, u32[]{:S(2)}) collective-permute-start(bf16[1,96,512]{2,1,0:T(8,128)(2,1)S(1)} %collective-permute-done.8), channel_id=1, source_target_pairs={{0,28},{4,0},{8,4},{12,8},{16,12},{20,16},{24,20},{28,24},{1,29},{... | collective-permute-start | bytes 294920 | tf_op jit(solution)/shard_map/ppermute | solution.py:17
  36.2 7.9 %collective-permute-start.6 = (bf16[1,96,512]{2,1,0:T(8,128)(2,1)S(1)}, bf16[1,96,512]{2,1,0:T(8,128)(2,1)S(1)}, u32[]{:S(2)}, u32[]{:S(2)}) collective-permute-start(bf16[1,96,512]{2,1,0:T(8,128)(2,1)S(1)} %collective-permute-done.5), channel_id=1, source_target_pairs={{0,4},{4,8},{8,12},{12,16},{16,20},{20,24},{24,28},{28,0},{1,5},{5... | collective-permute-start | bytes 294920 | tf_op jit(solution)/shard_map/ppermute | solution.py:17
  44.1 12.7 %collective-permute-start.10 = (bf16[8,1,96,512]{3,2,1,0:T(8,128)(2,1)S(1)}, bf16[8,1,96,512]{3,2,1,0:T(8,128)(2,1)}, u32[]{:S(2)}, u32[]{:S(2)}) collective-permute-start(bf16[8,1,96,512]{3,2,1,0:T(8,128)(2,1)S(1)} %bitcast_dynamic-update-slice_fusion), channel_id=1, source_target_pairs={{0,1},{1,2},{2,3},{3,0},{4,5},{5,6},{6,7},{7,4},{8,9},{9,10},{10,1... | collective-permute-start | bytes 2359304 | tf_op jit(solution)/shard_map/ppermute | solution.py:17
  46.0 12.8 %collective-permute-start.11 = (bf16[8,1,96,512]{3,2,1,0:T(8,128)(2,1)S(1)}, bf16[8,1,96,512]{3,2,1,0:T(8,128)(2,1)S(1)}, u32[]{:S(2)}, u32[]{:S(2)}) collective-permute-start(bf16[8,1,96,512]{3,2,1,0:T(8,128)(2,1)S(1)} %bitcast_dynamic-update-slice_fusion), channel_id=1, source_target_pairs={{0,3},{1,0},{2,1},{3,2},{4,7},{5,4},{6,5},{7,6},{8,11},{9,8},{10,9... | collective-permute-start | bytes 2359304 | tf_op jit(solution)/shard_map/ppermute | solution.py:17
  47.9 9.9 %collective-permute-start.15 = (bf16[2,1,96,512]{3,2,1,0:T(8,128)(2,1)}, bf16[2,1,96,512]{3,2,1,0:T(8,128)(2,1)}, u32[]{:S(2)}, u32[]{:S(2)}) collective-permute-start(bf16[2,1,96,512]{3,2,1,0:T(8,128)(2,1)} %get-tuple-element.29), channel_id=1, source_target_pairs={{0,2},{1,3},{2,0},{3,1},{36,38},{37,39},{38,36},{39,37},{72,74},{7... | collective-permute-start | bytes 589832 | tf_op jit(solution)/shard_map/ppermute | solution.py:81
  58.9 29.9 %collective-permute-start.20 = (bf16[768,512]{1,0:T(8,128)(2,1)S(1)}, bf16[768,512]{1,0:T(8,128)(2,1)}, u32[]{:S(2)}, u32[]{:S(2)}) collective-permute-start(bf16[768,512]{1,0:T(8,128)(2,1)S(1)} %bitcast.93), channel_id=1, source_target_pairs={{0,224},{1,225},{2,226},{3,227},{36,228},{37,229},{38,230},{39,231... | collective-permute-start | bytes 2359304 | tf_op jit(solution)/shard_map/ppermute | solution.py:81
  60.4 30.0 %collective-permute-start.19 = (bf16[768,512]{1,0:T(8,128)(2,1)S(1)}, bf16[768,512]{1,0:T(8,128)(2,1)}, u32[]{:S(2)}, u32[]{:S(2)}) collective-permute-start(bf16[768,512]{1,0:T(8,128)(2,1)S(1)} %bitcast.94), channel_id=1, source_target_pairs={{0,96},{1,97},{2,98},{3,99},{36,100},{37,101},{38,102},{39,103},{7... | collective-permute-start | bytes 2359304 | tf_op jit(solution)/shard_map/ppermute | solution.py:81
  62.0 33.5 %collective-permute-start.21 = (bf16[768,512]{1,0:T(8,128)(2,1)S(1)}, bf16[768,512]{1,0:T(8,128)(2,1)}, u32[]{:S(2)}, u32[]{:S(2)}) collective-permute-start(bf16[768,512]{1,0:T(8,128)(2,1)S(1)} %bitcast.95), channel_id=1, source_target_pairs={{0,160},{1,161},{2,162},{3,163},{36,164},{37,165},{38,166},{39,167... | collective-permute-start | bytes 2359304 | tf_op jit(solution)/shard_map/ppermute | solution.py:81
  72.8 10.9 %collective-permute-start.13 = (bf16[4,1,96,512]{3,2,1,0:T(8,128)(2,1)S(1)}, bf16[4,1,96,512]{3,2,1,0:T(8,128)(2,1)S(1)}, u32[]{:S(2)}, u32[]{:S(2)}) collective-permute-start(bf16[4,1,96,512]{3,2,1,0:T(8,128)(2,1)S(1)} %slice.19), channel_id=1, source_target_pairs={{0,3},{1,0},{2,1},{3,2},{4,7},{5,4},{6,5},{7,6},{8,11},{9,8},{10,9... | collective-permute-start | bytes 1179656 | tf_op jit(solution)/shard_map/ppermute | solution.py:17
  75.1 10.2 %collective-permute-start.12 = (bf16[4,1,96,512]{3,2,1,0:T(8,128)(2,1)S(1)}, bf16[4,1,96,512]{3,2,1,0:T(8,128)(2,1)S(1)}, u32[]{:S(2)}, u32[]{:S(2)}) collective-permute-start(bf16[4,1,96,512]{3,2,1,0:T(8,128)(2,1)S(1)} %slice.18), channel_id=1, source_target_pairs={{0,1},{1,2},{2,3},{3,0},{4,5},{5,6},{6,7},{7,4},{8,9},{9,10},{10,1... | collective-permute-start | bytes 1179656 | tf_op jit(solution)/shard_map/ppermute | solution.py:17
  83.7 19.0 %collective-permute-start.18 = (bf16[768,512]{1,0:T(8,128)(2,1)S(1)}, bf16[768,512]{1,0:T(8,128)(2,1)}, u32[]{:S(2)}, u32[]{:S(2)}) collective-permute-start(bf16[768,512]{1,0:T(8,128)(2,1)S(1)} %get-tuple-element.25), channel_id=1, source_target_pairs={{0,128},{1,129},{2,130},{3,131},{36,132},{37,133},{38,134},{39,135... | collective-permute-start | bytes 2359304 | tf_op jit(solution)/shard_map/ppermute | solution.py:81
  85.3 17.5 %collective-permute-start.17 = (bf16[768,512]{1,0:T(8,128)(2,1)S(1)}, bf16[768,512]{1,0:T(8,128)(2,1)}, u32[]{:S(2)}, u32[]{:S(2)}) collective-permute-start(bf16[768,512]{1,0:T(8,128)(2,1)S(1)} %get-tuple-element.25), channel_id=1, source_target_pairs={{0,192},{1,193},{2,194},{3,195},{36,196},{37,197},{38,198},{39,199... | collective-permute-start | bytes 2359304 | tf_op jit(solution)/shard_map/ppermute | solution.py:81
  88.8 14.0 %collective-permute-start.16 = (bf16[768,512]{1,0:T(8,128)(2,1)S(1)}, bf16[768,512]{1,0:T(8,128)(2,1)}, u32[]{:S(2)}, u32[]{:S(2)}) collective-permute-start(bf16[768,512]{1,0:T(8,128)(2,1)S(1)} %get-tuple-element.25), channel_id=1, source_target_pairs={{0,64},{1,65},{2,66},{3,67},{36,68},{37,69},{38,70},{39,71},{72,13... | collective-permute-start | bytes 2359304 | tf_op jit(solution)/shard_map/ppermute | solution.py:81
  90.4 12.3 %collective-permute-start.22 = (bf16[768,512]{1,0:T(8,128)(2,1)}, bf16[768,512]{1,0:T(8,128)(2,1)S(1)}, u32[]{:S(2)}, u32[]{:S(2)}) collective-permute-start(bf16[768,512]{1,0:T(8,128)(2,1)} %get-tuple-element.24), channel_id=1, source_target_pairs={{0,32},{1,33},{2,34},{3,35},{36,4},{37,5},{38,6},{39,7},{72,104},{... | collective-permute-start | bytes 2359304 | tf_op jit(solution)/shard_map/ppermute | solution.py:81
  95.5 10.0 %collective-permute-start.14 = (bf16[512,768]{1,0:T(8,128)(2,1)}, bf16[512,768]{1,0:T(8,128)(2,1)}, u32[]{:S(2)}, u32[]{:S(2)}) collective-permute-start(bf16[512,768]{1,0:T(8,128)(2,1)} %get-tuple-element.40), channel_id=1, source_target_pairs={{0,32},{32,0},{1,33},{33,1},{2,34},{34,2},{3,35},{35,3},{4,36},{36... | collective-permute-start | bytes 2359304 | tf_op jit(solution)/shard_map/ppermute | solution.py:90
  107.0 6.2 %collective-permute-start.23 = (bf16[128,768]{1,0:T(8,128)(2,1)S(1)}, bf16[128,768]{1,0:T(8,128)(2,1)S(1)}, u32[]{:S(2)}, u32[]{:S(2)}) collective-permute-start(bf16[128,768]{1,0:T(8,128)(2,1)S(1)} %get-tuple-element.26), channel_id=1, source_target_pairs={{0,128},{64,192},{128,0},{192,64},{1,129},{65,193},{129,1},{193,65... | collective-permute-start | bytes 589832 | tf_op jit(solution)/shard_map/ppermute | solution.py:17
  107.1 6.1 %collective-permute-start.25 = (bf16[128,768]{1,0:T(8,128)(2,1)S(1)}, bf16[128,768]{1,0:T(8,128)(2,1)S(1)}, u32[]{:S(2)}, u32[]{:S(2)}) collective-permute-start(bf16[128,768]{1,0:T(8,128)(2,1)S(1)} %get-tuple-element.27), channel_id=1, source_target_pairs={{0,192},{64,0},{128,64},{192,128},{1,193},{65,1},{129,65},{193,129... | collective-permute-start | bytes 589832 | tf_op jit(solution)/shard_map/ppermute | solution.py:17
  107.2 8.0 %collective-permute-start.24 = (bf16[128,768]{1,0:T(8,128)(2,1)S(1)}, bf16[128,768]{1,0:T(8,128)(2,1)S(1)}, u32[]{:S(2)}, u32[]{:S(2)}) collective-permute-start(bf16[128,768]{1,0:T(8,128)(2,1)S(1)} %get-tuple-element.28), channel_id=1, source_target_pairs={{0,64},{64,128},{128,192},{192,0},{1,65},{65,129},{129,193},{193,1... | collective-permute-start | bytes 589832 | tf_op jit(solution)/shard_map/ppermute | solution.py:17
  123.4 20.8 %all-to-all-start = ((bf16[8,32,512]{2,1,0:T(8,128)(2,1)}), bf16[8,32,512]{2,1,0:T(8,128)(2,1)S(1)}, u32[]{:S(2)}, u32[]{:S(2)}) async-start(bf16[8,32,512]{2,1,0:T(8,128)(2,1)} %broadcast_in_dim.68), calls=%async_computation | async-start | bytes 524288 | tf_op jit(solution)/shard_map/all_to_all | solution.py:117
  134.8 5.0 %collective-permute-start.26 = (bf16[64,768]{1,0:T(8,128)(2,1)S(1)}, bf16[64,768]{1,0:T(8,128)(2,1)S(1)}, u32[]{:S(2)}, u32[]{:S(2)}) collective-permute-start(bf16[64,768]{1,0:T(8,128)(2,1)S(1)} %dynamic-slice_bitcast_fusion.3), channel_id=1, source_target_pairs={{0,32},{32,0},{1,33},{33,1},{2,34},{34,2},{3,35},{35,3},{4,36},{36... | collective-permute-start | bytes 294920 | tf_op jit(solution)/shard_map/ppermute | solution.py:131
  144.2 5.3 %collective-permute-start.32 = (bf16[32,512]{1,0:T(8,128)(2,1)S(1)}, bf16[32,512]{1,0:T(8,128)(2,1)S(1)}, u32[]{:S(2)}, u32[]{:S(2)}) collective-permute-start(bf16[32,512]{1,0:T(8,128)(2,1)S(1)} %reduce_sum.12), channel_id=1, source_target_pairs={{0,3},{1,2},{2,1},{3,0},{4,7},{5,6},{6,5},{7,4},{8,11},{9,10},{10,... | collective-permute-start | bytes 98312 | tf_op jit(solution)/shard_map/ppermute | solution.py:105
  144.5 5.0 %collective-permute-start.31 = (bf16[32,512]{1,0:T(8,128)(2,1)S(1)}, bf16[32,512]{1,0:T(8,128)(2,1)S(1)}, u32[]{:S(2)}, u32[]{:S(2)}) collective-permute-start(bf16[32,512]{1,0:T(8,128)(2,1)S(1)} %reduce_sum.12), channel_id=1, source_target_pairs={{0,2},{1,3},{2,0},{3,1},{4,6},{5,7},{6,4},{7,5},{8,10},{9,11},{10,... | collective-permute-start | bytes 98312 | tf_op jit(solution)/shard_map/ppermute | solution.py:105
  149.6 9.4 %collective-permute-start.33 = (bf16[64,512]{1,0:T(8,128)(2,1)S(1)}, bf16[64,512]{1,0:T(8,128)(2,1)S(1)}, u32[]{:S(2)}, u32[]{:S(2)}) collective-permute-start(bf16[64,512]{1,0:T(8,128)(2,1)S(1)} %dynamic-slice_bitcast_fusion.4), channel_id=1, source_target_pairs={{0,32},{32,0},{1,33},{33,1},{2,34},{34,2},{3,35},{35,3},{4,36},{36... | collective-permute-start | bytes 196616 | tf_op jit(solution)/shard_map/ppermute | solution.py:131
  (15 other events, 143.8 us)
Sparse Core Ops, SparseCore 0:
  21.1 50.5 all-gather.1

commit v12 on v11

--- a/solution.py
+++ b/solution.py
@@ -1,6 +1,8 @@
 import jax
 import jax.numpy as jnp
 from jax import lax
+from jax.experimental import pallas as pl
+from jax.experimental.pallas import tpu as pltpu
 from jax.sharding import Mesh
 from jax.sharding import PartitionSpec as P
 
@@ -132,6 +134,47 @@
     return jnp.stack([jnp.where(core == 0, kept, got), jnp.where(core == 0, got, kept)])
 
 
+def streamed_product(block, panel, depth):
+    rows, inner = block.shape
+    width = panel.shape[1]
+
+    def step(block_ref, panel_ref, out_ref, total):
+        k = pl.program_id(0)
+        part = jnp.dot(block_ref[...], panel_ref[...], preferred_element_type=F32)
+
+        @pl.when(k == 0)
+        def _():
+            total[...] = part
+
+        @pl.when(k > 0)
+        def _():
+            total[...] += part
+
+        @pl.when(k == pl.num_programs(0) - 1)
+        def _():
+            out_ref[...] = total[...].T.astype(BF16)
+
+    return pl.pallas_call(
+        step,
+        grid=(inner // depth,),
+        in_specs=[
+            pl.BlockSpec((rows, depth), lambda k: (0, k)),
+            pl.BlockSpec((depth, width), lambda k: (k, 0)),
+        ],
+        out_specs=pl.BlockSpec((width, rows), lambda k: (0, 0)),
+        out_shape=jax.ShapeDtypeStruct((width, rows), BF16),
+        scratch_shapes=[pltpu.VMEM((rows, width), F32)],
+        compiler_params=pltpu.CompilerParams(
+            dimension_semantics=("arbitrary",), vmem_limit_bytes=32 << 20
+        ),
+        cost_estimate=pl.CostEstimate(
+            flops=2 * rows * inner * width,
+            transcendentals=0,
+            bytes_accessed=2 * (rows * inner + inner * width + rows * width),
+        ),
+    )(block, panel)
+
+
 def body(listing, pieces, factor_inv, inverse_block, diag_inv):
     piece_rows, width = pieces.shape[1:]
     row = lax.axis_index(ROW)
@@ -143,7 +186,11 @@
         labels = (first + jnp.arange(count, dtype=jnp.int32)) // width
         return jnp.any(chosen[:, :, None] == labels[None, None, :], axis=1).astype(F32)
 
-    own_keep = keep_of((row * ZS * YS + col) * piece_rows, piece_rows)
+    first_row = (row * ZS * YS + col) * piece_rows
+    ends = jnp.stack([first_row, first_row + piece_rows - 1]) // width
+    kept = jnp.any(chosen[:, :, None] == ends[None, None, :], axis=1).astype(F32)
+    in_last = first_row + jnp.arange(piece_rows, dtype=jnp.int32) >= ends[1] * width
+    own_keep = jnp.where(in_last[None, :], kept[:, 1:], kept[:, :1])
     normed = jnp.einsum("srk,skj->srj", pieces, factor_inv, preferred_element_type=F32)
     normed = (normed * own_keep[:, :, None]).astype(BF16)
     rows = inverse_block.shape[0]
@@ -168,7 +215,7 @@
     chunks = [near[0], near[1], far_chunk(near), near[2]]
     slab_0 = lax.dynamic_slice_in_dim(panel_0, y * rows, rows, 0)
     sent_0 = along_x(slab_0, 0, (1, -1, 2))
-    partial = [partial_of(panel_0)]
+    partial = [streamed_product(inverse_block, panel_0, 512)]
 
     chunks, partial[0] = lax.optimization_barrier((chunks, partial[0]))
     across = from_root(

time: 167 us -> 169 us (1.012)
  matrix products: 11.2 us -> 5.29 us
  Pallas kernels: 0 us -> 4.91 us
  local copies, waits for them, and re-layouts: 7.73 us -> 10.7 us
    dot_general x2 -> x1, matrix products: 9.75 us -> 3.79 us  [partial_of(): jnp.einsum('qj,pq->jp', panel, inverse_block, preferred_element_type=F32)]
    pallas_call x0 -> x1, Pallas kernels: none -> 4.91 us  [streamed_product(): pl.pallas_call(step, grid=(inner // depth,), in_specs=[pl.BlockSpec((rows...]
    ppermute x2, starting transfers between devices: 12.6 us -> 10.2 us  [own_slab_of_both(): got = lax.ppermute(given, 'core', [(0, 1), (1, 0)])]
    unnamed x22 -> x18, local copies, waits for them, and re-layouts: 1.09 us -> 3.11 us
  transfers between devices with their start and end apart: 36 -> 36, of which waited for: 16 -> 16; matrix products, arithmetic and copies ran while one was open for 13% -> 9% of each run, Pallas kernels for 0% -> 3%
where the time goes in v12:
time: 169 us
  starting transfers between devices  71.9 us (43%)
  waiting for transfers between devices  50.8 us (30%)
  between operations  15.4 us (9%)
  local copies, waits for them, and re-layouts  10.7 us (6%)
  other arithmetic  9.65 us (6%)
  matrix products  5.29 us (3%)
  Pallas kernels  4.91 us (3%)
    ppermute x17, waiting for transfers between devices, shift(): lax.ppermute(array, axis, [(i, (i + by) % size) for i in range(size)])  31.2 us
    ppermute x17, starting transfers between devices, shift(): lax.ppermute(array, axis, [(i, (i + by) % size) for i in range(size)])  22.9 us
    all_to_all x1, starting transfers between devices, summed_over_col(): part = lax.all_to_all(copies, 'z', split_axis=0, concat_axis=0, tiled=True)  12.4 us
    ppermute x8, starting transfers between devices, from_root(): return lax.ppermute(array, ALL, pairs)  11.1 us
    ppermute x2, starting transfers between devices, own_slab_of_both(): got = lax.ppermute(given, 'core', [(0, 1), (1, 0)])  10.2 us
    all_gather x1, waiting for transfers between devices, panel_y_then_z(): return lax.all_gather(part, 'z', axis=0, tiled=True)  8.2 us
    ppermute x1, starting transfers between devices, pair_sum(): lax.ppermute(jnp.where(first, partial[1], partial[0]), 'core', [(0, 1), (...  7.63 us
    ppermute x6, starting transfers between devices, exchanged(): return lax.ppermute(array, axis, [(i, i ^ by) for i in range(size)])  7.53 us
  transfers between devices with their start and end apart: 36, of which 16 were waited for; matrix products, arithmetic and copies ran while one was open for 9% of the time, Pallas kernels for 3%

profile of v12, /device:TPU:1, one launch (start us, length us, event | category | flops | bytes accessed | tf_op | source)
XLA Modules:
  0.0 168.7 jit_solution(5552944507634060805)
XLA Ops:
  11.0 3.8 %collective-permute-start.1 = (bf16[96,512]{1,0:T(8,128)(2,1)S(1)}, bf16[96,512]{1,0:T(8,128)(2,1)S(1)}, u32[]{:S(2)}, u32[]{:S(2)}) collective-permute-start(bf16[96,512]{1,0:T(8,128)(2,1)S(1)} %get-tuple-element.38), channel_id=1, source_target_pairs={{0,2},{1,3},{2,0},{3,1},{4,6},{5,7},{6,4},{7,5},{8,10},{9,11},{10,... | collective-permute-start | bytes 294920 | tf_op jit(solution)/shard_map/ppermute | solution.py:19
  15.2 2.3 %collective-permute-start.2 = (bf16[96,512]{1,0:T(8,128)(2,1)S(1)}, bf16[96,512]{1,0:T(8,128)(2,1)S(1)}, u32[]{:S(2)}, u32[]{:S(2)}) collective-permute-start(bf16[96,512]{1,0:T(8,128)(2,1)S(1)} %get-tuple-element.38), channel_id=1, source_target_pairs={{0,3},{1,0},{2,1},{3,2},{4,7},{5,4},{6,5},{7,6},{8,11},{9,8},{10,9... | collective-permute-start | bytes 294920 | tf_op jit(solution)/shard_map/ppermute | solution.py:19
  17.6 3.8 %collective-permute-done = bf16[96,512]{1,0:T(8,128)(2,1)S(1)} collective-permute-done((bf16[96,512]{1,0:T(8,128)(2,1)S(1)}, bf16[96,512]{1,0:T(8,128)(2,1)S(1)}, u32[]{:S(2)}, u32[]{:S(2)}) %collective-permute-start) | collective-permute-done | bytes 98336 | tf_op jit(solution)/shard_map/ppermute | solution.py:19
  22.4 3.8 %collective-permute-start.7 = (bf16[1,96,512]{2,1,0:T(8,128)(2,1)S(1)}, bf16[1,96,512]{2,1,0:T(8,128)(2,1)S(1)}, u32[]{:S(2)}, u32[]{:S(2)}) collective-permute-start(bf16[1,96,512]{2,1,0:T(8,128)(2,1)S(1)} %get-tuple-element.37), channel_id=1, source_target_pairs={{0,28},{4,0},{8,4},{12,8},{16,12},{20,16},{24,20},{28,24},{1,29},{... | collective-permute-start | bytes 294920 | tf_op jit(solution)/shard_map/ppermute | solution.py:19
  26.5 1.7 collective-permute-done.3
  28.1 2.8 %collective-permute-start.8 = (bf16[1,96,512]{2,1,0:T(8,128)(2,1)S(1)}, bf16[1,96,512]{2,1,0:T(8,128)(2,1)S(1)}, u32[]{:S(2)}, u32[]{:S(2)}) collective-permute-start(bf16[1,96,512]{2,1,0:T(8,128)(2,1)S(1)} %collective-permute-done.7), channel_id=1, source_target_pairs={{0,28},{4,0},{8,4},{12,8},{16,12},{20,16},{24,20},{28,24},{1,29},{... | collective-permute-start | bytes 294920 | tf_op jit(solution)/shard_map/ppermute | solution.py:19
  30.9 1.9 %collective-permute-done.4 = bf16[1,96,512]{2,1,0:T(8,128)(2,1)S(1)} collective-permute-done((bf16[1,96,512]{2,1,0:T(8,128)(2,1)S(1)}, bf16[1,96,512]{2,1,0:T(8,128)(2,1)S(1)}, u32[]{:S(2)}, u32[]{:S(2)}) %collective-permute-start.4) | collective-permute-done | bytes 98336 | tf_op jit(solution)/shard_map/ppermute | solution.py:19
  32.8 2.8 %collective-permute-start.9 = (bf16[1,96,512]{2,1,0:T(8,128)(2,1)S(1)}, bf16[1,96,512]{2,1,0:T(8,128)(2,1)S(1)}, u32[]{:S(2)}, u32[]{:S(2)}) collective-permute-start(bf16[1,96,512]{2,1,0:T(8,128)(2,1)S(1)} %collective-permute-done.8), channel_id=1, source_target_pairs={{0,28},{4,0},{8,4},{12,8},{16,12},{20,16},{24,20},{28,24},{1,29},{... | collective-permute-start | bytes 294920 | tf_op jit(solution)/shard_map/ppermute | solution.py:19
  35.6 1.9 %collective-permute-done.5 = bf16[1,96,512]{2,1,0:T(8,128)(2,1)S(1)} collective-permute-done((bf16[1,96,512]{2,1,0:T(8,128)(2,1)S(1)}, bf16[1,96,512]{2,1,0:T(8,128)(2,1)S(1)}, u32[]{:S(2)}, u32[]{:S(2)}) %collective-permute-start.5) | collective-permute-done | bytes 98336 | tf_op jit(solution)/shard_map/ppermute | solution.py:19
  37.5 7.8 %collective-permute-done.6 = bf16[1,96,512]{2,1,0:T(8,128)(2,1)S(1)} collective-permute-done((bf16[1,96,512]{2,1,0:T(8,128)(2,1)S(1)}, bf16[1,96,512]{2,1,0:T(8,128)(2,1)S(1)}, u32[]{:S(2)}, u32[]{:S(2)}) %collective-permute-start.6) | collective-permute-done | bytes 98336 | tf_op jit(solution)/shard_map/ppermute | solution.py:19
  45.4 1.9 %collective-permute-start.10 = (bf16[8,1,96,512]{3,2,1,0:T(8,128)(2,1)S(1)}, bf16[8,1,96,512]{3,2,1,0:T(8,128)(2,1)}, u32[]{:S(2)}, u32[]{:S(2)}) collective-permute-start(bf16[8,1,96,512]{3,2,1,0:T(8,128)(2,1)S(1)} %bitcast_dynamic-update-slice_fusion), channel_id=1, source_target_pairs={{0,1},{1,2},{2,3},{3,0},{4,5},{5,6},{6,7},{7,4},{8,9},{9,10},{10,1... | collective-permute-start | bytes 2359304 | tf_op jit(solution)/shard_map/ppermute | solution.py:19
  50.6 7.6 %collective-permute-done.10 = bf16[8,1,96,512]{3,2,1,0:T(8,128)(2,1)} collective-permute-done((bf16[8,1,96,512]{3,2,1,0:T(8,128)(2,1)S(1)}, bf16[8,1,96,512]{3,2,1,0:T(8,128)(2,1)}, u32[]{:S(2)}, u32[]{:S(2)}) %collective-permute-start.10) | collective-permute-done | bytes 786464 | tf_op jit(solution)/shard_map/ppermute | solution.py:19
  60.2 1.6 collective-permute-start.20
  64.8 8.2 %all-gather.2.cloned.1.call-done.panel_ref = bf16[3072,512]{1,0:T(8,128)(2,1)} async-done(((bf16[384,512]{1,0:T(8,128)(2,1)}), bf16[3072,512]{1,0:T(8,128)(2,1)}) %all-gather.2.cloned.1.call-update) | async-done | bytes 3145744 | tf_op jit(solution)/shard_map/all_gather | solution.py:55
  74.2 2.3 %collective-permute-start.13 = (bf16[4,1,96,512]{3,2,1,0:T(8,128)(2,1)S(1)}, bf16[4,1,96,512]{3,2,1,0:T(8,128)(2,1)S(1)}, u32[]{:S(2)}, u32[]{:S(2)}) collective-permute-start(bf16[4,1,96,512]{3,2,1,0:T(8,128)(2,1)S(1)} %slice.37), channel_id=1, source_target_pairs={{0,3},{1,0},{2,1},{3,2},{4,7},{5,4},{6,5},{7,6},{8,11},{9,8},{10,9... | collective-permute-start | bytes 1179656 | tf_op jit(solution)/shard_map/ppermute | solution.py:19
  76.5 2.6 %broadcast_select_fusion = (bf16[768,512]{1,0:T(8,128)(2,1)}, bf16[768,512]{1,0:T(8,128)(2,1)}) fusion(pred[]{:T(512)S(6)} %eq.63, bf16[2,4,96,512]{3,2,1,0:T(8,128)(2,1)S(1)} %dynamic-slice_dynamic-update-slice_fusion, bf16[3072,512]{1,0:T(8,128)(2,1)} %all-gather.2.cloned.1.call-done.panel_ref, s32[]{:T(128)S(6)} %select_n.308), kind=kLoop, calls=%fused_computation.8 | loop fusion | flops 393216 | bytes 3145733 | tf_op jit(solution)/shard_map/jit(_where)/select_n | solution.py:222
  79.2 2.3 %copy-done.2 = bf16[768,3072]{1,0:T(8,128)(2,1)S(1)} copy-done((bf16[768,3072]{1,0:T(8,128)(2,1)S(1)}, bf16[768,3072]{1,0:T(8,128)(2,1)}, u32[]{:S(2)}) %copy-start.2) | copy-done | bytes 4718616
  81.5 4.9 %shard_map.68 = bf16[512,768]{1,0:T(8,128)(2,1)S(1)} custom-call(bf16[768,3072]{1,0:T(8,128)(2,1)S(1)} %copy-done.2, bf16[3072,512]{1,0:T(8,128)(2,1)S(1)} %copy-done.1), custom_call_target="tpu_custom_call" | custom-call | flops 2415919104 | bytes 8650752 | tf_op jit(solution)/shard_map/pallas_call | solution.py:157
  88.0 1.6 collective-permute-start.17
  93.5 3.8 %broadcast_select_fusion.1 = (bf16[512,768]{1,0:T(8,128)(2,1)}, bf16[512,768]{1,0:T(8,128)(2,1)}) fusion(bf16[512,768]{1,0:T(8,128)(2,1)S(1)} %shard_map.68, pred[]{:T(512)S(6)} %eq.63, bf16[3072,512]{1,0:T(8,128)(2,1)S(1)} %bitcast.97, bf16[768,3072]{1,0:T(8,128)(2,1)S(1)} %copy-done.2), kind=kOutput, calls=%fused_computation.9 | convolution fusion | flops 2416705536 | bytes 10223617 | tf_op jit(solution)/shard_map/qj,pq->jp/dot_general | solution.py:199
  97.3 7.6 %collective-permute-start.14 = (bf16[512,768]{1,0:T(8,128)(2,1)}, bf16[512,768]{1,0:T(8,128)(2,1)}, u32[]{:S(2)}, u32[]{:S(2)}) collective-permute-start(bf16[512,768]{1,0:T(8,128)(2,1)} %get-tuple-element.42), channel_id=1, source_target_pairs={{0,32},{32,0},{1,33},{33,1},{2,34},{34,2},{3,35},{35,3},{4,36},{36... | collective-permute-start | bytes 2359304 | tf_op jit(solution)/shard_map/ppermute | solution.py:92
  105.0 2.7 %add_select_fusion = bf16[768,512]{1,0:T(8,128)(2,1)S(1)} fusion(bf16[768,512]{1,0:T(8,128)(2,1)} %collective-permute-done.22, bf16[768,512]{1,0:T(8,128)(2,1)} %collective-permute-done.21, bf16[768,512]{1,0:T(8,128)(2,1)} %collective-permute-done.19, bf16[768,512]{1,0:T(8,128)(2,1)} %collective-permute-done.20, bf16[768,512]{1,0:T(8,128)(2,1)} %collective-permute-done.18, ...), kind=kLoop, calls=%fused_computation.7 | loop fusion | flops 3145728 | bytes 7864322 | tf_op jit(solution)/shard_map/jit(_where)/select_n | solution.py:227
  111.0 4.4 %collective-permute-done.23 = bf16[128,768]{1,0:T(8,128)(2,1)S(1)} collective-permute-done((bf16[128,768]{1,0:T(8,128)(2,1)S(1)}, bf16[128,768]{1,0:T(8,128)(2,1)S(1)}, u32[]{:S(2)}, u32[]{:S(2)}) %collective-permute-start.23) | collective-permute-done | bytes 196640 | tf_op jit(solution)/shard_map/ppermute | solution.py:19
  115.4 2.0 %collective-permute-done.24 = bf16[128,768]{1,0:T(8,128)(2,1)S(1)} collective-permute-done((bf16[128,768]{1,0:T(8,128)(2,1)S(1)}, bf16[128,768]{1,0:T(8,128)(2,1)S(1)}, u32[]{:S(2)}, u32[]{:S(2)}) %collective-permute-start.24) | collective-permute-done | bytes 196640 | tf_op jit(solution)/shard_map/ppermute | solution.py:19
  119.1 1.9 %collective-permute-start.29 = (bf16[32,512]{1,0:T(8,128)(2,1)S(1)}, bf16[32,512]{1,0:T(8,128)(2,1)S(1)}, u32[]{:S(2)}, u32[]{:S(2)}) collective-permute-start(bf16[32,512]{1,0:T(8,128)(2,1)S(1)} %get-tuple-element.40), channel_id=1, source_target_pairs={{0,3},{1,2},{2,1},{3,0},{4,7},{5,6},{6,5},{7,4},{8,11},{9,10},{10,... | collective-permute-start | bytes 98312 | tf_op jit(solution)/shard_map/ppermute | solution.py:107
  123.1 2.2 %collective-permute-done.28 = bf16[32,512]{1,0:T(8,128)(2,1)S(1)} collective-permute-done((bf16[32,512]{1,0:T(8,128)(2,1)S(1)}, bf16[32,512]{1,0:T(8,128)(2,1)S(1)}, u32[]{:S(2)}, u32[]{:S(2)}) %collective-permute-start.28) | collective-permute-done | bytes 32800 | tf_op jit(solution)/shard_map/ppermute | solution.py:107
  126.0 12.4 %all-to-all-start = ((bf16[8,32,512]{2,1,0:T(8,128)(2,1)}), bf16[8,32,512]{2,1,0:T(8,128)(2,1)S(1)}, u32[]{:S(2)}, u32[]{:S(2)}) async-start(bf16[8,32,512]{2,1,0:T(8,128)(2,1)} %broadcast_in_dim.96), calls=%async_computation | async-start | bytes 524288 | tf_op jit(solution)/shard_map/all_to_all | solution.py:119
  138.4 3.5 %collective-permute-start.26 = (bf16[64,768]{1,0:T(8,128)(2,1)S(1)}, bf16[64,768]{1,0:T(8,128)(2,1)S(1)}, u32[]{:S(2)}, u32[]{:S(2)}) collective-permute-start(bf16[64,768]{1,0:T(8,128)(2,1)S(1)} %dynamic-slice_bitcast_fusion.3), channel_id=1, source_target_pairs={{0,32},{32,0},{1,33},{33,1},{2,34},{34,2},{3,35},{35,3},{4,36},{36... | collective-permute-start | bytes 294920 | tf_op jit(solution)/shard_map/ppermute | solution.py:133
  142.9 4.9 %all-to-all-done = bf16[8,32,512]{2,1,0:T(8,128)(2,1)S(1)} async-done(((bf16[8,32,512]{2,1,0:T(8,128)(2,1)}), bf16[8,32,512]{2,1,0:T(8,128)(2,1)S(1)}, u32[]{:S(2)}, u32[]{:S(2)}) %all-to-all-start) | async-done | bytes 262176 | tf_op jit(solution)/shard_map/all_to_all | solution.py:119
  148.1 2.5 %collective-permute-start.31 = (bf16[32,512]{1,0:T(8,128)(2,1)S(1)}, bf16[32,512]{1,0:T(8,128)(2,1)S(1)}, u32[]{:S(2)}, u32[]{:S(2)}) collective-permute-start(bf16[32,512]{1,0:T(8,128)(2,1)S(1)} %reduce_sum.12), channel_id=1, source_target_pairs={{0,2},{1,3},{2,0},{3,1},{4,6},{5,7},{6,4},{7,5},{8,10},{9,11},{10,... | collective-permute-start | bytes 98312 | tf_op jit(solution)/shard_map/ppermute | solution.py:107
  151.3 2.1 %collective-permute-done.30 = bf16[32,512]{1,0:T(8,128)(2,1)S(1)} collective-permute-done((bf16[32,512]{1,0:T(8,128)(2,1)S(1)}, bf16[32,512]{1,0:T(8,128)(2,1)S(1)}, u32[]{:S(2)}, u32[]{:S(2)}) %collective-permute-start.30) | collective-permute-done | bytes 32800 | tf_op jit(solution)/shard_map/ppermute | solution.py:107
  153.4 6.7 %collective-permute-start.33 = (bf16[64,512]{1,0:T(8,128)(2,1)S(1)}, bf16[64,512]{1,0:T(8,128)(2,1)S(1)}, u32[]{:S(2)}, u32[]{:S(2)}) collective-permute-start(bf16[64,512]{1,0:T(8,128)(2,1)S(1)} %dynamic-slice_bitcast_fusion.4), channel_id=1, source_target_pairs={{0,32},{32,0},{1,33},{33,1},{2,34},{34,2},{3,35},{35,3},{4,36},{36... | collective-permute-start | bytes 196616 | tf_op jit(solution)/shard_map/ppermute | solution.py:133
  (121 shorter events, 30.9 us)
Async XLA Ops:
  7.2 65.8 %all-gather.2.cloned.1.call-start = ((), (), s32[]{:S(2)}) async-start(), calls=%async_computation.1 | async-start | bytes 3538944 | tf_op jit(solution)/shard_map/all_gather | solution.py:55
  11.0 10.5 %collective-permute-start.1 = (bf16[96,512]{1,0:T(8,128)(2,1)S(1)}, bf16[96,512]{1,0:T(8,128)(2,1)S(1)}, u32[]{:S(2)}, u32[]{:S(2)}) collective-permute-start(bf16[96,512]{1,0:T(8,128)(2,1)S(1)} %get-tuple-element.38), channel_id=1, source_target_pairs={{0,2},{1,3},{2,0},{3,1},{4,6},{5,7},{6,4},{7,5},{8,10},{9,11},{10,... | collective-permute-start | bytes 294920 | tf_op jit(solution)/shard_map/ppermute | solution.py:19
  14.8 6.6 %collective-permute-start = (bf16[96,512]{1,0:T(8,128)(2,1)S(1)}, bf16[96,512]{1,0:T(8,128)(2,1)S(1)}, u32[]{:S(2)}, u32[]{:S(2)}) collective-permute-start(bf16[96,512]{1,0:T(8,128)(2,1)S(1)} %get-tuple-element.38), channel_id=1, source_target_pairs={{0,1},{1,2},{2,3},{3,0},{4,5},{5,6},{6,7},{7,4},{8,9},{9,10},{10,1... | collective-permute-start | bytes 294920 | tf_op jit(solution)/shard_map/ppermute | solution.py:19
  15.2 6.3 %collective-permute-start.2 = (bf16[96,512]{1,0:T(8,128)(2,1)S(1)}, bf16[96,512]{1,0:T(8,128)(2,1)S(1)}, u32[]{:S(2)}, u32[]{:S(2)}) collective-permute-start(bf16[96,512]{1,0:T(8,128)(2,1)S(1)} %get-tuple-element.38), channel_id=1, source_target_pairs={{0,3},{1,0},{2,1},{3,2},{4,7},{5,4},{6,5},{7,6},{8,11},{9,8},{10,9... | collective-permute-start | bytes 294920 | tf_op jit(solution)/shard_map/ppermute | solution.py:19
  22.3 5.9 %collective-permute-start.3 = (bf16[1,96,512]{2,1,0:T(8,128)(2,1)S(1)}, bf16[1,96,512]{2,1,0:T(8,128)(2,1)S(1)}, u32[]{:S(2)}, u32[]{:S(2)}) collective-permute-start(bf16[1,96,512]{2,1,0:T(8,128)(2,1)S(1)} %get-tuple-element.37), channel_id=1, source_target_pairs={{0,4},{4,8},{8,12},{12,16},{16,20},{20,24},{24,28},{28,0},{1,5},{5... | collective-permute-start | bytes 294920 | tf_op jit(solution)/shard_map/ppermute | solution.py:19
  22.4 5.8 %collective-permute-start.7 = (bf16[1,96,512]{2,1,0:T(8,128)(2,1)S(1)}, bf16[1,96,512]{2,1,0:T(8,128)(2,1)S(1)}, u32[]{:S(2)}, u32[]{:S(2)}) collective-permute-start(bf16[1,96,512]{2,1,0:T(8,128)(2,1)S(1)} %get-tuple-element.37), channel_id=1, source_target_pairs={{0,28},{4,0},{8,4},{12,8},{16,12},{20,16},{24,20},{28,24},{1,29},{... | collective-permute-start | bytes 294920 | tf_op jit(solution)/shard_map/ppermute | solution.py:19
  28.1 4.7 %collective-permute-start.4 = (bf16[1,96,512]{2,1,0:T(8,128)(2,1)S(1)}, bf16[1,96,512]{2,1,0:T(8,128)(2,1)S(1)}, u32[]{:S(2)}, u32[]{:S(2)}) collective-permute-start(bf16[1,96,512]{2,1,0:T(8,128)(2,1)S(1)} %collective-permute-done.3), channel_id=1, source_target_pairs={{0,4},{4,8},{8,12},{12,16},{16,20},{20,24},{24,28},{28,0},{1,5},{5... | collective-permute-start | bytes 294920 | tf_op jit(solution)/shard_map/ppermute | solution.py:19
  28.1 4.7 %collective-permute-start.8 = (bf16[1,96,512]{2,1,0:T(8,128)(2,1)S(1)}, bf16[1,96,512]{2,1,0:T(8,128)(2,1)S(1)}, u32[]{:S(2)}, u32[]{:S(2)}) collective-permute-start(bf16[1,96,512]{2,1,0:T(8,128)(2,1)S(1)} %collective-permute-done.7), channel_id=1, source_target_pairs={{0,28},{4,0},{8,4},{12,8},{16,12},{20,16},{24,20},{28,24},{1,29},{... | collective-permute-start | bytes 294920 | tf_op jit(solution)/shard_map/ppermute | solution.py:19
  32.8 4.7 %collective-permute-start.5 = (bf16[1,96,512]{2,1,0:T(8,128)(2,1)S(1)}, bf16[1,96,512]{2,1,0:T(8,128)(2,1)S(1)}, u32[]{:S(2)}, u32[]{:S(2)}) collective-permute-start(bf16[1,96,512]{2,1,0:T(8,128)(2,1)S(1)} %collective-permute-done.4), channel_id=1, source_target_pairs={{0,4},{4,8},{8,12},{12,16},{16,20},{20,24},{24,28},{28,0},{1,5},{5... | collective-permute-start | bytes 294920 | tf_op jit(solution)/shard_map/ppermute | solution.py:19
  32.8 12.6 %collective-permute-start.9 = (bf16[1,96,512]{2,1,0:T(8,128)(2,1)S(1)}, bf16[1,96,512]{2,1,0:T(8,128)(2,1)S(1)}, u32[]{:S(2)}, u32[]{:S(2)}) collective-permute-start(bf16[1,96,512]{2,1,0:T(8,128)(2,1)S(1)} %collective-permute-done.8), channel_id=1, source_target_pairs={{0,28},{4,0},{8,4},{12,8},{16,12},{20,16},{24,20},{28,24},{1,29},{... | collective-permute-start | bytes 294920 | tf_op jit(solution)/shard_map/ppermute | solution.py:19
  37.5 7.9 %collective-permute-start.6 = (bf16[1,96,512]{2,1,0:T(8,128)(2,1)S(1)}, bf16[1,96,512]{2,1,0:T(8,128)(2,1)S(1)}, u32[]{:S(2)}, u32[]{:S(2)}) collective-permute-start(bf16[1,96,512]{2,1,0:T(8,128)(2,1)S(1)} %collective-permute-done.5), channel_id=1, source_target_pairs={{0,4},{4,8},{8,12},{12,16},{16,20},{20,24},{24,28},{28,0},{1,5},{5... | collective-permute-start | bytes 294920 | tf_op jit(solution)/shard_map/ppermute | solution.py:19
  45.4 12.7 %collective-permute-start.10 = (bf16[8,1,96,512]{3,2,1,0:T(8,128)(2,1)S(1)}, bf16[8,1,96,512]{3,2,1,0:T(8,128)(2,1)}, u32[]{:S(2)}, u32[]{:S(2)}) collective-permute-start(bf16[8,1,96,512]{3,2,1,0:T(8,128)(2,1)S(1)} %bitcast_dynamic-update-slice_fusion), channel_id=1, source_target_pairs={{0,1},{1,2},{2,3},{3,0},{4,5},{5,6},{6,7},{7,4},{8,9},{9,10},{10,1... | collective-permute-start | bytes 2359304 | tf_op jit(solution)/shard_map/ppermute | solution.py:19
  47.3 12.8 %collective-permute-start.11 = (bf16[8,1,96,512]{3,2,1,0:T(8,128)(2,1)S(1)}, bf16[8,1,96,512]{3,2,1,0:T(8,128)(2,1)S(1)}, u32[]{:S(2)}, u32[]{:S(2)}) collective-permute-start(bf16[8,1,96,512]{3,2,1,0:T(8,128)(2,1)S(1)} %bitcast_dynamic-update-slice_fusion), channel_id=1, source_target_pairs={{0,3},{1,0},{2,1},{3,2},{4,7},{5,4},{6,5},{7,6},{8,11},{9,8},{10,9... | collective-permute-start | bytes 2359304 | tf_op jit(solution)/shard_map/ppermute | solution.py:19
  49.3 9.9 %collective-permute-start.15 = (bf16[2,1,96,512]{3,2,1,0:T(8,128)(2,1)}, bf16[2,1,96,512]{3,2,1,0:T(8,128)(2,1)}, u32[]{:S(2)}, u32[]{:S(2)}) collective-permute-start(bf16[2,1,96,512]{3,2,1,0:T(8,128)(2,1)} %get-tuple-element.31), channel_id=1, source_target_pairs={{0,2},{1,3},{2,0},{3,1},{36,38},{37,39},{38,36},{39,37},{72,74},{7... | collective-permute-start | bytes 589832 | tf_op jit(solution)/shard_map/ppermute | solution.py:83
  60.2 31.3 %collective-permute-start.20 = (bf16[768,512]{1,0:T(8,128)(2,1)S(1)}, bf16[768,512]{1,0:T(8,128)(2,1)}, u32[]{:S(2)}, u32[]{:S(2)}) collective-permute-start(bf16[768,512]{1,0:T(8,128)(2,1)S(1)} %bitcast.94), channel_id=1, source_target_pairs={{0,224},{1,225},{2,226},{3,227},{36,228},{37,229},{38,230},{39,231... | collective-permute-start | bytes 2359304 | tf_op jit(solution)/shard_map/ppermute | solution.py:83
  61.7 30.5 %collective-permute-start.19 = (bf16[768,512]{1,0:T(8,128)(2,1)S(1)}, bf16[768,512]{1,0:T(8,128)(2,1)}, u32[]{:S(2)}, u32[]{:S(2)}) collective-permute-start(bf16[768,512]{1,0:T(8,128)(2,1)S(1)} %bitcast.95), channel_id=1, source_target_pairs={{0,96},{1,97},{2,98},{3,99},{36,100},{37,101},{38,102},{39,103},{7... | collective-permute-start | bytes 2359304 | tf_op jit(solution)/shard_map/ppermute | solution.py:83
  63.3 34.1 %collective-permute-start.21 = (bf16[768,512]{1,0:T(8,128)(2,1)S(1)}, bf16[768,512]{1,0:T(8,128)(2,1)}, u32[]{:S(2)}, u32[]{:S(2)}) collective-permute-start(bf16[768,512]{1,0:T(8,128)(2,1)S(1)} %bitcast.96), channel_id=1, source_target_pairs={{0,160},{1,161},{2,162},{3,163},{36,164},{37,165},{38,166},{39,167... | collective-permute-start | bytes 2359304 | tf_op jit(solution)/shard_map/ppermute | solution.py:83
  74.2 12.2 %collective-permute-start.13 = (bf16[4,1,96,512]{3,2,1,0:T(8,128)(2,1)S(1)}, bf16[4,1,96,512]{3,2,1,0:T(8,128)(2,1)S(1)}, u32[]{:S(2)}, u32[]{:S(2)}) collective-permute-start(bf16[4,1,96,512]{3,2,1,0:T(8,128)(2,1)S(1)} %slice.37), channel_id=1, source_target_pairs={{0,3},{1,0},{2,1},{3,2},{4,7},{5,4},{6,5},{7,6},{8,11},{9,8},{10,9... | collective-permute-start | bytes 1179656 | tf_op jit(solution)/shard_map/ppermute | solution.py:19
  76.5 11.5 %collective-permute-start.12 = (bf16[4,1,96,512]{3,2,1,0:T(8,128)(2,1)S(1)}, bf16[4,1,96,512]{3,2,1,0:T(8,128)(2,1)S(1)}, u32[]{:S(2)}, u32[]{:S(2)}) collective-permute-start(bf16[4,1,96,512]{3,2,1,0:T(8,128)(2,1)S(1)} %slice.36), channel_id=1, source_target_pairs={{0,1},{1,2},{2,3},{3,0},{4,5},{5,6},{6,7},{7,4},{8,9},{9,10},{10,1... | collective-permute-start | bytes 1179656 | tf_op jit(solution)/shard_map/ppermute | solution.py:19
  86.4 18.5 %collective-permute-start.18 = (bf16[768,512]{1,0:T(8,128)(2,1)}, bf16[768,512]{1,0:T(8,128)(2,1)}, u32[]{:S(2)}, u32[]{:S(2)}) collective-permute-start(bf16[768,512]{1,0:T(8,128)(2,1)} %get-tuple-element.27), channel_id=1, source_target_pairs={{0,128},{1,129},{2,130},{3,131},{36,132},{37,133},{38,134},{39,135... | collective-permute-start | bytes 2359304 | tf_op jit(solution)/shard_map/ppermute | solution.py:83
  88.0 17.0 %collective-permute-start.17 = (bf16[768,512]{1,0:T(8,128)(2,1)}, bf16[768,512]{1,0:T(8,128)(2,1)}, u32[]{:S(2)}, u32[]{:S(2)}) collective-permute-start(bf16[768,512]{1,0:T(8,128)(2,1)} %get-tuple-element.27), channel_id=1, source_target_pairs={{0,192},{1,193},{2,194},{3,195},{36,196},{37,197},{38,198},{39,199... | collective-permute-start | bytes 2359304 | tf_op jit(solution)/shard_map/ppermute | solution.py:83
  91.5 13.5 %collective-permute-start.16 = (bf16[768,512]{1,0:T(8,128)(2,1)}, bf16[768,512]{1,0:T(8,128)(2,1)S(1)}, u32[]{:S(2)}, u32[]{:S(2)}) collective-permute-start(bf16[768,512]{1,0:T(8,128)(2,1)} %get-tuple-element.27), channel_id=1, source_target_pairs={{0,64},{1,65},{2,66},{3,67},{36,68},{37,69},{38,70},{39,71},{72,13... | collective-permute-start | bytes 2359304 | tf_op jit(solution)/shard_map/ppermute | solution.py:83
  92.2 12.7 %collective-permute-start.22 = (bf16[768,512]{1,0:T(8,128)(2,1)}, bf16[768,512]{1,0:T(8,128)(2,1)}, u32[]{:S(2)}, u32[]{:S(2)}) collective-permute-start(bf16[768,512]{1,0:T(8,128)(2,1)} %get-tuple-element.26), channel_id=1, source_target_pairs={{0,32},{1,33},{2,34},{3,35},{36,4},{37,5},{38,6},{39,7},{72,104},{... | collective-permute-start | bytes 2359304 | tf_op jit(solution)/shard_map/ppermute | solution.py:83
  97.3 10.4 %collective-permute-start.14 = (bf16[512,768]{1,0:T(8,128)(2,1)}, bf16[512,768]{1,0:T(8,128)(2,1)}, u32[]{:S(2)}, u32[]{:S(2)}) collective-permute-start(bf16[512,768]{1,0:T(8,128)(2,1)} %get-tuple-element.42), channel_id=1, source_target_pairs={{0,32},{32,0},{1,33},{33,1},{2,34},{34,2},{3,35},{35,3},{4,36},{36... | collective-permute-start | bytes 2359304 | tf_op jit(solution)/shard_map/ppermute | solution.py:92
  109.2 6.2 %collective-permute-start.23 = (bf16[128,768]{1,0:T(8,128)(2,1)S(1)}, bf16[128,768]{1,0:T(8,128)(2,1)S(1)}, u32[]{:S(2)}, u32[]{:S(2)}) collective-permute-start(bf16[128,768]{1,0:T(8,128)(2,1)S(1)} %get-tuple-element.28), channel_id=1, source_target_pairs={{0,128},{64,192},{128,0},{192,64},{1,129},{65,193},{129,1},{193,65... | collective-permute-start | bytes 589832 | tf_op jit(solution)/shard_map/ppermute | solution.py:19
  109.3 6.1 %collective-permute-start.25 = (bf16[128,768]{1,0:T(8,128)(2,1)S(1)}, bf16[128,768]{1,0:T(8,128)(2,1)S(1)}, u32[]{:S(2)}, u32[]{:S(2)}) collective-permute-start(bf16[128,768]{1,0:T(8,128)(2,1)S(1)} %get-tuple-element.29), channel_id=1, source_target_pairs={{0,192},{64,0},{128,64},{192,128},{1,193},{65,1},{129,65},{193,129... | collective-permute-start | bytes 589832 | tf_op jit(solution)/shard_map/ppermute | solution.py:19
  109.4 8.0 %collective-permute-start.24 = (bf16[128,768]{1,0:T(8,128)(2,1)S(1)}, bf16[128,768]{1,0:T(8,128)(2,1)S(1)}, u32[]{:S(2)}, u32[]{:S(2)}) collective-permute-start(bf16[128,768]{1,0:T(8,128)(2,1)S(1)} %get-tuple-element.30), channel_id=1, source_target_pairs={{0,64},{64,128},{128,192},{192,0},{1,65},{65,129},{129,193},{193,1... | collective-permute-start | bytes 589832 | tf_op jit(solution)/shard_map/ppermute | solution.py:19
  126.0 21.8 %all-to-all-start = ((bf16[8,32,512]{2,1,0:T(8,128)(2,1)}), bf16[8,32,512]{2,1,0:T(8,128)(2,1)S(1)}, u32[]{:S(2)}, u32[]{:S(2)}) async-start(bf16[8,32,512]{2,1,0:T(8,128)(2,1)} %broadcast_in_dim.96), calls=%async_computation | async-start | bytes 524288 | tf_op jit(solution)/shard_map/all_to_all | solution.py:119
  138.4 4.5 %collective-permute-start.26 = (bf16[64,768]{1,0:T(8,128)(2,1)S(1)}, bf16[64,768]{1,0:T(8,128)(2,1)S(1)}, u32[]{:S(2)}, u32[]{:S(2)}) collective-permute-start(bf16[64,768]{1,0:T(8,128)(2,1)S(1)} %dynamic-slice_bitcast_fusion.3), channel_id=1, source_target_pairs={{0,32},{32,0},{1,33},{33,1},{2,34},{34,2},{3,35},{35,3},{4,36},{36... | collective-permute-start | bytes 294920 | tf_op jit(solution)/shard_map/ppermute | solution.py:133
  147.9 5.5 %collective-permute-start.32 = (bf16[32,512]{1,0:T(8,128)(2,1)S(1)}, bf16[32,512]{1,0:T(8,128)(2,1)S(1)}, u32[]{:S(2)}, u32[]{:S(2)}) collective-permute-start(bf16[32,512]{1,0:T(8,128)(2,1)S(1)} %reduce_sum.12), channel_id=1, source_target_pairs={{0,3},{1,2},{2,1},{3,0},{4,7},{5,6},{6,5},{7,4},{8,11},{9,10},{10,... | collective-permute-start | bytes 98312 | tf_op jit(solution)/shard_map/ppermute | solution.py:107
  148.1 5.3 %collective-permute-start.31 = (bf16[32,512]{1,0:T(8,128)(2,1)S(1)}, bf16[32,512]{1,0:T(8,128)(2,1)S(1)}, u32[]{:S(2)}, u32[]{:S(2)}) collective-permute-start(bf16[32,512]{1,0:T(8,128)(2,1)S(1)} %reduce_sum.12), channel_id=1, source_target_pairs={{0,2},{1,3},{2,0},{3,1},{4,6},{5,7},{6,4},{7,5},{8,10},{9,11},{10,... | collective-permute-start | bytes 98312 | tf_op jit(solution)/shard_map/ppermute | solution.py:107
  153.4 7.6 %collective-permute-start.33 = (bf16[64,512]{1,0:T(8,128)(2,1)S(1)}, bf16[64,512]{1,0:T(8,128)(2,1)S(1)}, u32[]{:S(2)}, u32[]{:S(2)}) collective-permute-start(bf16[64,512]{1,0:T(8,128)(2,1)S(1)} %dynamic-slice_bitcast_fusion.4), channel_id=1, source_target_pairs={{0,32},{32,0},{1,33},{33,1},{2,34},{34,2},{3,35},{35,3},{4,36},{36... | collective-permute-start | bytes 196616 | tf_op jit(solution)/shard_map/ppermute | solution.py:133
  (13 other events, 102.7 us)
Sparse Core Ops, SparseCore 0:
  22.4 50.5 all-gather.1

commit v13 on v8

--- a/solution.py
+++ b/solution.py
@@ -53,15 +53,17 @@
     return lax.all_gather(part, "z", axis=0, tiled=True)
 
 
-def near_z_then_y(piece):
-    part = placed_by_owner(relay_ring(piece[None], "z", ZS, False), lax.axis_index("z"), 0)[:, None]
-    return [part, shift(part, "y", YS, 1), shift(part, "y", YS, -1)]
-
-
-def far_chunk(near):
-    half = near[0].shape[0] // 2
-    right = shift(near[1][:half], "y", YS, 1)
-    return jnp.concatenate([right, shift(near[2][half:], "y", YS, -1)], axis=0)
+def batches_of(ring):
+    early = jnp.concatenate([ring[d] for d in (2, 1, 0, 7, 6)], axis=0)
+    return early, jnp.concatenate([ring[d] for d in (5, 4, 3)], axis=0)
+
+
+def by_place(early, late):
+    z = lax.axis_index("z")
+    long = jnp.zeros((ZS + 4, *early.shape[1:]), early.dtype)
+    long = lax.dynamic_update_slice_in_dim(long, early, (z - 2) % ZS, 0)
+    long = lax.dynamic_update_slice_in_dim(long, late, (z + 3) % ZS, 0)
+    return jnp.concatenate([long[:4] + long[ZS:], long[4:ZS]], axis=0)
 
 
 def device(x, core, z, y):
@@ -152,7 +154,9 @@
         return jnp.einsum("qj,pq->jp", panel, inverse_block, preferred_element_type=F32).astype(BF16)
 
     first = core == 0
-    near = near_z_then_y(normed[1])
+    runs = [run[:, None] for run in batches_of(relay_ring(normed[1][None], "z", ZS, False))]
+    right, left = [[shift(run, "y", YS, by) for run in runs] for by in (1, -1)]
+    near = [by_place(*runs), by_place(*right), by_place(*left)]
 
     deep = rows // (piece_rows * YS)
     of_slab = lambda part, lane: lax.dynamic_slice_in_dim(part, lane * deep, deep, 0)
@@ -164,24 +168,23 @@
     sent_1 = along_x(slab_1, 1, (1, -1, -2))
 
     panel_0 = panel_y_then_z(normed[0])
-    panel_0, near = lax.optimization_barrier((panel_0, near))
-    chunks = [near[0], near[1], far_chunk(near), near[2]]
+    far = by_place(shift(right[0], "y", YS, 1), shift(left[1], "y", YS, -1))
+    panel_1 = placed_by_owner([near[0], near[1], far, near[2]], y, 1)
+    partial_1 = partial_of(panel_1.reshape(-1, width))
+    panel_0, partial_1, slab_1, sent_1[:2] = lax.optimization_barrier(
+        (panel_0, partial_1, slab_1, sent_1[:2])
+    )
     slab_0 = lax.dynamic_slice_in_dim(panel_0, y * rows, rows, 0)
     sent_0 = along_x(slab_0, 0, (1, -1, 2))
-    partial = [partial_of(panel_0)]
-
-    chunks, partial[0], sent_1 = lax.optimization_barrier((chunks, partial[0], sent_1))
     across = from_root(
         jnp.where(first, slab_1, slab_0), lambda x, c, z, y: (x, 1 - c, z, y)
     )
-    partial.append(partial_of(placed_by_owner(chunks, y, 1).reshape(panel_0.shape)))
-
-    partial[1], sent_0[:2] = lax.optimization_barrier((partial[1], sent_0[:2]))
-    pair = lax.optimization_barrier(pair_sum(partial))
-    sent = [*sent_1, *sent_0, across]
+    partial = [partial_of(panel_0), partial_1]
+
     home = row == z
     slab = jnp.where(first, slab_0, slab_1)
-    factor_slab = sum(sent, jnp.where(home, slab, jnp.zeros((), BF16)))
+    factor_slab = jnp.where(home, slab, sum([*sent_0, *sent_1], across))
+    pair = lax.optimization_barrier(pair_sum(partial))
     product = sum_over_x(pair)
     col_keep = lax.dynamic_index_in_dim(keep_of(col * rows, rows), core, 0)
     offdiag = lax.optimization_barrier((-(product * col_keep)).astype(BF16))

time: 170 us -> 186 us (1.094)
  starting transfers between devices: 76.1 us -> 90.2 us
  waiting for transfers between devices: 50.1 us -> 54.1 us
  local copies, waits for them, and re-layouts: 8.84 us -> 4.93 us
  matrix products: 12.1 us -> 14 us
    ppermute x2, starting transfers between devices: 12.5 us -> 22.4 us  [own_slab_of_both(): got = lax.ppermute(given, 'core', [(0, 1), (1, 0)])]
    ppermute x17 -> x19, waiting for transfers between devices: 33.8 us -> 43.4 us  [shift(): lax.ppermute(array, axis, [(i, (i + by) % size) for i in range(size)])]
    all_to_all x1, starting transfers between devices: 7.74 us -> 15.7 us  [summed_over_col(): part = lax.all_to_all(copies, 'z', split_axis=0, concat_axis=0, tiled=True)]
    ppermute x17 -> x19, starting transfers between devices: 27.5 us -> 22.8 us  [shift(): lax.ppermute(array, axis, [(i, (i + by) % size) for i in range(size)])]
    all_gather x1, waiting for transfers between devices: 7.09 us -> 3.39 us  [panel_y_then_z(): return lax.all_gather(part, 'z', axis=0, tiled=True)]
    all_to_all x1, waiting for transfers between devices: 3.59 us -> 0.01 us  [summed_over_col(): part = lax.all_to_all(copies, 'z', split_axis=0, concat_axis=0, tiled=True)]
    dynamic_update_slice x19 -> x5, local copies, waits for them, and re-layouts: 3.51 us -> 0.07 us  [placed_by_owner(): lax.dynamic_update_slice_in_dim(whole, chunk, (own - d) % size * width, a...]
    ppermute x1, starting transfers between devices: 11.5 us -> 9.6 us  [pair_sum(): lax.ppermute(jnp.where(first, partial[1], partial[0]), 'core', [(0, 1), (...]
  transfers between devices with their start and end apart: 36 -> 38, of which waited for: 17 -> 22; matrix products, arithmetic and copies ran while one was open for 11% -> 5% of each run, Pallas kernels for 0% -> 0%
where the time goes in v13:
time: 186 us
  starting transfers between devices  90.2 us (48%)
  waiting for transfers between devices  54.1 us (29%)
  between operations  14.8 us (8%)
  matrix products  14 us (8%)
  other arithmetic  7.49 us (4%)
  local copies, waits for them, and re-layouts  4.93 us (3%)
    ppermute x19, waiting for transfers between devices, shift(): lax.ppermute(array, axis, [(i, (i + by) % size) for i in range(size)])  43.4 us
    ppermute x19, starting transfers between devices, shift(): lax.ppermute(array, axis, [(i, (i + by) % size) for i in range(size)])  22.8 us
    ppermute x2, starting transfers between devices, own_slab_of_both(): got = lax.ppermute(given, 'core', [(0, 1), (1, 0)])  22.4 us
    all_to_all x1, starting transfers between devices, summed_over_col(): part = lax.all_to_all(copies, 'z', split_axis=0, concat_axis=0, tiled=True)  15.7 us
    ppermute x8, starting transfers between devices, from_root(): return lax.ppermute(array, ALL, pairs)  11.1 us
    dot_general x2, matrix products, partial_of(): jnp.einsum('qj,pq->jp', panel, inverse_block, preferred_element_type=F32)  9.75 us
    ppermute x1, starting transfers between devices, pair_sum(): lax.ppermute(jnp.where(first, partial[1], partial[0]), 'core', [(0, 1), (...  9.6 us
    ppermute x6, starting transfers between devices, exchanged(): return lax.ppermute(array, axis, [(i, i ^ by) for i in range(size)])  8.62 us
  transfers between devices with their start and end apart: 38, of which 22 were waited for; matrix products, arithmetic and copies ran while one was open for 5% of the time, Pallas kernels for 0%

profile of v13, /device:TPU:1, one launch (start us, length us, event | category | flops | bytes accessed | tf_op | source)
XLA Modules:
  0.0 185.5 jit_solution(14825175966380435720)
XLA Ops:
  9.7 2.5 %collective-permute-start.3 = (bf16[1,96,512]{2,1,0:T(8,128)(2,1)S(1)}, bf16[1,96,512]{2,1,0:T(8,128)(2,1)S(1)}, u32[]{:S(2)}, u32[]{:S(2)}) collective-permute-start(bf16[1,96,512]{2,1,0:T(8,128)(2,1)S(1)} %slice.61), channel_id=1, source_target_pairs={{0,4},{4,8},{8,12},{12,16},{16,20},{20,24},{24,28},{28,0},{1,5},{5... | collective-permute-start | bytes 294920 | tf_op jit(solution)/shard_map/ppermute | solution.py:17
  12.2 6.5 %collective-permute-done.3 = bf16[1,96,512]{2,1,0:T(8,128)(2,1)S(1)} collective-permute-done((bf16[1,96,512]{2,1,0:T(8,128)(2,1)S(1)}, bf16[1,96,512]{2,1,0:T(8,128)(2,1)S(1)}, u32[]{:S(2)}, u32[]{:S(2)}) %collective-permute-start.3) | collective-permute-done | bytes 98336 | tf_op jit(solution)/shard_map/ppermute | solution.py:17
  18.7 4.7 %collective-permute-done.4 = bf16[1,96,512]{2,1,0:T(8,128)(2,1)S(1)} collective-permute-done((bf16[1,96,512]{2,1,0:T(8,128)(2,1)S(1)}, bf16[1,96,512]{2,1,0:T(8,128)(2,1)S(1)}, u32[]{:S(2)}, u32[]{:S(2)}) %collective-permute-start.4) | collective-permute-done | bytes 98336 | tf_op jit(solution)/shard_map/ppermute | solution.py:17
  24.9 2.7 %collective-permute-start.1 = (bf16[96,512]{1,0:T(8,128)(2,1)S(1)}, bf16[96,512]{1,0:T(8,128)(2,1)S(1)}, u32[]{:S(2)}, u32[]{:S(2)}) collective-permute-start(bf16[96,512]{1,0:T(8,128)(2,1)S(1)} %get-tuple-element.32), channel_id=1, source_target_pairs={{0,2},{1,3},{2,0},{3,1},{4,6},{5,7},{6,4},{7,5},{8,10},{9,11},{10,... | collective-permute-start | bytes 294920 | tf_op jit(solution)/shard_map/ppermute | solution.py:17
  28.7 1.8 collective-permute-done.1
  32.4 3.4 %collective-permute-done.5 = bf16[1,96,512]{2,1,0:T(8,128)(2,1)S(1)} collective-permute-done((bf16[1,96,512]{2,1,0:T(8,128)(2,1)S(1)}, bf16[1,96,512]{2,1,0:T(8,128)(2,1)S(1)}, u32[]{:S(2)}, u32[]{:S(2)}) %collective-permute-start.5) | collective-permute-done | bytes 98336 | tf_op jit(solution)/shard_map/ppermute | solution.py:17
  37.0 2.9 %collective-permute-done.6 = bf16[1,96,512]{2,1,0:T(8,128)(2,1)S(1)} collective-permute-done((bf16[1,96,512]{2,1,0:T(8,128)(2,1)S(1)}, bf16[1,96,512]{2,1,0:T(8,128)(2,1)S(1)}, u32[]{:S(2)}, u32[]{:S(2)}) %collective-permute-start.6) | collective-permute-done | bytes 98336 | tf_op jit(solution)/shard_map/ppermute | solution.py:17
  40.4 2.3 %collective-permute-start.15 = (bf16[5,1,96,512]{3,2,0,1:T(8,128)(2,1)S(1)}, bf16[5,1,96,512]{3,2,0,1:T(8,128)(2,1)S(1)}, u32[]{:S(2)}, u32[]{:S(2)}) collective-permute-start(bf16[5,1,96,512]{3,2,0,1:T(8,128)(2,1)S(1)} %bitcast.105), channel_id=1, source_target_pairs={{0,3},{1,0},{2,1},{3,2},{4,7},{5,4},{6,5},{7,6},{8,11},{9,8},{10,9... | collective-permute-start | bytes 1474568 | tf_op jit(solution)/shard_map/ppermute | solution.py:17
  42.7 2.7 %collective-permute-start.7 = (bf16[1,96,512]{2,1,0:T(8,128)(2,1)S(1)}, bf16[1,96,512]{2,1,0:T(8,128)(2,1)S(1)}, u32[]{:S(2)}, u32[]{:S(2)}) collective-permute-start(bf16[1,96,512]{2,1,0:T(8,128)(2,1)S(1)} %collective-permute-done.6), channel_id=1, source_target_pairs={{0,28},{4,0},{8,4},{12,8},{16,12},{20,16},{24,20},{28,24},{1,29},{... | collective-permute-start | bytes 294920 | tf_op jit(solution)/shard_map/ppermute | solution.py:17
  45.6 1.8 collective-permute-done.8
  48.4 6.1 %collective-permute-done.9 = bf16[1,96,512]{2,1,0:T(8,128)(2,1)S(1)} collective-permute-done((bf16[1,96,512]{2,1,0:T(8,128)(2,1)S(1)}, bf16[1,96,512]{2,1,0:T(8,128)(2,1)S(1)}, u32[]{:S(2)}, u32[]{:S(2)}) %collective-permute-start.9) | collective-permute-done | bytes 98336 | tf_op jit(solution)/shard_map/ppermute | solution.py:17
  54.7 2.7 %collective-permute-start.13 = (bf16[3,1,96,512]{3,2,0,1:T(8,128)(2,1)S(1)}, bf16[3,1,96,512]{3,2,0,1:T(8,128)(2,1)S(1)}, u32[]{:S(2)}, u32[]{:S(2)}) collective-permute-start(bf16[3,1,96,512]{3,2,0,1:T(8,128)(2,1)S(1)} %bitcast.109), channel_id=1, source_target_pairs={{0,3},{1,0},{2,1},{3,2},{4,7},{5,4},{6,5},{7,6},{8,11},{9,8},{10,9... | collective-permute-start | bytes 884744 | tf_op jit(solution)/shard_map/ppermute | solution.py:17
  59.2 2.7 %collective-permute-done.11 = bf16[3,1,96,512]{3,2,0,1:T(8,128)(2,1)S(1)} collective-permute-done((bf16[3,1,96,512]{3,2,0,1:T(8,128)(2,1)S(1)}, bf16[3,1,96,512]{3,2,0,1:T(8,128)(2,1)S(1)}, u32[]{:S(2)}, u32[]{:S(2)}) %collective-permute-start.11) | collective-permute-done | bytes 294944 | tf_op jit(solution)/shard_map/ppermute | solution.py:17
  63.4 1.7 collective-permute-start.18
  65.1 2.6 %collective-permute-start.14 = (bf16[3,1,96,512]{3,2,0,1:T(8,128)(2,1)S(1)}, bf16[3,1,96,512]{3,2,0,1:T(8,128)(2,1)S(1)}, u32[]{:S(2)}, u32[]{:S(2)}) collective-permute-start(bf16[3,1,96,512]{3,2,0,1:T(8,128)(2,1)S(1)} %collective-permute-done.13), channel_id=1, source_target_pairs={{0,3},{1,0},{2,1},{3,2},{4,7},{5,4},{6,5},{7,6},{8,11},{9,8},{10,9... | collective-permute-start | bytes 884744 | tf_op jit(solution)/shard_map/ppermute | solution.py:17
  67.9 5.1 %collective-permute-done.12 = bf16[5,1,96,512]{3,2,0,1:T(8,128)(2,1)S(1)} collective-permute-done((bf16[5,1,96,512]{3,2,0,1:T(8,128)(2,1)S(1)}, bf16[5,1,96,512]{3,2,0,1:T(8,128)(2,1)S(1)}, u32[]{:S(2)}, u32[]{:S(2)}) %collective-permute-start.12) | collective-permute-done | bytes 491552 | tf_op jit(solution)/shard_map/ppermute | solution.py:17
  73.1 2.7 %collective-permute-done.14 = bf16[3,1,96,512]{3,2,0,1:T(8,128)(2,1)S(1)} collective-permute-done((bf16[3,1,96,512]{3,2,0,1:T(8,128)(2,1)S(1)}, bf16[3,1,96,512]{3,2,0,1:T(8,128)(2,1)S(1)}, u32[]{:S(2)}, u32[]{:S(2)}) %collective-permute-start.14) | collective-permute-done | bytes 294944 | tf_op jit(solution)/shard_map/ppermute | solution.py:17
  76.0 2.7 %convolution_convert_fusion.1 = bf16[512,768]{1,0:T(8,128)(2,1)S(1)} fusion(bf16[3072,512]{1,0:T(8,128)(2,1)S(1)} %bitcast.94, bf16[768,3072]{1,0:T(8,128)(2,1)S(1)} %bitcast.115), kind=kOutput, calls=%fused_computation.2 | convolution fusion | flops 2416312320 | bytes 8650752 | tf_op jit(solution)/shard_map/qj,pq->jp/dot_general | solution.py:154
  79.6 3.4 %all-gather.2.cloned.1.call-done = bf16[3072,512]{1,0:T(8,128)(2,1)} async-done(((bf16[384,512]{1,0:T(8,128)(2,1)}), bf16[3072,512]{1,0:T(8,128)(2,1)}) %all-gather.2.cloned.1.call-update) | async-done | bytes 3145744 | tf_op jit(solution)/shard_map/all_gather | solution.py:53
  83.0 7.1 %broadcast_select_fusion.1 = (bf16[512,768]{1,0:T(8,128)(2,1)}, bf16[512,768]{1,0:T(8,128)(2,1)}) fusion(bf16[512,768]{1,0:T(8,128)(2,1)S(1)} %convolution_convert_fusion.1, pred[]{:T(512)S(6)} %eq.63, bf16[3072,512]{1,0:T(8,128)(2,1)} %all-gather.2.cloned.1.call-done, bf16[768,3072]{1,0:T(8,128)(2,1)} %param.8), kind=kOutput, calls=%fused_computation.33 | convolution fusion | flops 2416705536 | bytes 10223617 | tf_op jit(solution)/shard_map/qj,pq->jp/dot_general | solution.py:154
  90.1 9.6 %collective-permute-start.19 = (bf16[512,768]{1,0:T(8,128)(2,1)}, bf16[512,768]{1,0:T(8,128)(2,1)S(1)}, u32[]{:S(2)}, u32[]{:S(2)}) collective-permute-start(bf16[512,768]{1,0:T(8,128)(2,1)} %get-tuple-element.36), channel_id=1, source_target_pairs={{0,32},{32,0},{1,33},{33,1},{2,34},{34,2},{3,35},{35,3},{4,36},{36... | collective-permute-start | bytes 2359304 | tf_op jit(solution)/shard_map/ppermute | solution.py:92
  104.3 1.8 collective-permute-start.21
  107.0 2.5 %broadcast_select_fusion = (bf16[768,512]{1,0:T(8,128)(2,1)}, bf16[768,512]{1,0:T(8,128)(2,1)}) fusion(bf16[768,512]{1,0:T(8,128)(2,1)S(1)} %bitcast.100, pred[]{:T(512)S(6)} %eq.63, bf16[3072,512]{1,0:T(8,128)(2,1)} %all-gather.2.cloned.1.call-done, s32[]{:T(128)S(6)} %select_n.280), kind=kLoop, calls=%fused_computation.30 | loop fusion | flops 393216 | bytes 3145733 | tf_op jit(solution)/shard_map/jit(_where)/select_n | solution.py:180
  113.0 3.5 %collective-permute-done.21 = bf16[128,768]{1,0:T(8,128)(2,1)S(1)} collective-permute-done((bf16[128,768]{1,0:T(8,128)(2,1)S(1)}, bf16[128,768]{1,0:T(8,128)(2,1)S(1)}, u32[]{:S(2)}, u32[]{:S(2)}) %collective-permute-start.21) | collective-permute-done | bytes 196640 | tf_op jit(solution)/shard_map/ppermute | solution.py:17
  119.9 3.0 %fusion.1 = bf16[128,512]{1,0:T(8,128)(2,1)S(1)} fusion(bf16[128,768]{1,0:T(8,128)(2,1)S(1)} %fusion.18, bf16[768,512]{1,0:T(8,128)(2,1)} %collective-permute-done.28, bf16[768,512]{1,0:T(8,128)(2,1)} %collective-permute-done.18, bf16[768,512]{1,0:T(8,128)(2,1)} %copy-done.5, bf16[768,512]{1,0:T(8,128)(2,1)} %collective-permute-done.27, ...), kind=kOutput, calls=%fused_computation.6 | convolution fusion | flops 103940096 | bytes 7405570 | tf_op jit(solution)/shard_map/dot_general | solution.py:192
  123.6 4.0 %collective-permute-start.30 = (bf16[32,512]{1,0:T(8,128)(2,1)S(1)}, bf16[32,512]{1,0:T(8,128)(2,1)S(1)}, u32[]{:S(2)}, u32[]{:S(2)}) collective-permute-start(bf16[32,512]{1,0:T(8,128)(2,1)S(1)} %get-tuple-element.35), channel_id=1, source_target_pairs={{0,2},{1,3},{2,0},{3,1},{4,6},{5,7},{6,4},{7,5},{8,10},{9,11},{10,... | collective-permute-start | bytes 98312 | tf_op jit(solution)/shard_map/ppermute | solution.py:107
  127.7 1.6 collective-permute-done.30
  129.3 2.3 %collective-permute-done.31 = bf16[32,512]{1,0:T(8,128)(2,1)S(1)} collective-permute-done((bf16[32,512]{1,0:T(8,128)(2,1)S(1)}, bf16[32,512]{1,0:T(8,128)(2,1)S(1)}, u32[]{:S(2)}, u32[]{:S(2)}) %collective-permute-start.31) | collective-permute-done | bytes 32800 | tf_op jit(solution)/shard_map/ppermute | solution.py:107
  132.4 15.7 %all-to-all-start = ((bf16[8,32,512]{2,1,0:T(8,128)(2,1)}), bf16[8,32,512]{2,1,0:T(8,128)(2,1)S(1)}, u32[]{:S(2)}, u32[]{:S(2)}) async-start(bf16[8,32,512]{2,1,0:T(8,128)(2,1)} %broadcast_in_dim.47), calls=%async_computation | async-start | bytes 524288 | tf_op jit(solution)/shard_map/all_to_all | solution.py:119
  148.1 11.7 %collective-permute-start.23 = (bf16[64,768]{1,0:T(8,128)(2,1)S(1)}, bf16[64,768]{1,0:T(8,128)(2,1)S(1)}, u32[]{:S(2)}, u32[]{:S(2)}) collective-permute-start(bf16[64,768]{1,0:T(8,128)(2,1)S(1)} %dynamic-slice_bitcast_fusion.3), channel_id=1, source_target_pairs={{0,32},{32,0},{1,33},{33,1},{2,34},{34,2},{3,35},{35,3},{4,36},{36... | collective-permute-start | bytes 294920 | tf_op jit(solution)/shard_map/ppermute | solution.py:133
  161.8 3.0 %collective-permute-start.34 = (bf16[32,512]{1,0:T(8,128)(2,1)S(1)}, bf16[32,512]{1,0:T(8,128)(2,1)S(1)}, u32[]{:S(2)}, u32[]{:S(2)}) collective-permute-start(bf16[32,512]{1,0:T(8,128)(2,1)S(1)} %reduce_sum.12), channel_id=1, source_target_pairs={{0,3},{1,2},{2,1},{3,0},{4,7},{5,6},{6,5},{7,4},{8,11},{9,10},{10,... | collective-permute-start | bytes 98312 | tf_op jit(solution)/shard_map/ppermute | solution.py:107
  166.4 10.6 %collective-permute-start.35 = (bf16[64,512]{1,0:T(8,128)(2,1)S(1)}, bf16[64,512]{1,0:T(8,128)(2,1)S(1)}, u32[]{:S(2)}, u32[]{:S(2)}) collective-permute-start(bf16[64,512]{1,0:T(8,128)(2,1)S(1)} %dynamic-slice_bitcast_fusion.4), channel_id=1, source_target_pairs={{0,32},{32,0},{1,33},{33,1},{2,34},{34,2},{3,35},{35,3},{4,36},{36... | collective-permute-start | bytes 196616 | tf_op jit(solution)/shard_map/ppermute | solution.py:133
  (131 shorter events, 33.2 us)
Async XLA Ops:
  7.2 75.8 %all-gather.2.cloned.1.call-start = ((), (), s32[]{:S(2)}) async-start(), calls=%async_computation.1 | async-start | bytes 3538944 | tf_op jit(solution)/shard_map/all_gather | solution.py:53
  9.7 9.0 %collective-permute-start.3 = (bf16[1,96,512]{2,1,0:T(8,128)(2,1)S(1)}, bf16[1,96,512]{2,1,0:T(8,128)(2,1)S(1)}, u32[]{:S(2)}, u32[]{:S(2)}) collective-permute-start(bf16[1,96,512]{2,1,0:T(8,128)(2,1)S(1)} %slice.61), channel_id=1, source_target_pairs={{0,4},{4,8},{8,12},{12,16},{16,20},{20,24},{24,28},{28,0},{1,5},{5... | collective-permute-start | bytes 294920 | tf_op jit(solution)/shard_map/ppermute | solution.py:17
  18.7 4.7 %collective-permute-start.4 = (bf16[1,96,512]{2,1,0:T(8,128)(2,1)S(1)}, bf16[1,96,512]{2,1,0:T(8,128)(2,1)S(1)}, u32[]{:S(2)}, u32[]{:S(2)}) collective-permute-start(bf16[1,96,512]{2,1,0:T(8,128)(2,1)S(1)} %collective-permute-done.3), channel_id=1, source_target_pairs={{0,4},{4,8},{8,12},{12,16},{16,20},{20,24},{24,28},{28,0},{1,5},{5... | collective-permute-start | bytes 294920 | tf_op jit(solution)/shard_map/ppermute | solution.py:17
  23.4 5.3 %collective-permute-start = (bf16[96,512]{1,0:T(8,128)(2,1)S(1)}, bf16[96,512]{1,0:T(8,128)(2,1)S(1)}, u32[]{:S(2)}, u32[]{:S(2)}) collective-permute-start(bf16[96,512]{1,0:T(8,128)(2,1)S(1)} %get-tuple-element.32), channel_id=1, source_target_pairs={{0,1},{1,2},{2,3},{3,0},{4,5},{5,6},{6,7},{7,4},{8,9},{9,10},{10,1... | collective-permute-start | bytes 294920 | tf_op jit(solution)/shard_map/ppermute | solution.py:17
  24.9 5.6 %collective-permute-start.1 = (bf16[96,512]{1,0:T(8,128)(2,1)S(1)}, bf16[96,512]{1,0:T(8,128)(2,1)S(1)}, u32[]{:S(2)}, u32[]{:S(2)}) collective-permute-start(bf16[96,512]{1,0:T(8,128)(2,1)S(1)} %get-tuple-element.32), channel_id=1, source_target_pairs={{0,2},{1,3},{2,0},{3,1},{4,6},{5,7},{6,4},{7,5},{8,10},{9,11},{10,... | collective-permute-start | bytes 294920 | tf_op jit(solution)/shard_map/ppermute | solution.py:17
  35.8 4.2 %collective-permute-start.6 = (bf16[1,96,512]{2,1,0:T(8,128)(2,1)S(1)}, bf16[1,96,512]{2,1,0:T(8,128)(2,1)S(1)}, u32[]{:S(2)}, u32[]{:S(2)}) collective-permute-start(bf16[1,96,512]{2,1,0:T(8,128)(2,1)S(1)} %collective-permute-done.5), channel_id=1, source_target_pairs={{0,28},{4,0},{8,4},{12,8},{16,12},{20,16},{24,20},{28,24},{1,29},{... | collective-permute-start | bytes 294920 | tf_op jit(solution)/shard_map/ppermute | solution.py:17
  40.0 19.0 %collective-permute-start.10 = (bf16[5,1,96,512]{3,2,0,1:T(8,128)(2,1)S(1)}, bf16[5,1,96,512]{3,2,0,1:T(8,128)(2,1)S(1)}, u32[]{:S(2)}, u32[]{:S(2)}) collective-permute-start(bf16[5,1,96,512]{3,2,0,1:T(8,128)(2,1)S(1)} %bitcast.104), channel_id=1, source_target_pairs={{0,1},{1,2},{2,3},{3,0},{4,5},{5,6},{6,7},{7,4},{8,9},{9,10},{10,1... | collective-permute-start | bytes 1474568 | tf_op jit(solution)/shard_map/ppermute | solution.py:17
  40.4 21.8 %collective-permute-start.15 = (bf16[5,1,96,512]{3,2,0,1:T(8,128)(2,1)S(1)}, bf16[5,1,96,512]{3,2,0,1:T(8,128)(2,1)S(1)}, u32[]{:S(2)}, u32[]{:S(2)}) collective-permute-start(bf16[5,1,96,512]{3,2,0,1:T(8,128)(2,1)S(1)} %bitcast.105), channel_id=1, source_target_pairs={{0,3},{1,0},{2,1},{3,2},{4,7},{5,4},{6,5},{7,6},{8,11},{9,8},{10,9... | collective-permute-start | bytes 1474568 | tf_op jit(solution)/shard_map/ppermute | solution.py:17
  42.7 4.7 %collective-permute-start.8 = (bf16[1,96,512]{2,1,0:T(8,128)(2,1)S(1)}, bf16[1,96,512]{2,1,0:T(8,128)(2,1)S(1)}, u32[]{:S(2)}, u32[]{:S(2)}) collective-permute-start(bf16[1,96,512]{2,1,0:T(8,128)(2,1)S(1)} %collective-permute-done.4), channel_id=1, source_target_pairs={{0,4},{4,8},{8,12},{12,16},{16,20},{20,24},{24,28},{28,0},{1,5},{5... | collective-permute-start | bytes 294920 | tf_op jit(solution)/shard_map/ppermute | solution.py:17
  42.7 5.7 %collective-permute-start.7 = (bf16[1,96,512]{2,1,0:T(8,128)(2,1)S(1)}, bf16[1,96,512]{2,1,0:T(8,128)(2,1)S(1)}, u32[]{:S(2)}, u32[]{:S(2)}) collective-permute-start(bf16[1,96,512]{2,1,0:T(8,128)(2,1)S(1)} %collective-permute-done.6), channel_id=1, source_target_pairs={{0,28},{4,0},{8,4},{12,8},{16,12},{20,16},{24,20},{28,24},{1,29},{... | collective-permute-start | bytes 294920 | tf_op jit(solution)/shard_map/ppermute | solution.py:17
  47.4 7.1 %collective-permute-start.9 = (bf16[1,96,512]{2,1,0:T(8,128)(2,1)S(1)}, bf16[1,96,512]{2,1,0:T(8,128)(2,1)S(1)}, u32[]{:S(2)}, u32[]{:S(2)}) collective-permute-start(bf16[1,96,512]{2,1,0:T(8,128)(2,1)S(1)} %collective-permute-done.8), channel_id=1, source_target_pairs={{0,4},{4,8},{8,12},{12,16},{16,20},{20,24},{24,28},{28,0},{1,5},{5... | collective-permute-start | bytes 294920 | tf_op jit(solution)/shard_map/ppermute | solution.py:17
  54.6 7.3 %collective-permute-start.11 = (bf16[3,1,96,512]{3,2,0,1:T(8,128)(2,1)S(1)}, bf16[3,1,96,512]{3,2,0,1:T(8,128)(2,1)S(1)}, u32[]{:S(2)}, u32[]{:S(2)}) collective-permute-start(bf16[3,1,96,512]{3,2,0,1:T(8,128)(2,1)S(1)} %bitcast.108), channel_id=1, source_target_pairs={{0,1},{1,2},{2,3},{3,0},{4,5},{5,6},{6,7},{7,4},{8,9},{9,10},{10,1... | collective-permute-start | bytes 884744 | tf_op jit(solution)/shard_map/ppermute | solution.py:17
  54.7 7.7 %collective-permute-start.13 = (bf16[3,1,96,512]{3,2,0,1:T(8,128)(2,1)S(1)}, bf16[3,1,96,512]{3,2,0,1:T(8,128)(2,1)S(1)}, u32[]{:S(2)}, u32[]{:S(2)}) collective-permute-start(bf16[3,1,96,512]{3,2,0,1:T(8,128)(2,1)S(1)} %bitcast.109), channel_id=1, source_target_pairs={{0,3},{1,0},{2,1},{3,2},{4,7},{5,4},{6,5},{7,6},{8,11},{9,8},{10,9... | collective-permute-start | bytes 884744 | tf_op jit(solution)/shard_map/ppermute | solution.py:17
  57.7 4.4 %collective-permute-start.16 = (bf16[2,1,96,512]{3,2,1,0:T(8,128)(2,1)S(1)}, bf16[2,1,96,512]{3,2,1,0:T(8,128)(2,1)S(1)}, u32[]{:S(2)}, u32[]{:S(2)}) collective-permute-start(bf16[2,1,96,512]{3,2,1,0:T(8,128)(2,1)S(1)} %get-tuple-element.25), channel_id=1, source_target_pairs={{0,2},{1,3},{2,0},{3,1},{36,38},{37,39},{38,36},{39,37},{72,74},{7... | collective-permute-start | bytes 589832 | tf_op jit(solution)/shard_map/ppermute | solution.py:83
  62.0 11.0 %collective-permute-start.12 = (bf16[5,1,96,512]{3,2,0,1:T(8,128)(2,1)S(1)}, bf16[5,1,96,512]{3,2,0,1:T(8,128)(2,1)S(1)}, u32[]{:S(2)}, u32[]{:S(2)}) collective-permute-start(bf16[5,1,96,512]{3,2,0,1:T(8,128)(2,1)S(1)} %collective-permute-done.10), channel_id=1, source_target_pairs={{0,1},{1,2},{2,3},{3,0},{4,5},{5,6},{6,7},{7,4},{8,9},{9,10},{10,1... | collective-permute-start | bytes 1474568 | tf_op jit(solution)/shard_map/ppermute | solution.py:17
  62.6 16.1 %collective-permute-start.17 = (bf16[768,512]{1,0:T(8,128)(2,1)S(1)}, bf16[768,512]{1,0:T(8,128)(2,1)S(1)}, u32[]{:S(2)}, u32[]{:S(2)}) collective-permute-start(bf16[768,512]{1,0:T(8,128)(2,1)S(1)} %bitcast.97), channel_id=1, source_target_pairs={{0,96},{1,97},{2,98},{3,99},{36,100},{37,101},{38,102},{39,103},{7... | collective-permute-start | bytes 2359304 | tf_op jit(solution)/shard_map/ppermute | solution.py:83
  63.4 16.2 %collective-permute-start.18 = (bf16[768,512]{1,0:T(8,128)(2,1)S(1)}, bf16[768,512]{1,0:T(8,128)(2,1)}, u32[]{:S(2)}, u32[]{:S(2)}) collective-permute-start(bf16[768,512]{1,0:T(8,128)(2,1)S(1)} %bitcast.98), channel_id=1, source_target_pairs={{0,224},{1,225},{2,226},{3,227},{36,228},{37,229},{38,230},{39,231... | collective-permute-start | bytes 2359304 | tf_op jit(solution)/shard_map/ppermute | solution.py:83
  65.1 10.6 %collective-permute-start.14 = (bf16[3,1,96,512]{3,2,0,1:T(8,128)(2,1)S(1)}, bf16[3,1,96,512]{3,2,0,1:T(8,128)(2,1)S(1)}, u32[]{:S(2)}, u32[]{:S(2)}) collective-permute-start(bf16[3,1,96,512]{3,2,0,1:T(8,128)(2,1)S(1)} %collective-permute-done.13), channel_id=1, source_target_pairs={{0,3},{1,0},{2,1},{3,2},{4,7},{5,4},{6,5},{7,6},{8,11},{9,8},{10,9... | collective-permute-start | bytes 884744 | tf_op jit(solution)/shard_map/ppermute | solution.py:17
  90.1 11.7 %collective-permute-start.19 = (bf16[512,768]{1,0:T(8,128)(2,1)}, bf16[512,768]{1,0:T(8,128)(2,1)S(1)}, u32[]{:S(2)}, u32[]{:S(2)}) collective-permute-start(bf16[512,768]{1,0:T(8,128)(2,1)} %get-tuple-element.36), channel_id=1, source_target_pairs={{0,32},{32,0},{1,33},{33,1},{2,34},{34,2},{3,35},{35,3},{4,36},{36... | collective-permute-start | bytes 2359304 | tf_op jit(solution)/shard_map/ppermute | solution.py:92
  99.7 20.1 %collective-permute-start.28 = (bf16[768,512]{1,0:T(8,128)(2,1)S(1)}, bf16[768,512]{1,0:T(8,128)(2,1)}, u32[]{:S(2)}, u32[]{:S(2)}) collective-permute-start(bf16[768,512]{1,0:T(8,128)(2,1)S(1)} %bitcast.99), channel_id=1, source_target_pairs={{0,160},{1,161},{2,162},{3,163},{36,164},{37,165},{38,166},{39,167... | collective-permute-start | bytes 2359304 | tf_op jit(solution)/shard_map/ppermute | solution.py:83
  104.2 7.2 %collective-permute-start.20 = (bf16[128,768]{1,0:T(8,128)(2,1)S(1)}, bf16[128,768]{1,0:T(8,128)(2,1)S(1)}, u32[]{:S(2)}, u32[]{:S(2)}) collective-permute-start(bf16[128,768]{1,0:T(8,128)(2,1)S(1)} %get-tuple-element.22), channel_id=1, source_target_pairs={{0,128},{64,192},{128,0},{192,64},{1,129},{65,193},{129,1},{193,65... | collective-permute-start | bytes 589832 | tf_op jit(solution)/shard_map/ppermute | solution.py:17
  104.3 12.1 %collective-permute-start.21 = (bf16[128,768]{1,0:T(8,128)(2,1)S(1)}, bf16[128,768]{1,0:T(8,128)(2,1)S(1)}, u32[]{:S(2)}, u32[]{:S(2)}) collective-permute-start(bf16[128,768]{1,0:T(8,128)(2,1)S(1)} %get-tuple-element.24), channel_id=1, source_target_pairs={{0,64},{64,128},{128,192},{192,0},{1,65},{65,129},{129,193},{193,1... | collective-permute-start | bytes 589832 | tf_op jit(solution)/shard_map/ppermute | solution.py:17
  106.1 11.9 %collective-permute-start.22 = (bf16[128,768]{1,0:T(8,128)(2,1)S(1)}, bf16[128,768]{1,0:T(8,128)(2,1)S(1)}, u32[]{:S(2)}, u32[]{:S(2)}) collective-permute-start(bf16[128,768]{1,0:T(8,128)(2,1)S(1)} %get-tuple-element.23), channel_id=1, source_target_pairs={{0,192},{64,0},{128,64},{192,128},{1,193},{65,1},{129,65},{193,129... | collective-permute-start | bytes 589832 | tf_op jit(solution)/shard_map/ppermute | solution.py:17
  109.6 10.3 %collective-permute-start.24 = (bf16[768,512]{1,0:T(8,128)(2,1)}, bf16[768,512]{1,0:T(8,128)(2,1)}, u32[]{:S(2)}, u32[]{:S(2)}) collective-permute-start(bf16[768,512]{1,0:T(8,128)(2,1)} %get-tuple-element.12), channel_id=1, source_target_pairs={{0,32},{1,33},{2,34},{3,35},{36,4},{37,5},{38,6},{39,7},{72,104},{... | collective-permute-start | bytes 2359304 | tf_op jit(solution)/shard_map/ppermute | solution.py:83
  111.4 8.4 %collective-permute-start.25 = (bf16[768,512]{1,0:T(8,128)(2,1)}, bf16[768,512]{1,0:T(8,128)(2,1)}, u32[]{:S(2)}, u32[]{:S(2)}) collective-permute-start(bf16[768,512]{1,0:T(8,128)(2,1)} %get-tuple-element.13), channel_id=1, source_target_pairs={{0,64},{1,65},{2,66},{3,67},{36,68},{37,69},{38,70},{39,71},{72,13... | collective-permute-start | bytes 2359304 | tf_op jit(solution)/shard_map/ppermute | solution.py:83
  123.0 4.7 %collective-permute-start.29 = (bf16[32,512]{1,0:T(8,128)(2,1)S(1)}, bf16[32,512]{1,0:T(8,128)(2,1)S(1)}, u32[]{:S(2)}, u32[]{:S(2)}) collective-permute-start(bf16[32,512]{1,0:T(8,128)(2,1)S(1)} %get-tuple-element.33), channel_id=1, source_target_pairs={{0,1},{1,0},{2,3},{3,2},{4,5},{5,4},{6,7},{7,6},{8,9},{9,8},{10,11... | collective-permute-start | bytes 98312 | tf_op jit(solution)/shard_map/ppermute | solution.py:107
  123.6 5.7 %collective-permute-start.30 = (bf16[32,512]{1,0:T(8,128)(2,1)S(1)}, bf16[32,512]{1,0:T(8,128)(2,1)S(1)}, u32[]{:S(2)}, u32[]{:S(2)}) collective-permute-start(bf16[32,512]{1,0:T(8,128)(2,1)S(1)} %get-tuple-element.35), channel_id=1, source_target_pairs={{0,2},{1,3},{2,0},{3,1},{4,6},{5,7},{6,4},{7,5},{8,10},{9,11},{10,... | collective-permute-start | bytes 98312 | tf_op jit(solution)/shard_map/ppermute | solution.py:107
  132.4 28.4 %all-to-all-start = ((bf16[8,32,512]{2,1,0:T(8,128)(2,1)}), bf16[8,32,512]{2,1,0:T(8,128)(2,1)S(1)}, u32[]{:S(2)}, u32[]{:S(2)}) async-start(bf16[8,32,512]{2,1,0:T(8,128)(2,1)} %broadcast_in_dim.47), calls=%async_computation | async-start | bytes 524288 | tf_op jit(solution)/shard_map/all_to_all | solution.py:119
  148.1 12.7 %collective-permute-start.23 = (bf16[64,768]{1,0:T(8,128)(2,1)S(1)}, bf16[64,768]{1,0:T(8,128)(2,1)S(1)}, u32[]{:S(2)}, u32[]{:S(2)}) collective-permute-start(bf16[64,768]{1,0:T(8,128)(2,1)S(1)} %dynamic-slice_bitcast_fusion.3), channel_id=1, source_target_pairs={{0,32},{32,0},{1,33},{33,1},{2,34},{34,2},{3,35},{35,3},{4,36},{36... | collective-permute-start | bytes 294920 | tf_op jit(solution)/shard_map/ppermute | solution.py:133
  160.9 4.7 %collective-permute-start.33 = (bf16[32,512]{1,0:T(8,128)(2,1)S(1)}, bf16[32,512]{1,0:T(8,128)(2,1)S(1)}, u32[]{:S(2)}, u32[]{:S(2)}) collective-permute-start(bf16[32,512]{1,0:T(8,128)(2,1)S(1)} %reduce_sum.12), channel_id=1, source_target_pairs={{0,2},{1,3},{2,0},{3,1},{4,6},{5,7},{6,4},{7,5},{8,10},{9,11},{10,... | collective-permute-start | bytes 98312 | tf_op jit(solution)/shard_map/ppermute | solution.py:107
  161.8 4.5 %collective-permute-start.34 = (bf16[32,512]{1,0:T(8,128)(2,1)S(1)}, bf16[32,512]{1,0:T(8,128)(2,1)S(1)}, u32[]{:S(2)}, u32[]{:S(2)}) collective-permute-start(bf16[32,512]{1,0:T(8,128)(2,1)S(1)} %reduce_sum.12), channel_id=1, source_target_pairs={{0,3},{1,2},{2,1},{3,0},{4,7},{5,6},{6,5},{7,4},{8,11},{9,10},{10,... | collective-permute-start | bytes 98312 | tf_op jit(solution)/shard_map/ppermute | solution.py:107
  166.4 11.5 %collective-permute-start.35 = (bf16[64,512]{1,0:T(8,128)(2,1)S(1)}, bf16[64,512]{1,0:T(8,128)(2,1)S(1)}, u32[]{:S(2)}, u32[]{:S(2)}) collective-permute-start(bf16[64,512]{1,0:T(8,128)(2,1)S(1)} %dynamic-slice_bitcast_fusion.4), channel_id=1, source_target_pairs={{0,32},{32,0},{1,33},{33,1},{2,34},{34,2},{3,35},{35,3},{4,36},{36... | collective-permute-start | bytes 196616 | tf_op jit(solution)/shard_map/ppermute | solution.py:133
  (14 other events, 114.8 us)
Sparse Core Ops, SparseCore 0:
  32.4 50.5 all-gather.1

commit v14 on v13

--- a/solution.py
+++ b/solution.py
@@ -179,7 +179,8 @@
     across = from_root(
         jnp.where(first, slab_1, slab_0), lambda x, c, z, y: (x, 1 - c, z, y)
     )
-    partial = [partial_of(panel_0), partial_1]
+    partial_0, sent_0[:2] = lax.optimization_barrier((partial_of(panel_0), sent_0[:2]))
+    partial = [partial_0, partial_1]
 
     home = row == z
     slab = jnp.where(first, slab_0, slab_1)

time: 186 us -> 192 us (1.032)
  starting transfers between devices: 90.2 us -> 95.2 us
  other arithmetic: 7.49 us -> 9.47 us
    ppermute x1, starting transfers between devices: 9.6 us -> 17.4 us  [pair_sum(): lax.ppermute(jnp.where(first, partial[1], partial[0]), 'core', [(0, 1), (...]
    ppermute x19, starting transfers between devices: 22.8 us -> 29.8 us  [shift(): lax.ppermute(array, axis, [(i, (i + by) % size) for i in range(size)])]
    ppermute x2, starting transfers between devices: 22.4 us -> 15.7 us  [own_slab_of_both(): got = lax.ppermute(given, 'core', [(0, 1), (1, 0)])]
    ppermute x19, waiting for transfers between devices: 43.4 us -> 41.3 us  [shift(): lax.ppermute(array, axis, [(i, (i + by) % size) for i in range(size)])]
    dot_general x2, matrix products: 9.75 us -> 7.71 us  [partial_of(): jnp.einsum('qj,pq->jp', panel, inverse_block, preferred_element_type=F32)]
  transfers between devices with their start and end apart: 38 -> 38, of which waited for: 22 -> 23; matrix products, arithmetic and copies ran while one was open for 5% -> 8% of each run, Pallas kernels for 0% -> 0%
where the time goes in v14:
time: 192 us; the launch traced here: 191 us
  starting transfers between devices  95.2 us (50%)
  waiting for transfers between devices  52.9 us (28%)
  between operations  14.9 us (8%)
  matrix products  12.2 us (6%)
  other arithmetic  9.47 us (5%)
  local copies, waits for them, and re-layouts  6.51 us (3%)
    ppermute x19, waiting for transfers between devices, shift(): lax.ppermute(array, axis, [(i, (i + by) % size) for i in range(size)])  41.3 us
    ppermute x19, starting transfers between devices, shift(): lax.ppermute(array, axis, [(i, (i + by) % size) for i in range(size)])  29.8 us
    ppermute x1, starting transfers between devices, pair_sum(): lax.ppermute(jnp.where(first, partial[1], partial[0]), 'core', [(0, 1), (...  17.4 us
    ppermute x2, starting transfers between devices, own_slab_of_both(): got = lax.ppermute(given, 'core', [(0, 1), (1, 0)])  15.7 us
    all_to_all x1, starting transfers between devices, summed_over_col(): part = lax.all_to_all(copies, 'z', split_axis=0, concat_axis=0, tiled=True)  14.5 us
    ppermute x8, starting transfers between devices, from_root(): return lax.ppermute(array, ALL, pairs)  9.97 us
    ppermute x6, starting transfers between devices, exchanged(): return lax.ppermute(array, axis, [(i, i ^ by) for i in range(size)])  7.88 us
    dot_general x2, matrix products, partial_of(): jnp.einsum('qj,pq->jp', panel, inverse_block, preferred_element_type=F32)  7.71 us
  transfers between devices with their start and end apart: 38, of which 23 were waited for; matrix products, arithmetic and copies ran while one was open for 8% of the time, Pallas kernels for 0%

profile of v14, /device:TPU:1, one launch (start us, length us, event | category | flops | bytes accessed | tf_op | source)
XLA Modules:
  0.0 191.2 jit_solution(10558565935812322944)
XLA Ops:
  9.7 2.5 %collective-permute-start.3 = (bf16[1,96,512]{2,1,0:T(8,128)(2,1)S(1)}, bf16[1,96,512]{2,1,0:T(8,128)(2,1)S(1)}, u32[]{:S(2)}, u32[]{:S(2)}) collective-permute-start(bf16[1,96,512]{2,1,0:T(8,128)(2,1)S(1)} %slice.61), channel_id=1, source_target_pairs={{0,4},{4,8},{8,12},{12,16},{16,20},{20,24},{24,28},{28,0},{1,5},{5... | collective-permute-start | bytes 294920 | tf_op jit(solution)/shard_map/ppermute | solution.py:17
  12.2 6.5 %collective-permute-done.3 = bf16[1,96,512]{2,1,0:T(8,128)(2,1)S(1)} collective-permute-done((bf16[1,96,512]{2,1,0:T(8,128)(2,1)S(1)}, bf16[1,96,512]{2,1,0:T(8,128)(2,1)S(1)}, u32[]{:S(2)}, u32[]{:S(2)}) %collective-permute-start.3) | collective-permute-done | bytes 98336 | tf_op jit(solution)/shard_map/ppermute | solution.py:17
  18.7 4.7 %collective-permute-done.4 = bf16[1,96,512]{2,1,0:T(8,128)(2,1)S(1)} collective-permute-done((bf16[1,96,512]{2,1,0:T(8,128)(2,1)S(1)}, bf16[1,96,512]{2,1,0:T(8,128)(2,1)S(1)}, u32[]{:S(2)}, u32[]{:S(2)}) %collective-permute-start.4) | collective-permute-done | bytes 98336 | tf_op jit(solution)/shard_map/ppermute | solution.py:17
  24.9 2.7 %collective-permute-start.1 = (bf16[96,512]{1,0:T(8,128)(2,1)S(1)}, bf16[96,512]{1,0:T(8,128)(2,1)S(1)}, u32[]{:S(2)}, u32[]{:S(2)}) collective-permute-start(bf16[96,512]{1,0:T(8,128)(2,1)S(1)} %get-tuple-element.38), channel_id=1, source_target_pairs={{0,2},{1,3},{2,0},{3,1},{4,6},{5,7},{6,4},{7,5},{8,10},{9,11},{10,... | collective-permute-start | bytes 294920 | tf_op jit(solution)/shard_map/ppermute | solution.py:17
  28.7 1.8 collective-permute-done.1
  32.4 3.4 %collective-permute-done.5 = bf16[1,96,512]{2,1,0:T(8,128)(2,1)S(1)} collective-permute-done((bf16[1,96,512]{2,1,0:T(8,128)(2,1)S(1)}, bf16[1,96,512]{2,1,0:T(8,128)(2,1)S(1)}, u32[]{:S(2)}, u32[]{:S(2)}) %collective-permute-start.5) | collective-permute-done | bytes 98336 | tf_op jit(solution)/shard_map/ppermute | solution.py:17
  37.0 2.9 %collective-permute-done.6 = bf16[1,96,512]{2,1,0:T(8,128)(2,1)S(1)} collective-permute-done((bf16[1,96,512]{2,1,0:T(8,128)(2,1)S(1)}, bf16[1,96,512]{2,1,0:T(8,128)(2,1)S(1)}, u32[]{:S(2)}, u32[]{:S(2)}) %collective-permute-start.6) | collective-permute-done | bytes 98336 | tf_op jit(solution)/shard_map/ppermute | solution.py:17
  40.4 2.3 %collective-permute-start.15 = (bf16[5,1,96,512]{3,2,0,1:T(8,128)(2,1)S(1)}, bf16[5,1,96,512]{3,2,0,1:T(8,128)(2,1)S(1)}, u32[]{:S(2)}, u32[]{:S(2)}) collective-permute-start(bf16[5,1,96,512]{3,2,0,1:T(8,128)(2,1)S(1)} %bitcast.100), channel_id=1, source_target_pairs={{0,3},{1,0},{2,1},{3,2},{4,7},{5,4},{6,5},{7,6},{8,11},{9,8},{10,9... | collective-permute-start | bytes 1474568 | tf_op jit(solution)/shard_map/ppermute | solution.py:17
  42.7 2.7 %collective-permute-start.7 = (bf16[1,96,512]{2,1,0:T(8,128)(2,1)S(1)}, bf16[1,96,512]{2,1,0:T(8,128)(2,1)S(1)}, u32[]{:S(2)}, u32[]{:S(2)}) collective-permute-start(bf16[1,96,512]{2,1,0:T(8,128)(2,1)S(1)} %collective-permute-done.6), channel_id=1, source_target_pairs={{0,28},{4,0},{8,4},{12,8},{16,12},{20,16},{24,20},{28,24},{1,29},{... | collective-permute-start | bytes 294920 | tf_op jit(solution)/shard_map/ppermute | solution.py:17
  45.6 1.8 collective-permute-done.8
  48.4 6.1 %collective-permute-done.9 = bf16[1,96,512]{2,1,0:T(8,128)(2,1)S(1)} collective-permute-done((bf16[1,96,512]{2,1,0:T(8,128)(2,1)S(1)}, bf16[1,96,512]{2,1,0:T(8,128)(2,1)S(1)}, u32[]{:S(2)}, u32[]{:S(2)}) %collective-permute-start.9) | collective-permute-done | bytes 98336 | tf_op jit(solution)/shard_map/ppermute | solution.py:17
  54.7 2.7 %collective-permute-start.13 = (bf16[3,1,96,512]{3,2,0,1:T(8,128)(2,1)S(1)}, bf16[3,1,96,512]{3,2,0,1:T(8,128)(2,1)S(1)}, u32[]{:S(2)}, u32[]{:S(2)}) collective-permute-start(bf16[3,1,96,512]{3,2,0,1:T(8,128)(2,1)S(1)} %bitcast.104), channel_id=1, source_target_pairs={{0,3},{1,0},{2,1},{3,2},{4,7},{5,4},{6,5},{7,6},{8,11},{9,8},{10,9... | collective-permute-start | bytes 884744 | tf_op jit(solution)/shard_map/ppermute | solution.py:17
  67.8 2.6 %collective-permute-start.14 = (bf16[3,1,96,512]{3,2,0,1:T(8,128)(2,1)S(1)}, bf16[3,1,96,512]{3,2,0,1:T(8,128)(2,1)S(1)}, u32[]{:S(2)}, u32[]{:S(2)}) collective-permute-start(bf16[3,1,96,512]{3,2,0,1:T(8,128)(2,1)S(1)} %collective-permute-done.13), channel_id=1, source_target_pairs={{0,3},{1,0},{2,1},{3,2},{4,7},{5,4},{6,5},{7,6},{8,11},{9,8},{10,9... | collective-permute-start | bytes 884744 | tf_op jit(solution)/shard_map/ppermute | solution.py:17
  70.6 2.4 %collective-permute-done.12 = bf16[5,1,96,512]{3,2,0,1:T(8,128)(2,1)S(1)} collective-permute-done((bf16[5,1,96,512]{3,2,0,1:T(8,128)(2,1)S(1)}, bf16[5,1,96,512]{3,2,0,1:T(8,128)(2,1)S(1)}, u32[]{:S(2)}, u32[]{:S(2)}) %collective-permute-start.12) | collective-permute-done | bytes 491552 | tf_op jit(solution)/shard_map/ppermute | solution.py:17
  73.1 4.4 %collective-permute-done.14 = bf16[3,1,96,512]{3,2,0,1:T(8,128)(2,1)S(1)} collective-permute-done((bf16[3,1,96,512]{3,2,0,1:T(8,128)(2,1)S(1)}, bf16[3,1,96,512]{3,2,0,1:T(8,128)(2,1)S(1)}, u32[]{:S(2)}, u32[]{:S(2)}) %collective-permute-start.14) | collective-permute-done | bytes 294944 | tf_op jit(solution)/shard_map/ppermute | solution.py:17
  77.8 2.7 %convolution_convert_fusion.1 = bf16[512,768]{1,0:T(8,128)(2,1)S(1)} fusion(bf16[3072,512]{1,0:T(8,128)(2,1)S(1)} %bitcast.94, bf16[768,3072]{1,0:T(8,128)(2,1)S(1)} %bitcast.110), kind=kOutput, calls=%fused_computation.2 | convolution fusion | flops 2416312320 | bytes 8650752 | tf_op jit(solution)/shard_map/qj,pq->jp/dot_general | solution.py:154
  80.5 2.5 %all-gather.2.cloned.1.call-done = bf16[3072,512]{1,0:T(8,128)(2,1)} async-done(((bf16[384,512]{1,0:T(8,128)(2,1)}), bf16[3072,512]{1,0:T(8,128)(2,1)}) %all-gather.2.cloned.1.call-update) | async-done | bytes 3145744 | tf_op jit(solution)/shard_map/all_gather | solution.py:53
  83.0 2.4 %broadcast_select_fusion = (bf16[768,512]{1,0:T(8,128)(2,1)}, bf16[768,512]{1,0:T(8,128)(2,1)S(1)}) fusion(bf16[768,512]{1,0:T(8,128)(2,1)} %bitcast.12, pred[]{:T(512)S(6)} %eq.63, bf16[3072,512]{1,0:T(8,128)(2,1)} %all-gather.2.cloned.1.call-done, s32[]{:T(128)S(6)} %select_n.262), kind=kLoop, calls=%fused_computation.30 | loop fusion | flops 393216 | bytes 3145733 | tf_op jit(solution)/shard_map/jit(_where)/select_n | solution.py:180
  86.8 5.1 %convolution_convert_fusion = bf16[512,768]{1,0:T(8,128)(2,1)S(1)} fusion(bf16[3072,512]{1,0:T(8,128)(2,1)S(1)} %copy-done.5, bf16[768,3072]{1,0:T(8,128)(2,1)} %param.8), kind=kOutput, calls=%fused_computation.1 | convolution fusion | flops 2416312320 | bytes 8650752 | tf_op jit(solution)/shard_map/qj,pq->jp/dot_general | solution.py:154
  93.7 17.4 %collective-permute-start.21 = (bf16[512,768]{1,0:T(8,128)(2,1)S(1)}, bf16[512,768]{1,0:T(8,128)(2,1)}, u32[]{:S(2)}, u32[]{:S(2)}) collective-permute-start(bf16[512,768]{1,0:T(8,128)(2,1)S(1)} %broadcast_select_fusion.1), channel_id=1, source_target_pairs={{0,32},{32,0},{1,33},{33,1},{2,34},{34,2},{3,35},{35,3},{4,36},{36... | collective-permute-start | bytes 2359304 | tf_op jit(solution)/shard_map/ppermute | solution.py:92
  117.2 4.2 %collective-permute-start.23 = (bf16[128,768]{1,0:T(8,128)(2,1)S(1)}, bf16[128,768]{1,0:T(8,128)(2,1)S(1)}, u32[]{:S(2)}, u32[]{:S(2)}) collective-permute-start(bf16[128,768]{1,0:T(8,128)(2,1)S(1)} %get-tuple-element.30), channel_id=1, source_target_pairs={{0,64},{64,128},{128,192},{192,0},{1,65},{65,129},{129,193},{193,1... | collective-permute-start | bytes 589832 | tf_op jit(solution)/shard_map/ppermute | solution.py:17
  121.4 1.9 collective-permute-done.22
  123.3 5.6 %collective-permute-start.24 = (bf16[128,768]{1,0:T(8,128)(2,1)S(1)}, bf16[128,768]{1,0:T(8,128)(2,1)S(1)}, u32[]{:S(2)}, u32[]{:S(2)}) collective-permute-start(bf16[128,768]{1,0:T(8,128)(2,1)S(1)} %get-tuple-element.29), channel_id=1, source_target_pairs={{0,192},{64,0},{128,64},{192,128},{1,193},{65,1},{129,65},{193,129... | collective-permute-start | bytes 589832 | tf_op jit(solution)/shard_map/ppermute | solution.py:17
  129.5 2.0 %collective-permute-done.24 = bf16[128,768]{1,0:T(8,128)(2,1)S(1)} collective-permute-done((bf16[128,768]{1,0:T(8,128)(2,1)S(1)}, bf16[128,768]{1,0:T(8,128)(2,1)S(1)}, u32[]{:S(2)}, u32[]{:S(2)}) %collective-permute-start.24) | collective-permute-done | bytes 196640 | tf_op jit(solution)/shard_map/ppermute | solution.py:17
  131.7 3.3 %fusion.1 = bf16[128,512]{1,0:T(8,128)(2,1)S(1)} fusion(bf16[128,768]{1,0:T(8,128)(2,1)S(1)} %fusion.18, bf16[768,512]{1,0:T(8,128)(2,1)} %collective-permute-done.28, bf16[768,512]{1,0:T(8,128)(2,1)} %collective-permute-done.18, bf16[768,512]{1,0:T(8,128)(2,1)} %collective-permute-done.17, bf16[768,512]{1,0:T(8,128)(2,1)} %collective-permute-done.27, ...), kind=kOutput, calls=%fused_computation.6 | convolution fusion | flops 103940096 | bytes 7405570 | tf_op jit(solution)/shard_map/dot_general | solution.py:193
  135.3 2.9 %collective-permute-start.30 = (bf16[32,512]{1,0:T(8,128)(2,1)S(1)}, bf16[32,512]{1,0:T(8,128)(2,1)S(1)}, u32[]{:S(2)}, u32[]{:S(2)}) collective-permute-start(bf16[32,512]{1,0:T(8,128)(2,1)S(1)} %get-tuple-element.41), channel_id=1, source_target_pairs={{0,2},{1,3},{2,0},{3,1},{4,6},{5,7},{6,4},{7,5},{8,10},{9,11},{10,... | collective-permute-start | bytes 98312 | tf_op jit(solution)/shard_map/ppermute | solution.py:107
  139.9 2.3 %collective-permute-done.31 = bf16[32,512]{1,0:T(8,128)(2,1)S(1)} collective-permute-done((bf16[32,512]{1,0:T(8,128)(2,1)S(1)}, bf16[32,512]{1,0:T(8,128)(2,1)S(1)}, u32[]{:S(2)}, u32[]{:S(2)}) %collective-permute-start.31) | collective-permute-done | bytes 32800 | tf_op jit(solution)/shard_map/ppermute | solution.py:107
  143.0 14.5 %all-to-all-start = ((bf16[8,32,512]{2,1,0:T(8,128)(2,1)}), bf16[8,32,512]{2,1,0:T(8,128)(2,1)S(1)}, u32[]{:S(2)}, u32[]{:S(2)}) async-start(bf16[8,32,512]{2,1,0:T(8,128)(2,1)} %broadcast_in_dim.47), calls=%async_computation | async-start | bytes 524288 | tf_op jit(solution)/shard_map/all_to_all | solution.py:119
  157.5 6.6 %collective-permute-start.25 = (bf16[64,768]{1,0:T(8,128)(2,1)S(1)}, bf16[64,768]{1,0:T(8,128)(2,1)S(1)}, u32[]{:S(2)}, u32[]{:S(2)}) collective-permute-start(bf16[64,768]{1,0:T(8,128)(2,1)S(1)} %dynamic-slice_bitcast_fusion.3), channel_id=1, source_target_pairs={{0,32},{32,0},{1,33},{33,1},{2,34},{34,2},{3,35},{35,3},{4,36},{36... | collective-permute-start | bytes 294920 | tf_op jit(solution)/shard_map/ppermute | solution.py:133
  166.9 2.3 %collective-permute-start.33 = (bf16[32,512]{1,0:T(8,128)(2,1)S(1)}, bf16[32,512]{1,0:T(8,128)(2,1)S(1)}, u32[]{:S(2)}, u32[]{:S(2)}) collective-permute-start(bf16[32,512]{1,0:T(8,128)(2,1)S(1)} %reduce_sum.12), channel_id=1, source_target_pairs={{0,2},{1,3},{2,0},{3,1},{4,6},{5,7},{6,4},{7,5},{8,10},{9,11},{10,... | collective-permute-start | bytes 98312 | tf_op jit(solution)/shard_map/ppermute | solution.py:107
  171.3 2.2 %collective-permute-done.34 = bf16[32,512]{1,0:T(8,128)(2,1)S(1)} collective-permute-done((bf16[32,512]{1,0:T(8,128)(2,1)S(1)}, bf16[32,512]{1,0:T(8,128)(2,1)S(1)}, u32[]{:S(2)}, u32[]{:S(2)}) %collective-permute-start.34) | collective-permute-done | bytes 32800 | tf_op jit(solution)/shard_map/ppermute | solution.py:107
  173.5 9.1 %collective-permute-start.35 = (bf16[64,512]{1,0:T(8,128)(2,1)S(1)}, bf16[64,512]{1,0:T(8,128)(2,1)S(1)}, u32[]{:S(2)}, u32[]{:S(2)}) collective-permute-start(bf16[64,512]{1,0:T(8,128)(2,1)S(1)} %dynamic-slice_bitcast_fusion.4), channel_id=1, source_target_pairs={{0,32},{32,0},{1,33},{33,1},{2,34},{34,2},{3,35},{35,3},{4,36},{36... | collective-permute-start | bytes 196616 | tf_op jit(solution)/shard_map/ppermute | solution.py:133
  (138 shorter events, 39.8 us)
Async XLA Ops:
  7.2 75.8 %all-gather.2.cloned.1.call-start = ((), (), s32[]{:S(2)}) async-start(), calls=%async_computation.1 | async-start | bytes 3538944 | tf_op jit(solution)/shard_map/all_gather | solution.py:53
  9.7 9.0 %collective-permute-start.3 = (bf16[1,96,512]{2,1,0:T(8,128)(2,1)S(1)}, bf16[1,96,512]{2,1,0:T(8,128)(2,1)S(1)}, u32[]{:S(2)}, u32[]{:S(2)}) collective-permute-start(bf16[1,96,512]{2,1,0:T(8,128)(2,1)S(1)} %slice.61), channel_id=1, source_target_pairs={{0,4},{4,8},{8,12},{12,16},{16,20},{20,24},{24,28},{28,0},{1,5},{5... | collective-permute-start | bytes 294920 | tf_op jit(solution)/shard_map/ppermute | solution.py:17
  18.7 4.7 %collective-permute-start.4 = (bf16[1,96,512]{2,1,0:T(8,128)(2,1)S(1)}, bf16[1,96,512]{2,1,0:T(8,128)(2,1)S(1)}, u32[]{:S(2)}, u32[]{:S(2)}) collective-permute-start(bf16[1,96,512]{2,1,0:T(8,128)(2,1)S(1)} %collective-permute-done.3), channel_id=1, source_target_pairs={{0,4},{4,8},{8,12},{12,16},{16,20},{20,24},{24,28},{28,0},{1,5},{5... | collective-permute-start | bytes 294920 | tf_op jit(solution)/shard_map/ppermute | solution.py:17
  23.4 5.3 %collective-permute-start = (bf16[96,512]{1,0:T(8,128)(2,1)S(1)}, bf16[96,512]{1,0:T(8,128)(2,1)S(1)}, u32[]{:S(2)}, u32[]{:S(2)}) collective-permute-start(bf16[96,512]{1,0:T(8,128)(2,1)S(1)} %get-tuple-element.38), channel_id=1, source_target_pairs={{0,1},{1,2},{2,3},{3,0},{4,5},{5,6},{6,7},{7,4},{8,9},{9,10},{10,1... | collective-permute-start | bytes 294920 | tf_op jit(solution)/shard_map/ppermute | solution.py:17
  24.9 5.6 %collective-permute-start.1 = (bf16[96,512]{1,0:T(8,128)(2,1)S(1)}, bf16[96,512]{1,0:T(8,128)(2,1)S(1)}, u32[]{:S(2)}, u32[]{:S(2)}) collective-permute-start(bf16[96,512]{1,0:T(8,128)(2,1)S(1)} %get-tuple-element.38), channel_id=1, source_target_pairs={{0,2},{1,3},{2,0},{3,1},{4,6},{5,7},{6,4},{7,5},{8,10},{9,11},{10,... | collective-permute-start | bytes 294920 | tf_op jit(solution)/shard_map/ppermute | solution.py:17
  35.8 4.2 %collective-permute-start.6 = (bf16[1,96,512]{2,1,0:T(8,128)(2,1)S(1)}, bf16[1,96,512]{2,1,0:T(8,128)(2,1)S(1)}, u32[]{:S(2)}, u32[]{:S(2)}) collective-permute-start(bf16[1,96,512]{2,1,0:T(8,128)(2,1)S(1)} %collective-permute-done.5), channel_id=1, source_target_pairs={{0,28},{4,0},{8,4},{12,8},{16,12},{20,16},{24,20},{28,24},{1,29},{... | collective-permute-start | bytes 294920 | tf_op jit(solution)/shard_map/ppermute | solution.py:17
  40.0 20.6 %collective-permute-start.10 = (bf16[5,1,96,512]{3,2,0,1:T(8,128)(2,1)S(1)}, bf16[5,1,96,512]{3,2,0,1:T(8,128)(2,1)S(1)}, u32[]{:S(2)}, u32[]{:S(2)}) collective-permute-start(bf16[5,1,96,512]{3,2,0,1:T(8,128)(2,1)S(1)} %bitcast.99), channel_id=1, source_target_pairs={{0,1},{1,2},{2,3},{3,0},{4,5},{5,6},{6,7},{7,4},{8,9},{9,10},{10,1... | collective-permute-start | bytes 1474568 | tf_op jit(solution)/shard_map/ppermute | solution.py:17
  40.4 23.1 %collective-permute-start.15 = (bf16[5,1,96,512]{3,2,0,1:T(8,128)(2,1)S(1)}, bf16[5,1,96,512]{3,2,0,1:T(8,128)(2,1)S(1)}, u32[]{:S(2)}, u32[]{:S(2)}) collective-permute-start(bf16[5,1,96,512]{3,2,0,1:T(8,128)(2,1)S(1)} %bitcast.100), channel_id=1, source_target_pairs={{0,3},{1,0},{2,1},{3,2},{4,7},{5,4},{6,5},{7,6},{8,11},{9,8},{10,9... | collective-permute-start | bytes 1474568 | tf_op jit(solution)/shard_map/ppermute | solution.py:17
  42.7 4.7 %collective-permute-start.8 = (bf16[1,96,512]{2,1,0:T(8,128)(2,1)S(1)}, bf16[1,96,512]{2,1,0:T(8,128)(2,1)S(1)}, u32[]{:S(2)}, u32[]{:S(2)}) collective-permute-start(bf16[1,96,512]{2,1,0:T(8,128)(2,1)S(1)} %collective-permute-done.4), channel_id=1, source_target_pairs={{0,4},{4,8},{8,12},{12,16},{16,20},{20,24},{24,28},{28,0},{1,5},{5... | collective-permute-start | bytes 294920 | tf_op jit(solution)/shard_map/ppermute | solution.py:17
  42.7 5.7 %collective-permute-start.7 = (bf16[1,96,512]{2,1,0:T(8,128)(2,1)S(1)}, bf16[1,96,512]{2,1,0:T(8,128)(2,1)S(1)}, u32[]{:S(2)}, u32[]{:S(2)}) collective-permute-start(bf16[1,96,512]{2,1,0:T(8,128)(2,1)S(1)} %collective-permute-done.6), channel_id=1, source_target_pairs={{0,28},{4,0},{8,4},{12,8},{16,12},{20,16},{24,20},{28,24},{1,29},{... | collective-permute-start | bytes 294920 | tf_op jit(solution)/shard_map/ppermute | solution.py:17
  47.4 7.1 %collective-permute-start.9 = (bf16[1,96,512]{2,1,0:T(8,128)(2,1)S(1)}, bf16[1,96,512]{2,1,0:T(8,128)(2,1)S(1)}, u32[]{:S(2)}, u32[]{:S(2)}) collective-permute-start(bf16[1,96,512]{2,1,0:T(8,128)(2,1)S(1)} %collective-permute-done.8), channel_id=1, source_target_pairs={{0,4},{4,8},{8,12},{12,16},{16,20},{20,24},{24,28},{28,0},{1,5},{5... | collective-permute-start | bytes 294920 | tf_op jit(solution)/shard_map/ppermute | solution.py:17
  54.6 7.3 %collective-permute-start.11 = (bf16[3,1,96,512]{3,2,0,1:T(8,128)(2,1)S(1)}, bf16[3,1,96,512]{3,2,0,1:T(8,128)(2,1)S(1)}, u32[]{:S(2)}, u32[]{:S(2)}) collective-permute-start(bf16[3,1,96,512]{3,2,0,1:T(8,128)(2,1)S(1)} %bitcast.103), channel_id=1, source_target_pairs={{0,1},{1,2},{2,3},{3,0},{4,5},{5,6},{6,7},{7,4},{8,9},{9,10},{10,1... | collective-permute-start | bytes 884744 | tf_op jit(solution)/shard_map/ppermute | solution.py:17
  54.7 9.0 %collective-permute-start.13 = (bf16[3,1,96,512]{3,2,0,1:T(8,128)(2,1)S(1)}, bf16[3,1,96,512]{3,2,0,1:T(8,128)(2,1)S(1)}, u32[]{:S(2)}, u32[]{:S(2)}) collective-permute-start(bf16[3,1,96,512]{3,2,0,1:T(8,128)(2,1)S(1)} %bitcast.104), channel_id=1, source_target_pairs={{0,3},{1,0},{2,1},{3,2},{4,7},{5,4},{6,5},{7,6},{8,11},{9,8},{10,9... | collective-permute-start | bytes 884744 | tf_op jit(solution)/shard_map/ppermute | solution.py:17
  62.0 11.0 %collective-permute-start.12 = (bf16[5,1,96,512]{3,2,0,1:T(8,128)(2,1)S(1)}, bf16[5,1,96,512]{3,2,0,1:T(8,128)(2,1)S(1)}, u32[]{:S(2)}, u32[]{:S(2)}) collective-permute-start(bf16[5,1,96,512]{3,2,0,1:T(8,128)(2,1)S(1)} %collective-permute-done.10), channel_id=1, source_target_pairs={{0,1},{1,2},{2,3},{3,0},{4,5},{5,6},{6,7},{7,4},{8,9},{9,10},{10,1... | collective-permute-start | bytes 1474568 | tf_op jit(solution)/shard_map/ppermute | solution.py:17
  64.6 15.9 %collective-permute-start.17 = (bf16[768,512]{1,0:T(8,128)(2,1)}, bf16[768,512]{1,0:T(8,128)(2,1)}, u32[]{:S(2)}, u32[]{:S(2)}) collective-permute-start(bf16[768,512]{1,0:T(8,128)(2,1)} %bitcast.12), channel_id=1, source_target_pairs={{0,96},{1,97},{2,98},{3,99},{36,100},{37,101},{38,102},{39,103},{7... | collective-permute-start | bytes 2359304 | tf_op jit(solution)/shard_map/ppermute | solution.py:83
  66.3 14.2 %collective-permute-start.18 = (bf16[768,512]{1,0:T(8,128)(2,1)}, bf16[768,512]{1,0:T(8,128)(2,1)}, u32[]{:S(2)}, u32[]{:S(2)}) collective-permute-start(bf16[768,512]{1,0:T(8,128)(2,1)} %bitcast.12), channel_id=1, source_target_pairs={{0,224},{1,225},{2,226},{3,227},{36,228},{37,229},{38,230},{39,231... | collective-permute-start | bytes 2359304 | tf_op jit(solution)/shard_map/ppermute | solution.py:83
  67.8 9.7 %collective-permute-start.14 = (bf16[3,1,96,512]{3,2,0,1:T(8,128)(2,1)S(1)}, bf16[3,1,96,512]{3,2,0,1:T(8,128)(2,1)S(1)}, u32[]{:S(2)}, u32[]{:S(2)}) collective-permute-start(bf16[3,1,96,512]{3,2,0,1:T(8,128)(2,1)S(1)} %collective-permute-done.13), channel_id=1, source_target_pairs={{0,3},{1,0},{2,1},{3,2},{4,7},{5,4},{6,5},{7,6},{8,11},{9,8},{10,9... | collective-permute-start | bytes 884744 | tf_op jit(solution)/shard_map/ppermute | solution.py:17
  85.4 6.5 %collective-permute-start.19 = (bf16[768,512]{1,0:T(8,128)(2,1)S(1)}, bf16[768,512]{1,0:T(8,128)(2,1)S(1)}, u32[]{:S(2)}, u32[]{:S(2)}) collective-permute-start(bf16[768,512]{1,0:T(8,128)(2,1)S(1)} %get-tuple-element.19), channel_id=1, source_target_pairs={{0,64},{1,65},{2,66},{3,67},{36,68},{37,69},{38,70},{39,71},{72,13... | collective-permute-start | bytes 2359304 | tf_op jit(solution)/shard_map/ppermute | solution.py:83
  86.1 5.8 %collective-permute-start.20 = (bf16[768,512]{1,0:T(8,128)(2,1)S(1)}, bf16[768,512]{1,0:T(8,128)(2,1)S(1)}, u32[]{:S(2)}, u32[]{:S(2)}) collective-permute-start(bf16[768,512]{1,0:T(8,128)(2,1)S(1)} %get-tuple-element.19), channel_id=1, source_target_pairs={{0,192},{1,193},{2,194},{3,195},{36,196},{37,197},{38,198},{39,199... | collective-permute-start | bytes 2359304 | tf_op jit(solution)/shard_map/ppermute | solution.py:83
  93.7 21.9 %collective-permute-start.21 = (bf16[512,768]{1,0:T(8,128)(2,1)S(1)}, bf16[512,768]{1,0:T(8,128)(2,1)}, u32[]{:S(2)}, u32[]{:S(2)}) collective-permute-start(bf16[512,768]{1,0:T(8,128)(2,1)S(1)} %broadcast_select_fusion.1), channel_id=1, source_target_pairs={{0,32},{32,0},{1,33},{33,1},{2,34},{34,2},{3,35},{35,3},{4,36},{36... | collective-permute-start | bytes 2359304 | tf_op jit(solution)/shard_map/ppermute | solution.py:92
  111.1 20.5 %collective-permute-start.28 = (bf16[768,512]{1,0:T(8,128)(2,1)}, bf16[768,512]{1,0:T(8,128)(2,1)}, u32[]{:S(2)}, u32[]{:S(2)}) collective-permute-start(bf16[768,512]{1,0:T(8,128)(2,1)} %bitcast.12), channel_id=1, source_target_pairs={{0,160},{1,161},{2,162},{3,163},{36,164},{37,165},{38,166},{39,167... | collective-permute-start | bytes 2359304 | tf_op jit(solution)/shard_map/ppermute | solution.py:83
  112.6 19.0 %collective-permute-start.27 = (bf16[768,512]{1,0:T(8,128)(2,1)}, bf16[768,512]{1,0:T(8,128)(2,1)}, u32[]{:S(2)}, u32[]{:S(2)}) collective-permute-start(bf16[768,512]{1,0:T(8,128)(2,1)} %copy-done.2), channel_id=1, source_target_pairs={{0,128},{1,129},{2,130},{3,131},{36,132},{37,133},{38,134},{39,135... | collective-permute-start | bytes 2359304 | tf_op jit(solution)/shard_map/ppermute | solution.py:83
  114.2 17.5 %collective-permute-start.26 = (bf16[768,512]{1,0:T(8,128)(2,1)}, bf16[768,512]{1,0:T(8,128)(2,1)}, u32[]{:S(2)}, u32[]{:S(2)}) collective-permute-start(bf16[768,512]{1,0:T(8,128)(2,1)} %get-tuple-element.18), channel_id=1, source_target_pairs={{0,32},{1,33},{2,34},{3,35},{36,4},{37,5},{38,6},{39,7},{72,104},{... | collective-permute-start | bytes 2359304 | tf_op jit(solution)/shard_map/ppermute | solution.py:83
  117.1 6.2 %collective-permute-start.22 = (bf16[128,768]{1,0:T(8,128)(2,1)S(1)}, bf16[128,768]{1,0:T(8,128)(2,1)S(1)}, u32[]{:S(2)}, u32[]{:S(2)}) collective-permute-start(bf16[128,768]{1,0:T(8,128)(2,1)S(1)} %get-tuple-element.28), channel_id=1, source_target_pairs={{0,128},{64,192},{128,0},{192,64},{1,129},{65,193},{129,1},{193,65... | collective-permute-start | bytes 589832 | tf_op jit(solution)/shard_map/ppermute | solution.py:17
  117.2 12.2 %collective-permute-start.23 = (bf16[128,768]{1,0:T(8,128)(2,1)S(1)}, bf16[128,768]{1,0:T(8,128)(2,1)S(1)}, u32[]{:S(2)}, u32[]{:S(2)}) collective-permute-start(bf16[128,768]{1,0:T(8,128)(2,1)S(1)} %get-tuple-element.30), channel_id=1, source_target_pairs={{0,64},{64,128},{128,192},{192,0},{1,65},{65,129},{129,193},{193,1... | collective-permute-start | bytes 589832 | tf_op jit(solution)/shard_map/ppermute | solution.py:17
  123.3 8.2 %collective-permute-start.24 = (bf16[128,768]{1,0:T(8,128)(2,1)S(1)}, bf16[128,768]{1,0:T(8,128)(2,1)S(1)}, u32[]{:S(2)}, u32[]{:S(2)}) collective-permute-start(bf16[128,768]{1,0:T(8,128)(2,1)S(1)} %get-tuple-element.29), channel_id=1, source_target_pairs={{0,192},{64,0},{128,64},{192,128},{1,193},{65,1},{129,65},{193,129... | collective-permute-start | bytes 589832 | tf_op jit(solution)/shard_map/ppermute | solution.py:17
  135.3 4.6 %collective-permute-start.30 = (bf16[32,512]{1,0:T(8,128)(2,1)S(1)}, bf16[32,512]{1,0:T(8,128)(2,1)S(1)}, u32[]{:S(2)}, u32[]{:S(2)}) collective-permute-start(bf16[32,512]{1,0:T(8,128)(2,1)S(1)} %get-tuple-element.41), channel_id=1, source_target_pairs={{0,2},{1,3},{2,0},{3,1},{4,6},{5,7},{6,4},{7,5},{8,10},{9,11},{10,... | collective-permute-start | bytes 98312 | tf_op jit(solution)/shard_map/ppermute | solution.py:107
  143.0 23.8 %all-to-all-start = ((bf16[8,32,512]{2,1,0:T(8,128)(2,1)}), bf16[8,32,512]{2,1,0:T(8,128)(2,1)S(1)}, u32[]{:S(2)}, u32[]{:S(2)}) async-start(bf16[8,32,512]{2,1,0:T(8,128)(2,1)} %broadcast_in_dim.47), calls=%async_computation | async-start | bytes 524288 | tf_op jit(solution)/shard_map/all_to_all | solution.py:119
  157.5 7.5 %collective-permute-start.25 = (bf16[64,768]{1,0:T(8,128)(2,1)S(1)}, bf16[64,768]{1,0:T(8,128)(2,1)S(1)}, u32[]{:S(2)}, u32[]{:S(2)}) collective-permute-start(bf16[64,768]{1,0:T(8,128)(2,1)S(1)} %dynamic-slice_bitcast_fusion.3), channel_id=1, source_target_pairs={{0,32},{32,0},{1,33},{33,1},{2,34},{34,2},{3,35},{35,3},{4,36},{36... | collective-permute-start | bytes 294920 | tf_op jit(solution)/shard_map/ppermute | solution.py:133
  166.9 4.4 %collective-permute-start.33 = (bf16[32,512]{1,0:T(8,128)(2,1)S(1)}, bf16[32,512]{1,0:T(8,128)(2,1)S(1)}, u32[]{:S(2)}, u32[]{:S(2)}) collective-permute-start(bf16[32,512]{1,0:T(8,128)(2,1)S(1)} %reduce_sum.12), channel_id=1, source_target_pairs={{0,2},{1,3},{2,0},{3,1},{4,6},{5,7},{6,4},{7,5},{8,10},{9,11},{10,... | collective-permute-start | bytes 98312 | tf_op jit(solution)/shard_map/ppermute | solution.py:107
  169.2 4.3 %collective-permute-start.34 = (bf16[32,512]{1,0:T(8,128)(2,1)S(1)}, bf16[32,512]{1,0:T(8,128)(2,1)S(1)}, u32[]{:S(2)}, u32[]{:S(2)}) collective-permute-start(bf16[32,512]{1,0:T(8,128)(2,1)S(1)} %reduce_sum.12), channel_id=1, source_target_pairs={{0,3},{1,2},{2,1},{3,0},{4,7},{5,6},{6,5},{7,4},{8,11},{9,10},{10,... | collective-permute-start | bytes 98312 | tf_op jit(solution)/shard_map/ppermute | solution.py:107
  173.5 10.0 %collective-permute-start.35 = (bf16[64,512]{1,0:T(8,128)(2,1)S(1)}, bf16[64,512]{1,0:T(8,128)(2,1)S(1)}, u32[]{:S(2)}, u32[]{:S(2)}) collective-permute-start(bf16[64,512]{1,0:T(8,128)(2,1)S(1)} %dynamic-slice_bitcast_fusion.4), channel_id=1, source_target_pairs={{0,32},{32,0},{1,33},{33,1},{2,34},{34,2},{3,35},{35,3},{4,36},{36... | collective-permute-start | bytes 196616 | tf_op jit(solution)/shard_map/ppermute | solution.py:133
  (17 other events, 136.3 us)
Sparse Core Ops, SparseCore 0:
  32.4 50.5 all-gather.1

commit v15 on v9

--- a/solution.py
+++ b/solution.py
@@ -179,11 +179,11 @@
     )
     partial = [partial_of(panel_0)]
 
-    chunks, partial[0], sent_1 = lax.optimization_barrier((chunks, partial[0], sent_1))
+    sent = [*sent_1, *sent_0, across]
+    chunks, partial[0], sent = lax.optimization_barrier((chunks, partial[0], sent))
     partial.append(partial_of(placed_by_owner(chunks, y, 1).reshape(panel_0.shape)))
 
-    sent = [*sent_1, *sent_0, across]
-    pair, sent = lax.optimization_barrier((pair_sum(partial), sent))
+    pair = lax.optimization_barrier(pair_sum(partial))
     product = sum_over_x(pair)
     own_tile = jnp.where(first, tiles_0[0], tiles_1[0])
     factor_tile = sum(sent, jnp.where(row == z, own_tile, jnp.zeros((), BF16)))

time: 172 us -> 175 us (1.017)
  waiting for transfers between devices: 53.4 us -> 59.2 us
    all_to_all x1, starting transfers between devices: 12.6 us -> 5.16 us  [summed_over_col(): part = lax.all_to_all(copies, 'z', split_axis=0, concat_axis=0, tiled=True)]
    ppermute x1, starting transfers between devices: 2.7 us -> 6.37 us  [pair_sum(): lax.ppermute(jnp.where(first, partial[1], partial[0]), 'core', [(0, 1), (...]
    ppermute x23, starting transfers between devices: 30.9 us -> 34.5 us  [shift(): lax.ppermute(array, axis, [(i, (i + by) % size) for i in range(size)])]
    ppermute x23, waiting for transfers between devices: 36.7 us -> 40 us  [shift(): lax.ppermute(array, axis, [(i, (i + by) % size) for i in range(size)])]
    ppermute x1, waiting for transfers between devices: 0.01 us -> 2.03 us  [pair_sum(): lax.ppermute(jnp.where(first, partial[1], partial[0]), 'core', [(0, 1), (...]
  transfers between devices with their start and end apart: 42 -> 42, of which waited for: 18 -> 18; matrix products, arithmetic and copies ran while one was open for 11% -> 9% of each run, Pallas kernels for 0% -> 0%
where the time goes in v15:
time: 175 us
  starting transfers between devices  69.6 us (40%)
  waiting for transfers between devices  59.2 us (34%)
  between operations  15 us (9%)
  local copies, waits for them, and re-layouts  13.7 us (8%)
  matrix products  11.7 us (7%)
  other arithmetic  5.68 us (3%)
    ppermute x23, waiting for transfers between devices, shift(): lax.ppermute(array, axis, [(i, (i + by) % size) for i in range(size)])  40 us
    ppermute x23, starting transfers between devices, shift(): lax.ppermute(array, axis, [(i, (i + by) % size) for i in range(size)])  34.5 us
    all_gather x1, waiting for transfers between devices, panel_y_then_z(): return lax.all_gather(part, 'z', axis=0, tiled=True)  10.9 us
    dot_general x2, matrix products, partial_of(): jnp.dot(inverse_block, panel, preferred_element_type=F32).astype(BF16)  8.6 us
    ppermute x6, starting transfers between devices, exchanged(): return lax.ppermute(array, axis, [(i, i ^ by) for i in range(size)])  7.88 us
    ppermute x2, starting transfers between devices, own_slab_of_both(): got = lax.ppermute(given, 'core', [(0, 1), (1, 0)])  7.84 us
    ppermute x8, starting transfers between devices, from_root(): return lax.ppermute(array, ALL, pairs)  7.8 us
    ppermute x1, starting transfers between devices, pair_sum(): lax.ppermute(jnp.where(first, partial[1], partial[0]), 'core', [(0, 1), (...  6.37 us
  transfers between devices with their start and end apart: 42, of which 18 were waited for; matrix products, arithmetic and copies ran while one was open for 9% of the time, Pallas kernels for 0%

profile of v15, /device:TPU:1, one launch (start us, length us, event | category | flops | bytes accessed | tf_op | source)
XLA Modules:
  0.0 174.9 jit_solution(724234931061532233)
XLA Ops:
  9.7 2.2 %collective-permute-start = (bf16[96,512]{1,0:T(8,128)(2,1)S(1)}, bf16[96,512]{1,0:T(8,128)(2,1)S(1)}, u32[]{:S(2)}, u32[]{:S(2)}) collective-permute-start(bf16[96,512]{1,0:T(8,128)(2,1)S(1)} %get-tuple-element.67), channel_id=1, source_target_pairs={{0,1},{1,2},{2,3},{3,0},{4,5},{5,6},{6,7},{7,4},{8,9},{9,10},{10,1... | collective-permute-start | bytes 294920 | tf_op jit(solution)/shard_map/ppermute | solution.py:17
  11.9 2.6 %collective-permute-start.1 = (bf16[96,512]{1,0:T(8,128)(2,1)S(1)}, bf16[96,512]{1,0:T(8,128)(2,1)S(1)}, u32[]{:S(2)}, u32[]{:S(2)}) collective-permute-start(bf16[96,512]{1,0:T(8,128)(2,1)S(1)} %get-tuple-element.67), channel_id=1, source_target_pairs={{0,2},{1,3},{2,0},{3,1},{4,6},{5,7},{6,4},{7,5},{8,10},{9,11},{10,... | collective-permute-start | bytes 294920 | tf_op jit(solution)/shard_map/ppermute | solution.py:17
  15.7 2.8 %collective-permute-done.1 = bf16[96,512]{1,0:T(8,128)(2,1)S(1)} collective-permute-done((bf16[96,512]{1,0:T(8,128)(2,1)S(1)}, bf16[96,512]{1,0:T(8,128)(2,1)S(1)}, u32[]{:S(2)}, u32[]{:S(2)}) %collective-permute-start.1) | collective-permute-done | bytes 98336 | tf_op jit(solution)/shard_map/ppermute | solution.py:17
  21.0 4.0 %collective-permute-start.7 = (bf16[1,96,512]{2,1,0:T(8,128)(2,1)S(1)}, bf16[1,96,512]{2,1,0:T(8,128)(2,1)S(1)}, u32[]{:S(2)}, u32[]{:S(2)}) collective-permute-start(bf16[1,96,512]{2,1,0:T(8,128)(2,1)S(1)} %get-tuple-element.66), channel_id=1, source_target_pairs={{0,28},{4,0},{8,4},{12,8},{16,12},{20,16},{24,20},{28,24},{1,29},{... | collective-permute-start | bytes 294920 | tf_op jit(solution)/shard_map/ppermute | solution.py:17
  27.0 2.8 %collective-permute-start.8 = (bf16[1,96,512]{2,1,0:T(8,128)(2,1)S(1)}, bf16[1,96,512]{2,1,0:T(8,128)(2,1)S(1)}, u32[]{:S(2)}, u32[]{:S(2)}) collective-permute-start(bf16[1,96,512]{2,1,0:T(8,128)(2,1)S(1)} %collective-permute-done.7), channel_id=1, source_target_pairs={{0,28},{4,0},{8,4},{12,8},{16,12},{20,16},{24,20},{28,24},{1,29},{... | collective-permute-start | bytes 294920 | tf_op jit(solution)/shard_map/ppermute | solution.py:17
  29.8 1.9 %collective-permute-done.4 = bf16[1,96,512]{2,1,0:T(8,128)(2,1)S(1)} collective-permute-done((bf16[1,96,512]{2,1,0:T(8,128)(2,1)S(1)}, bf16[1,96,512]{2,1,0:T(8,128)(2,1)S(1)}, u32[]{:S(2)}, u32[]{:S(2)}) %collective-permute-start.4) | collective-permute-done | bytes 98336 | tf_op jit(solution)/shard_map/ppermute | solution.py:17
  31.7 2.8 %collective-permute-start.9 = (bf16[1,96,512]{2,1,0:T(8,128)(2,1)S(1)}, bf16[1,96,512]{2,1,0:T(8,128)(2,1)S(1)}, u32[]{:S(2)}, u32[]{:S(2)}) collective-permute-start(bf16[1,96,512]{2,1,0:T(8,128)(2,1)S(1)} %collective-permute-done.8), channel_id=1, source_target_pairs={{0,28},{4,0},{8,4},{12,8},{16,12},{20,16},{24,20},{28,24},{1,29},{... | collective-permute-start | bytes 294920 | tf_op jit(solution)/shard_map/ppermute | solution.py:17
  34.4 1.9 %collective-permute-done.5 = bf16[1,96,512]{2,1,0:T(8,128)(2,1)S(1)} collective-permute-done((bf16[1,96,512]{2,1,0:T(8,128)(2,1)S(1)}, bf16[1,96,512]{2,1,0:T(8,128)(2,1)S(1)}, u32[]{:S(2)}, u32[]{:S(2)}) %collective-permute-start.5) | collective-permute-done | bytes 98336 | tf_op jit(solution)/shard_map/ppermute | solution.py:17
  36.4 8.0 %collective-permute-done.6 = bf16[1,96,512]{2,1,0:T(8,128)(2,1)S(1)} collective-permute-done((bf16[1,96,512]{2,1,0:T(8,128)(2,1)S(1)}, bf16[1,96,512]{2,1,0:T(8,128)(2,1)S(1)}, u32[]{:S(2)}, u32[]{:S(2)}) %collective-permute-start.6) | collective-permute-done | bytes 98336 | tf_op jit(solution)/shard_map/ppermute | solution.py:17
  45.2 2.1 %collective-permute-start.11 = (bf16[8,1,96,512]{3,2,1,0:T(8,128)(2,1)S(1)}, bf16[8,1,96,512]{3,2,1,0:T(8,128)(2,1)S(1)}, u32[]{:S(2)}, u32[]{:S(2)}) collective-permute-start(bf16[8,1,96,512]{3,2,1,0:T(8,128)(2,1)S(1)} %bitcast_dynamic-update-slice_fusion), channel_id=1, source_target_pairs={{0,3},{1,0},{2,1},{3,2},{4,7},{5,4},{6,5},{7,6},{8,11},{9,8},{10,9... | collective-permute-start | bytes 2359304 | tf_op jit(solution)/shard_map/ppermute | solution.py:17
  49.4 7.8 %collective-permute-done.10 = bf16[8,1,96,512]{3,2,1,0:T(8,128)(2,1)} collective-permute-done((bf16[8,1,96,512]{3,2,1,0:T(8,128)(2,1)S(1)}, bf16[8,1,96,512]{3,2,1,0:T(8,128)(2,1)}, u32[]{:S(2)}, u32[]{:S(2)}) %collective-permute-start.10) | collective-permute-done | bytes 786464 | tf_op jit(solution)/shard_map/ppermute | solution.py:17
  60.0 10.9 %all-gather.2.cloned.1.call-done = bf16[3072,512]{1,0:T(8,128)(2,1)} async-done(((bf16[384,512]{1,0:T(8,128)(2,1)}), bf16[3072,512]{1,0:T(8,128)(2,1)}) %all-gather.2.cloned.1.call-update) | async-done | bytes 3145744 | tf_op jit(solution)/shard_map/all_gather | solution.py:53
  80.7 2.2 %collective-permute-done.13 = bf16[4,1,96,512]{3,2,1,0:T(8,128)(2,1)S(1)} collective-permute-done((bf16[4,1,96,512]{3,2,1,0:T(8,128)(2,1)S(1)}, bf16[4,1,96,512]{3,2,1,0:T(8,128)(2,1)S(1)}, u32[]{:S(2)}, u32[]{:S(2)}) %collective-permute-start.13) | collective-permute-done | bytes 393248 | tf_op jit(solution)/shard_map/ppermute | solution.py:17
  85.0 5.9 %fusion = bf16[768,512]{0,1:T(8,128)(2,1)S(1)} fusion(bf16[3072,512]{1,0:T(8,128)(2,1)} %all-gather.2.cloned.1.call-done, bf16[768,3072]{1,0:T(8,128)(2,1)} %param.8), kind=kOutput, calls=%fused_computation.4 | convolution fusion | flops 2416312320 | bytes 8650752 | tf_op jit(solution)/shard_map/dot_general | solution.py:154
  94.4 2.7 %broadcast_select_fusion = (bf16[768,512]{0,1:T(8,128)(2,1)S(1)}, bf16[768,512]{0,1:T(8,128)(2,1)S(1)}) fusion(bf16[768,512]{0,1:T(8,128)(2,1)S(1)} %fusion, pred[]{:T(512)S(6)} %eq.83, bf16[3072,512]{1,0:T(8,128)(2,1)S(1)} %bitcast.110, bf16[768,3072]{1,0:T(8,128)(2,1)S(1)} %bitcast.123), kind=kOutput, calls=%fused_computation.10 | convolution fusion | flops 2416705536 | bytes 10223617 | tf_op jit(solution)/shard_map/dot_general | solution.py:154
  97.1 6.4 %collective-permute-start.22 = (bf16[768,512]{0,1:T(8,128)(2,1)S(1)}, bf16[768,512]{0,1:T(8,128)(2,1)}, u32[]{:S(2)}, u32[]{:S(2)}) collective-permute-start(bf16[768,512]{0,1:T(8,128)(2,1)S(1)} %get-tuple-element.71), channel_id=1, source_target_pairs={{0,32},{32,0},{1,33},{33,1},{2,34},{34,2},{3,35},{35,3},{4,36},{36... | collective-permute-start | bytes 2359304 | tf_op jit(solution)/shard_map/ppermute | solution.py:92
  103.5 2.0 %collective-permute-done.22 = bf16[768,512]{0,1:T(8,128)(2,1)} collective-permute-done((bf16[768,512]{0,1:T(8,128)(2,1)S(1)}, bf16[768,512]{0,1:T(8,128)(2,1)}, u32[]{:S(2)}, u32[]{:S(2)}) %collective-permute-start.22) | collective-permute-done | bytes 786464 | tf_op jit(solution)/shard_map/ppermute | solution.py:92
  107.3 1.9 %collective-permute-start.23 = (bf16[192,512]{1,0:T(8,128)(2,1)S(1)}, bf16[192,512]{1,0:T(8,128)(2,1)S(1)}, u32[]{:S(2)}, u32[]{:S(2)}) collective-permute-start(bf16[192,512]{1,0:T(8,128)(2,1)S(1)} %get-tuple-element.46), channel_id=1, source_target_pairs={{0,128},{64,192},{128,0},{192,64},{1,129},{65,193},{129,1},{193,65... | collective-permute-start | bytes 589832 | tf_op jit(solution)/shard_map/ppermute | solution.py:17
  109.2 2.7 %collective-permute-start.25 = (bf16[192,512]{1,0:T(8,128)(2,1)S(1)}, bf16[192,512]{1,0:T(8,128)(2,1)S(1)}, u32[]{:S(2)}, u32[]{:S(2)}) collective-permute-start(bf16[192,512]{1,0:T(8,128)(2,1)S(1)} %get-tuple-element.47), channel_id=1, source_target_pairs={{0,192},{64,0},{128,64},{192,128},{1,193},{65,1},{129,65},{193,129... | collective-permute-start | bytes 589832 | tf_op jit(solution)/shard_map/ppermute | solution.py:17
  112.0 2.8 %collective-permute-done.23 = bf16[192,512]{1,0:T(8,128)(2,1)S(1)} collective-permute-done((bf16[192,512]{1,0:T(8,128)(2,1)S(1)}, bf16[192,512]{1,0:T(8,128)(2,1)S(1)}, u32[]{:S(2)}, u32[]{:S(2)}) %collective-permute-start.23) | collective-permute-done | bytes 196640 | tf_op jit(solution)/shard_map/ppermute | solution.py:17
  114.8 5.2 %collective-permute-done.24 = bf16[192,512]{1,0:T(8,128)(2,1)S(1)} collective-permute-done((bf16[192,512]{1,0:T(8,128)(2,1)S(1)}, bf16[192,512]{1,0:T(8,128)(2,1)S(1)}, u32[]{:S(2)}, u32[]{:S(2)}) %collective-permute-start.24) | collective-permute-done | bytes 196640 | tf_op jit(solution)/shard_map/ppermute | solution.py:17
  123.2 2.7 %collective-permute-start.32 = (bf16[128,512]{1,0:T(8,128)(2,1)S(1)}, bf16[128,512]{1,0:T(8,128)(2,1)S(1)}, u32[]{:S(2)}, u32[]{:S(2)}) collective-permute-start(bf16[128,512]{1,0:T(8,128)(2,1)S(1)} %get-tuple-element.56), channel_id=1, source_target_pairs={{0,192},{64,0},{128,64},{192,128},{1,193},{65,1},{129,65},{193,129... | collective-permute-start | bytes 393224 | tf_op jit(solution)/shard_map/ppermute | solution.py:17
  125.9 2.3 %collective-permute-done.30 = bf16[128,512]{1,0:T(8,128)(2,1)S(1)} collective-permute-done((bf16[128,512]{1,0:T(8,128)(2,1)S(1)}, bf16[128,512]{1,0:T(8,128)(2,1)S(1)}, u32[]{:S(2)}, u32[]{:S(2)}) %collective-permute-start.30) | collective-permute-done | bytes 131104 | tf_op jit(solution)/shard_map/ppermute | solution.py:17
  128.2 3.5 %collective-permute-done.31 = bf16[128,512]{1,0:T(8,128)(2,1)S(1)} collective-permute-done((bf16[128,512]{1,0:T(8,128)(2,1)S(1)}, bf16[128,512]{1,0:T(8,128)(2,1)S(1)}, u32[]{:S(2)}, u32[]{:S(2)}) %collective-permute-start.31) | collective-permute-done | bytes 131104 | tf_op jit(solution)/shard_map/ppermute | solution.py:17
  131.9 2.4 %collective-permute-start.34 = (bf16[32,512]{1,0:T(8,128)(2,1)S(1)}, bf16[32,512]{1,0:T(8,128)(2,1)S(1)}, u32[]{:S(2)}, u32[]{:S(2)}) collective-permute-start(bf16[32,512]{1,0:T(8,128)(2,1)S(1)} %get-tuple-element.70), channel_id=1, source_target_pairs={{0,2},{1,3},{2,0},{3,1},{4,6},{5,7},{6,4},{7,5},{8,10},{9,11},{10,... | collective-permute-start | bytes 98312 | tf_op jit(solution)/shard_map/ppermute | solution.py:107
  137.2 2.0 %collective-permute-start.28 = (bf16[192,128]{1,0:T(8,128)(2,1)S(1)}, bf16[192,128]{1,0:T(8,128)(2,1)S(1)}, u32[]{:S(2)}, u32[]{:S(2)}) collective-permute-start(bf16[192,128]{1,0:T(8,128)(2,1)S(1)} %get-tuple-element.62), channel_id=1, source_target_pairs={{0,192},{64,0},{128,64},{192,128},{1,193},{65,1},{129,65},{193,129... | collective-permute-start | bytes 147464 | tf_op jit(solution)/shard_map/ppermute | solution.py:17
  139.9 5.2 %all-to-all-start = ((bf16[8,32,512]{2,1,0:T(8,128)(2,1)}), bf16[8,32,512]{2,1,0:T(8,128)(2,1)S(1)}, u32[]{:S(2)}, u32[]{:S(2)}) async-start(bf16[8,32,512]{2,1,0:T(8,128)(2,1)} %broadcast_in_dim.77), calls=%async_computation | async-start | bytes 524288 | tf_op jit(solution)/shard_map/all_to_all | solution.py:119
  148.4 2.5 %collective-permute-start.29 = (bf16[64,768]{1,0:T(8,128)(2,1)S(1)}, bf16[64,768]{1,0:T(8,128)(2,1)S(1)}, u32[]{:S(2)}, u32[]{:S(2)}) collective-permute-start(bf16[64,768]{1,0:T(8,128)(2,1)S(1)} %dynamic-slice_bitcast_fusion.6), channel_id=1, source_target_pairs={{0,32},{32,0},{1,33},{33,1},{2,34},{34,2},{3,35},{35,3},{4,36},{36... | collective-permute-start | bytes 294920 | tf_op jit(solution)/shard_map/ppermute | solution.py:133
  152.0 2.6 %all-to-all-done = bf16[8,32,512]{2,1,0:T(8,128)(2,1)S(1)} async-done(((bf16[8,32,512]{2,1,0:T(8,128)(2,1)}), bf16[8,32,512]{2,1,0:T(8,128)(2,1)S(1)}, u32[]{:S(2)}, u32[]{:S(2)}) %all-to-all-start) | async-done | bytes 262176 | tf_op jit(solution)/shard_map/all_to_all | solution.py:119
  154.7 2.4 %collective-permute-start.37 = (bf16[32,512]{1,0:T(8,128)(2,1)S(1)}, bf16[32,512]{1,0:T(8,128)(2,1)S(1)}, u32[]{:S(2)}, u32[]{:S(2)}) collective-permute-start(bf16[32,512]{1,0:T(8,128)(2,1)S(1)} %reduce_sum.12), channel_id=1, source_target_pairs={{0,2},{1,3},{2,0},{3,1},{4,6},{5,7},{6,4},{7,5},{8,10},{9,11},{10,... | collective-permute-start | bytes 98312 | tf_op jit(solution)/shard_map/ppermute | solution.py:107
  159.0 2.0 %collective-permute-done.38 = bf16[32,512]{1,0:T(8,128)(2,1)S(1)} collective-permute-done((bf16[32,512]{1,0:T(8,128)(2,1)S(1)}, bf16[32,512]{1,0:T(8,128)(2,1)S(1)}, u32[]{:S(2)}, u32[]{:S(2)}) %collective-permute-start.38) | collective-permute-done | bytes 32800 | tf_op jit(solution)/shard_map/ppermute | solution.py:107
  161.1 5.3 %collective-permute-start.39 = (bf16[64,512]{1,0:T(8,128)(2,1)S(1)}, bf16[64,512]{1,0:T(8,128)(2,1)S(1)}, u32[]{:S(2)}, u32[]{:S(2)}) collective-permute-start(bf16[64,512]{1,0:T(8,128)(2,1)S(1)} %dynamic-slice_bitcast_fusion.7), channel_id=1, source_target_pairs={{0,32},{32,0},{1,33},{33,1},{2,34},{34,2},{3,35},{35,3},{4,36},{36... | collective-permute-start | bytes 196616 | tf_op jit(solution)/shard_map/ppermute | solution.py:133
  (159 shorter events, 45.6 us)
Async XLA Ops:
  7.2 63.7 %all-gather.2.cloned.1.call-start = ((), (), s32[]{:S(2)}) async-start(), calls=%async_computation.1 | async-start | bytes 3538944 | tf_op jit(solution)/shard_map/all_gather | solution.py:53
  9.7 6.0 %collective-permute-start = (bf16[96,512]{1,0:T(8,128)(2,1)S(1)}, bf16[96,512]{1,0:T(8,128)(2,1)S(1)}, u32[]{:S(2)}, u32[]{:S(2)}) collective-permute-start(bf16[96,512]{1,0:T(8,128)(2,1)S(1)} %get-tuple-element.67), channel_id=1, source_target_pairs={{0,1},{1,2},{2,3},{3,0},{4,5},{5,6},{6,7},{7,4},{8,9},{9,10},{10,1... | collective-permute-start | bytes 294920 | tf_op jit(solution)/shard_map/ppermute | solution.py:17
  11.9 6.6 %collective-permute-start.1 = (bf16[96,512]{1,0:T(8,128)(2,1)S(1)}, bf16[96,512]{1,0:T(8,128)(2,1)S(1)}, u32[]{:S(2)}, u32[]{:S(2)}) collective-permute-start(bf16[96,512]{1,0:T(8,128)(2,1)S(1)} %get-tuple-element.67), channel_id=1, source_target_pairs={{0,2},{1,3},{2,0},{3,1},{4,6},{5,7},{6,4},{7,5},{8,10},{9,11},{10,... | collective-permute-start | bytes 294920 | tf_op jit(solution)/shard_map/ppermute | solution.py:17
  19.3 7.7 %collective-permute-start.3 = (bf16[1,96,512]{2,1,0:T(8,128)(2,1)S(1)}, bf16[1,96,512]{2,1,0:T(8,128)(2,1)S(1)}, u32[]{:S(2)}, u32[]{:S(2)}) collective-permute-start(bf16[1,96,512]{2,1,0:T(8,128)(2,1)S(1)} %get-tuple-element.66), channel_id=1, source_target_pairs={{0,4},{4,8},{8,12},{12,16},{16,20},{20,24},{24,28},{28,0},{1,5},{5... | collective-permute-start | bytes 294920 | tf_op jit(solution)/shard_map/ppermute | solution.py:17
  21.0 6.0 %collective-permute-start.7 = (bf16[1,96,512]{2,1,0:T(8,128)(2,1)S(1)}, bf16[1,96,512]{2,1,0:T(8,128)(2,1)S(1)}, u32[]{:S(2)}, u32[]{:S(2)}) collective-permute-start(bf16[1,96,512]{2,1,0:T(8,128)(2,1)S(1)} %get-tuple-element.66), channel_id=1, source_target_pairs={{0,28},{4,0},{8,4},{12,8},{16,12},{20,16},{24,20},{28,24},{1,29},{... | collective-permute-start | bytes 294920 | tf_op jit(solution)/shard_map/ppermute | solution.py:17
  31.7 12.7 %collective-permute-start.9 = (bf16[1,96,512]{2,1,0:T(8,128)(2,1)S(1)}, bf16[1,96,512]{2,1,0:T(8,128)(2,1)S(1)}, u32[]{:S(2)}, u32[]{:S(2)}) collective-permute-start(bf16[1,96,512]{2,1,0:T(8,128)(2,1)S(1)} %collective-permute-done.8), channel_id=1, source_target_pairs={{0,28},{4,0},{8,4},{12,8},{16,12},{20,16},{24,20},{28,24},{1,29},{... | collective-permute-start | bytes 294920 | tf_op jit(solution)/shard_map/ppermute | solution.py:17
  36.3 8.1 %collective-permute-start.6 = (bf16[1,96,512]{2,1,0:T(8,128)(2,1)S(1)}, bf16[1,96,512]{2,1,0:T(8,128)(2,1)S(1)}, u32[]{:S(2)}, u32[]{:S(2)}) collective-permute-start(bf16[1,96,512]{2,1,0:T(8,128)(2,1)S(1)} %collective-permute-done.5), channel_id=1, source_target_pairs={{0,4},{4,8},{8,12},{12,16},{16,20},{20,24},{24,28},{28,0},{1,5},{5... | collective-permute-start | bytes 294920 | tf_op jit(solution)/shard_map/ppermute | solution.py:17
  44.5 12.6 %collective-permute-start.10 = (bf16[8,1,96,512]{3,2,1,0:T(8,128)(2,1)S(1)}, bf16[8,1,96,512]{3,2,1,0:T(8,128)(2,1)}, u32[]{:S(2)}, u32[]{:S(2)}) collective-permute-start(bf16[8,1,96,512]{3,2,1,0:T(8,128)(2,1)S(1)} %bitcast_dynamic-update-slice_fusion), channel_id=1, source_target_pairs={{0,1},{1,2},{2,3},{3,0},{4,5},{5,6},{6,7},{7,4},{8,9},{9,10},{10,1... | collective-permute-start | bytes 2359304 | tf_op jit(solution)/shard_map/ppermute | solution.py:17
  45.2 13.9 %collective-permute-start.11 = (bf16[8,1,96,512]{3,2,1,0:T(8,128)(2,1)S(1)}, bf16[8,1,96,512]{3,2,1,0:T(8,128)(2,1)S(1)}, u32[]{:S(2)}, u32[]{:S(2)}) collective-permute-start(bf16[8,1,96,512]{3,2,1,0:T(8,128)(2,1)S(1)} %bitcast_dynamic-update-slice_fusion), channel_id=1, source_target_pairs={{0,3},{1,0},{2,1},{3,2},{4,7},{5,4},{6,5},{7,6},{8,11},{9,8},{10,9... | collective-permute-start | bytes 2359304 | tf_op jit(solution)/shard_map/ppermute | solution.py:17
  48.0 10.0 %collective-permute-start.12 = (bf16[2,1,96,512]{3,2,1,0:T(8,128)(2,1)}, bf16[2,1,96,512]{3,2,1,0:T(8,128)(2,1)}, u32[]{:S(2)}, u32[]{:S(2)}) collective-permute-start(bf16[2,1,96,512]{3,2,1,0:T(8,128)(2,1)} %get-tuple-element.53), channel_id=1, source_target_pairs={{0,2},{1,3},{2,0},{3,1},{36,38},{37,39},{38,36},{39,37},{72,74},{7... | collective-permute-start | bytes 589832 | tf_op jit(solution)/shard_map/ppermute | solution.py:81
  71.9 11.0 %collective-permute-start.13 = (bf16[4,1,96,512]{3,2,1,0:T(8,128)(2,1)S(1)}, bf16[4,1,96,512]{3,2,1,0:T(8,128)(2,1)S(1)}, u32[]{:S(2)}, u32[]{:S(2)}) collective-permute-start(bf16[4,1,96,512]{3,2,1,0:T(8,128)(2,1)S(1)} %slice.18), channel_id=1, source_target_pairs={{0,1},{1,2},{2,3},{3,0},{4,5},{5,6},{6,7},{7,4},{8,9},{9,10},{10,1... | collective-permute-start | bytes 1179656 | tf_op jit(solution)/shard_map/ppermute | solution.py:17
  73.2 10.4 %collective-permute-start.14 = (bf16[4,1,96,512]{3,2,1,0:T(8,128)(2,1)S(1)}, bf16[4,1,96,512]{3,2,1,0:T(8,128)(2,1)S(1)}, u32[]{:S(2)}, u32[]{:S(2)}) collective-permute-start(bf16[4,1,96,512]{3,2,1,0:T(8,128)(2,1)S(1)} %slice.19), channel_id=1, source_target_pairs={{0,3},{1,0},{2,1},{3,2},{4,7},{5,4},{6,5},{7,6},{8,11},{9,8},{10,9... | collective-permute-start | bytes 1179656 | tf_op jit(solution)/shard_map/ppermute | solution.py:17
  77.9 13.1 %collective-permute-start.20 = (bf16[192,512]{1,0:T(8,128)(2,1)S(1)}, bf16[192,512]{1,0:T(8,128)(2,1)S(1)}, u32[]{:S(2)}, u32[]{:S(2)}) collective-permute-start(bf16[192,512]{1,0:T(8,128)(2,1)S(1)} %get-tuple-element.43), channel_id=1, source_target_pairs={{0,192},{1,193},{2,194},{3,195},{36,196},{37,197},{38,198},{39,199... | collective-permute-start | bytes 589832 | tf_op jit(solution)/shard_map/ppermute | solution.py:81
  78.6 12.5 %collective-permute-start.21 = (bf16[192,512]{1,0:T(8,128)(2,1)S(1)}, bf16[192,512]{1,0:T(8,128)(2,1)S(1)}, u32[]{:S(2)}, u32[]{:S(2)}) collective-permute-start(bf16[192,512]{1,0:T(8,128)(2,1)S(1)} %get-tuple-element.42), channel_id=1, source_target_pairs={{0,32},{1,33},{2,34},{3,35},{36,4},{37,5},{38,6},{39,7},{72,104},{... | collective-permute-start | bytes 589832 | tf_op jit(solution)/shard_map/ppermute | solution.py:81
  80.0 11.0 %collective-permute-start.15 = (bf16[192,512]{1,0:T(8,128)(2,1)S(1)}, bf16[192,512]{1,0:T(8,128)(2,1)S(1)}, u32[]{:S(2)}, u32[]{:S(2)}) collective-permute-start(bf16[192,512]{1,0:T(8,128)(2,1)S(1)} %copy-done.7), channel_id=1, source_target_pairs={{0,96},{1,97},{2,98},{3,99},{36,100},{37,101},{38,102},{39,103},{7... | collective-permute-start | bytes 589832 | tf_op jit(solution)/shard_map/ppermute | solution.py:81
  82.9 8.2 %collective-permute-start.16 = (bf16[192,512]{1,0:T(8,128)(2,1)S(1)}, bf16[192,512]{1,0:T(8,128)(2,1)S(1)}, u32[]{:S(2)}, u32[]{:S(2)}) collective-permute-start(bf16[192,512]{1,0:T(8,128)(2,1)S(1)} %copy-done.6), channel_id=1, source_target_pairs={{0,160},{1,161},{2,162},{3,163},{36,164},{37,165},{38,166},{39,167... | collective-permute-start | bytes 589832 | tf_op jit(solution)/shard_map/ppermute | solution.py:81
  83.6 9.0 %collective-permute-start.17 = (bf16[192,512]{1,0:T(8,128)(2,1)S(1)}, bf16[192,512]{1,0:T(8,128)(2,1)}, u32[]{:S(2)}, u32[]{:S(2)}) collective-permute-start(bf16[192,512]{1,0:T(8,128)(2,1)S(1)} %copy-done.5), channel_id=1, source_target_pairs={{0,224},{1,225},{2,226},{3,227},{36,228},{37,229},{38,230},{39,231... | collective-permute-start | bytes 589832 | tf_op jit(solution)/shard_map/ppermute | solution.py:81
  97.1 8.4 %collective-permute-start.22 = (bf16[768,512]{0,1:T(8,128)(2,1)S(1)}, bf16[768,512]{0,1:T(8,128)(2,1)}, u32[]{:S(2)}, u32[]{:S(2)}) collective-permute-start(bf16[768,512]{0,1:T(8,128)(2,1)S(1)} %get-tuple-element.71), channel_id=1, source_target_pairs={{0,32},{32,0},{1,33},{33,1},{2,34},{34,2},{3,35},{35,3},{4,36},{36... | collective-permute-start | bytes 2359304 | tf_op jit(solution)/shard_map/ppermute | solution.py:92
  107.3 7.5 %collective-permute-start.23 = (bf16[192,512]{1,0:T(8,128)(2,1)S(1)}, bf16[192,512]{1,0:T(8,128)(2,1)S(1)}, u32[]{:S(2)}, u32[]{:S(2)}) collective-permute-start(bf16[192,512]{1,0:T(8,128)(2,1)S(1)} %get-tuple-element.46), channel_id=1, source_target_pairs={{0,128},{64,192},{128,0},{192,64},{1,129},{65,193},{129,1},{193,65... | collective-permute-start | bytes 589832 | tf_op jit(solution)/shard_map/ppermute | solution.py:17
  109.2 10.7 %collective-permute-start.24 = (bf16[192,512]{1,0:T(8,128)(2,1)S(1)}, bf16[192,512]{1,0:T(8,128)(2,1)S(1)}, u32[]{:S(2)}, u32[]{:S(2)}) collective-permute-start(bf16[192,512]{1,0:T(8,128)(2,1)S(1)} %get-tuple-element.48), channel_id=1, source_target_pairs={{0,64},{64,128},{128,192},{192,0},{1,65},{65,129},{129,193},{193,1... | collective-permute-start | bytes 589832 | tf_op jit(solution)/shard_map/ppermute | solution.py:17
  109.2 10.7 %collective-permute-start.25 = (bf16[192,512]{1,0:T(8,128)(2,1)S(1)}, bf16[192,512]{1,0:T(8,128)(2,1)S(1)}, u32[]{:S(2)}, u32[]{:S(2)}) collective-permute-start(bf16[192,512]{1,0:T(8,128)(2,1)S(1)} %get-tuple-element.47), channel_id=1, source_target_pairs={{0,192},{64,0},{128,64},{192,128},{1,193},{65,1},{129,65},{193,129... | collective-permute-start | bytes 589832 | tf_op jit(solution)/shard_map/ppermute | solution.py:17
  122.0 6.2 %collective-permute-start.30 = (bf16[128,512]{1,0:T(8,128)(2,1)S(1)}, bf16[128,512]{1,0:T(8,128)(2,1)S(1)}, u32[]{:S(2)}, u32[]{:S(2)}) collective-permute-start(bf16[128,512]{1,0:T(8,128)(2,1)S(1)} %get-tuple-element.55), channel_id=1, source_target_pairs={{0,128},{64,192},{128,0},{192,64},{1,129},{65,193},{129,1},{193,65... | collective-permute-start | bytes 393224 | tf_op jit(solution)/shard_map/ppermute | solution.py:17
  123.2 8.5 %collective-permute-start.31 = (bf16[128,512]{1,0:T(8,128)(2,1)S(1)}, bf16[128,512]{1,0:T(8,128)(2,1)S(1)}, u32[]{:S(2)}, u32[]{:S(2)}) collective-permute-start(bf16[128,512]{1,0:T(8,128)(2,1)S(1)} %get-tuple-element.57), channel_id=1, source_target_pairs={{0,64},{64,128},{128,192},{192,0},{1,65},{65,129},{129,193},{193,1... | collective-permute-start | bytes 393224 | tf_op jit(solution)/shard_map/ppermute | solution.py:17
  123.2 8.5 %collective-permute-start.32 = (bf16[128,512]{1,0:T(8,128)(2,1)S(1)}, bf16[128,512]{1,0:T(8,128)(2,1)S(1)}, u32[]{:S(2)}, u32[]{:S(2)}) collective-permute-start(bf16[128,512]{1,0:T(8,128)(2,1)S(1)} %get-tuple-element.56), channel_id=1, source_target_pairs={{0,192},{64,0},{128,64},{192,128},{1,193},{65,1},{129,65},{193,129... | collective-permute-start | bytes 393224 | tf_op jit(solution)/shard_map/ppermute | solution.py:17
  131.8 5.4 %collective-permute-start.33 = (bf16[32,512]{1,0:T(8,128)(2,1)S(1)}, bf16[32,512]{1,0:T(8,128)(2,1)S(1)}, u32[]{:S(2)}, u32[]{:S(2)}) collective-permute-start(bf16[32,512]{1,0:T(8,128)(2,1)S(1)} %get-tuple-element.68), channel_id=1, source_target_pairs={{0,1},{1,0},{2,3},{3,2},{4,5},{5,4},{6,7},{7,6},{8,9},{9,8},{10,11... | collective-permute-start | bytes 98312 | tf_op jit(solution)/shard_map/ppermute | solution.py:107
  131.9 7.3 %collective-permute-start.34 = (bf16[32,512]{1,0:T(8,128)(2,1)S(1)}, bf16[32,512]{1,0:T(8,128)(2,1)S(1)}, u32[]{:S(2)}, u32[]{:S(2)}) collective-permute-start(bf16[32,512]{1,0:T(8,128)(2,1)S(1)} %get-tuple-element.70), channel_id=1, source_target_pairs={{0,2},{1,3},{2,0},{3,1},{4,6},{5,7},{6,4},{7,5},{8,10},{9,11},{10,... | collective-permute-start | bytes 98312 | tf_op jit(solution)/shard_map/ppermute | solution.py:107
  134.3 4.8 %collective-permute-start.35 = (bf16[32,512]{1,0:T(8,128)(2,1)S(1)}, bf16[32,512]{1,0:T(8,128)(2,1)S(1)}, u32[]{:S(2)}, u32[]{:S(2)}) collective-permute-start(bf16[32,512]{1,0:T(8,128)(2,1)S(1)} %get-tuple-element.69), channel_id=1, source_target_pairs={{0,3},{1,2},{2,1},{3,0},{4,7},{5,6},{6,5},{7,4},{8,11},{9,10},{10,... | collective-permute-start | bytes 98312 | tf_op jit(solution)/shard_map/ppermute | solution.py:107
  135.8 10.1 %collective-permute-start.26 = (bf16[192,128]{1,0:T(8,128)(2,1)S(1)}, bf16[192,128]{1,0:T(8,128)(2,1)S(1)}, u32[]{:S(2)}, u32[]{:S(2)}) collective-permute-start(bf16[192,128]{1,0:T(8,128)(2,1)S(1)} %get-tuple-element.64), channel_id=1, source_target_pairs={{0,64},{64,128},{128,192},{192,0},{1,65},{65,129},{129,193},{193,1... | collective-permute-start | bytes 147464 | tf_op jit(solution)/shard_map/ppermute | solution.py:17
  135.9 10.9 %collective-permute-start.27 = (bf16[192,128]{1,0:T(8,128)(2,1)S(1)}, bf16[192,128]{1,0:T(8,128)(2,1)S(1)}, u32[]{:S(2)}, u32[]{:S(2)}) collective-permute-start(bf16[192,128]{1,0:T(8,128)(2,1)S(1)} %get-tuple-element.63), channel_id=1, source_target_pairs={{0,128},{64,192},{128,0},{192,64},{1,129},{65,193},{129,1},{193,65... | collective-permute-start | bytes 147464 | tf_op jit(solution)/shard_map/ppermute | solution.py:17
  137.2 10.2 %collective-permute-start.28 = (bf16[192,128]{1,0:T(8,128)(2,1)S(1)}, bf16[192,128]{1,0:T(8,128)(2,1)S(1)}, u32[]{:S(2)}, u32[]{:S(2)}) collective-permute-start(bf16[192,128]{1,0:T(8,128)(2,1)S(1)} %get-tuple-element.62), channel_id=1, source_target_pairs={{0,192},{64,0},{128,64},{192,128},{1,193},{65,1},{129,65},{193,129... | collective-permute-start | bytes 147464 | tf_op jit(solution)/shard_map/ppermute | solution.py:17
  139.9 14.6 %all-to-all-start = ((bf16[8,32,512]{2,1,0:T(8,128)(2,1)}), bf16[8,32,512]{2,1,0:T(8,128)(2,1)S(1)}, u32[]{:S(2)}, u32[]{:S(2)}) async-start(bf16[8,32,512]{2,1,0:T(8,128)(2,1)} %broadcast_in_dim.77), calls=%async_computation | async-start | bytes 524288 | tf_op jit(solution)/shard_map/all_to_all | solution.py:119
  161.1 6.2 %collective-permute-start.39 = (bf16[64,512]{1,0:T(8,128)(2,1)S(1)}, bf16[64,512]{1,0:T(8,128)(2,1)S(1)}, u32[]{:S(2)}, u32[]{:S(2)}) collective-permute-start(bf16[64,512]{1,0:T(8,128)(2,1)S(1)} %dynamic-slice_bitcast_fusion.7), channel_id=1, source_target_pairs={{0,32},{32,0},{1,33},{33,1},{2,34},{34,2},{3,35},{35,3},{4,36},{36... | collective-permute-start | bytes 196616 | tf_op jit(solution)/shard_map/ppermute | solution.py:133
  (27 other events, 252.4 us)
Sparse Core Ops, SparseCore 0:
  19.4 51.3 all-gather.1

commit v16 on v11

--- a/solution.py
+++ b/solution.py
@@ -86,9 +86,9 @@
 
 
 def pair_sum(partial):
-    first = lax.axis_index("core") == 0
-    given = lax.ppermute(jnp.where(first, partial[1], partial[0]), "core", [(0, 1), (1, 0)])
-    pair = jnp.where(first, partial[0], partial[1]).astype(F32) + given.astype(F32)
+    given = lax.ppermute(partial[0], "core", [(1, 0)]).astype(F32)
+    given = given + lax.ppermute(partial[1], "core", [(0, 1)]).astype(F32)
+    pair = jnp.where(lax.axis_index("core") == 0, partial[0], partial[1]).astype(F32) + given
     return pair.astype(BF16)
 
 

time: 167 us -> 168 us (level)
    ppermute x1 -> x2, starting transfers between devices: 7.18 us -> 12.7 us  [the longest x1 11.4 us: pair_sum(): given = lax.ppermute(partial[0], 'core', [(1, 0)]).astype(F32)]
    all_to_all x1, starting transfers between devices: 11.4 us -> 8.94 us  [summed_over_col(): part = lax.all_to_all(copies, 'z', split_axis=0, concat_axis=0, tiled=True)]
    ppermute x2, starting transfers between devices: 12.6 us -> 10.7 us  [own_slab_of_both(): got = lax.ppermute(given, 'core', [(0, 1), (1, 0)])]
  transfers between devices with their start and end apart: 36 -> 37, of which waited for: 16 -> 17; matrix products, arithmetic and copies ran while one was open for 13% -> 13% of each run, Pallas kernels for 0% -> 0%
where the time goes in v16:
time: 168 us
  starting transfers between devices  73.1 us (44%)
  waiting for transfers between devices  51.3 us (31%)
  between operations  14.9 us (9%)
  matrix products  11.9 us (7%)
  other arithmetic  8.78 us (5%)
  local copies, waits for them, and re-layouts  7.74 us (5%)
    ppermute x17, waiting for transfers between devices, shift(): lax.ppermute(array, axis, [(i, (i + by) % size) for i in range(size)])  31.9 us
    ppermute x17, starting transfers between devices, shift(): lax.ppermute(array, axis, [(i, (i + by) % size) for i in range(size)])  22.9 us
    ppermute x1, starting transfers between devices, pair_sum(): given = lax.ppermute(partial[0], 'core', [(1, 0)]).astype(F32)  11.4 us
    ppermute x8, starting transfers between devices, from_root(): return lax.ppermute(array, ALL, pairs)  11.2 us
    ppermute x2, starting transfers between devices, own_slab_of_both(): got = lax.ppermute(given, 'core', [(0, 1), (1, 0)])  10.7 us
    dot_general x2, matrix products, partial_of(): jnp.einsum('qj,pq->jp', panel, inverse_block, preferred_element_type=F32)  10.4 us
    all_to_all x1, starting transfers between devices, summed_over_col(): part = lax.all_to_all(copies, 'z', split_axis=0, concat_axis=0, tiled=True)  8.94 us
    all_gather x1, waiting for transfers between devices, panel_y_then_z(): return lax.all_gather(part, 'z', axis=0, tiled=True)  8.16 us
  transfers between devices with their start and end apart: 37, of which 17 were waited for; matrix products, arithmetic and copies ran while one was open for 13% of the time, Pallas kernels for 0%

profile of v16, /device:TPU:1, one launch (start us, length us, event | category | flops | bytes accessed | tf_op | source)
XLA Modules:
  0.0 167.7 jit_solution(12589849207053200358)
XLA Ops:
  9.7 3.8 %collective-permute-start.1 = (bf16[96,512]{1,0:T(8,128)(2,1)S(1)}, bf16[96,512]{1,0:T(8,128)(2,1)S(1)}, u32[]{:S(2)}, u32[]{:S(2)}) collective-permute-start(bf16[96,512]{1,0:T(8,128)(2,1)S(1)} %get-tuple-element.36), channel_id=1, source_target_pairs={{0,2},{1,3},{2,0},{3,1},{4,6},{5,7},{6,4},{7,5},{8,10},{9,11},{10,... | collective-permute-start | bytes 294920 | tf_op jit(solution)/shard_map/ppermute | solution.py:17
  13.9 2.3 %collective-permute-start.2 = (bf16[96,512]{1,0:T(8,128)(2,1)S(1)}, bf16[96,512]{1,0:T(8,128)(2,1)S(1)}, u32[]{:S(2)}, u32[]{:S(2)}) collective-permute-start(bf16[96,512]{1,0:T(8,128)(2,1)S(1)} %get-tuple-element.36), channel_id=1, source_target_pairs={{0,3},{1,0},{2,1},{3,2},{4,7},{5,4},{6,5},{7,6},{8,11},{9,8},{10,9... | collective-permute-start | bytes 294920 | tf_op jit(solution)/shard_map/ppermute | solution.py:17
  16.3 3.8 %collective-permute-done = bf16[96,512]{1,0:T(8,128)(2,1)S(1)} collective-permute-done((bf16[96,512]{1,0:T(8,128)(2,1)S(1)}, bf16[96,512]{1,0:T(8,128)(2,1)S(1)}, u32[]{:S(2)}, u32[]{:S(2)}) %collective-permute-start) | collective-permute-done | bytes 98336 | tf_op jit(solution)/shard_map/ppermute | solution.py:17
  21.1 3.8 %collective-permute-start.7 = (bf16[1,96,512]{2,1,0:T(8,128)(2,1)S(1)}, bf16[1,96,512]{2,1,0:T(8,128)(2,1)S(1)}, u32[]{:S(2)}, u32[]{:S(2)}) collective-permute-start(bf16[1,96,512]{2,1,0:T(8,128)(2,1)S(1)} %get-tuple-element.35), channel_id=1, source_target_pairs={{0,28},{4,0},{8,4},{12,8},{16,12},{20,16},{24,20},{28,24},{1,29},{... | collective-permute-start | bytes 294920 | tf_op jit(solution)/shard_map/ppermute | solution.py:17
  25.2 1.7 %collective-permute-done.3 = bf16[1,96,512]{2,1,0:T(8,128)(2,1)S(1)} collective-permute-done((bf16[1,96,512]{2,1,0:T(8,128)(2,1)S(1)}, bf16[1,96,512]{2,1,0:T(8,128)(2,1)S(1)}, u32[]{:S(2)}, u32[]{:S(2)}) %collective-permute-start.3) | collective-permute-done | bytes 98336 | tf_op jit(solution)/shard_map/ppermute | solution.py:17
  26.8 2.8 %collective-permute-start.8 = (bf16[1,96,512]{2,1,0:T(8,128)(2,1)S(1)}, bf16[1,96,512]{2,1,0:T(8,128)(2,1)S(1)}, u32[]{:S(2)}, u32[]{:S(2)}) collective-permute-start(bf16[1,96,512]{2,1,0:T(8,128)(2,1)S(1)} %collective-permute-done.7), channel_id=1, source_target_pairs={{0,28},{4,0},{8,4},{12,8},{16,12},{20,16},{24,20},{28,24},{1,29},{... | collective-permute-start | bytes 294920 | tf_op jit(solution)/shard_map/ppermute | solution.py:17
  29.6 1.9 %collective-permute-done.4 = bf16[1,96,512]{2,1,0:T(8,128)(2,1)S(1)} collective-permute-done((bf16[1,96,512]{2,1,0:T(8,128)(2,1)S(1)}, bf16[1,96,512]{2,1,0:T(8,128)(2,1)S(1)}, u32[]{:S(2)}, u32[]{:S(2)}) %collective-permute-start.4) | collective-permute-done | bytes 98336 | tf_op jit(solution)/shard_map/ppermute | solution.py:17
  31.5 2.8 %collective-permute-start.9 = (bf16[1,96,512]{2,1,0:T(8,128)(2,1)S(1)}, bf16[1,96,512]{2,1,0:T(8,128)(2,1)S(1)}, u32[]{:S(2)}, u32[]{:S(2)}) collective-permute-start(bf16[1,96,512]{2,1,0:T(8,128)(2,1)S(1)} %collective-permute-done.8), channel_id=1, source_target_pairs={{0,28},{4,0},{8,4},{12,8},{16,12},{20,16},{24,20},{28,24},{1,29},{... | collective-permute-start | bytes 294920 | tf_op jit(solution)/shard_map/ppermute | solution.py:17
  34.3 1.9 %collective-permute-done.5 = bf16[1,96,512]{2,1,0:T(8,128)(2,1)S(1)} collective-permute-done((bf16[1,96,512]{2,1,0:T(8,128)(2,1)S(1)}, bf16[1,96,512]{2,1,0:T(8,128)(2,1)S(1)}, u32[]{:S(2)}, u32[]{:S(2)}) %collective-permute-start.5) | collective-permute-done | bytes 98336 | tf_op jit(solution)/shard_map/ppermute | solution.py:17
  36.2 7.8 %collective-permute-done.6 = bf16[1,96,512]{2,1,0:T(8,128)(2,1)S(1)} collective-permute-done((bf16[1,96,512]{2,1,0:T(8,128)(2,1)S(1)}, bf16[1,96,512]{2,1,0:T(8,128)(2,1)S(1)}, u32[]{:S(2)}, u32[]{:S(2)}) %collective-permute-start.6) | collective-permute-done | bytes 98336 | tf_op jit(solution)/shard_map/ppermute | solution.py:17
  44.1 1.9 %collective-permute-start.10 = (bf16[8,1,96,512]{3,2,1,0:T(8,128)(2,1)S(1)}, bf16[8,1,96,512]{3,2,1,0:T(8,128)(2,1)}, u32[]{:S(2)}, u32[]{:S(2)}) collective-permute-start(bf16[8,1,96,512]{3,2,1,0:T(8,128)(2,1)S(1)} %bitcast_dynamic-update-slice_fusion), channel_id=1, source_target_pairs={{0,1},{1,2},{2,3},{3,0},{4,5},{5,6},{6,7},{7,4},{8,9},{9,10},{10,1... | collective-permute-start | bytes 2359304 | tf_op jit(solution)/shard_map/ppermute | solution.py:17
  49.3 7.6 %collective-permute-done.10 = bf16[8,1,96,512]{3,2,1,0:T(8,128)(2,1)} collective-permute-done((bf16[8,1,96,512]{3,2,1,0:T(8,128)(2,1)S(1)}, bf16[8,1,96,512]{3,2,1,0:T(8,128)(2,1)}, u32[]{:S(2)}, u32[]{:S(2)}) %collective-permute-start.10) | collective-permute-done | bytes 786464 | tf_op jit(solution)/shard_map/ppermute | solution.py:17
  60.4 1.6 collective-permute-start.20
  63.5 8.2 %all-gather.2.cloned.1.call-done = bf16[3072,512]{1,0:T(8,128)(2,1)} async-done(((bf16[384,512]{1,0:T(8,128)(2,1)}), bf16[3072,512]{1,0:T(8,128)(2,1)}) %all-gather.2.cloned.1.call-update) | async-done | bytes 3145744 | tf_op jit(solution)/shard_map/all_gather | solution.py:53
  72.8 2.3 %collective-permute-start.13 = (bf16[4,1,96,512]{3,2,1,0:T(8,128)(2,1)S(1)}, bf16[4,1,96,512]{3,2,1,0:T(8,128)(2,1)S(1)}, u32[]{:S(2)}, u32[]{:S(2)}) collective-permute-start(bf16[4,1,96,512]{3,2,1,0:T(8,128)(2,1)S(1)} %slice.19), channel_id=1, source_target_pairs={{0,3},{1,0},{2,1},{3,2},{4,7},{5,4},{6,5},{7,6},{8,11},{9,8},{10,9... | collective-permute-start | bytes 1179656 | tf_op jit(solution)/shard_map/ppermute | solution.py:17
  75.1 6.8 %convolution_convert_fusion.1 = bf16[512,768]{1,0:T(8,128)(2,1)} fusion(bf16[3072,512]{1,0:T(8,128)(2,1)} %all-gather.2.cloned.1.call-done, bf16[768,3072]{1,0:T(8,128)(2,1)} %param.8), kind=kOutput, calls=%fused_computation.2 | convolution fusion | flops 2416312320 | bytes 8650752 | tf_op jit(solution)/shard_map/qj,pq->jp/dot_general | solution.py:152
  84.7 1.6 collective-permute-start.19
  88.9 1.6 collective-permute-start.17
  90.5 3.5 %convolution_convert_fusion = bf16[512,768]{1,0:T(8,128)(2,1)} fusion(bf16[3072,512]{1,0:T(8,128)(2,1)S(1)} %bitcast.98, bf16[768,3072]{1,0:T(8,128)(2,1)S(1)} %bitcast.108), kind=kOutput, calls=%fused_computation.1 | convolution fusion | flops 2416312320 | bytes 8650752 | tf_op jit(solution)/shard_map/qj,pq->jp/dot_general | solution.py:152
  94.0 11.4 %collective-permute-start.14 = (bf16[512,768]{1,0:T(8,128)(2,1)}, bf16[512,768]{1,0:T(8,128)(2,1)}, u32[]{:S(2)}, u32[]{:S(2)}) collective-permute-start(bf16[512,768]{1,0:T(8,128)(2,1)} %convolution_convert_fusion.1), channel_id=1, source_target_pairs={{32,0},{33,1},{34,2},{35,3},{36,4},{37,5},{38,6},{39,7},{40,8},{41... | collective-permute-start | bytes 2359304 | tf_op jit(solution)/shard_map/ppermute | solution.py:89
  106.9 2.6 %add_select_fusion = bf16[768,512]{1,0:T(8,128)(2,1)S(1)} fusion(bf16[768,512]{1,0:T(8,128)(2,1)} %collective-permute-done.23, bf16[768,512]{1,0:T(8,128)(2,1)} %collective-permute-done.22, bf16[768,512]{1,0:T(8,128)(2,1)} %collective-permute-done.20, bf16[768,512]{1,0:T(8,128)(2,1)} %collective-permute-done.21, bf16[768,512]{1,0:T(8,128)(2,1)} %collective-permute-done.19, ...), kind=kLoop, calls=%fused_computation.8 | loop fusion | flops 3145728 | bytes 7864322 | tf_op jit(solution)/shard_map/jit(_where)/select_n | solution.py:180
  110.0 2.0 %add_convert_fusion = bf16[512,768]{1,0:T(8,128)(2,1)S(1)} fusion(bf16[512,768]{1,0:T(8,128)(2,1)} %collective-permute-done.15, bf16[512,768]{1,0:T(8,128)(2,1)} %collective-permute-done.14, bf16[512,768]{1,0:T(8,128)(2,1)} %convolution_convert_fusion.1, bf16[512,768]{1,0:T(8,128)(2,1)} %convolution_convert_fusion, pred[]{:T(512)S(6)} %eq.63), kind=kLoop, calls=%fused_computation | loop fusion | flops 2752512 | bytes 3932161 | tf_op jit(solution)/shard_map/convert_element_type | solution.py:92
  113.9 4.4 %collective-permute-done.24 = bf16[128,768]{1,0:T(8,128)(2,1)S(1)} collective-permute-done((bf16[128,768]{1,0:T(8,128)(2,1)S(1)}, bf16[128,768]{1,0:T(8,128)(2,1)S(1)}, u32[]{:S(2)}, u32[]{:S(2)}) %collective-permute-start.24) | collective-permute-done | bytes 196640 | tf_op jit(solution)/shard_map/ppermute | solution.py:17
  118.3 2.6 %collective-permute-done.25 = bf16[128,768]{1,0:T(8,128)(2,1)S(1)} collective-permute-done((bf16[128,768]{1,0:T(8,128)(2,1)S(1)}, bf16[128,768]{1,0:T(8,128)(2,1)S(1)}, u32[]{:S(2)}, u32[]{:S(2)}) %collective-permute-start.25) | collective-permute-done | bytes 196640 | tf_op jit(solution)/shard_map/ppermute | solution.py:17
  121.5 1.7 %collective-permute-start.30 = (bf16[32,512]{1,0:T(8,128)(2,1)S(1)}, bf16[32,512]{1,0:T(8,128)(2,1)S(1)}, u32[]{:S(2)}, u32[]{:S(2)}) collective-permute-start(bf16[32,512]{1,0:T(8,128)(2,1)S(1)} %get-tuple-element.38), channel_id=1, source_target_pairs={{0,3},{1,2},{2,1},{3,0},{4,7},{5,6},{6,5},{7,4},{8,11},{9,10},{10,... | collective-permute-start | bytes 98312 | tf_op jit(solution)/shard_map/ppermute | solution.py:105
  125.8 1.7 %collective-permute-done.29 = bf16[32,512]{1,0:T(8,128)(2,1)S(1)} collective-permute-done((bf16[32,512]{1,0:T(8,128)(2,1)S(1)}, bf16[32,512]{1,0:T(8,128)(2,1)S(1)}, u32[]{:S(2)}, u32[]{:S(2)}) %collective-permute-start.29) | collective-permute-done | bytes 32800 | tf_op jit(solution)/shard_map/ppermute | solution.py:105
  128.3 8.9 %all-to-all-start = ((bf16[8,32,512]{2,1,0:T(8,128)(2,1)}), bf16[8,32,512]{2,1,0:T(8,128)(2,1)S(1)}, u32[]{:S(2)}, u32[]{:S(2)}) async-start(bf16[8,32,512]{2,1,0:T(8,128)(2,1)} %broadcast_in_dim.68), calls=%async_computation | async-start | bytes 524288 | tf_op jit(solution)/shard_map/all_to_all | solution.py:117
  137.2 3.7 %collective-permute-start.27 = (bf16[64,768]{1,0:T(8,128)(2,1)S(1)}, bf16[64,768]{1,0:T(8,128)(2,1)S(1)}, u32[]{:S(2)}, u32[]{:S(2)}) collective-permute-start(bf16[64,768]{1,0:T(8,128)(2,1)S(1)} %dynamic-slice_bitcast_fusion.3), channel_id=1, source_target_pairs={{0,32},{32,0},{1,33},{33,1},{2,34},{34,2},{3,35},{35,3},{4,36},{36... | collective-permute-start | bytes 294920 | tf_op jit(solution)/shard_map/ppermute | solution.py:131
  141.9 4.8 %all-to-all-done = bf16[8,32,512]{2,1,0:T(8,128)(2,1)S(1)} async-done(((bf16[8,32,512]{2,1,0:T(8,128)(2,1)}), bf16[8,32,512]{2,1,0:T(8,128)(2,1)S(1)}, u32[]{:S(2)}, u32[]{:S(2)}) %all-to-all-start) | async-done | bytes 262176 | tf_op jit(solution)/shard_map/all_to_all | solution.py:117
  147.8 1.6 collective-permute-start.32
  150.1 2.0 %collective-permute-done.31 = bf16[32,512]{1,0:T(8,128)(2,1)S(1)} collective-permute-done((bf16[32,512]{1,0:T(8,128)(2,1)S(1)}, bf16[32,512]{1,0:T(8,128)(2,1)S(1)}, u32[]{:S(2)}, u32[]{:S(2)}) %collective-permute-start.31) | collective-permute-done | bytes 32800 | tf_op jit(solution)/shard_map/ppermute | solution.py:105
  152.2 7.0 %collective-permute-start.34 = (bf16[64,512]{1,0:T(8,128)(2,1)S(1)}, bf16[64,512]{1,0:T(8,128)(2,1)S(1)}, u32[]{:S(2)}, u32[]{:S(2)}) collective-permute-start(bf16[64,512]{1,0:T(8,128)(2,1)S(1)} %dynamic-slice_bitcast_fusion.4), channel_id=1, source_target_pairs={{0,32},{32,0},{1,33},{33,1},{2,34},{34,2},{3,35},{35,3},{4,36},{36... | collective-permute-start | bytes 196616 | tf_op jit(solution)/shard_map/ppermute | solution.py:131
  (118 shorter events, 30.6 us)
Async XLA Ops:
  7.2 64.5 %all-gather.2.cloned.1.call-start = ((), (), s32[]{:S(2)}) async-start(), calls=%async_computation.1 | async-start | bytes 3538944 | tf_op jit(solution)/shard_map/all_gather | solution.py:53
  9.7 10.5 %collective-permute-start.1 = (bf16[96,512]{1,0:T(8,128)(2,1)S(1)}, bf16[96,512]{1,0:T(8,128)(2,1)S(1)}, u32[]{:S(2)}, u32[]{:S(2)}) collective-permute-start(bf16[96,512]{1,0:T(8,128)(2,1)S(1)} %get-tuple-element.36), channel_id=1, source_target_pairs={{0,2},{1,3},{2,0},{3,1},{4,6},{5,7},{6,4},{7,5},{8,10},{9,11},{10,... | collective-permute-start | bytes 294920 | tf_op jit(solution)/shard_map/ppermute | solution.py:17
  13.5 6.6 %collective-permute-start = (bf16[96,512]{1,0:T(8,128)(2,1)S(1)}, bf16[96,512]{1,0:T(8,128)(2,1)S(1)}, u32[]{:S(2)}, u32[]{:S(2)}) collective-permute-start(bf16[96,512]{1,0:T(8,128)(2,1)S(1)} %get-tuple-element.36), channel_id=1, source_target_pairs={{0,1},{1,2},{2,3},{3,0},{4,5},{5,6},{6,7},{7,4},{8,9},{9,10},{10,1... | collective-permute-start | bytes 294920 | tf_op jit(solution)/shard_map/ppermute | solution.py:17
  13.9 6.3 %collective-permute-start.2 = (bf16[96,512]{1,0:T(8,128)(2,1)S(1)}, bf16[96,512]{1,0:T(8,128)(2,1)S(1)}, u32[]{:S(2)}, u32[]{:S(2)}) collective-permute-start(bf16[96,512]{1,0:T(8,128)(2,1)S(1)} %get-tuple-element.36), channel_id=1, source_target_pairs={{0,3},{1,0},{2,1},{3,2},{4,7},{5,4},{6,5},{7,6},{8,11},{9,8},{10,9... | collective-permute-start | bytes 294920 | tf_op jit(solution)/shard_map/ppermute | solution.py:17
  21.0 5.9 %collective-permute-start.3 = (bf16[1,96,512]{2,1,0:T(8,128)(2,1)S(1)}, bf16[1,96,512]{2,1,0:T(8,128)(2,1)S(1)}, u32[]{:S(2)}, u32[]{:S(2)}) collective-permute-start(bf16[1,96,512]{2,1,0:T(8,128)(2,1)S(1)} %get-tuple-element.35), channel_id=1, source_target_pairs={{0,4},{4,8},{8,12},{12,16},{16,20},{20,24},{24,28},{28,0},{1,5},{5... | collective-permute-start | bytes 294920 | tf_op jit(solution)/shard_map/ppermute | solution.py:17
  21.1 5.8 %collective-permute-start.7 = (bf16[1,96,512]{2,1,0:T(8,128)(2,1)S(1)}, bf16[1,96,512]{2,1,0:T(8,128)(2,1)S(1)}, u32[]{:S(2)}, u32[]{:S(2)}) collective-permute-start(bf16[1,96,512]{2,1,0:T(8,128)(2,1)S(1)} %get-tuple-element.35), channel_id=1, source_target_pairs={{0,28},{4,0},{8,4},{12,8},{16,12},{20,16},{24,20},{28,24},{1,29},{... | collective-permute-start | bytes 294920 | tf_op jit(solution)/shard_map/ppermute | solution.py:17
  26.8 4.7 %collective-permute-start.4 = (bf16[1,96,512]{2,1,0:T(8,128)(2,1)S(1)}, bf16[1,96,512]{2,1,0:T(8,128)(2,1)S(1)}, u32[]{:S(2)}, u32[]{:S(2)}) collective-permute-start(bf16[1,96,512]{2,1,0:T(8,128)(2,1)S(1)} %collective-permute-done.3), channel_id=1, source_target_pairs={{0,4},{4,8},{8,12},{12,16},{16,20},{20,24},{24,28},{28,0},{1,5},{5... | collective-permute-start | bytes 294920 | tf_op jit(solution)/shard_map/ppermute | solution.py:17
  26.8 4.7 %collective-permute-start.8 = (bf16[1,96,512]{2,1,0:T(8,128)(2,1)S(1)}, bf16[1,96,512]{2,1,0:T(8,128)(2,1)S(1)}, u32[]{:S(2)}, u32[]{:S(2)}) collective-permute-start(bf16[1,96,512]{2,1,0:T(8,128)(2,1)S(1)} %collective-permute-done.7), channel_id=1, source_target_pairs={{0,28},{4,0},{8,4},{12,8},{16,12},{20,16},{24,20},{28,24},{1,29},{... | collective-permute-start | bytes 294920 | tf_op jit(solution)/shard_map/ppermute | solution.py:17
  31.5 4.7 %collective-permute-start.5 = (bf16[1,96,512]{2,1,0:T(8,128)(2,1)S(1)}, bf16[1,96,512]{2,1,0:T(8,128)(2,1)S(1)}, u32[]{:S(2)}, u32[]{:S(2)}) collective-permute-start(bf16[1,96,512]{2,1,0:T(8,128)(2,1)S(1)} %collective-permute-done.4), channel_id=1, source_target_pairs={{0,4},{4,8},{8,12},{12,16},{16,20},{20,24},{24,28},{28,0},{1,5},{5... | collective-permute-start | bytes 294920 | tf_op jit(solution)/shard_map/ppermute | solution.py:17
  31.5 12.6 %collective-permute-start.9 = (bf16[1,96,512]{2,1,0:T(8,128)(2,1)S(1)}, bf16[1,96,512]{2,1,0:T(8,128)(2,1)S(1)}, u32[]{:S(2)}, u32[]{:S(2)}) collective-permute-start(bf16[1,96,512]{2,1,0:T(8,128)(2,1)S(1)} %collective-permute-done.8), channel_id=1, source_target_pairs={{0,28},{4,0},{8,4},{12,8},{16,12},{20,16},{24,20},{28,24},{1,29},{... | collective-permute-start | bytes 294920 | tf_op jit(solution)/shard_map/ppermute | solution.py:17
  36.2 7.9 %collective-permute-start.6 = (bf16[1,96,512]{2,1,0:T(8,128)(2,1)S(1)}, bf16[1,96,512]{2,1,0:T(8,128)(2,1)S(1)}, u32[]{:S(2)}, u32[]{:S(2)}) collective-permute-start(bf16[1,96,512]{2,1,0:T(8,128)(2,1)S(1)} %collective-permute-done.5), channel_id=1, source_target_pairs={{0,4},{4,8},{8,12},{12,16},{16,20},{20,24},{24,28},{28,0},{1,5},{5... | collective-permute-start | bytes 294920 | tf_op jit(solution)/shard_map/ppermute | solution.py:17
  44.1 12.7 %collective-permute-start.10 = (bf16[8,1,96,512]{3,2,1,0:T(8,128)(2,1)S(1)}, bf16[8,1,96,512]{3,2,1,0:T(8,128)(2,1)}, u32[]{:S(2)}, u32[]{:S(2)}) collective-permute-start(bf16[8,1,96,512]{3,2,1,0:T(8,128)(2,1)S(1)} %bitcast_dynamic-update-slice_fusion), channel_id=1, source_target_pairs={{0,1},{1,2},{2,3},{3,0},{4,5},{5,6},{6,7},{7,4},{8,9},{9,10},{10,1... | collective-permute-start | bytes 2359304 | tf_op jit(solution)/shard_map/ppermute | solution.py:17
  46.1 12.8 %collective-permute-start.11 = (bf16[8,1,96,512]{3,2,1,0:T(8,128)(2,1)S(1)}, bf16[8,1,96,512]{3,2,1,0:T(8,128)(2,1)S(1)}, u32[]{:S(2)}, u32[]{:S(2)}) collective-permute-start(bf16[8,1,96,512]{3,2,1,0:T(8,128)(2,1)S(1)} %bitcast_dynamic-update-slice_fusion), channel_id=1, source_target_pairs={{0,3},{1,0},{2,1},{3,2},{4,7},{5,4},{6,5},{7,6},{8,11},{9,8},{10,9... | collective-permute-start | bytes 2359304 | tf_op jit(solution)/shard_map/ppermute | solution.py:17
  48.0 9.9 %collective-permute-start.16 = (bf16[2,1,96,512]{3,2,1,0:T(8,128)(2,1)}, bf16[2,1,96,512]{3,2,1,0:T(8,128)(2,1)}, u32[]{:S(2)}, u32[]{:S(2)}) collective-permute-start(bf16[2,1,96,512]{3,2,1,0:T(8,128)(2,1)} %get-tuple-element.29), channel_id=1, source_target_pairs={{0,2},{1,3},{2,0},{3,1},{36,38},{37,39},{38,36},{39,37},{72,74},{7... | collective-permute-start | bytes 589832 | tf_op jit(solution)/shard_map/ppermute | solution.py:81
  58.9 29.3 %collective-permute-start.21 = (bf16[768,512]{1,0:T(8,128)(2,1)S(1)}, bf16[768,512]{1,0:T(8,128)(2,1)}, u32[]{:S(2)}, u32[]{:S(2)}) collective-permute-start(bf16[768,512]{1,0:T(8,128)(2,1)S(1)} %bitcast.93), channel_id=1, source_target_pairs={{0,224},{1,225},{2,226},{3,227},{36,228},{37,229},{38,230},{39,231... | collective-permute-start | bytes 2359304 | tf_op jit(solution)/shard_map/ppermute | solution.py:81
  60.4 28.5 %collective-permute-start.20 = (bf16[768,512]{1,0:T(8,128)(2,1)S(1)}, bf16[768,512]{1,0:T(8,128)(2,1)}, u32[]{:S(2)}, u32[]{:S(2)}) collective-permute-start(bf16[768,512]{1,0:T(8,128)(2,1)S(1)} %bitcast.94), channel_id=1, source_target_pairs={{0,96},{1,97},{2,98},{3,99},{36,100},{37,101},{38,102},{39,103},{7... | collective-permute-start | bytes 2359304 | tf_op jit(solution)/shard_map/ppermute | solution.py:81
  62.0 32.0 %collective-permute-start.22 = (bf16[768,512]{1,0:T(8,128)(2,1)S(1)}, bf16[768,512]{1,0:T(8,128)(2,1)}, u32[]{:S(2)}, u32[]{:S(2)}) collective-permute-start(bf16[768,512]{1,0:T(8,128)(2,1)S(1)} %bitcast.95), channel_id=1, source_target_pairs={{0,160},{1,161},{2,162},{3,163},{36,164},{37,165},{38,166},{39,167... | collective-permute-start | bytes 2359304 | tf_op jit(solution)/shard_map/ppermute | solution.py:81
  72.8 10.6 %collective-permute-start.13 = (bf16[4,1,96,512]{3,2,1,0:T(8,128)(2,1)S(1)}, bf16[4,1,96,512]{3,2,1,0:T(8,128)(2,1)S(1)}, u32[]{:S(2)}, u32[]{:S(2)}) collective-permute-start(bf16[4,1,96,512]{3,2,1,0:T(8,128)(2,1)S(1)} %slice.19), channel_id=1, source_target_pairs={{0,3},{1,0},{2,1},{3,2},{4,7},{5,4},{6,5},{7,6},{8,11},{9,8},{10,9... | collective-permute-start | bytes 1179656 | tf_op jit(solution)/shard_map/ppermute | solution.py:17
  75.1 9.6 %collective-permute-start.12 = (bf16[4,1,96,512]{3,2,1,0:T(8,128)(2,1)S(1)}, bf16[4,1,96,512]{3,2,1,0:T(8,128)(2,1)S(1)}, u32[]{:S(2)}, u32[]{:S(2)}) collective-permute-start(bf16[4,1,96,512]{3,2,1,0:T(8,128)(2,1)S(1)} %slice.18), channel_id=1, source_target_pairs={{0,1},{1,2},{2,3},{3,0},{4,5},{5,6},{6,7},{7,4},{8,9},{9,10},{10,1... | collective-permute-start | bytes 1179656 | tf_op jit(solution)/shard_map/ppermute | solution.py:17
  83.4 22.1 %collective-permute-start.23 = (bf16[768,512]{1,0:T(8,128)(2,1)S(1)}, bf16[768,512]{1,0:T(8,128)(2,1)}, u32[]{:S(2)}, u32[]{:S(2)}) collective-permute-start(bf16[768,512]{1,0:T(8,128)(2,1)S(1)} %get-tuple-element.24), channel_id=1, source_target_pairs={{0,32},{1,33},{2,34},{3,35},{36,4},{37,5},{38,6},{39,7},{72,104},{... | collective-permute-start | bytes 2359304 | tf_op jit(solution)/shard_map/ppermute | solution.py:81
  84.7 22.2 %collective-permute-start.19 = (bf16[768,512]{1,0:T(8,128)(2,1)S(1)}, bf16[768,512]{1,0:T(8,128)(2,1)}, u32[]{:S(2)}, u32[]{:S(2)}) collective-permute-start(bf16[768,512]{1,0:T(8,128)(2,1)S(1)} %get-tuple-element.25), channel_id=1, source_target_pairs={{0,128},{1,129},{2,130},{3,131},{36,132},{37,133},{38,134},{39,135... | collective-permute-start | bytes 2359304 | tf_op jit(solution)/shard_map/ppermute | solution.py:81
  88.2 18.7 %collective-permute-start.18 = (bf16[768,512]{1,0:T(8,128)(2,1)S(1)}, bf16[768,512]{1,0:T(8,128)(2,1)S(1)}, u32[]{:S(2)}, u32[]{:S(2)}) collective-permute-start(bf16[768,512]{1,0:T(8,128)(2,1)S(1)} %get-tuple-element.25), channel_id=1, source_target_pairs={{0,192},{1,193},{2,194},{3,195},{36,196},{37,197},{38,198},{39,199... | collective-permute-start | bytes 2359304 | tf_op jit(solution)/shard_map/ppermute | solution.py:81
  88.9 18.0 %collective-permute-start.17 = (bf16[768,512]{1,0:T(8,128)(2,1)S(1)}, bf16[768,512]{1,0:T(8,128)(2,1)}, u32[]{:S(2)}, u32[]{:S(2)}) collective-permute-start(bf16[768,512]{1,0:T(8,128)(2,1)S(1)} %get-tuple-element.25), channel_id=1, source_target_pairs={{0,64},{1,65},{2,66},{3,67},{36,68},{37,69},{38,70},{39,71},{72,13... | collective-permute-start | bytes 2359304 | tf_op jit(solution)/shard_map/ppermute | solution.py:81
  94.0 15.5 %collective-permute-start.14 = (bf16[512,768]{1,0:T(8,128)(2,1)}, bf16[512,768]{1,0:T(8,128)(2,1)}, u32[]{:S(2)}, u32[]{:S(2)}) collective-permute-start(bf16[512,768]{1,0:T(8,128)(2,1)} %convolution_convert_fusion.1), channel_id=1, source_target_pairs={{32,0},{33,1},{34,2},{35,3},{36,4},{37,5},{38,6},{39,7},{40,8},{41... | collective-permute-start | bytes 2359304 | tf_op jit(solution)/shard_map/ppermute | solution.py:89
  105.5 4.5 %collective-permute-start.15 = (bf16[512,768]{1,0:T(8,128)(2,1)}, bf16[512,768]{1,0:T(8,128)(2,1)}, u32[]{:S(2)}, u32[]{:S(2)}) collective-permute-start(bf16[512,768]{1,0:T(8,128)(2,1)} %convolution_convert_fusion), channel_id=1, source_target_pairs={{0,32},{1,33},{2,34},{3,35},{4,36},{5,37},{6,38},{7,39},{8,40},{9,... | collective-permute-start | bytes 2359304 | tf_op jit(solution)/shard_map/ppermute | solution.py:90
  112.1 6.2 %collective-permute-start.24 = (bf16[128,768]{1,0:T(8,128)(2,1)S(1)}, bf16[128,768]{1,0:T(8,128)(2,1)S(1)}, u32[]{:S(2)}, u32[]{:S(2)}) collective-permute-start(bf16[128,768]{1,0:T(8,128)(2,1)S(1)} %get-tuple-element.26), channel_id=1, source_target_pairs={{0,128},{64,192},{128,0},{192,64},{1,129},{65,193},{129,1},{193,65... | collective-permute-start | bytes 589832 | tf_op jit(solution)/shard_map/ppermute | solution.py:17
  112.2 6.1 %collective-permute-start.26 = (bf16[128,768]{1,0:T(8,128)(2,1)S(1)}, bf16[128,768]{1,0:T(8,128)(2,1)S(1)}, u32[]{:S(2)}, u32[]{:S(2)}) collective-permute-start(bf16[128,768]{1,0:T(8,128)(2,1)S(1)} %get-tuple-element.27), channel_id=1, source_target_pairs={{0,192},{64,0},{128,64},{192,128},{1,193},{65,1},{129,65},{193,129... | collective-permute-start | bytes 589832 | tf_op jit(solution)/shard_map/ppermute | solution.py:17
  112.2 8.7 %collective-permute-start.25 = (bf16[128,768]{1,0:T(8,128)(2,1)S(1)}, bf16[128,768]{1,0:T(8,128)(2,1)S(1)}, u32[]{:S(2)}, u32[]{:S(2)}) collective-permute-start(bf16[128,768]{1,0:T(8,128)(2,1)S(1)} %get-tuple-element.28), channel_id=1, source_target_pairs={{0,64},{64,128},{128,192},{192,0},{1,65},{65,129},{129,193},{193,1... | collective-permute-start | bytes 589832 | tf_op jit(solution)/shard_map/ppermute | solution.py:17
  128.3 18.4 %all-to-all-start = ((bf16[8,32,512]{2,1,0:T(8,128)(2,1)}), bf16[8,32,512]{2,1,0:T(8,128)(2,1)S(1)}, u32[]{:S(2)}, u32[]{:S(2)}) async-start(bf16[8,32,512]{2,1,0:T(8,128)(2,1)} %broadcast_in_dim.68), calls=%async_computation | async-start | bytes 524288 | tf_op jit(solution)/shard_map/all_to_all | solution.py:117
  137.2 4.7 %collective-permute-start.27 = (bf16[64,768]{1,0:T(8,128)(2,1)S(1)}, bf16[64,768]{1,0:T(8,128)(2,1)S(1)}, u32[]{:S(2)}, u32[]{:S(2)}) collective-permute-start(bf16[64,768]{1,0:T(8,128)(2,1)S(1)} %dynamic-slice_bitcast_fusion.3), channel_id=1, source_target_pairs={{0,32},{32,0},{1,33},{33,1},{2,34},{34,2},{3,35},{35,3},{4,36},{36... | collective-permute-start | bytes 294920 | tf_op jit(solution)/shard_map/ppermute | solution.py:131
  146.7 5.4 %collective-permute-start.33 = (bf16[32,512]{1,0:T(8,128)(2,1)S(1)}, bf16[32,512]{1,0:T(8,128)(2,1)S(1)}, u32[]{:S(2)}, u32[]{:S(2)}) collective-permute-start(bf16[32,512]{1,0:T(8,128)(2,1)S(1)} %reduce_sum.12), channel_id=1, source_target_pairs={{0,3},{1,2},{2,1},{3,0},{4,7},{5,6},{6,5},{7,4},{8,11},{9,10},{10,... | collective-permute-start | bytes 98312 | tf_op jit(solution)/shard_map/ppermute | solution.py:105
  152.2 7.9 %collective-permute-start.34 = (bf16[64,512]{1,0:T(8,128)(2,1)S(1)}, bf16[64,512]{1,0:T(8,128)(2,1)S(1)}, u32[]{:S(2)}, u32[]{:S(2)}) collective-permute-start(bf16[64,512]{1,0:T(8,128)(2,1)S(1)} %dynamic-slice_bitcast_fusion.4), channel_id=1, source_target_pairs={{0,32},{32,0},{1,33},{33,1},{2,34},{34,2},{3,35},{35,3},{4,36},{36... | collective-permute-start | bytes 196616 | tf_op jit(solution)/shard_map/ppermute | solution.py:131
  (13 other events, 126.4 us)
Sparse Core Ops, SparseCore 0:
  21.1 50.5 all-gather.1
